TPU v7x, 256 devices: a whole 4x4x8 slice. The times are simulated.
256 devices in a mesh: pool: 4 (over x), section: 2 (over core), tensor: 32 (over z, y).
Axes of the slice: x: 4, y: 4, z: 8, core: 2. Of those that a mesh axis runs over, the one named last changes fastest.
Arguments:
- hidden_input: bfloat16 [2048, 8192], P('pool', 'tensor'), may hold values from -6 to 6
- attention_output: bfloat16 [2, 2048, 8192], P('section', 'pool', 'tensor'), may hold values from -6 to 6
- projection_weight: bfloat16 [2, 8192, 8192], P('section', 'tensor'), may hold values from -0.125 to 0.125
- lowrank_down_factor: bfloat16 [2, 128, 64, 8192], P('section', 'pool', None, 'tensor'), may hold values from -0.0625 to 0.0625
- lowrank_up_factor: bfloat16 [2, 128, 64, 8192], P('section', 'pool', None, 'tensor'), may hold values from -0.75 to 0.75
- residual_block_mats: bfloat16 [2, 128, 32, 128, 128], P('section', 'pool', 'tensor'), may hold values from -0.5 to 0.5
- diagonal_block_index: int32 [2, 128, 32], P('section', 'pool', 'tensor'), may hold values from 0 to 63, as said below
- row_variant_index: int32 [2048], P('pool'), may hold values from 0 to 127, as said below
Outputs:
- hidden_out: bfloat16 [2, 2048, 8192], P('section', 'pool', 'tensor')
Inputs may be any that keep to these rules, and one draw needn't show every extreme that they name: `row_variant_index`: within each aligned block of 512 rows the ids never fall; at most 256 rows of a block name variants of one owner q (ids q * 32 to (q + 1) * 32 - 1), and some owner receives exactly 256 rows from every block. `diagonal_block_index`: entry j of each list lies in j * 2 to (j + 1) * 2 - 1.
All inputs are finite; a program needn't handle non-finite values.
Results may differ from a plain program's by a relative error of at most 0.017.
Values may be sent and summed in bfloat16 or wider, within the bound.
No kernel may reach another device: no remote copies, remote signals or barrier semaphores. Data moves between devices by JAX's collectives and lax.ppermute only.
A program may use at most 128 MiB of HBM per device.

v0:
```python
import functools

import jax
import jax.numpy as jnp
from jax import lax
from jax.experimental import pallas as pl
from jax.experimental.pallas import tpu as pltpu
from jax.sharding import Mesh
from jax.sharding import PartitionSpec as P


Z, Y = "tensor_0", "tensor_1"
TENSOR = (Z, Y)
NZ, NY, NX = 8, 4, 4
ROWS, WIDTH, TILE = 512, 256, 256
WINDOW = 256
IDROWS = 16
VARS, RANK, BLK = 32, 64, 128
HOPS = (1, 3, 2)
F32, BF16 = jnp.float32, jnp.bfloat16
ANY = pl.BlockSpec(memory_space=pl.ANY)
HBM = pl.BlockSpec(memory_space=pltpu.HBM)
SMEM = pl.BlockSpec(memory_space=pltpu.SMEM)


def shift(value, axis, steps):
    count = lax.axis_size(axis)
    return lax.ppermute(value, axis, [(i, (i + steps) % count) for i in range(count)])


def cost(flops, nbytes):
    return pl.CostEstimate(flops=flops, bytes_accessed=nbytes, transcendentals=0)


def shape(dims, dtype=BF16):
    return pltpu.VMEM(dims, dtype)


def whole(dims, at=None):
    at = at or (0,) * len(dims)
    return pl.BlockSpec(dims, lambda: at)


def tiles_of(group):
    z = lax.axis_index(Z)
    return lax.rem(z + (4 - group), NZ), lax.rem(z + (group + NZ - 3), NZ)


def column(ztile, ytile):
    return pl.multiple_of((ztile * NY + ytile) * TILE, TILE)


def placed(value, spec):
    space = pltpu.HBM if spec is HBM else pltpu.VMEM
    if spec is SMEM:
        return value
    return pltpu.with_memory_space_constraint(value, space)


def call(kernel, args, in_specs, outs, out_specs, scratch, work, limit, after=()):
    n, m = len(args), len(after)
    args = [placed(arg, spec) for arg, spec in zip(args, in_specs)]

    def body(*refs):
        kernel(*refs[:n], *refs[n + m :])

    return pl.pallas_call(
        body,
        out_shape=outs,
        in_specs=list(in_specs) + [ANY] * m,
        out_specs=out_specs,
        scratch_shapes=scratch,
        cost_estimate=cost(*work),
        compiler_params=pltpu.CompilerParams(vmem_limit_bytes=limit << 20),
    )(*args, *after)


def pack_kernel(groups, ahead, extra, *refs):
    w_ref = refs[0]
    n_in = 1 + bool(ahead or extra)
    outs = refs[n_in : n_in + 4 * len(groups)]
    sems = refs[-1]
    y = lax.axis_index(Y)
    copies = []
    for gi, group in enumerate(groups):
        for ki, hop in enumerate((0,) + HOPS):
            out = outs[gi * 4 + ki]
            before = ahead if hop else 0
            if before:
                copies.append((refs[1], out.at[pl.ds(0, ROWS), :]))
            for ti, ztile in enumerate(tiles_of(group)):
                col = column(ztile, lax.rem(y + hop, NY))
                first = ti * TILE + before
                copies.append((w_ref.at[:, pl.ds(col, TILE)], out.at[pl.ds(first, TILE), :]))
    copies = [
        pltpu.make_async_copy(source, target, sems.at[i])
        for i, (source, target) in enumerate(copies)
    ]
    for copy in copies:
        copy.start()
    if extra:
        for ki in range(1, 4):
            outs[ki][2 * TILE : 2 * TILE + extra, :] = refs[1][...]
    for copy in copies:
        copy.wait()


def pack(groups, weight, features=None, low=None, after=()):
    ahead = 0 if features is None else ROWS
    extra = 0 if low is None else WINDOW
    rows = 2 * TILE + ahead + extra
    args, specs = [weight], [HBM]
    if ahead:
        args.append(features)
        specs.append(HBM)
    if extra:
        args.append(low)
        specs.append(whole((WINDOW, 256)))
    dims = [(2 * TILE, TILE)] + [(rows, TILE)] * 3
    dims = dims * len(groups)
    return call(
        functools.partial(pack_kernel, groups, ahead, extra),
        args,
        specs,
        [shape(d) for d in dims],
        [whole(d) for d in dims],
        [pltpu.SemaphoreType.DMA((len(groups) * 12,))],
        (0, 8 * len(groups) * rows * TILE),
        8,
        after,
    )


def project_kernel(group, which, has_in, *refs):
    own_ref, x_ref = refs[:2]
    peers = refs[2:5]
    pos = 5
    blocks = peers
    if group:
        blocks = refs[5:8]
        pos = 8
    base = 0 if group else ROWS
    carried = []
    for _ in which:
        carried.append(refs[pos] if has_in else None)
        pos += 1 if has_in else 0
    outs = refs[pos : pos + len(which)]
    rhs = []
    for ti in which:
        rows = slice(base + ti * TILE, base + (ti + 1) * TILE)
        mine = own_ref[ti * TILE : (ti + 1) * TILE, :]
        rhs.append(jnp.concatenate([mine] + [block[rows, :] for block in blocks], axis=0))
    lhs = jnp.concatenate([x_ref[...]] + [peer[0:ROWS, :] for peer in peers], axis=1)
    for n in range(len(which)):
        total = jnp.dot(lhs, rhs[n], preferred_element_type=F32)
        if has_in:
            total = total + carried[n][...].astype(F32)
        outs[n][...] = total.astype(outs[n].dtype)


def project(group, which, own, features, first_got, got, carried, after=(), out_dtype=BF16):
    half = (ROWS, WIDTH)
    in_specs = [whole((2 * TILE, TILE)), whole(half)] + [whole((2 * ROWS, TILE))] * 3
    args = [own, features, *first_got]
    if group:
        in_specs += [whole(got[0].shape)] * 3
        args += list(got)
    in_specs += [whole(half)] * len(carried)
    args += list(carried)
    n = len(which)
    return call(
        functools.partial(project_kernel, group, which, bool(carried)),
        args,
        in_specs,
        [shape((ROWS, TILE), out_dtype)] * n,
        [whole((ROWS, TILE))] * n,
        [],
        (2 * ROWS * 1024 * TILE * n, 2 << 20),
        8,
        after,
    )


def window_start(ids, owner):
    before = jnp.sum((ids < owner * VARS).astype(jnp.int32))
    return jnp.minimum(before, ROWS - WINDOW)


def dispatch_kernel(ids_ref, x_ref, *outs):
    me = lax.axis_index("pool")
    ids = ids_ref[...]
    features = x_ref[...]
    for k in range(NX):
        owner = lax.rem(me + k, NX)
        start = window_start(ids, owner)
        at = lax.broadcasted_iota(jnp.int32, (WINDOW, ROWS), 0) + start
        hot = (at == lax.broadcasted_iota(jnp.int32, (WINDOW, ROWS), 1)).astype(F32).astype(BF16)
        outs[k][0:WINDOW, :] = jnp.dot(hot, features, preferred_element_type=F32).astype(BF16)
        local = jnp.broadcast_to((ids - owner * VARS).astype(F32), (IDROWS, ROWS)).astype(BF16)
        outs[k][WINDOW : WINDOW + IDROWS, :] = lax.dot_general(
            local, hot, (((1,), (1,)), ((), ())), preferred_element_type=F32
        ).astype(BF16)


def dispatch(ids, features, after=()):
    return call(
        dispatch_kernel,
        (ids, features),
        [whole((1, ROWS)), whole((ROWS, WIDTH))],
        [shape((WINDOW + IDROWS, WIDTH))] * NX,
        [whole((WINDOW + IDROWS, WIDTH))] * NX,
        [],
        (2 * 1024 * 512 * 256, 1 << 20),
        6,
        after,
    )


def variant_columns(item_ref, lanes):
    row = jnp.broadcast_to(item_ref[WINDOW : WINDOW + 1, :].astype(F32), (WINDOW, WINDOW))
    diagonal = lax.broadcasted_iota(jnp.int32, (WINDOW, WINDOW), 0) == lax.broadcasted_iota(
        jnp.int32, (WINDOW, WINDOW), 1
    )
    spread = jnp.where(diagonal, row, 0.0).astype(BF16)
    return jnp.dot(spread, jnp.ones((WINDOW, lanes), BF16), preferred_element_type=F32)


def down_kernel(i0, i1, i2, i3, down_ref, out_ref, var_ref, acc_ref):
    items = (i0, i1, i2, i3)
    for k in range(NX):
        var_ref[k] = variant_columns(items[k], 256)
        acc_ref[k] = jnp.zeros((WINDOW, 256), F32)
    lane = lax.broadcasted_iota(jnp.int32, (1, 256), 1)
    part = lax.div(lane, jnp.int32(RANK)).astype(F32)

    def step(j, carry):
        factor = down_ref[pl.ds(pl.multiple_of(j * 256, 256), 256), :]
        wanted = part + (j * 4).astype(F32)
        for k in range(NX):
            value = lax.dot_general(
                items[k][0:WINDOW, :],
                factor,
                (((1,), (1,)), ((), ())),
                preferred_element_type=F32,
            )
            acc_ref[k] += jnp.where(var_ref[k] == wanted, value, 0.0)
        return carry

    lax.fori_loop(0, VARS * RANK // 256, step, 0)
    folded = []
    for k in range(NX):
        two = acc_ref[k, :, 0:128] + acc_ref[k, :, 128:256]
        folded.append(two + pltpu.roll(two, RANK, 1))
    low = lax.broadcasted_iota(jnp.int32, (WINDOW, 128), 1) < RANK
    for h in range(2):
        packed = jnp.where(low, folded[h], folded[h + 2]).astype(BF16)
        out_ref[:, h * 128 : (h + 1) * 128] = packed


def down(items, factor, after=()):
    return call(
        down_kernel,
        (*items, factor),
        [whole((WINDOW + IDROWS, WIDTH))] * NX + [whole((VARS * RANK, WIDTH))],
        shape((WINDOW, 256)),
        whole((WINDOW, 256)),
        [pltpu.VMEM((NX, WINDOW, 256), F32), pltpu.VMEM((NX, WINDOW, 256), F32)],
        (2 * 1024 * 256 * 2048, 2 << 20),
        8,
        after,
    )


def block_kernel(i0, i1, i2, i3, mats_ref, place_ref, out_ref, var_ref, rhs_ref):
    items = (i0, i1, i2, i3)
    shard = lax.axis_index(Z) * NY + lax.axis_index(Y)
    for k in range(NX):
        var_ref[k] = variant_columns(items[k], 128)
        out_ref[k] = jnp.zeros((WINDOW, 256), F32)

    def lanes_of(v):
        return pl.ds(pl.multiple_of((place_ref[v] - shard * 2) * BLK, BLK), BLK)

    def fill(v, carry):
        rhs_ref[v] = jnp.zeros((BLK, 256), BF16)
        rhs_ref[v, :, lanes_of(v)] = mats_ref[v]
        return carry

    lax.fori_loop(0, VARS, fill, 0)

    def step(c, carry):
        rhs = rhs_ref[pl.ds(c * 4, 4)].reshape(4 * BLK, 256)
        for k in range(NX):
            pieces = []
            for i in range(4):
                v = c * 4 + i
                piece = items[k][0:WINDOW, lanes_of(v)].astype(F32)
                pieces.append(jnp.where(var_ref[k] == v.astype(F32), piece, 0.0).astype(BF16))
            lhs = jnp.concatenate(pieces, axis=1)
            out_ref[k] += jnp.dot(lhs, rhs, preferred_element_type=F32)
        return carry

    lax.fori_loop(0, VARS // 4, step, 0)


def block_terms(items, mats, places, after=()):
    return call(
        block_kernel,
        (*items, mats, places),
        [whole((WINDOW + IDROWS, WIDTH))] * NX + [whole((VARS, BLK, BLK)), SMEM],
        shape((NX, WINDOW, 256), F32),
        whole((NX, WINDOW, 256)),
        [pltpu.VMEM((NX, WINDOW, 128), F32), pltpu.VMEM((VARS, BLK, 256), BF16)],
        (2 * 1024 * 4096 * 256, 3 << 20),
        10,
        after,
    )


def add_kernel(a_ref, b_ref, out_ref):
    out_ref[...] = (a_ref[...].astype(F32) + b_ref[...].astype(F32)).astype(BF16)


def exchanged_sum(value, axis, bit, after=()):
    count = lax.axis_size(axis)
    other = lax.ppermute(value, axis, [(i, i ^ bit) for i in range(count)])
    return call(
        add_kernel,
        (value, other),
        [whole((WINDOW, 256))] * 2,
        shape((WINDOW, 256)),
        whole((WINDOW, 256)),
        [],
        (1 << 16, 3 << 17),
        2,
        after,
    )


def up_kernel(*refs):
    items, lows = refs[:4], refs[4:8]
    up_ref, block_ref = refs[8:10]
    outs = refs[10:14]
    acc_ref, var_ref, two_ref = refs[14:]
    low = lows[0][...].astype(F32)
    for other in lows[1:]:
        low = low + other[2 * TILE : 2 * TILE + WINDOW, :].astype(F32)
    low = low.astype(BF16).astype(F32)
    first = lax.broadcasted_iota(jnp.int32, (WINDOW, 128), 1) < RANK
    for h in range(2):
        packed = low[:, h * 128 : (h + 1) * 128]
        turned = pltpu.roll(packed, RANK, 1)
        two_ref[h] = jnp.where(first, packed, turned)
        two_ref[h + 2] = jnp.where(first, turned, packed)
    for k in range(NX):
        var_ref[k] = variant_columns(items[k], 128)
        acc_ref[k] = block_ref[k]
    half = lax.div(lax.broadcasted_iota(jnp.int32, (1, 128), 1), jnp.int32(RANK)).astype(F32)

    def step(c, carry):
        rhs = up_ref[pl.ds(pl.multiple_of(c * 512, 512), 512), :]
        for k in range(NX):
            pieces = []
            for i in range(4):
                wanted = half + (c * 8 + i * 2).astype(F32)
                pieces.append(jnp.where(var_ref[k] == wanted, two_ref[k], 0.0).astype(BF16))
            lhs = jnp.concatenate(pieces, axis=1)
            acc_ref[k] += jnp.dot(lhs, rhs, preferred_element_type=F32)
        return carry

    lax.fori_loop(0, VARS * RANK // 512, step, 0)
    for k in range(NX):
        outs[k][...] = acc_ref[k].astype(BF16)


def up(items, low, lows, factor, blocks, after=()):
    return call(
        up_kernel,
        (*items, low, *lows, factor, blocks),
        [whole((WINDOW + IDROWS, WIDTH))] * NX
        + [whole((WINDOW, 256))]
        + [whole(lows[0].shape)] * 3
        + [whole((VARS * RANK, WIDTH)), whole((NX, WINDOW, 256))],
        [shape((WINDOW, WIDTH))] * NX,
        [whole((WINDOW, WIDTH))] * NX,
        [pltpu.VMEM((NX, WINDOW, 256), F32), pltpu.VMEM((NX, WINDOW, 128), F32), pltpu.VMEM((NX, WINDOW, 128), F32)],
        (2 * 1024 * 256 * 2048, 3 << 20),
        10,
        after,
    )


def combine_kernel(ids_ref, h_ref, own_ref, plus_ref, r0, r1, r2, r3, first_ref, branch_ref):
    me = lax.axis_index("pool")
    ids = ids_ref[...]
    branch = own_ref[...] + plus_ref[...].astype(F32)
    delta = None
    for k, back in enumerate((r0, r1, r2, r3)):
        start = window_start(ids, lax.rem(me + k, NX))
        at = lax.broadcasted_iota(jnp.int32, (ROWS, WINDOW), 1) + start
        hot = (at == lax.broadcasted_iota(jnp.int32, (ROWS, WINDOW), 0)).astype(F32).astype(BF16)
        part = jnp.dot(hot, back[...], preferred_element_type=F32)
        delta = part if delta is None else delta + part
    branch = branch + delta
    branch_ref[...] = branch
    first_ref[...] = (h_ref[...].astype(F32) + branch).astype(BF16)


def combine(ids, hidden, own, plus, returned, after=()):
    half = (ROWS, WIDTH)
    return call(
        combine_kernel,
        (ids, hidden, own, plus, *returned),
        [whole((1, ROWS))] + [whole(half)] * 3 + [whole((WINDOW, WIDTH))] * NX,
        [shape(half), shape(half, F32)],
        [whole(half)] * 2,
        [],
        (2 * 512 * 1024 * 256, 2 << 20),
        8,
        after,
    )


def steps(
    hidden_input,
    attention_output,
    projection_weight,
    lowrank_down_factor,
    lowrank_up_factor,
    residual_block_mats,
    diagonal_block_index,
    row_variant_index,
):
    features = attention_output[0]
    weight = projection_weight[0]
    down_factor = lowrank_down_factor[0].reshape(VARS * RANK, WIDTH)
    up_factor = lowrank_up_factor[0].reshape(VARS * RANK, WIDTH)
    mats = residual_block_mats[0][:, 0]
    places = diagonal_block_index[0][:, 0]
    ids = row_variant_index.reshape(1, ROWS)

    own0, *first = pack((0,), weight, features)
    first_got = [shift(value, Y, hop) for value, hop in zip(first, HOPS)]
    sent = dispatch(ids, features, (first[0],))
    items = [sent[0]] + [shift(sent[k], "pool", k) for k in (1, 2, 3)]
    own1, *second = pack((1,), weight, None, None, (sent[0],))
    got1 = [shift(value, Y, hop) for value, hop in zip(second, HOPS)]
    low = down(items, down_factor)
    low1 = exchanged_sum(low, Z, 1)
    blocks = block_terms(items, mats, places, (low,))
    low2 = exchanged_sum(low1, Z, 2, (blocks,))
    low3 = exchanged_sum(low2, Z, 4)

    plus, minus = project(0, (0, 1), own0, features, first_got, None, (), (low2,))
    carried = (shift(plus, Z, 1), shift(minus, Z, -1))
    own2, *third = pack((2,), weight, None, low3)
    got2 = [shift(value, Y, hop) for value, hop in zip(third, HOPS)]
    own3, *fourth = pack((3,), weight, None, None, (third[0],))
    got3 = [shift(value, Y, hop) for value, hop in zip(fourth, HOPS)]
    plus, minus = project(1, (0, 1), own1, features, first_got, got1, carried)
    carried = (shift(plus, Z, 1), shift(minus, Z, -1))
    plus, minus = project(2, (0, 1), own2, features, first_got, got2, carried)
    carried = (shift(plus, Z, 1), shift(minus, Z, -1))
    served = up(items, low3, got2, up_factor, blocks, (plus,))
    returned = [served[0]] + [shift(served[k], "pool", -k) for k in (1, 2, 3)]
    (plus,) = project(3, (0,), own3, features, first_got, got3, carried[:1], (served[1],))
    arrived = shift(plus, Z, 1)
    (own,) = project(3, (1,), own3, features, first_got, got3, carried[1:], (plus,), F32)
    plus = arrived

    first_out, branch = combine(ids, hidden_input, own, plus, returned)
    carried = lax.ppermute(first_out, "section", [(0, 1)])
    begin = jnp.where(lax.axis_index("section") == 0, hidden_input, carried)
    return (begin.astype(F32) + branch).astype(BF16)[None]


def solution(mesh):
    finer = Mesh(
        mesh.devices.reshape(mesh.shape["pool"], mesh.shape["section"], NZ, NY),
        ("pool", "section", Z, Y),
    )
    placed = (
        P("pool", TENSOR),
        P("section", "pool", TENSOR),
        P("section", TENSOR, None),
        P("section", "pool", None, TENSOR),
        P("section", "pool", None, TENSOR),
        P("section", "pool", TENSOR, None, None),
        P("section", "pool", TENSOR),
        P("pool"),
    )
    return jax.shard_map(
        steps,
        mesh=finer,
        in_specs=placed,
        out_specs=P("section", "pool", TENSOR),
        check_vma=False,
    )
```

profile of v0, /device:TPU:1, one launch (start us, length us, event | category | flops | bytes accessed | tf_op | source)
XLA Modules:
  0.0 100.3 jit_solution(5719922473444462948)
XLA Ops:
  0.0 1.7 %shard_map.82 = (bf16[512,256]{1,0:T(8,128)(2,1)S(1)}, bf16[1024,256]{1,0:T(8,128)(2,1)S(1)}, bf16[1024,256]{1,0:T(8,128)(2,1)S(1)}, bf16[1024,256]{1,0:T(8,128)(2,1)S(1)}) custom-call(bf16[256,8192]{1,0:T(8,128)(2,1)} %bitcast.22, bf16[512,256]{1,0:T(8,128)(2,1)} %bitcast.9), custom_call_target="tpu_custom_call" | custom-call | bytes 2097152 | tf_op jit(solution)/shard_map/pallas_call | solution.py:67
  2.7 2.1 %collective-permute-start = (bf16[272,256]{1,0:T(8,128)(2,1)S(1)}, bf16[272,256]{1,0:T(8,128)(2,1)S(1)}, u32[]{:S(2)}, u32[]{:S(2)}) collective-permute-start(bf16[272,256]{1,0:T(8,128)(2,1)S(1)} %get-tuple-element.39), channel_id=1, source_target_pairs={{0,64},{64,128},{128,192},{192,0},{1,65},{65,129},{129,193},{193,1... | collective-permute-start | bytes 417800 | tf_op jit(solution)/shard_map/ppermute | solution.py:28
  4.8 2.4 %collective-permute-start.1 = (bf16[272,256]{1,0:T(8,128)(2,1)S(1)}, bf16[272,256]{1,0:T(8,128)(2,1)S(1)}, u32[]{:S(2)}, u32[]{:S(2)}) collective-permute-start(bf16[272,256]{1,0:T(8,128)(2,1)S(1)} %get-tuple-element.40), channel_id=1, source_target_pairs={{0,128},{64,192},{128,0},{192,64},{1,129},{65,193},{129,1},{193,65... | collective-permute-start | bytes 417800 | tf_op jit(solution)/shard_map/ppermute | solution.py:28
  8.4 1.3 %collective-permute-start.6 = (bf16[1024,256]{1,0:T(8,128)(2,1)S(1)}, bf16[1024,256]{1,0:T(8,128)(2,1)S(1)}, u32[]{:S(2)}, u32[]{:S(2)}) collective-permute-start(bf16[1024,256]{1,0:T(8,128)(2,1)S(1)} %get-tuple-element.37.refs_2_), channel_id=1, source_target_pairs={{0,1},{1,2},{2,3},{3,0},{4,5},{5,6},{6,7},{7,4},{8,9},{9,10},{10,1... | collective-permute-start | bytes 1572872 | tf_op jit(solution)/shard_map/ppermute | solution.py:28
  9.7 1.4 %collective-permute-start.7 = (bf16[1024,256]{1,0:T(8,128)(2,1)S(1)}, bf16[1024,256]{1,0:T(8,128)(2,1)S(1)}, u32[]{:S(2)}, u32[]{:S(2)}) collective-permute-start(bf16[1024,256]{1,0:T(8,128)(2,1)S(1)} %get-tuple-element.44), channel_id=1, source_target_pairs={{0,3},{1,0},{2,1},{3,2},{4,7},{5,4},{6,5},{7,6},{8,11},{9,8},{10,9... | collective-permute-start | bytes 1572872 | tf_op jit(solution)/shard_map/ppermute | solution.py:28
  11.1 1.6 %collective-permute-start.8 = (bf16[1024,256]{1,0:T(8,128)(2,1)S(1)}, bf16[1024,256]{1,0:T(8,128)(2,1)S(1)}, u32[]{:S(2)}, u32[]{:S(2)}) collective-permute-start(bf16[1024,256]{1,0:T(8,128)(2,1)S(1)} %get-tuple-element.45), channel_id=1, source_target_pairs={{0,2},{1,3},{2,0},{3,1},{4,6},{5,7},{6,4},{7,5},{8,10},{9,11},{10,... | collective-permute-start | bytes 1572872 | tf_op jit(solution)/shard_map/ppermute | solution.py:28
  13.3 3.3 %shard_map.84.refs_0_.refs_6_ = bf16[256,256]{1,0:T(8,128)(2,1)S(1)} custom-call(bf16[272,256]{1,0:T(8,128)(2,1)S(1)} %get-tuple-element.38.refs_0_.refs_1_, bf16[272,256]{1,0:T(8,128)(2,1)S(1)} %collective-permute-done.refs_1_, bf16[272,256]{1,0:T(8,128)(2,1)S(1)} %collective-permute-done.1.refs_2_, bf16[272,256]{1,0:T(8,128)(2,1)S(1)} %collective-permute-done.2.refs_3_, ...), custom_call_target="tpu_custom_call" | custom-call | flops 1073741824 | bytes 2097152 | tf_op jit(solution)/shard_map/pallas_call | solution.py:67
  16.6 1.7 %collective-permute-start.3 = (bf16[256,256]{1,0:T(8,128)(2,1)S(1)}, bf16[256,256]{1,0:T(8,128)(2,1)S(1)}, u32[]{:S(2)}, u32[]{:S(2)}) collective-permute-start(bf16[256,256]{1,0:T(8,128)(2,1)S(1)} %shard_map.84.refs_0_.refs_6_), channel_id=1, source_target_pairs={{0,4},{4,0},{8,12},{12,8},{16,20},{20,16},{24,28},{28,24},{1,5},{5... | collective-permute-start | bytes 393224 | tf_op jit(solution)/shard_map/ppermute | solution.py:326
  18.4 2.7 %collective-permute-done.3.refs_1_ = bf16[256,256]{1,0:T(8,128)(2,1)S(1)} collective-permute-done((bf16[256,256]{1,0:T(8,128)(2,1)S(1)}, bf16[256,256]{1,0:T(8,128)(2,1)S(1)}, u32[]{:S(2)}, u32[]{:S(2)}) %collective-permute-start.3) | collective-permute-done | bytes 131104 | tf_op jit(solution)/shard_map/ppermute | solution.py:326
  21.0 3.1 %collective-permute-start.4 = (bf16[256,256]{1,0:T(8,128)(2,1)S(1)}, bf16[256,256]{1,0:T(8,128)(2,1)S(1)}, u32[]{:S(2)}, u32[]{:S(2)}) collective-permute-start(bf16[256,256]{1,0:T(8,128)(2,1)S(1)} %shard_map.85.refs_0_), channel_id=1, source_target_pairs={{0,8},{4,12},{8,0},{12,4},{16,24},{20,28},{24,16},{28,20},{1,9},{5... | collective-permute-start | bytes 393224 | tf_op jit(solution)/shard_map/ppermute | solution.py:326
  24.1 5.2 %shard_map.86.refs_2_.refs_9_ = f32[4,256,256]{2,1,0:T(8,128)S(1)} custom-call(bf16[272,256]{1,0:T(8,128)(2,1)S(1)} %get-tuple-element.38.refs_0_.refs_1_, bf16[272,256]{1,0:T(8,128)(2,1)S(1)} %collective-permute-done.refs_1_, bf16[272,256]{1,0:T(8,128)(2,1)S(1)} %collective-permute-done.1.refs_2_, bf16[272,256]{1,0:T(8,128)(2,1)S(1)} %collective-permute-done.2.refs_3_, ...), custom_call_target="tpu_custom_call" | custom-call | flops 2147483648 | bytes 3145728 | tf_op jit(solution)/shard_map/pallas_call | solution.py:67
  29.4 5.0 %collective-permute-start.5 = (bf16[256,256]{1,0:T(8,128)(2,1)S(1)}, bf16[256,256]{1,0:T(8,128)(2,1)S(1)}, u32[]{:S(2)}, u32[]{:S(2)}) collective-permute-start(bf16[256,256]{1,0:T(8,128)(2,1)S(1)} %shard_map.87.refs_0_.refs_5_), channel_id=1, source_target_pairs={{0,16},{4,20},{8,24},{12,28},{16,0},{20,4},{24,8},{28,12},{1,17},{... | collective-permute-start | bytes 393224 | tf_op jit(solution)/shard_map/ppermute | solution.py:326
  34.4 1.4 %shard_map.91 = (bf16[512,256]{1,0:T(8,128)(2,1)S(1)}, bf16[512,256]{1,0:T(8,128)(2,1)S(1)}, bf16[512,256]{1,0:T(8,128)(2,1)S(1)}, bf16[512,256]{1,0:T(8,128)(2,1)S(1)}) custom-call(bf16[256,8192]{1,0:T(8,128)(2,1)} %bitcast.23, bf16[272,256]{1,0:T(8,128)(2,1)S(1)} %get-tuple-element.38.refs_0_.refs_1_), custom_call_target="tpu_custom_call" | custom-call | bytes 1048576 | tf_op jit(solution)/shard_map/pallas_call | solution.py:67
  35.8 1.3 %collective-permute-start.15 = (bf16[512,256]{1,0:T(8,128)(2,1)S(1)}, bf16[512,256]{1,0:T(8,128)(2,1)S(1)}, u32[]{:S(2)}, u32[]{:S(2)}) collective-permute-start(bf16[512,256]{1,0:T(8,128)(2,1)S(1)} %get-tuple-element.53), channel_id=1, source_target_pairs={{0,1},{1,2},{2,3},{3,0},{4,5},{5,6},{6,7},{7,4},{8,9},{9,10},{10,1... | collective-permute-start | bytes 786440 | tf_op jit(solution)/shard_map/ppermute | solution.py:28
  37.2 1.6 %collective-permute-start.16 = (bf16[512,256]{1,0:T(8,128)(2,1)S(1)}, bf16[512,256]{1,0:T(8,128)(2,1)S(1)}, u32[]{:S(2)}, u32[]{:S(2)}) collective-permute-start(bf16[512,256]{1,0:T(8,128)(2,1)S(1)} %get-tuple-element.54), channel_id=1, source_target_pairs={{0,3},{1,0},{2,1},{3,2},{4,7},{5,4},{6,5},{7,6},{8,11},{9,8},{10,9... | collective-permute-start | bytes 786440 | tf_op jit(solution)/shard_map/ppermute | solution.py:28
  38.7 1.5 %collective-permute-start.17 = (bf16[512,256]{1,0:T(8,128)(2,1)S(1)}, bf16[512,256]{1,0:T(8,128)(2,1)S(1)}, u32[]{:S(2)}, u32[]{:S(2)}) collective-permute-start(bf16[512,256]{1,0:T(8,128)(2,1)S(1)} %get-tuple-element.55), channel_id=1, source_target_pairs={{0,2},{1,3},{2,0},{3,1},{4,6},{5,7},{6,4},{7,5},{8,10},{9,11},{10,... | collective-permute-start | bytes 786440 | tf_op jit(solution)/shard_map/ppermute | solution.py:28
  41.8 2.0 %collective-permute-start.19 = (bf16[512,256]{1,0:T(8,128)(2,1)S(1)}, bf16[512,256]{1,0:T(8,128)(2,1)S(1)}, u32[]{:S(2)}, u32[]{:S(2)}) collective-permute-start(bf16[512,256]{1,0:T(8,128)(2,1)S(1)} %get-tuple-element.58), channel_id=1, source_target_pairs={{0,28},{4,0},{8,4},{12,8},{16,12},{20,16},{24,20},{28,24},{1,29},{... | collective-permute-start | bytes 786440 | tf_op jit(solution)/shard_map/ppermute | solution.py:28
  43.8 1.4 %shard_map.89 = (bf16[512,256]{1,0:T(8,128)(2,1)S(1)}, bf16[768,256]{1,0:T(8,128)(2,1)S(1)}, bf16[768,256]{1,0:T(8,128)(2,1)S(1)}, bf16[768,256]{1,0:T(8,128)(2,1)S(1)}) custom-call(bf16[256,8192]{1,0:T(8,128)(2,1)} %bitcast.24, bf16[256,256]{1,0:T(8,128)(2,1)S(1)} %shard_map.88.refs_1_.refs_4_), custom_call_target="tpu_custom_call" | custom-call | bytes 1572864 | tf_op jit(solution)/shard_map/pallas_call | solution.py:67
  45.7 2.3 %collective-permute-start.13 = (bf16[768,256]{1,0:T(8,128)(2,1)S(1)}, bf16[768,256]{1,0:T(8,128)(2,1)S(1)}, u32[]{:S(2)}, u32[]{:S(2)}) collective-permute-start(bf16[768,256]{1,0:T(8,128)(2,1)S(1)} %get-tuple-element.50), channel_id=1, source_target_pairs={{0,3},{1,0},{2,1},{3,2},{4,7},{5,4},{6,5},{7,6},{8,11},{9,8},{10,9... | collective-permute-start | bytes 1179656 | tf_op jit(solution)/shard_map/ppermute | solution.py:28
  49.7 1.4 %collective-permute-start.20 = (bf16[512,256]{1,0:T(8,128)(2,1)S(1)}, bf16[512,256]{1,0:T(8,128)(2,1)S(1)}, u32[]{:S(2)}, u32[]{:S(2)}) collective-permute-start(bf16[512,256]{1,0:T(8,128)(2,1)S(1)} %get-tuple-element.59), channel_id=1, source_target_pairs={{0,4},{4,8},{8,12},{12,16},{16,20},{20,24},{24,28},{28,0},{1,5},{5... | collective-permute-start | bytes 786440 | tf_op jit(solution)/shard_map/ppermute | solution.py:28
  51.0 1.4 %collective-permute-start.21 = (bf16[512,256]{1,0:T(8,128)(2,1)S(1)}, bf16[512,256]{1,0:T(8,128)(2,1)S(1)}, u32[]{:S(2)}, u32[]{:S(2)}) collective-permute-start(bf16[512,256]{1,0:T(8,128)(2,1)S(1)} %get-tuple-element.60), channel_id=1, source_target_pairs={{0,28},{4,0},{8,4},{12,8},{16,12},{20,16},{24,20},{28,24},{1,29},{... | collective-permute-start | bytes 786440 | tf_op jit(solution)/shard_map/ppermute | solution.py:28
  52.4 1.4 %shard_map.90 = (bf16[512,256]{1,0:T(8,128)(2,1)S(1)}, bf16[512,256]{1,0:T(8,128)(2,1)S(1)}, bf16[512,256]{1,0:T(8,128)(2,1)S(1)}, bf16[512,256]{1,0:T(8,128)(2,1)S(1)}) custom-call(bf16[256,8192]{1,0:T(8,128)(2,1)} %bitcast.25, bf16[768,256]{1,0:T(8,128)(2,1)S(1)} %get-tuple-element.42.refs_1_), custom_call_target="tpu_custom_call" | custom-call | bytes 1048576 | tf_op jit(solution)/shard_map/pallas_call | solution.py:67
  53.8 4.5 %collective-permute-done.12.refs_5_ = bf16[768,256]{1,0:T(8,128)(2,1)S(1)} collective-permute-done((bf16[768,256]{1,0:T(8,128)(2,1)S(1)}, bf16[768,256]{1,0:T(8,128)(2,1)S(1)}, u32[]{:S(2)}, u32[]{:S(2)}) %collective-permute-start.12) | collective-permute-done | bytes 393248 | tf_op jit(solution)/shard_map/ppermute | solution.py:28
  59.4 6.3 %collective-permute-done.14.refs_7_ = bf16[768,256]{1,0:T(8,128)(2,1)S(1)} collective-permute-done((bf16[768,256]{1,0:T(8,128)(2,1)S(1)}, bf16[768,256]{1,0:T(8,128)(2,1)S(1)}, u32[]{:S(2)}, u32[]{:S(2)}) %collective-permute-start.14) | collective-permute-done | bytes 393248 | tf_op jit(solution)/shard_map/ppermute | solution.py:28
  67.9 2.3 %collective-permute-start.22 = (bf16[512,256]{1,0:T(8,128)(2,1)S(1)}, bf16[512,256]{1,0:T(8,128)(2,1)S(1)}, u32[]{:S(2)}, u32[]{:S(2)}) collective-permute-start(bf16[512,256]{1,0:T(8,128)(2,1)S(1)} %get-tuple-element.61), channel_id=1, source_target_pairs={{0,28},{4,0},{8,4},{12,8},{16,12},{20,16},{24,20},{28,24},{1,29},{... | collective-permute-start | bytes 786440 | tf_op jit(solution)/shard_map/ppermute | solution.py:28
  70.2 2.3 %shard_map.95 = (bf16[256,256]{1,0:T(8,128)(2,1)S(1)}, bf16[256,256]{1,0:T(8,128)(2,1)S(1)}, bf16[256,256]{1,0:T(8,128)(2,1)S(1)}, bf16[256,256]{1,0:T(8,128)(2,1)S(1)}) custom-call(bf16[272,256]{1,0:T(8,128)(2,1)S(1)} %get-tuple-element.38.refs_0_.refs_1_, bf16[272,256]{1,0:T(8,128)(2,1)S(1)} %collective-permute-done.refs_1_, ...), custom_call_target="tpu_custom_call" | custom-call | flops 1073741824 | bytes 3145728 | tf_op jit(solution)/shard_map/pallas_call | solution.py:67
  72.5 3.6 %collective-permute-done.9.refs_5_ = bf16[512,256]{1,0:T(8,128)(2,1)S(1)} collective-permute-done((bf16[512,256]{1,0:T(8,128)(2,1)S(1)}, bf16[512,256]{1,0:T(8,128)(2,1)S(1)}, u32[]{:S(2)}, u32[]{:S(2)}) %collective-permute-start.9) | collective-permute-done | bytes 262176 | tf_op jit(solution)/shard_map/ppermute | solution.py:28
  77.4 2.6 %collective-permute-start.25 = (bf16[256,256]{1,0:T(8,128)(2,1)S(1)}, bf16[256,256]{1,0:T(8,128)(2,1)S(1)}, u32[]{:S(2)}, u32[]{:S(2)}) collective-permute-start(bf16[256,256]{1,0:T(8,128)(2,1)S(1)} %get-tuple-element.63.refs_9_), channel_id=1, source_target_pairs={{0,192},{64,0},{128,64},{192,128},{1,193},{65,1},{129,65},{193,129... | collective-permute-start | bytes 393224 | tf_op jit(solution)/shard_map/ppermute | solution.py:28
  80.0 4.1 %collective-permute-start.26 = (bf16[256,256]{1,0:T(8,128)(2,1)S(1)}, bf16[256,256]{1,0:T(8,128)(2,1)S(1)}, u32[]{:S(2)}, u32[]{:S(2)}) collective-permute-start(bf16[256,256]{1,0:T(8,128)(2,1)S(1)} %get-tuple-element.65), channel_id=1, source_target_pairs={{0,128},{64,192},{128,0},{192,64},{1,129},{65,193},{129,1},{193,65... | collective-permute-start | bytes 393224 | tf_op jit(solution)/shard_map/ppermute | solution.py:28
  84.7 1.8 %collective-permute-done.26.refs_6_ = bf16[256,256]{1,0:T(8,128)(2,1)S(1)} collective-permute-done((bf16[256,256]{1,0:T(8,128)(2,1)S(1)}, bf16[256,256]{1,0:T(8,128)(2,1)S(1)}, u32[]{:S(2)}, u32[]{:S(2)}) %collective-permute-start.26) | collective-permute-done | bytes 131104 | tf_op jit(solution)/shard_map/ppermute | solution.py:28
  86.5 3.0 %collective-permute-done.27.refs_7_ = bf16[256,256]{1,0:T(8,128)(2,1)S(1)} collective-permute-done((bf16[256,256]{1,0:T(8,128)(2,1)S(1)}, bf16[256,256]{1,0:T(8,128)(2,1)S(1)}, u32[]{:S(2)}, u32[]{:S(2)}) %collective-permute-start.27) | collective-permute-done | bytes 131104 | tf_op jit(solution)/shard_map/ppermute | solution.py:28
  91.3 8.2 %collective-permute-done.28 = bf16[512,256]{1,0:T(8,128)(2,1)S(1)} collective-permute-done((bf16[512,256]{1,0:T(8,128)(2,1)S(1)}, bf16[512,256]{1,0:T(8,128)(2,1)S(1)}, u32[]{:S(2)}, u32[]{:S(2)}) %collective-permute-start.28) | collective-permute-done | bytes 262176 | tf_op jit(solution)/shard_map/ppermute | solution.py:472
  (58 shorter events, 14.0 us)
Async XLA Ops:
  0.0 24.1 %copy-start.5 = (bf16[1,32,1,128,128]{4,3,2,1,0:T(8,128)(2,1)S(1)}, bf16[1,32,1,128,128]{4,3,2,1,0:T(8,128)(2,1)}, u32[]{:S(2)}) copy-start(bf16[1,32,1,128,128]{4,3,2,1,0:T(8,128)(2,1)} %param.13) | copy-start | bytes 3145732
  0.0 24.1 %copy-start.6 = (s32[1,32,1]{1,2,0:T(1,128)S(1)}, s32[1,32,1]{1,2,0:T(1,128)}, u32[]{:S(2)}) copy-start(s32[1,32,1]{1,2,0:T(1,128)} %param.14) | copy-start | bytes 388
  2.7 8.5 %collective-permute-start = (bf16[272,256]{1,0:T(8,128)(2,1)S(1)}, bf16[272,256]{1,0:T(8,128)(2,1)S(1)}, u32[]{:S(2)}, u32[]{:S(2)}) collective-permute-start(bf16[272,256]{1,0:T(8,128)(2,1)S(1)} %get-tuple-element.39), channel_id=1, source_target_pairs={{0,64},{64,128},{128,192},{192,0},{1,65},{65,129},{129,193},{193,1... | collective-permute-start | bytes 417800 | tf_op jit(solution)/shard_map/ppermute | solution.py:28
  4.8 8.5 %collective-permute-start.1 = (bf16[272,256]{1,0:T(8,128)(2,1)S(1)}, bf16[272,256]{1,0:T(8,128)(2,1)S(1)}, u32[]{:S(2)}, u32[]{:S(2)}) collective-permute-start(bf16[272,256]{1,0:T(8,128)(2,1)S(1)} %get-tuple-element.40), channel_id=1, source_target_pairs={{0,128},{64,192},{128,0},{192,64},{1,129},{65,193},{129,1},{193,65... | collective-permute-start | bytes 417800 | tf_op jit(solution)/shard_map/ppermute | solution.py:28
  7.2 6.1 %collective-permute-start.2 = (bf16[272,256]{1,0:T(8,128)(2,1)S(1)}, bf16[272,256]{1,0:T(8,128)(2,1)S(1)}, u32[]{:S(2)}, u32[]{:S(2)}) collective-permute-start(bf16[272,256]{1,0:T(8,128)(2,1)S(1)} %get-tuple-element.41), channel_id=1, source_target_pairs={{0,192},{64,0},{128,64},{192,128},{1,193},{65,1},{129,65},{193,129... | collective-permute-start | bytes 417800 | tf_op jit(solution)/shard_map/ppermute | solution.py:28
  8.4 28.8 %collective-permute-start.6 = (bf16[1024,256]{1,0:T(8,128)(2,1)S(1)}, bf16[1024,256]{1,0:T(8,128)(2,1)S(1)}, u32[]{:S(2)}, u32[]{:S(2)}) collective-permute-start(bf16[1024,256]{1,0:T(8,128)(2,1)S(1)} %get-tuple-element.37.refs_2_), channel_id=1, source_target_pairs={{0,1},{1,2},{2,3},{3,0},{4,5},{5,6},{6,7},{7,4},{8,9},{9,10},{10,1... | collective-permute-start | bytes 1572872 | tf_op jit(solution)/shard_map/ppermute | solution.py:28
  9.7 29.0 %collective-permute-start.7 = (bf16[1024,256]{1,0:T(8,128)(2,1)S(1)}, bf16[1024,256]{1,0:T(8,128)(2,1)S(1)}, u32[]{:S(2)}, u32[]{:S(2)}) collective-permute-start(bf16[1024,256]{1,0:T(8,128)(2,1)S(1)} %get-tuple-element.44), channel_id=1, source_target_pairs={{0,3},{1,0},{2,1},{3,2},{4,7},{5,4},{6,5},{7,6},{8,11},{9,8},{10,9... | collective-permute-start | bytes 1572872 | tf_op jit(solution)/shard_map/ppermute | solution.py:28
  11.1 29.1 %collective-permute-start.8 = (bf16[1024,256]{1,0:T(8,128)(2,1)S(1)}, bf16[1024,256]{1,0:T(8,128)(2,1)S(1)}, u32[]{:S(2)}, u32[]{:S(2)}) collective-permute-start(bf16[1024,256]{1,0:T(8,128)(2,1)S(1)} %get-tuple-element.45), channel_id=1, source_target_pairs={{0,2},{1,3},{2,0},{3,1},{4,6},{5,7},{6,4},{7,5},{8,10},{9,11},{10,... | collective-permute-start | bytes 1572872 | tf_op jit(solution)/shard_map/ppermute | solution.py:28
  16.6 4.4 %collective-permute-start.3 = (bf16[256,256]{1,0:T(8,128)(2,1)S(1)}, bf16[256,256]{1,0:T(8,128)(2,1)S(1)}, u32[]{:S(2)}, u32[]{:S(2)}) collective-permute-start(bf16[256,256]{1,0:T(8,128)(2,1)S(1)} %shard_map.84.refs_0_.refs_6_), channel_id=1, source_target_pairs={{0,4},{4,0},{8,12},{12,8},{16,20},{20,16},{24,28},{28,24},{1,5},{5... | collective-permute-start | bytes 393224 | tf_op jit(solution)/shard_map/ppermute | solution.py:326
  21.0 8.3 %collective-permute-start.4 = (bf16[256,256]{1,0:T(8,128)(2,1)S(1)}, bf16[256,256]{1,0:T(8,128)(2,1)S(1)}, u32[]{:S(2)}, u32[]{:S(2)}) collective-permute-start(bf16[256,256]{1,0:T(8,128)(2,1)S(1)} %shard_map.85.refs_0_), channel_id=1, source_target_pairs={{0,8},{4,12},{8,0},{12,4},{16,24},{20,28},{24,16},{28,20},{1,9},{5... | collective-permute-start | bytes 393224 | tf_op jit(solution)/shard_map/ppermute | solution.py:326
  29.4 12.4 %collective-permute-start.5 = (bf16[256,256]{1,0:T(8,128)(2,1)S(1)}, bf16[256,256]{1,0:T(8,128)(2,1)S(1)}, u32[]{:S(2)}, u32[]{:S(2)}) collective-permute-start(bf16[256,256]{1,0:T(8,128)(2,1)S(1)} %shard_map.87.refs_0_.refs_5_), channel_id=1, source_target_pairs={{0,16},{4,20},{8,24},{12,28},{16,0},{20,4},{24,8},{28,12},{1,17},{... | collective-permute-start | bytes 393224 | tf_op jit(solution)/shard_map/ppermute | solution.py:326
  35.8 9.4 %collective-permute-start.15 = (bf16[512,256]{1,0:T(8,128)(2,1)S(1)}, bf16[512,256]{1,0:T(8,128)(2,1)S(1)}, u32[]{:S(2)}, u32[]{:S(2)}) collective-permute-start(bf16[512,256]{1,0:T(8,128)(2,1)S(1)} %get-tuple-element.53), channel_id=1, source_target_pairs={{0,1},{1,2},{2,3},{3,0},{4,5},{5,6},{6,7},{7,4},{8,9},{9,10},{10,1... | collective-permute-start | bytes 786440 | tf_op jit(solution)/shard_map/ppermute | solution.py:28
  37.2 8.5 %collective-permute-start.16 = (bf16[512,256]{1,0:T(8,128)(2,1)S(1)}, bf16[512,256]{1,0:T(8,128)(2,1)S(1)}, u32[]{:S(2)}, u32[]{:S(2)}) collective-permute-start(bf16[512,256]{1,0:T(8,128)(2,1)S(1)} %get-tuple-element.54), channel_id=1, source_target_pairs={{0,3},{1,0},{2,1},{3,2},{4,7},{5,4},{6,5},{7,6},{8,11},{9,8},{10,9... | collective-permute-start | bytes 786440 | tf_op jit(solution)/shard_map/ppermute | solution.py:28
  38.7 9.3 %collective-permute-start.17 = (bf16[512,256]{1,0:T(8,128)(2,1)S(1)}, bf16[512,256]{1,0:T(8,128)(2,1)S(1)}, u32[]{:S(2)}, u32[]{:S(2)}) collective-permute-start(bf16[512,256]{1,0:T(8,128)(2,1)S(1)} %get-tuple-element.55), channel_id=1, source_target_pairs={{0,2},{1,3},{2,0},{3,1},{4,6},{5,7},{6,4},{7,5},{8,10},{9,11},{10,... | collective-permute-start | bytes 786440 | tf_op jit(solution)/shard_map/ppermute | solution.py:28
  41.0 7.9 %collective-permute-start.18 = (bf16[512,256]{1,0:T(8,128)(2,1)S(1)}, bf16[512,256]{1,0:T(8,128)(2,1)S(1)}, u32[]{:S(2)}, u32[]{:S(2)}) collective-permute-start(bf16[512,256]{1,0:T(8,128)(2,1)S(1)} %get-tuple-element.57), channel_id=1, source_target_pairs={{0,4},{4,8},{8,12},{12,16},{16,20},{20,24},{24,28},{28,0},{1,5},{5... | collective-permute-start | bytes 786440 | tf_op jit(solution)/shard_map/ppermute | solution.py:28
  41.8 7.2 %collective-permute-start.19 = (bf16[512,256]{1,0:T(8,128)(2,1)S(1)}, bf16[512,256]{1,0:T(8,128)(2,1)S(1)}, u32[]{:S(2)}, u32[]{:S(2)}) collective-permute-start(bf16[512,256]{1,0:T(8,128)(2,1)S(1)} %get-tuple-element.58), channel_id=1, source_target_pairs={{0,28},{4,0},{8,4},{12,8},{16,12},{20,16},{24,20},{28,24},{1,29},{... | collective-permute-start | bytes 786440 | tf_op jit(solution)/shard_map/ppermute | solution.py:28
  45.2 13.1 %collective-permute-start.12 = (bf16[768,256]{1,0:T(8,128)(2,1)S(1)}, bf16[768,256]{1,0:T(8,128)(2,1)S(1)}, u32[]{:S(2)}, u32[]{:S(2)}) collective-permute-start(bf16[768,256]{1,0:T(8,128)(2,1)S(1)} %get-tuple-element.42.refs_1_), channel_id=1, source_target_pairs={{0,1},{1,2},{2,3},{3,0},{4,5},{5,6},{6,7},{7,4},{8,9},{9,10},{10,1... | collective-permute-start | bytes 1179656 | tf_op jit(solution)/shard_map/ppermute | solution.py:28
  45.7 12.7 %collective-permute-start.13 = (bf16[768,256]{1,0:T(8,128)(2,1)S(1)}, bf16[768,256]{1,0:T(8,128)(2,1)S(1)}, u32[]{:S(2)}, u32[]{:S(2)}) collective-permute-start(bf16[768,256]{1,0:T(8,128)(2,1)S(1)} %get-tuple-element.50), channel_id=1, source_target_pairs={{0,3},{1,0},{2,1},{3,2},{4,7},{5,4},{6,5},{7,6},{8,11},{9,8},{10,9... | collective-permute-start | bytes 1179656 | tf_op jit(solution)/shard_map/ppermute | solution.py:28
  48.0 17.8 %collective-permute-start.14 = (bf16[768,256]{1,0:T(8,128)(2,1)S(1)}, bf16[768,256]{1,0:T(8,128)(2,1)S(1)}, u32[]{:S(2)}, u32[]{:S(2)}) collective-permute-start(bf16[768,256]{1,0:T(8,128)(2,1)S(1)} %get-tuple-element.51), channel_id=1, source_target_pairs={{0,2},{1,3},{2,0},{3,1},{4,6},{5,7},{6,4},{7,5},{8,10},{9,11},{10,... | collective-permute-start | bytes 1179656 | tf_op jit(solution)/shard_map/ppermute | solution.py:28
  49.7 17.0 %collective-permute-start.20 = (bf16[512,256]{1,0:T(8,128)(2,1)S(1)}, bf16[512,256]{1,0:T(8,128)(2,1)S(1)}, u32[]{:S(2)}, u32[]{:S(2)}) collective-permute-start(bf16[512,256]{1,0:T(8,128)(2,1)S(1)} %get-tuple-element.59), channel_id=1, source_target_pairs={{0,4},{4,8},{8,12},{12,16},{16,20},{20,24},{24,28},{28,0},{1,5},{5... | collective-permute-start | bytes 786440 | tf_op jit(solution)/shard_map/ppermute | solution.py:28
  51.0 19.2 %copy-start.2 = (bf16[1,32,64,256]{3,2,1,0:T(8,128)(2,1)S(1)}, bf16[1,32,64,256]{3,2,1,0:T(8,128)(2,1)}, u32[]{:S(2)}) copy-start(bf16[1,32,64,256]{3,2,1,0:T(8,128)(2,1)} %param.12) | copy-start | bytes 3145732
  51.0 15.7 %collective-permute-start.21 = (bf16[512,256]{1,0:T(8,128)(2,1)S(1)}, bf16[512,256]{1,0:T(8,128)(2,1)S(1)}, u32[]{:S(2)}, u32[]{:S(2)}) collective-permute-start(bf16[512,256]{1,0:T(8,128)(2,1)S(1)} %get-tuple-element.60), channel_id=1, source_target_pairs={{0,28},{4,0},{8,4},{12,8},{16,12},{20,16},{24,20},{28,24},{1,29},{... | collective-permute-start | bytes 786440 | tf_op jit(solution)/shard_map/ppermute | solution.py:28
  58.4 14.1 %collective-permute-start.10 = (bf16[512,256]{1,0:T(8,128)(2,1)S(1)}, bf16[512,256]{1,0:T(8,128)(2,1)S(1)}, u32[]{:S(2)}, u32[]{:S(2)}) collective-permute-start(bf16[512,256]{1,0:T(8,128)(2,1)S(1)} %get-tuple-element.47), channel_id=1, source_target_pairs={{0,3},{1,0},{2,1},{3,2},{4,7},{5,4},{6,5},{7,6},{8,11},{9,8},{10,9... | collective-permute-start | bytes 786440 | tf_op jit(solution)/shard_map/ppermute | solution.py:28
  58.4 14.1 %collective-permute-start.11 = (bf16[512,256]{1,0:T(8,128)(2,1)S(1)}, bf16[512,256]{1,0:T(8,128)(2,1)S(1)}, u32[]{:S(2)}, u32[]{:S(2)}) collective-permute-start(bf16[512,256]{1,0:T(8,128)(2,1)S(1)} %get-tuple-element.48), channel_id=1, source_target_pairs={{0,2},{1,3},{2,0},{3,1},{4,6},{5,7},{6,4},{7,5},{8,10},{9,11},{10,... | collective-permute-start | bytes 786440 | tf_op jit(solution)/shard_map/ppermute | solution.py:28
  65.8 10.4 %collective-permute-start.9 = (bf16[512,256]{1,0:T(8,128)(2,1)S(1)}, bf16[512,256]{1,0:T(8,128)(2,1)S(1)}, u32[]{:S(2)}, u32[]{:S(2)}) collective-permute-start(bf16[512,256]{1,0:T(8,128)(2,1)S(1)} %get-tuple-element.46), channel_id=1, source_target_pairs={{0,1},{1,2},{2,3},{3,0},{4,5},{5,6},{6,7},{7,4},{8,9},{9,10},{10,1... | collective-permute-start | bytes 786440 | tf_op jit(solution)/shard_map/ppermute | solution.py:28
  67.4 8.7 %collective-permute-start.23 = (bf16[512,256]{1,0:T(8,128)(2,1)S(1)}, bf16[512,256]{1,0:T(8,128)(2,1)S(1)}, u32[]{:S(2)}, u32[]{:S(2)}) collective-permute-start(bf16[512,256]{1,0:T(8,128)(2,1)S(1)} %get-tuple-element.62.refs_10_), channel_id=1, source_target_pairs={{0,4},{4,8},{8,12},{12,16},{16,20},{20,24},{24,28},{28,0},{1,5},{5... | collective-permute-start | bytes 786440 | tf_op jit(solution)/shard_map/ppermute | solution.py:28
  67.9 16.2 %collective-permute-start.22 = (bf16[512,256]{1,0:T(8,128)(2,1)S(1)}, bf16[512,256]{1,0:T(8,128)(2,1)S(1)}, u32[]{:S(2)}, u32[]{:S(2)}) collective-permute-start(bf16[512,256]{1,0:T(8,128)(2,1)S(1)} %get-tuple-element.61), channel_id=1, source_target_pairs={{0,28},{4,0},{8,4},{12,8},{16,12},{20,16},{24,20},{28,24},{1,29},{... | collective-permute-start | bytes 786440 | tf_op jit(solution)/shard_map/ppermute | solution.py:28
  76.6 12.9 %collective-permute-start.24 = (bf16[512,256]{1,0:T(8,128)(2,1)S(1)}, bf16[512,256]{1,0:T(8,128)(2,1)S(1)}, u32[]{:S(2)}, u32[]{:S(2)}) collective-permute-start(bf16[512,256]{1,0:T(8,128)(2,1)S(1)} %shard_map.96.refs_9_), channel_id=1, source_target_pairs={{0,4},{4,8},{8,12},{12,16},{16,20},{20,24},{24,28},{28,0},{1,5},{5... | collective-permute-start | bytes 786440 | tf_op jit(solution)/shard_map/ppermute | solution.py:28
  77.4 7.3 %collective-permute-start.25 = (bf16[256,256]{1,0:T(8,128)(2,1)S(1)}, bf16[256,256]{1,0:T(8,128)(2,1)S(1)}, u32[]{:S(2)}, u32[]{:S(2)}) collective-permute-start(bf16[256,256]{1,0:T(8,128)(2,1)S(1)} %get-tuple-element.63.refs_9_), channel_id=1, source_target_pairs={{0,192},{64,0},{128,64},{192,128},{1,193},{65,1},{129,65},{193,129... | collective-permute-start | bytes 393224 | tf_op jit(solution)/shard_map/ppermute | solution.py:28
  80.0 6.5 %collective-permute-start.26 = (bf16[256,256]{1,0:T(8,128)(2,1)S(1)}, bf16[256,256]{1,0:T(8,128)(2,1)S(1)}, u32[]{:S(2)}, u32[]{:S(2)}) collective-permute-start(bf16[256,256]{1,0:T(8,128)(2,1)S(1)} %get-tuple-element.65), channel_id=1, source_target_pairs={{0,128},{64,192},{128,0},{192,64},{1,129},{65,193},{129,1},{193,65... | collective-permute-start | bytes 393224 | tf_op jit(solution)/shard_map/ppermute | solution.py:28
  84.1 5.3 %collective-permute-start.27 = (bf16[256,256]{1,0:T(8,128)(2,1)S(1)}, bf16[256,256]{1,0:T(8,128)(2,1)S(1)}, u32[]{:S(2)}, u32[]{:S(2)}) collective-permute-start(bf16[256,256]{1,0:T(8,128)(2,1)S(1)} %get-tuple-element.66), channel_id=1, source_target_pairs={{0,64},{64,128},{128,192},{192,0},{1,65},{65,129},{129,193},{193,1... | collective-permute-start | bytes 393224 | tf_op jit(solution)/shard_map/ppermute | solution.py:28
  90.0 9.5 %collective-permute-start.28 = (bf16[512,256]{1,0:T(8,128)(2,1)S(1)}, bf16[512,256]{1,0:T(8,128)(2,1)S(1)}, u32[]{:S(2)}, u32[]{:S(2)}) collective-permute-start(bf16[512,256]{1,0:T(8,128)(2,1)S(1)} %get-tuple-element.67), channel_id=1, source_target_pairs={{0,32},{1,33},{2,34},{3,35},{4,36},{5,37},{6,38},{7,39},{8,40},{9,... | collective-permute-start | bytes 786440 | tf_op jit(solution)/shard_map/ppermute | solution.py:472
  (4 other events, 33.9 us)
where the time goes:
time: 101 us; the launch traced here: 100 us
  starting transfers between devices  47.2 us (47%)
  waiting for transfers between devices  30.8 us (30%)
  Pallas kernels  21.2 us (21%)
    ppermute x25, starting transfers between devices, shift(): lax.ppermute(value, axis, [(i, (i + steps) % count) for i in range(count)])  36.1 us
    pallas_call x17, Pallas kernels, call(): pl.pallas_call(body, out_shape=outs, in_specs=list(in_specs) + [ANY] * m,...  21.2 us
    ppermute x25, waiting for transfers between devices, shift(): lax.ppermute(value, axis, [(i, (i + steps) % count) for i in range(count)])  19.9 us
    ppermute x3, starting transfers between devices, exchanged_sum(): other = lax.ppermute(value, axis, [(i, i ^ bit) for i in range(count)])  9.85 us
    ppermute x1, waiting for transfers between devices, steps(): carried = lax.ppermute(first_out, 'section', [(0, 1)])  8.24 us
    ppermute x3, waiting for transfers between devices, exchanged_sum(): other = lax.ppermute(value, axis, [(i, i ^ bit) for i in range(count)])  2.66 us
  transfers between devices with their start and end apart: 29, of which 9 were waited for; matrix products, arithmetic and copies ran while one was open for 0% of the time, Pallas kernels for 18%

commit v1 on v0

v1 whole, which is shorter than its diff:
```python
import functools

import jax
import jax.numpy as jnp
from jax import lax
from jax.experimental import pallas as pl
from jax.experimental.pallas import tpu as pltpu
from jax.sharding import Mesh
from jax.sharding import PartitionSpec as P


Z, Y = "tensor_0", "tensor_1"
TENSOR = (Z, Y)
NZ, NY, NX = 8, 4, 4
ROWS, WIDTH, TILE = 512, 256, 256
WINDOW = 256
IDROWS = 16
VARS, RANK, BLK = 32, 64, 128
HOPS = (1, 3, 2)
F32, BF16 = jnp.float32, jnp.bfloat16
ANY = pl.BlockSpec(memory_space=pl.ANY)
HBM = pl.BlockSpec(memory_space=pltpu.HBM)
SMEM = pl.BlockSpec(memory_space=pltpu.SMEM)


def shift(value, axis, steps):
    count = lax.axis_size(axis)
    return lax.ppermute(value, axis, [(i, (i + steps) % count) for i in range(count)])


def cost(flops, nbytes):
    return pl.CostEstimate(flops=flops, bytes_accessed=nbytes, transcendentals=0)


def shape(dims, dtype=BF16):
    return pltpu.VMEM(dims, dtype)


def whole(dims, at=None):
    at = at or (0,) * len(dims)
    return pl.BlockSpec(dims, lambda: at)


def tiles_of(group):
    z = lax.axis_index(Z)
    return lax.rem(z + (4 - group), NZ), lax.rem(z + (group + NZ - 3), NZ)


def column(ztile, ytile):
    return pl.multiple_of((ztile * NY + ytile) * TILE, TILE)


def placed(value, spec):
    space = pltpu.HBM if spec is HBM else pltpu.VMEM
    if spec is SMEM:
        return value
    return pltpu.with_memory_space_constraint(value, space)


def call(kernel, args, in_specs, outs, out_specs, scratch, work, limit, after=()):
    n, m = len(args), len(after)
    args = [placed(arg, spec) for arg, spec in zip(args, in_specs)]

    def body(*refs):
        kernel(*refs[:n], *refs[n + m :])

    return pl.pallas_call(
        body,
        out_shape=outs,
        in_specs=list(in_specs) + [ANY] * m,
        out_specs=out_specs,
        scratch_shapes=scratch,
        cost_estimate=cost(*work),
        compiler_params=pltpu.CompilerParams(vmem_limit_bytes=limit << 20),
    )(*args, *after)


def parity():
    return lax.rem(lax.axis_index("pool"), 2)


def pack_kernel(groups, ahead, *refs):
    w_ref = refs[0]
    n_in = 2 if ahead else 1
    outs = refs[n_in : n_in + 3]
    owns = refs[n_in + 3 : n_in + 3 + len(groups)]
    sems = refs[-1]
    y, odd = lax.axis_index(Y), parity()
    copies = []
    for gi, group in enumerate(groups):
        plus, minus = tiles_of(group)
        mine = plus * (1 - odd) + minus * odd
        for ki, hop in enumerate(HOPS):
            if ahead and gi == 0:
                copies.append((refs[1], outs[ki].at[pl.ds(0, ROWS), :]))
            source = w_ref.at[:, pl.ds(column(mine, lax.rem(y + hop, NY)), TILE)]
            copies.append((source, outs[ki].at[pl.ds(ahead + gi * TILE, TILE), :]))
    for gi, group in enumerate(groups):
        for ti, ztile in enumerate(tiles_of(group)):
            source = w_ref.at[:, pl.ds(column(ztile, y), TILE)]
            copies.append((source, owns[gi].at[pl.ds(ti * TILE, TILE), :]))
    copies = [
        pltpu.make_async_copy(source, target, sems.at[i])
        for i, (source, target) in enumerate(copies)
    ]
    for copy in copies:
        copy.start()
    for copy in copies:
        copy.wait()


def pack(groups, weight, features=None, after=()):
    ahead = 0 if features is None else ROWS
    args, specs = [weight], [HBM]
    if ahead:
        args.append(features)
        specs.append(HBM)
    rows = ahead + len(groups) * TILE
    dims = [(rows, TILE)] * 3 + [(2 * TILE, TILE)] * len(groups)
    got = call(
        functools.partial(pack_kernel, groups, ahead),
        args,
        specs,
        [shape(d) for d in dims],
        [whole(d) for d in dims],
        [pltpu.SemaphoreType.DMA((3 + 5 * len(groups),))],
        (0, 6 * rows * TILE),
        8,
        after,
    )
    return got[:3], got[3:]


def join_kernel(base, a_ref, b_ref, c_ref, *outs):
    for gi, out in enumerate(outs):
        for ki, ref in enumerate((a_ref, b_ref, c_ref)):
            rows = slice(base + gi * TILE, base + (gi + 1) * TILE)
            out[ki * TILE : (ki + 1) * TILE, :] = ref[rows, :]


def join(got, base, after=()):
    return call(
        functools.partial(join_kernel, base),
        tuple(got),
        [whole(got[0].shape)] * 3,
        [shape((3 * TILE, TILE))] * 2,
        [whole((3 * TILE, TILE))] * 2,
        [],
        (0, 3 << 20),
        4,
        after,
    )


def swapped(value, second_pairing):
    if second_pairing:
        pairs = [(0, 3), (3, 0), (1, 2), (2, 1)]
    else:
        pairs = [(0, 1), (1, 0), (2, 3), (3, 2)]
    return lax.ppermute(value, "pool", pairs)


def project_kernel(which, has_in, own_ref, x_ref, p0, p1, p2, mine_ref, other_ref, *refs):
    n = len(which)
    carried, outs = (refs[:n], refs[n:]) if has_in else ((None,) * n, refs)
    even = parity() == 0
    mine, other = mine_ref[...], other_ref[...]
    lhs = jnp.concatenate([x_ref[...]] + [peer[0:ROWS, :] for peer in (p0, p1, p2)], axis=1)
    for c_ref, out, ti in zip(carried, outs, which):
        remote = lax.select(even, mine, other) if ti == 0 else lax.select(even, other, mine)
        rhs = jnp.concatenate([own_ref[ti * TILE : (ti + 1) * TILE, :], remote], axis=0)
        total = jnp.dot(lhs, rhs, preferred_element_type=F32)
        if has_in:
            total = total + c_ref[...].astype(F32)
        out[...] = total.astype(out.dtype)


def project(which, own, features, first_got, mine, other, carried, after=(), out_dtype=BF16):
    half = (ROWS, WIDTH)
    n = len(which)
    return call(
        functools.partial(project_kernel, which, bool(carried)),
        (own, features, *first_got, mine, other, *carried),
        [whole(half)] * 2
        + [whole(first_got[0].shape)] * 3
        + [whole((3 * TILE, TILE))] * 2
        + [whole(half)] * len(carried),
        [shape((ROWS, TILE), out_dtype)] * n,
        [whole((ROWS, TILE))] * n,
        [],
        (2 * ROWS * 1024 * TILE * n, 2 << 20),
        8,
        after,
    )


def window_start(ids, owner):
    before = jnp.sum((ids < owner * VARS).astype(jnp.int32))
    return jnp.minimum(before, ROWS - WINDOW)


def dispatch_kernel(ids_ref, x_ref, *outs):
    me = lax.axis_index("pool")
    ids = ids_ref[...]
    features = x_ref[...]
    for k in range(NX):
        owner = lax.rem(me + k, NX)
        start = window_start(ids, owner)
        at = lax.broadcasted_iota(jnp.int32, (WINDOW, ROWS), 0) + start
        hot = (at == lax.broadcasted_iota(jnp.int32, (WINDOW, ROWS), 1)).astype(F32).astype(BF16)
        outs[k][0:WINDOW, :] = jnp.dot(hot, features, preferred_element_type=F32).astype(BF16)
        local = jnp.broadcast_to((ids - owner * VARS).astype(F32), (IDROWS, ROWS)).astype(BF16)
        outs[k][WINDOW : WINDOW + IDROWS, :] = lax.dot_general(
            local, hot, (((1,), (1,)), ((), ())), preferred_element_type=F32
        ).astype(BF16)


def dispatch(ids, features, after=()):
    return call(
        dispatch_kernel,
        (ids, features),
        [whole((1, ROWS)), whole((ROWS, WIDTH))],
        [shape((WINDOW + IDROWS, WIDTH))] * NX,
        [whole((WINDOW + IDROWS, WIDTH))] * NX,
        [],
        (2 * 1024 * 512 * 256, 1 << 20),
        6,
        after,
    )


def spread_columns(row, lanes):
    diagonal = lax.broadcasted_iota(jnp.int32, (WINDOW, WINDOW), 0) == lax.broadcasted_iota(
        jnp.int32, (WINDOW, WINDOW), 1
    )
    row = jnp.broadcast_to(row.astype(F32), (WINDOW, WINDOW))
    spread = jnp.where(diagonal, row, 0.0).astype(BF16)
    return jnp.dot(spread, jnp.ones((WINDOW, lanes), BF16), preferred_element_type=F32)


def variant_columns(item_ref, lanes):
    return spread_columns(item_ref[WINDOW : WINDOW + 1, :], lanes)


def down_kernel(i0, i1, i2, i3, down_ref, out_ref, item_ref, fold_ref):
    for k, item in enumerate((i0, i1, i2, i3)):
        item_ref[k] = item[...]
    lane = lax.broadcasted_iota(jnp.int32, (1, 256), 1)
    part = lax.div(lane, jnp.int32(RANK)).astype(F32)

    def window(k, carry):
        item = item_ref.at[k]
        variant = variant_columns(item, 256)
        features = item[0:WINDOW, :]
        total = None
        for j in range(VARS * RANK // 256):
            value = lax.dot_general(
                features,
                down_ref[j * 256 : (j + 1) * 256, :],
                (((1,), (1,)), ((), ())),
                preferred_element_type=F32,
            )
            value = jnp.where(variant == part + float(j * 4), value, 0.0)
            total = value if total is None else total + value
        two = total[:, 0:128] + total[:, 128:256]
        fold_ref[k] = two + pltpu.roll(two, RANK, 1)
        return carry

    lax.fori_loop(0, NX, window, 0)
    low = lax.broadcasted_iota(jnp.int32, (WINDOW, 128), 1) < RANK
    for h in range(2):
        packed = jnp.where(low, fold_ref[h], fold_ref[h + 2]).astype(BF16)
        out_ref[:, h * 128 : (h + 1) * 128] = packed


def down(items, factor, after=()):
    return call(
        down_kernel,
        (*items, factor),
        [whole((WINDOW + IDROWS, WIDTH))] * NX + [whole((VARS * RANK, WIDTH))],
        shape((WINDOW, 256)),
        whole((WINDOW, 256)),
        [pltpu.VMEM((NX, WINDOW + IDROWS, WIDTH), BF16), pltpu.VMEM((NX, WINDOW, 128), F32)],
        (2 * 1024 * 256 * 2048, 2 << 20),
        8,
        after,
    )


def block_kernel(i0, i1, i2, i3, mats_ref, place_ref, out_ref, item_ref, rhs_ref):
    for k, item in enumerate((i0, i1, i2, i3)):
        item_ref[k] = item[...]
    shard = lax.axis_index(Z) * NY + lax.axis_index(Y)

    def lanes_of(v):
        return pl.ds(pl.multiple_of((place_ref[v] - shard * 2) * BLK, BLK), BLK)

    for v in range(VARS):
        rhs_ref[v * BLK : (v + 1) * BLK, :] = jnp.zeros((BLK, 256), BF16)
        rhs_ref[v * BLK : (v + 1) * BLK, lanes_of(v)] = mats_ref[v]

    def window(k, carry):
        item = item_ref.at[k]
        variant = variant_columns(item, 128)
        pieces = []
        for v in range(VARS):
            piece = item[0:WINDOW, lanes_of(v)].astype(F32)
            pieces.append(jnp.where(variant == float(v), piece, 0.0).astype(BF16))
        lhs = jnp.concatenate(pieces, axis=1)
        out_ref[k] = jnp.dot(lhs, rhs_ref[...], preferred_element_type=F32)
        return carry

    lax.fori_loop(0, NX, window, 0)


def block_terms(items, mats, places, after=()):
    return call(
        block_kernel,
        (*items, mats, places),
        [whole((WINDOW + IDROWS, WIDTH))] * NX + [whole((VARS, BLK, BLK)), SMEM],
        shape((NX, WINDOW, 256), F32),
        whole((NX, WINDOW, 256)),
        [pltpu.VMEM((NX, WINDOW + IDROWS, WIDTH), BF16), pltpu.VMEM((VARS * BLK, 256), BF16)],
        (2 * 1024 * 4096 * 256, 3 << 20),
        10,
        after,
    )


def add_kernel(a_ref, b_ref, out_ref):
    out_ref[...] = (a_ref[...].astype(F32) + b_ref[...].astype(F32)).astype(BF16)


def exchanged_sum(value, axis, bit, after=()):
    count = lax.axis_size(axis)
    other = lax.ppermute(value, axis, [(i, i ^ bit) for i in range(count)])
    return call(
        add_kernel,
        (value, other),
        [whole((WINDOW, 256))] * 2,
        shape((WINDOW, 256)),
        whole((WINDOW, 256)),
        [],
        (1 << 16, 3 << 17),
        2,
        after,
    )


def up_kernel(i0, i1, i2, i3, low_ref, up_ref, block_ref, *refs):
    outs, (item_ref, two_ref, out_ref) = refs[:NX], refs[NX:]
    for k, item in enumerate((i0, i1, i2, i3)):
        item_ref[k] = item[WINDOW : WINDOW + IDROWS, :]
    first = lax.broadcasted_iota(jnp.int32, (WINDOW, 128), 1) < RANK
    for h in range(2):
        packed = low_ref[:, h * 128 : (h + 1) * 128].astype(F32)
        turned = pltpu.roll(packed, RANK, 1)
        two_ref[h] = jnp.where(first, packed, turned)
        two_ref[h + 2] = jnp.where(first, turned, packed)
    half = lax.div(lax.broadcasted_iota(jnp.int32, (1, 128), 1), jnp.int32(RANK)).astype(F32)

    def window(k, carry):
        variant = spread_columns(item_ref[k, 0:1, :], 128)
        two = two_ref[k]
        pieces = []
        for i in range(VARS // 2):
            pieces.append(jnp.where(variant == half + float(2 * i), two, 0.0).astype(BF16))
        lhs = jnp.concatenate(pieces, axis=1)
        total = block_ref[k] + jnp.dot(lhs, up_ref[...], preferred_element_type=F32)
        out_ref[k] = total.astype(BF16)
        return carry

    lax.fori_loop(0, NX, window, 0)
    for k in range(NX):
        outs[k][...] = out_ref[k]


def up(items, low, factor, blocks, after=()):
    return call(
        up_kernel,
        (*items, low, factor, blocks),
        [whole((WINDOW + IDROWS, WIDTH))] * NX
        + [whole((WINDOW, 256)), whole((VARS * RANK, WIDTH)), whole((NX, WINDOW, 256))],
        [shape((WINDOW, WIDTH))] * NX,
        [whole((WINDOW, WIDTH))] * NX,
        [
            pltpu.VMEM((NX, IDROWS, WIDTH), BF16),
            pltpu.VMEM((NX, WINDOW, 128), F32),
            pltpu.VMEM((NX, WINDOW, WIDTH), BF16),
        ],
        (2 * 1024 * 256 * 2048, 3 << 20),
        10,
        after,
    )


def combine_kernel(ids_ref, h_ref, own_ref, plus_ref, r0, r1, r2, r3, first_ref, branch_ref):
    me = lax.axis_index("pool")
    ids = ids_ref[...]
    branch = own_ref[...] + plus_ref[...].astype(F32)
    delta = None
    for k, back in enumerate((r0, r1, r2, r3)):
        start = window_start(ids, lax.rem(me + k, NX))
        at = lax.broadcasted_iota(jnp.int32, (ROWS, WINDOW), 1) + start
        hot = (at == lax.broadcasted_iota(jnp.int32, (ROWS, WINDOW), 0)).astype(F32).astype(BF16)
        part = jnp.dot(hot, back[...], preferred_element_type=F32)
        delta = part if delta is None else delta + part
    branch = branch + delta
    branch_ref[...] = branch
    first_ref[...] = (h_ref[...].astype(F32) + branch).astype(BF16)


def combine(ids, hidden, own, plus, returned, after=()):
    half = (ROWS, WIDTH)
    return call(
        combine_kernel,
        (ids, hidden, own, plus, *returned),
        [whole((1, ROWS))] + [whole(half)] * 3 + [whole((WINDOW, WIDTH))] * NX,
        [shape(half), shape(half, F32)],
        [whole(half)] * 2,
        [],
        (2 * 512 * 1024 * 256, 2 << 20),
        8,
        after,
    )


def steps(
    hidden_input,
    attention_output,
    projection_weight,
    lowrank_down_factor,
    lowrank_up_factor,
    residual_block_mats,
    diagonal_block_index,
    row_variant_index,
):
    features = attention_output[0]
    weight = projection_weight[0]
    down_factor = lowrank_down_factor[0].reshape(VARS * RANK, WIDTH)
    up_factor = lowrank_up_factor[0].reshape(VARS * RANK, WIDTH)
    mats = residual_block_mats[0][:, 0]
    places = diagonal_block_index[0][:, 0]
    ids = row_variant_index.reshape(1, ROWS)

    first, (own0, own1) = pack((0, 1), weight, features)
    got = [shift(value, Y, hop) for value, hop in zip(first, HOPS)]
    sent = dispatch(ids, features, (first[0],))
    items = [sent[0]] + [shift(sent[k], "pool", k) for k in (1, 2, 3)]
    second, (own2, own3) = pack((2, 3), weight, None, (sent[0],))
    later = [shift(value, Y, hop) for value, hop in zip(second, HOPS)]
    low = down(items, down_factor, (second[0],))
    low1 = exchanged_sum(low, Z, 1)
    blocks = block_terms(items, mats, places, (low,))
    low2 = exchanged_sum(low1, Z, 2)
    mine0, mine1 = join(got, ROWS, (low1, blocks))
    other0 = swapped(mine0, False)
    other1 = swapped(mine1, True)
    low3 = exchanged_sum(low2, Z, 4)
    plus, minus = project((0, 1), own0, features, got, mine0, other0, (), (low2,))
    carried = (shift(plus, Z, 1), shift(minus, Z, -1))
    mine2, mine3 = join(later, 0, (plus,))
    other2 = swapped(mine2, False)
    other3 = swapped(mine3, True)
    low4 = exchanged_sum(low3, Y, 1)
    plus, minus = project((0, 1), own1, features, got, mine1, other1, carried)
    carried = (shift(plus, Z, 1), shift(minus, Z, -1))
    low5 = exchanged_sum(low4, Y, 2)
    plus, minus = project((0, 1), own2, features, got, mine2, other2, carried)
    carried = (shift(plus, Z, 1), shift(minus, Z, -1))
    served = up(items, low5, up_factor, blocks, (plus,))
    returned = [served[0]] + [shift(served[k], "pool", -k) for k in (1, 2, 3)]
    (plus,) = project(
        (0,), own3, features, got, mine3, other3, carried[:1], (served[1],)
    )
    arrived = shift(plus, Z, 1)
    (own,) = project((1,), own3, features, got, mine3, other3, carried[1:], (plus,), F32)
    plus = arrived

    first_out, branch = combine(ids, hidden_input, own, plus, returned)
    carried = lax.ppermute(first_out, "section", [(0, 1)])
    begin = jnp.where(lax.axis_index("section") == 0, hidden_input, carried)
    return (begin.astype(F32) + branch).astype(BF16)[None]


def solution(mesh):
    finer = Mesh(
        mesh.devices.reshape(mesh.shape["pool"], mesh.shape["section"], NZ, NY),
        ("pool", "section", Z, Y),
    )
    placed = (
        P("pool", TENSOR),
        P("section", "pool", TENSOR),
        P("section", TENSOR, None),
        P("section", "pool", None, TENSOR),
        P("section", "pool", None, TENSOR),
        P("section", "pool", TENSOR, None, None),
        P("section", "pool", TENSOR),
        P("pool"),
    )
    return jax.shard_map(
        steps,
        mesh=finer,
        in_specs=placed,
        out_specs=P("section", "pool", TENSOR),
        check_vma=False,
    )
```

time: 101 us -> 103 us (1.020)
  waiting for transfers between devices: 30.8 us -> 35.7 us
  Pallas kernels: 21.2 us -> 17.2 us
  starting transfers between devices: 47.2 us -> 48.6 us
    ppermute x25 -> x19, starting transfers between devices: 36.1 us -> 27.8 us  [shift(): lax.ppermute(value, axis, [(i, (i + steps) % count) for i in range(count)])]
    ppermute x0 -> x4, starting transfers between devices: none -> 4.95 us  [swapped(): return lax.ppermute(value, 'pool', pairs)]
    ppermute x3 -> x5, waiting for transfers between devices: 2.66 us -> 7.46 us  [exchanged_sum(): other = lax.ppermute(value, axis, [(i, i ^ bit) for i in range(count)])]
    ppermute x3 -> x5, starting transfers between devices: 9.85 us -> 14.6 us  [exchanged_sum(): other = lax.ppermute(value, axis, [(i, i ^ bit) for i in range(count)])]
    pallas_call x17 -> x19, Pallas kernels: 21.2 us -> 17.2 us  [call(): pl.pallas_call(body, out_shape=outs, in_specs=list(in_specs) + [ANY] * m,...]
    ppermute x25 -> x19, waiting for transfers between devices: 19.9 us -> 16 us  [shift(): lax.ppermute(value, axis, [(i, (i + steps) % count) for i in range(count)])]
    ppermute x1, waiting for transfers between devices: 8.24 us -> 12.1 us  [steps(): carried = lax.ppermute(first_out, 'section', [(0, 1)])]
  transfers between devices with their start and end apart: 29 -> 29, of which waited for: 9 -> 12; matrix products, arithmetic and copies ran while one was open for 0% -> 0% of each run, Pallas kernels for 18% -> 14%
where the time goes in v1:
time: 103 us
  starting transfers between devices  48.6 us (47%)
  waiting for transfers between devices  35.7 us (35%)
  Pallas kernels  17.2 us (17%)
    ppermute x19, starting transfers between devices, shift(): lax.ppermute(value, axis, [(i, (i + steps) % count) for i in range(count)])  27.8 us
    pallas_call x19, Pallas kernels, call(): pl.pallas_call(body, out_shape=outs, in_specs=list(in_specs) + [ANY] * m,...  17.2 us
    ppermute x19, waiting for transfers between devices, shift(): lax.ppermute(value, axis, [(i, (i + steps) % count) for i in range(count)])  16 us
    ppermute x5, starting transfers between devices, exchanged_sum(): other = lax.ppermute(value, axis, [(i, i ^ bit) for i in range(count)])  14.6 us
    ppermute x1, waiting for transfers between devices, steps(): carried = lax.ppermute(first_out, 'section', [(0, 1)])  12.1 us
    ppermute x5, waiting for transfers between devices, exchanged_sum(): other = lax.ppermute(value, axis, [(i, i ^ bit) for i in range(count)])  7.46 us
    ppermute x4, starting transfers between devices, swapped(): return lax.ppermute(value, 'pool', pairs)  4.95 us
  transfers between devices with their start and end apart: 29, of which 12 were waited for; matrix products, arithmetic and copies ran while one was open for 0% of the time, Pallas kernels for 14%

profile of v1, /device:TPU:1, one launch (start us, length us, event | category | flops | bytes accessed | tf_op | source)
XLA Modules:
  0.0 102.6 jit_solution(5064392451444945158)
XLA Ops:
  0.0 1.8 %shard_map.82 = (bf16[1024,256]{1,0:T(8,128)(2,1)S(1)}, bf16[1024,256]{1,0:T(8,128)(2,1)S(1)}, bf16[1024,256]{1,0:T(8,128)(2,1)S(1)}, bf16[512,256]{1,0:T(8,128)(2,1)S(1)}, bf16[512,256]{1,0:T(8,128)(2,1)S(1)}) custom-call(bf16[256,8192]{1,0:T(8,128)(2,1)} %bitcast.22, bf16[512,256]{1,0:T(8,128)(2,1)} %bitcast.9), custom_call_target="tpu_custom_call" | custom-call | bytes 1572864 | tf_op jit(solution)/shard_map/pallas_call | solution.py:67
  2.7 2.1 %collective-permute-start.6 = (bf16[272,256]{1,0:T(8,128)(2,1)S(1)}, bf16[272,256]{1,0:T(8,128)(2,1)S(1)}, u32[]{:S(2)}, u32[]{:S(2)}) collective-permute-start(bf16[272,256]{1,0:T(8,128)(2,1)S(1)} %get-tuple-element.44), channel_id=1, source_target_pairs={{0,64},{64,128},{128,192},{192,0},{1,65},{65,129},{129,193},{193,1... | collective-permute-start | bytes 417800 | tf_op jit(solution)/shard_map/ppermute | solution.py:28
  6.1 1.4 %collective-permute-start.1 = (bf16[1024,256]{1,0:T(8,128)(2,1)S(1)}, bf16[1024,256]{1,0:T(8,128)(2,1)S(1)}, u32[]{:S(2)}, u32[]{:S(2)}) collective-permute-start(bf16[1024,256]{1,0:T(8,128)(2,1)S(1)} %get-tuple-element.38), channel_id=1, source_target_pairs={{0,3},{1,0},{2,1},{3,2},{4,7},{5,4},{6,5},{7,6},{8,11},{9,8},{10,9... | collective-permute-start | bytes 1572872 | tf_op jit(solution)/shard_map/ppermute | solution.py:28
  7.5 1.6 %collective-permute-start.2 = (bf16[1024,256]{1,0:T(8,128)(2,1)S(1)}, bf16[1024,256]{1,0:T(8,128)(2,1)S(1)}, u32[]{:S(2)}, u32[]{:S(2)}) collective-permute-start(bf16[1024,256]{1,0:T(8,128)(2,1)S(1)} %get-tuple-element.39), channel_id=1, source_target_pairs={{0,2},{1,3},{2,0},{3,1},{4,6},{5,7},{6,4},{7,5},{8,10},{9,11},{10,... | collective-permute-start | bytes 1572872 | tf_op jit(solution)/shard_map/ppermute | solution.py:28
  9.2 2.4 %collective-permute-start.7 = (bf16[272,256]{1,0:T(8,128)(2,1)S(1)}, bf16[272,256]{1,0:T(8,128)(2,1)S(1)}, u32[]{:S(2)}, u32[]{:S(2)}) collective-permute-start(bf16[272,256]{1,0:T(8,128)(2,1)S(1)} %get-tuple-element.45), channel_id=1, source_target_pairs={{0,128},{64,192},{128,0},{192,64},{1,129},{65,193},{129,1},{193,65... | collective-permute-start | bytes 417800 | tf_op jit(solution)/shard_map/ppermute | solution.py:28
  12.8 1.5 %shard_map.84 = (bf16[512,256]{1,0:T(8,128)(2,1)S(1)}, bf16[512,256]{1,0:T(8,128)(2,1)S(1)}, bf16[512,256]{1,0:T(8,128)(2,1)S(1)}, bf16[512,256]{1,0:T(8,128)(2,1)S(1)}, bf16[512,256]{1,0:T(8,128)(2,1)S(1)}) custom-call(bf16[256,8192]{1,0:T(8,128)(2,1)} %bitcast.23, bf16[272,256]{1,0:T(8,128)(2,1)S(1)} %get-tuple-element.36.refs_1_.refs_0_), custom_call_target="tpu_custom_call" | custom-call | bytes 786432 | tf_op jit(solution)/shard_map/pallas_call | solution.py:67
  14.6 2.4 %collective-permute-done.8.refs_3_ = bf16[272,256]{1,0:T(8,128)(2,1)S(1)} collective-permute-done((bf16[272,256]{1,0:T(8,128)(2,1)S(1)}, bf16[272,256]{1,0:T(8,128)(2,1)S(1)}, u32[]{:S(2)}, u32[]{:S(2)}) %collective-permute-start.8) | collective-permute-done | bytes 139296 | tf_op jit(solution)/shard_map/ppermute | solution.py:28
  17.0 2.5 %shard_map.85.refs_0_.refs_6_ = bf16[256,256]{1,0:T(8,128)(2,1)S(1)} custom-call(bf16[272,256]{1,0:T(8,128)(2,1)S(1)} %get-tuple-element.36.refs_1_.refs_0_, bf16[272,256]{1,0:T(8,128)(2,1)S(1)} %collective-permute-done.6.refs_1_, bf16[272,256]{1,0:T(8,128)(2,1)S(1)} %collective-permute-done.7.refs_2_, bf16[272,256]{1,0:T(8,128)(2,1)S(1)} %collective-permute-done.8.refs_3_, ...), custom_call_target="tpu_custom_call" | custom-call | flops 1073741824 | bytes 2097152 | tf_op jit(solution)/shard_map/pallas_call | solution.py:67
  19.5 1.7 %collective-permute-start.9 = (bf16[256,256]{1,0:T(8,128)(2,1)S(1)}, bf16[256,256]{1,0:T(8,128)(2,1)S(1)}, u32[]{:S(2)}, u32[]{:S(2)}) collective-permute-start(bf16[256,256]{1,0:T(8,128)(2,1)S(1)} %shard_map.85.refs_0_.refs_6_), channel_id=1, source_target_pairs={{0,4},{4,0},{8,12},{12,8},{16,20},{20,16},{24,28},{28,24},{1,5},{5... | collective-permute-start | bytes 393224 | tf_op jit(solution)/shard_map/ppermute | solution.py:336
  21.2 4.3 %shard_map.87.refs_4_.refs_6_ = f32[4,256,256]{2,1,0:T(8,128)S(1)} custom-call(bf16[272,256]{1,0:T(8,128)(2,1)S(1)} %get-tuple-element.36.refs_1_.refs_0_, bf16[272,256]{1,0:T(8,128)(2,1)S(1)} %collective-permute-done.6.refs_1_, bf16[272,256]{1,0:T(8,128)(2,1)S(1)} %collective-permute-done.7.refs_2_, bf16[272,256]{1,0:T(8,128)(2,1)S(1)} %collective-permute-done.8.refs_3_, ...), custom_call_target="tpu_custom_call" | custom-call | flops 2147483648 | bytes 3145728 | tf_op jit(solution)/shard_map/pallas_call | solution.py:67
  25.6 5.5 %collective-permute-done.2.refs_2_.refs_4_ = bf16[1024,256]{1,0:T(8,128)(2,1)S(1)} collective-permute-done((bf16[1024,256]{1,0:T(8,128)(2,1)S(1)}, bf16[1024,256]{1,0:T(8,128)(2,1)S(1)}, u32[]{:S(2)}, u32[]{:S(2)}) %collective-permute-start.2) | collective-permute-done | bytes 524320 | tf_op jit(solution)/shard_map/ppermute | solution.py:28
  31.1 1.3 %collective-permute-start.10 = (bf16[768,256]{1,0:T(8,128)(2,1)S(1)}, bf16[768,256]{1,0:T(8,128)(2,1)S(1)}, u32[]{:S(2)}, u32[]{:S(2)}) collective-permute-start(bf16[768,256]{1,0:T(8,128)(2,1)S(1)} %get-tuple-element.47.refs_5_), channel_id=1, source_target_pairs={{0,64},{64,0},{128,192},{192,128},{1,65},{65,1},{129,193},{193,129... | collective-permute-start | bytes 1179656 | tf_op jit(solution)/shard_map/ppermute | solution.py:160
  33.0 3.0 %collective-permute-start.11 = (bf16[256,256]{1,0:T(8,128)(2,1)S(1)}, bf16[256,256]{1,0:T(8,128)(2,1)S(1)}, u32[]{:S(2)}, u32[]{:S(2)}) collective-permute-start(bf16[256,256]{1,0:T(8,128)(2,1)S(1)} %shard_map.86.refs_3_.refs_0_), channel_id=1, source_target_pairs={{0,8},{4,12},{8,0},{12,4},{16,24},{20,28},{24,16},{28,20},{1,9},{5... | collective-permute-start | bytes 393224 | tf_op jit(solution)/shard_map/ppermute | solution.py:336
  35.9 1.5 %collective-permute-start.14 = (bf16[768,256]{1,0:T(8,128)(2,1)S(1)}, bf16[768,256]{1,0:T(8,128)(2,1)S(1)}, u32[]{:S(2)}, u32[]{:S(2)}) collective-permute-start(bf16[768,256]{1,0:T(8,128)(2,1)S(1)} %get-tuple-element.53.refs_5_), channel_id=1, source_target_pairs={{0,192},{192,0},{64,128},{128,64},{1,193},{193,1},{65,129},{129,65... | collective-permute-start | bytes 1179656 | tf_op jit(solution)/shard_map/ppermute | solution.py:160
  37.5 2.1 %collective-permute-start.4 = (bf16[512,256]{1,0:T(8,128)(2,1)S(1)}, bf16[512,256]{1,0:T(8,128)(2,1)S(1)}, u32[]{:S(2)}, u32[]{:S(2)}) collective-permute-start(bf16[512,256]{1,0:T(8,128)(2,1)S(1)} %get-tuple-element.41), channel_id=1, source_target_pairs={{0,3},{1,0},{2,1},{3,2},{4,7},{5,4},{6,5},{7,6},{8,11},{9,8},{10,9... | collective-permute-start | bytes 786440 | tf_op jit(solution)/shard_map/ppermute | solution.py:28
  40.7 2.3 %collective-permute-start.15 = (bf16[512,256]{1,0:T(8,128)(2,1)S(1)}, bf16[512,256]{1,0:T(8,128)(2,1)S(1)}, u32[]{:S(2)}, u32[]{:S(2)}) collective-permute-start(bf16[512,256]{1,0:T(8,128)(2,1)S(1)} %get-tuple-element.48.refs_3_), channel_id=1, source_target_pairs={{0,4},{4,8},{8,12},{12,16},{16,20},{20,24},{24,28},{28,0},{1,5},{5... | collective-permute-start | bytes 786440 | tf_op jit(solution)/shard_map/ppermute | solution.py:28
  43.1 4.3 %collective-permute-start.16 = (bf16[512,256]{1,0:T(8,128)(2,1)S(1)}, bf16[512,256]{1,0:T(8,128)(2,1)S(1)}, u32[]{:S(2)}, u32[]{:S(2)}) collective-permute-start(bf16[512,256]{1,0:T(8,128)(2,1)S(1)} %get-tuple-element.54), channel_id=1, source_target_pairs={{0,28},{4,0},{8,4},{12,8},{16,12},{20,16},{24,20},{28,24},{1,29},{... | collective-permute-start | bytes 786440 | tf_op jit(solution)/shard_map/ppermute | solution.py:28
  48.1 3.0 %collective-permute-done.15.refs_7_ = bf16[512,256]{1,0:T(8,128)(2,1)S(1)} collective-permute-done((bf16[512,256]{1,0:T(8,128)(2,1)S(1)}, bf16[512,256]{1,0:T(8,128)(2,1)S(1)}, u32[]{:S(2)}, u32[]{:S(2)}) %collective-permute-start.15) | collective-permute-done | bytes 262176 | tf_op jit(solution)/shard_map/ppermute | solution.py:28
  51.9 3.1 %collective-permute-start.18 = (bf16[512,256]{1,0:T(8,128)(2,1)S(1)}, bf16[512,256]{1,0:T(8,128)(2,1)S(1)}, u32[]{:S(2)}, u32[]{:S(2)}) collective-permute-start(bf16[512,256]{1,0:T(8,128)(2,1)S(1)} %get-tuple-element.56), channel_id=1, source_target_pairs={{0,28},{4,0},{8,4},{12,8},{16,12},{20,16},{24,20},{28,24},{1,29},{... | collective-permute-start | bytes 786440 | tf_op jit(solution)/shard_map/ppermute | solution.py:28
  55.0 3.8 %collective-permute-start.21 = (bf16[256,256]{1,0:T(8,128)(2,1)S(1)}, bf16[256,256]{1,0:T(8,128)(2,1)S(1)}, u32[]{:S(2)}, u32[]{:S(2)}) collective-permute-start(bf16[256,256]{1,0:T(8,128)(2,1)S(1)} %shard_map.89.refs_7_.refs_0_), channel_id=1, source_target_pairs={{0,16},{4,20},{8,24},{12,28},{16,0},{20,4},{24,8},{28,12},{1,17},{... | collective-permute-start | bytes 393224 | tf_op jit(solution)/shard_map/ppermute | solution.py:336
  58.8 1.5 %collective-permute-start.12 = (bf16[768,256]{1,0:T(8,128)(2,1)S(1)}, bf16[768,256]{1,0:T(8,128)(2,1)S(1)}, u32[]{:S(2)}, u32[]{:S(2)}) collective-permute-start(bf16[768,256]{1,0:T(8,128)(2,1)S(1)} %get-tuple-element.49.refs_5_), channel_id=1, source_target_pairs={{0,192},{192,0},{64,128},{128,64},{1,193},{193,1},{65,129},{129,65... | collective-permute-start | bytes 1179656 | tf_op jit(solution)/shard_map/ppermute | solution.py:160
  60.3 2.8 %collective-permute-done.21.refs_1_ = bf16[256,256]{1,0:T(8,128)(2,1)S(1)} collective-permute-done((bf16[256,256]{1,0:T(8,128)(2,1)S(1)}, bf16[256,256]{1,0:T(8,128)(2,1)S(1)}, u32[]{:S(2)}, u32[]{:S(2)}) %collective-permute-start.21) | collective-permute-done | bytes 131104 | tf_op jit(solution)/shard_map/ppermute | solution.py:336
  63.1 1.4 %collective-permute-start.22 = (bf16[256,256]{1,0:T(8,128)(2,1)S(1)}, bf16[256,256]{1,0:T(8,128)(2,1)S(1)}, u32[]{:S(2)}, u32[]{:S(2)}) collective-permute-start(bf16[256,256]{1,0:T(8,128)(2,1)S(1)} %shard_map.94.refs_0_), channel_id=1, source_target_pairs={{0,1},{1,0},{2,3},{3,2},{4,5},{5,4},{6,7},{7,6},{8,9},{9,8},{10,11... | collective-permute-start | bytes 393224 | tf_op jit(solution)/shard_map/ppermute | solution.py:336
  65.3 2.0 %collective-permute-done.22.refs_1_ = bf16[256,256]{1,0:T(8,128)(2,1)S(1)} collective-permute-done((bf16[256,256]{1,0:T(8,128)(2,1)S(1)}, bf16[256,256]{1,0:T(8,128)(2,1)S(1)}, u32[]{:S(2)}, u32[]{:S(2)}) %collective-permute-start.22) | collective-permute-done | bytes 131104 | tf_op jit(solution)/shard_map/ppermute | solution.py:336
  67.4 4.7 %collective-permute-start.23 = (bf16[256,256]{1,0:T(8,128)(2,1)S(1)}, bf16[256,256]{1,0:T(8,128)(2,1)S(1)}, u32[]{:S(2)}, u32[]{:S(2)}) collective-permute-start(bf16[256,256]{1,0:T(8,128)(2,1)S(1)} %shard_map.95.refs_0_), channel_id=1, source_target_pairs={{0,2},{1,3},{2,0},{3,1},{4,6},{5,7},{6,4},{7,5},{8,10},{9,11},{10,... | collective-permute-start | bytes 393224 | tf_op jit(solution)/shard_map/ppermute | solution.py:336
  72.1 2.7 %collective-permute-done.23.refs_1_ = bf16[256,256]{1,0:T(8,128)(2,1)S(1)} collective-permute-done((bf16[256,256]{1,0:T(8,128)(2,1)S(1)}, bf16[256,256]{1,0:T(8,128)(2,1)S(1)}, u32[]{:S(2)}, u32[]{:S(2)}) %collective-permute-start.23) | collective-permute-done | bytes 131104 | tf_op jit(solution)/shard_map/ppermute | solution.py:336
  74.7 1.7 %collective-permute-start.19 = (bf16[512,256]{1,0:T(8,128)(2,1)S(1)}, bf16[512,256]{1,0:T(8,128)(2,1)S(1)}, u32[]{:S(2)}, u32[]{:S(2)}) collective-permute-start(bf16[512,256]{1,0:T(8,128)(2,1)S(1)} %get-tuple-element.57), channel_id=1, source_target_pairs={{0,28},{4,0},{8,4},{12,8},{16,12},{20,16},{24,20},{28,24},{1,29},{... | collective-permute-start | bytes 786440 | tf_op jit(solution)/shard_map/ppermute | solution.py:28
  76.5 2.5 %shard_map.97 = (bf16[256,256]{1,0:T(8,128)(2,1)S(1)}, bf16[256,256]{1,0:T(8,128)(2,1)S(1)}, bf16[256,256]{1,0:T(8,128)(2,1)S(1)}, bf16[256,256]{1,0:T(8,128)(2,1)S(1)}) custom-call(bf16[272,256]{1,0:T(8,128)(2,1)S(1)} %get-tuple-element.36.refs_1_.refs_0_, bf16[272,256]{1,0:T(8,128)(2,1)S(1)} %collective-permute-done.6.refs_1_, ...), custom_call_target="tpu_custom_call" | custom-call | flops 1073741824 | bytes 3145728 | tf_op jit(solution)/shard_map/pallas_call | solution.py:67
  79.5 1.6 %collective-permute-start.25 = (bf16[256,256]{1,0:T(8,128)(2,1)S(1)}, bf16[256,256]{1,0:T(8,128)(2,1)S(1)}, u32[]{:S(2)}, u32[]{:S(2)}) collective-permute-start(bf16[256,256]{1,0:T(8,128)(2,1)S(1)} %get-tuple-element.59.refs_8_), channel_id=1, source_target_pairs={{0,192},{64,0},{128,64},{192,128},{1,193},{65,1},{129,65},{193,129... | collective-permute-start | bytes 393224 | tf_op jit(solution)/shard_map/ppermute | solution.py:28
  83.4 3.1 %collective-permute-done.26.refs_6_ = bf16[256,256]{1,0:T(8,128)(2,1)S(1)} collective-permute-done((bf16[256,256]{1,0:T(8,128)(2,1)S(1)}, bf16[256,256]{1,0:T(8,128)(2,1)S(1)}, u32[]{:S(2)}, u32[]{:S(2)}) %collective-permute-start.26) | collective-permute-done | bytes 131104 | tf_op jit(solution)/shard_map/ppermute | solution.py:28
  86.5 1.3 %collective-permute-done.27.refs_7_ = bf16[256,256]{1,0:T(8,128)(2,1)S(1)} collective-permute-done((bf16[256,256]{1,0:T(8,128)(2,1)S(1)}, bf16[256,256]{1,0:T(8,128)(2,1)S(1)}, u32[]{:S(2)}, u32[]{:S(2)}) %collective-permute-start.27) | collective-permute-done | bytes 131104 | tf_op jit(solution)/shard_map/ppermute | solution.py:28
  89.7 12.1 %collective-permute-done.28 = bf16[512,256]{1,0:T(8,128)(2,1)S(1)} collective-permute-done((bf16[512,256]{1,0:T(8,128)(2,1)S(1)}, bf16[512,256]{1,0:T(8,128)(2,1)S(1)}, u32[]{:S(2)}, u32[]{:S(2)}) %collective-permute-start.28) | collective-permute-done | bytes 262176 | tf_op jit(solution)/shard_map/ppermute | solution.py:481
  (60 shorter events, 13.3 us)
Async XLA Ops:
  2.7 18.5 %copy-start.4 = (bf16[1,32,1,128,128]{4,3,2,1,0:T(8,128)(2,1)S(1)}, bf16[1,32,1,128,128]{4,3,2,1,0:T(8,128)(2,1)}, u32[]{:S(2)}) copy-start(bf16[1,32,1,128,128]{4,3,2,1,0:T(8,128)(2,1)} %param.13) | copy-start | bytes 3145732
  2.7 18.5 %copy-start.6 = (s32[1,32,1]{1,2,0:T(1,128)S(1)}, s32[1,32,1]{1,2,0:T(1,128)}, u32[]{:S(2)}) copy-start(s32[1,32,1]{1,2,0:T(1,128)} %param.14) | copy-start | bytes 388
  2.7 8.9 %collective-permute-start.6 = (bf16[272,256]{1,0:T(8,128)(2,1)S(1)}, bf16[272,256]{1,0:T(8,128)(2,1)S(1)}, u32[]{:S(2)}, u32[]{:S(2)}) collective-permute-start(bf16[272,256]{1,0:T(8,128)(2,1)S(1)} %get-tuple-element.44), channel_id=1, source_target_pairs={{0,64},{64,128},{128,192},{192,0},{1,65},{65,129},{129,193},{193,1... | collective-permute-start | bytes 417800 | tf_op jit(solution)/shard_map/ppermute | solution.py:28
  4.8 20.7 %collective-permute-start = (bf16[1024,256]{1,0:T(8,128)(2,1)S(1)}, bf16[1024,256]{1,0:T(8,128)(2,1)S(1)}, u32[]{:S(2)}, u32[]{:S(2)}) collective-permute-start(bf16[1024,256]{1,0:T(8,128)(2,1)S(1)} %get-tuple-element.35.refs_2_), channel_id=1, source_target_pairs={{0,1},{1,2},{2,3},{3,0},{4,5},{5,6},{6,7},{7,4},{8,9},{9,10},{10,1... | collective-permute-start | bytes 1572872 | tf_op jit(solution)/shard_map/ppermute | solution.py:28
  6.1 19.4 %collective-permute-start.1 = (bf16[1024,256]{1,0:T(8,128)(2,1)S(1)}, bf16[1024,256]{1,0:T(8,128)(2,1)S(1)}, u32[]{:S(2)}, u32[]{:S(2)}) collective-permute-start(bf16[1024,256]{1,0:T(8,128)(2,1)S(1)} %get-tuple-element.38), channel_id=1, source_target_pairs={{0,3},{1,0},{2,1},{3,2},{4,7},{5,4},{6,5},{7,6},{8,11},{9,8},{10,9... | collective-permute-start | bytes 1572872 | tf_op jit(solution)/shard_map/ppermute | solution.py:28
  7.5 23.5 %collective-permute-start.2 = (bf16[1024,256]{1,0:T(8,128)(2,1)S(1)}, bf16[1024,256]{1,0:T(8,128)(2,1)S(1)}, u32[]{:S(2)}, u32[]{:S(2)}) collective-permute-start(bf16[1024,256]{1,0:T(8,128)(2,1)S(1)} %get-tuple-element.39), channel_id=1, source_target_pairs={{0,2},{1,3},{2,0},{3,1},{4,6},{5,7},{6,4},{7,5},{8,10},{9,11},{10,... | collective-permute-start | bytes 1572872 | tf_op jit(solution)/shard_map/ppermute | solution.py:28
  9.2 5.4 %collective-permute-start.7 = (bf16[272,256]{1,0:T(8,128)(2,1)S(1)}, bf16[272,256]{1,0:T(8,128)(2,1)S(1)}, u32[]{:S(2)}, u32[]{:S(2)}) collective-permute-start(bf16[272,256]{1,0:T(8,128)(2,1)S(1)} %get-tuple-element.45), channel_id=1, source_target_pairs={{0,128},{64,192},{128,0},{192,64},{1,129},{65,193},{129,1},{193,65... | collective-permute-start | bytes 417800 | tf_op jit(solution)/shard_map/ppermute | solution.py:28
  11.6 5.3 %collective-permute-start.8 = (bf16[272,256]{1,0:T(8,128)(2,1)S(1)}, bf16[272,256]{1,0:T(8,128)(2,1)S(1)}, u32[]{:S(2)}, u32[]{:S(2)}) collective-permute-start(bf16[272,256]{1,0:T(8,128)(2,1)S(1)} %get-tuple-element.46), channel_id=1, source_target_pairs={{0,192},{64,0},{128,64},{192,128},{1,193},{65,1},{129,65},{193,129... | collective-permute-start | bytes 417800 | tf_op jit(solution)/shard_map/ppermute | solution.py:28
  19.5 6.0 %collective-permute-start.9 = (bf16[256,256]{1,0:T(8,128)(2,1)S(1)}, bf16[256,256]{1,0:T(8,128)(2,1)S(1)}, u32[]{:S(2)}, u32[]{:S(2)}) collective-permute-start(bf16[256,256]{1,0:T(8,128)(2,1)S(1)} %shard_map.85.refs_0_.refs_6_), channel_id=1, source_target_pairs={{0,4},{4,0},{8,12},{12,8},{16,20},{20,16},{24,28},{28,24},{1,5},{5... | collective-permute-start | bytes 393224 | tf_op jit(solution)/shard_map/ppermute | solution.py:336
  31.1 9.0 %collective-permute-start.10 = (bf16[768,256]{1,0:T(8,128)(2,1)S(1)}, bf16[768,256]{1,0:T(8,128)(2,1)S(1)}, u32[]{:S(2)}, u32[]{:S(2)}) collective-permute-start(bf16[768,256]{1,0:T(8,128)(2,1)S(1)} %get-tuple-element.47.refs_5_), channel_id=1, source_target_pairs={{0,64},{64,0},{128,192},{192,128},{1,65},{65,1},{129,193},{193,129... | collective-permute-start | bytes 1179656 | tf_op jit(solution)/shard_map/ppermute | solution.py:160
  32.4 10.7 %collective-permute-start.3 = (bf16[512,256]{1,0:T(8,128)(2,1)S(1)}, bf16[512,256]{1,0:T(8,128)(2,1)S(1)}, u32[]{:S(2)}, u32[]{:S(2)}) collective-permute-start(bf16[512,256]{1,0:T(8,128)(2,1)S(1)} %get-tuple-element.40.refs_5_), channel_id=1, source_target_pairs={{0,1},{1,2},{2,3},{3,0},{4,5},{5,6},{6,7},{7,4},{8,9},{9,10},{10,1... | collective-permute-start | bytes 786440 | tf_op jit(solution)/shard_map/ppermute | solution.py:28
  33.0 6.6 %collective-permute-start.11 = (bf16[256,256]{1,0:T(8,128)(2,1)S(1)}, bf16[256,256]{1,0:T(8,128)(2,1)S(1)}, u32[]{:S(2)}, u32[]{:S(2)}) collective-permute-start(bf16[256,256]{1,0:T(8,128)(2,1)S(1)} %shard_map.86.refs_3_.refs_0_), channel_id=1, source_target_pairs={{0,8},{4,12},{8,0},{12,4},{16,24},{20,28},{24,16},{28,20},{1,9},{5... | collective-permute-start | bytes 393224 | tf_op jit(solution)/shard_map/ppermute | solution.py:336
  35.9 12.1 %collective-permute-start.14 = (bf16[768,256]{1,0:T(8,128)(2,1)S(1)}, bf16[768,256]{1,0:T(8,128)(2,1)S(1)}, u32[]{:S(2)}, u32[]{:S(2)}) collective-permute-start(bf16[768,256]{1,0:T(8,128)(2,1)S(1)} %get-tuple-element.53.refs_5_), channel_id=1, source_target_pairs={{0,192},{192,0},{64,128},{128,64},{1,193},{193,1},{65,129},{129,65... | collective-permute-start | bytes 1179656 | tf_op jit(solution)/shard_map/ppermute | solution.py:160
  37.5 9.9 %collective-permute-start.4 = (bf16[512,256]{1,0:T(8,128)(2,1)S(1)}, bf16[512,256]{1,0:T(8,128)(2,1)S(1)}, u32[]{:S(2)}, u32[]{:S(2)}) collective-permute-start(bf16[512,256]{1,0:T(8,128)(2,1)S(1)} %get-tuple-element.41), channel_id=1, source_target_pairs={{0,3},{1,0},{2,1},{3,2},{4,7},{5,4},{6,5},{7,6},{8,11},{9,8},{10,9... | collective-permute-start | bytes 786440 | tf_op jit(solution)/shard_map/ppermute | solution.py:28
  39.6 7.8 %collective-permute-start.5 = (bf16[512,256]{1,0:T(8,128)(2,1)S(1)}, bf16[512,256]{1,0:T(8,128)(2,1)S(1)}, u32[]{:S(2)}, u32[]{:S(2)}) collective-permute-start(bf16[512,256]{1,0:T(8,128)(2,1)S(1)} %get-tuple-element.42), channel_id=1, source_target_pairs={{0,2},{1,3},{2,0},{3,1},{4,6},{5,7},{6,4},{7,5},{8,10},{9,11},{10,... | collective-permute-start | bytes 786440 | tf_op jit(solution)/shard_map/ppermute | solution.py:28
  40.7 10.3 %collective-permute-start.15 = (bf16[512,256]{1,0:T(8,128)(2,1)S(1)}, bf16[512,256]{1,0:T(8,128)(2,1)S(1)}, u32[]{:S(2)}, u32[]{:S(2)}) collective-permute-start(bf16[512,256]{1,0:T(8,128)(2,1)S(1)} %get-tuple-element.48.refs_3_), channel_id=1, source_target_pairs={{0,4},{4,8},{8,12},{12,16},{16,20},{20,24},{24,28},{28,0},{1,5},{5... | collective-permute-start | bytes 786440 | tf_op jit(solution)/shard_map/ppermute | solution.py:28
  43.1 8.0 %collective-permute-start.16 = (bf16[512,256]{1,0:T(8,128)(2,1)S(1)}, bf16[512,256]{1,0:T(8,128)(2,1)S(1)}, u32[]{:S(2)}, u32[]{:S(2)}) collective-permute-start(bf16[512,256]{1,0:T(8,128)(2,1)S(1)} %get-tuple-element.54), channel_id=1, source_target_pairs={{0,28},{4,0},{8,4},{12,8},{16,12},{20,16},{24,20},{28,24},{1,29},{... | collective-permute-start | bytes 786440 | tf_op jit(solution)/shard_map/ppermute | solution.py:28
  47.4 29.0 %copy-start.5 = (bf16[1,32,64,256]{3,2,1,0:T(8,128)(2,1)S(1)}, bf16[1,32,64,256]{3,2,1,0:T(8,128)(2,1)}, u32[]{:S(2)}) copy-start(bf16[1,32,64,256]{3,2,1,0:T(8,128)(2,1)} %param.12) | copy-start | bytes 3145732
  47.5 17.0 %collective-permute-start.13 = (bf16[768,256]{1,0:T(8,128)(2,1)S(1)}, bf16[768,256]{1,0:T(8,128)(2,1)S(1)}, u32[]{:S(2)}, u32[]{:S(2)}) collective-permute-start(bf16[768,256]{1,0:T(8,128)(2,1)S(1)} %get-tuple-element.51.refs_5_), channel_id=1, source_target_pairs={{0,64},{64,0},{128,192},{192,128},{1,65},{65,1},{129,193},{193,129... | collective-permute-start | bytes 1179656 | tf_op jit(solution)/shard_map/ppermute | solution.py:160
  51.8 12.7 %collective-permute-start.17 = (bf16[512,256]{1,0:T(8,128)(2,1)S(1)}, bf16[512,256]{1,0:T(8,128)(2,1)S(1)}, u32[]{:S(2)}, u32[]{:S(2)}) collective-permute-start(bf16[512,256]{1,0:T(8,128)(2,1)S(1)} %get-tuple-element.55), channel_id=1, source_target_pairs={{0,4},{4,8},{8,12},{12,16},{16,20},{20,24},{24,28},{28,0},{1,5},{5... | collective-permute-start | bytes 786440 | tf_op jit(solution)/shard_map/ppermute | solution.py:28
  51.9 12.7 %collective-permute-start.18 = (bf16[512,256]{1,0:T(8,128)(2,1)S(1)}, bf16[512,256]{1,0:T(8,128)(2,1)S(1)}, u32[]{:S(2)}, u32[]{:S(2)}) collective-permute-start(bf16[512,256]{1,0:T(8,128)(2,1)S(1)} %get-tuple-element.56), channel_id=1, source_target_pairs={{0,28},{4,0},{8,4},{12,8},{16,12},{20,16},{24,20},{28,24},{1,29},{... | collective-permute-start | bytes 786440 | tf_op jit(solution)/shard_map/ppermute | solution.py:28
  55.0 8.1 %collective-permute-start.21 = (bf16[256,256]{1,0:T(8,128)(2,1)S(1)}, bf16[256,256]{1,0:T(8,128)(2,1)S(1)}, u32[]{:S(2)}, u32[]{:S(2)}) collective-permute-start(bf16[256,256]{1,0:T(8,128)(2,1)S(1)} %shard_map.89.refs_7_.refs_0_), channel_id=1, source_target_pairs={{0,16},{4,20},{8,24},{12,28},{16,0},{20,4},{24,8},{28,12},{1,17},{... | collective-permute-start | bytes 393224 | tf_op jit(solution)/shard_map/ppermute | solution.py:336
  58.8 20.1 %collective-permute-start.12 = (bf16[768,256]{1,0:T(8,128)(2,1)S(1)}, bf16[768,256]{1,0:T(8,128)(2,1)S(1)}, u32[]{:S(2)}, u32[]{:S(2)}) collective-permute-start(bf16[768,256]{1,0:T(8,128)(2,1)S(1)} %get-tuple-element.49.refs_5_), channel_id=1, source_target_pairs={{0,192},{192,0},{64,128},{128,64},{1,193},{193,1},{65,129},{129,65... | collective-permute-start | bytes 1179656 | tf_op jit(solution)/shard_map/ppermute | solution.py:160
  63.1 4.2 %collective-permute-start.22 = (bf16[256,256]{1,0:T(8,128)(2,1)S(1)}, bf16[256,256]{1,0:T(8,128)(2,1)S(1)}, u32[]{:S(2)}, u32[]{:S(2)}) collective-permute-start(bf16[256,256]{1,0:T(8,128)(2,1)S(1)} %shard_map.94.refs_0_), channel_id=1, source_target_pairs={{0,1},{1,0},{2,3},{3,2},{4,5},{5,4},{6,7},{7,6},{8,9},{9,8},{10,11... | collective-permute-start | bytes 393224 | tf_op jit(solution)/shard_map/ppermute | solution.py:336
  65.2 13.7 %collective-permute-start.20 = (bf16[512,256]{1,0:T(8,128)(2,1)S(1)}, bf16[512,256]{1,0:T(8,128)(2,1)S(1)}, u32[]{:S(2)}, u32[]{:S(2)}) collective-permute-start(bf16[512,256]{1,0:T(8,128)(2,1)S(1)} %get-tuple-element.58.refs_7_), channel_id=1, source_target_pairs={{0,4},{4,8},{8,12},{12,16},{16,20},{20,24},{24,28},{28,0},{1,5},{5... | collective-permute-start | bytes 786440 | tf_op jit(solution)/shard_map/ppermute | solution.py:28
  67.4 7.3 %collective-permute-start.23 = (bf16[256,256]{1,0:T(8,128)(2,1)S(1)}, bf16[256,256]{1,0:T(8,128)(2,1)S(1)}, u32[]{:S(2)}, u32[]{:S(2)}) collective-permute-start(bf16[256,256]{1,0:T(8,128)(2,1)S(1)} %shard_map.95.refs_0_), channel_id=1, source_target_pairs={{0,2},{1,3},{2,0},{3,1},{4,6},{5,7},{6,4},{7,5},{8,10},{9,11},{10,... | collective-permute-start | bytes 393224 | tf_op jit(solution)/shard_map/ppermute | solution.py:336
  74.7 7.8 %collective-permute-start.19 = (bf16[512,256]{1,0:T(8,128)(2,1)S(1)}, bf16[512,256]{1,0:T(8,128)(2,1)S(1)}, u32[]{:S(2)}, u32[]{:S(2)}) collective-permute-start(bf16[512,256]{1,0:T(8,128)(2,1)S(1)} %get-tuple-element.57), channel_id=1, source_target_pairs={{0,28},{4,0},{8,4},{12,8},{16,12},{20,16},{24,20},{28,24},{1,29},{... | collective-permute-start | bytes 786440 | tf_op jit(solution)/shard_map/ppermute | solution.py:28
  79.4 8.4 %collective-permute-start.24 = (bf16[512,256]{1,0:T(8,128)(2,1)S(1)}, bf16[512,256]{1,0:T(8,128)(2,1)S(1)}, u32[]{:S(2)}, u32[]{:S(2)}) collective-permute-start(bf16[512,256]{1,0:T(8,128)(2,1)S(1)} %shard_map.98.refs_8_), channel_id=1, source_target_pairs={{0,4},{4,8},{8,12},{12,16},{16,20},{20,24},{24,28},{28,0},{1,5},{5... | collective-permute-start | bytes 786440 | tf_op jit(solution)/shard_map/ppermute | solution.py:28
  79.5 3.9 %collective-permute-start.25 = (bf16[256,256]{1,0:T(8,128)(2,1)S(1)}, bf16[256,256]{1,0:T(8,128)(2,1)S(1)}, u32[]{:S(2)}, u32[]{:S(2)}) collective-permute-start(bf16[256,256]{1,0:T(8,128)(2,1)S(1)} %get-tuple-element.59.refs_8_), channel_id=1, source_target_pairs={{0,192},{64,0},{128,64},{192,128},{1,193},{65,1},{129,65},{193,129... | collective-permute-start | bytes 393224 | tf_op jit(solution)/shard_map/ppermute | solution.py:28
  81.1 5.4 %collective-permute-start.26 = (bf16[256,256]{1,0:T(8,128)(2,1)S(1)}, bf16[256,256]{1,0:T(8,128)(2,1)S(1)}, u32[]{:S(2)}, u32[]{:S(2)}) collective-permute-start(bf16[256,256]{1,0:T(8,128)(2,1)S(1)} %get-tuple-element.61), channel_id=1, source_target_pairs={{0,128},{64,192},{128,0},{192,64},{1,129},{65,193},{129,1},{193,65... | collective-permute-start | bytes 393224 | tf_op jit(solution)/shard_map/ppermute | solution.py:28
  82.2 5.6 %collective-permute-start.27 = (bf16[256,256]{1,0:T(8,128)(2,1)S(1)}, bf16[256,256]{1,0:T(8,128)(2,1)S(1)}, u32[]{:S(2)}, u32[]{:S(2)}) collective-permute-start(bf16[256,256]{1,0:T(8,128)(2,1)S(1)} %get-tuple-element.62), channel_id=1, source_target_pairs={{0,64},{64,128},{128,192},{192,0},{1,65},{65,129},{129,193},{193,1... | collective-permute-start | bytes 393224 | tf_op jit(solution)/shard_map/ppermute | solution.py:28
  88.4 13.4 %collective-permute-start.28 = (bf16[512,256]{1,0:T(8,128)(2,1)S(1)}, bf16[512,256]{1,0:T(8,128)(2,1)S(1)}, u32[]{:S(2)}, u32[]{:S(2)}) collective-permute-start(bf16[512,256]{1,0:T(8,128)(2,1)S(1)} %get-tuple-element.63), channel_id=1, source_target_pairs={{0,32},{1,33},{2,34},{3,35},{4,36},{5,37},{6,38},{7,39},{8,40},{9,... | collective-permute-start | bytes 786440 | tf_op jit(solution)/shard_map/ppermute | solution.py:481
  (4 other events, 29.4 us)

commit v2 on v1

--- a/solution.py
+++ b/solution.py
@@ -131,20 +131,30 @@
     return got[:3], got[3:]
 
 
-def join_kernel(base, a_ref, b_ref, c_ref, *outs):
-    for gi, out in enumerate(outs):
+def join_kernel(base, halves, a_ref, b_ref, c_ref, *outs):
+    pos = 0
+    for gi, split in enumerate(halves):
         for ki, ref in enumerate((a_ref, b_ref, c_ref)):
-            rows = slice(base + gi * TILE, base + (gi + 1) * TILE)
-            out[ki * TILE : (ki + 1) * TILE, :] = ref[rows, :]
-
-
-def join(got, base, after=()):
-    return call(
-        functools.partial(join_kernel, base),
+            first = base + gi * TILE
+            if split:
+                for side in range(2):
+                    rows = slice(first + side * BLK, first + (side + 1) * BLK)
+                    outs[pos + side][ki * BLK : (ki + 1) * BLK, :] = ref[rows, :]
+            else:
+                outs[pos][ki * TILE : (ki + 1) * TILE, :] = ref[first : first + TILE, :]
+        pos += 2 if split else 1
+
+
+def join(got, base, halves, after=()):
+    dims = []
+    for split in halves:
+        dims += [(3 * BLK, TILE)] * 2 if split else [(3 * TILE, TILE)]
+    return call(
+        functools.partial(join_kernel, base, halves),
         tuple(got),
         [whole(got[0].shape)] * 3,
-        [shape((3 * TILE, TILE))] * 2,
-        [whole((3 * TILE, TILE))] * 2,
+        [shape(d) for d in dims],
+        [whole(d) for d in dims],
         [],
         (0, 3 << 20),
         4,
@@ -160,11 +170,23 @@
     return lax.ppermute(value, "pool", pairs)
 
 
-def project_kernel(which, has_in, own_ref, x_ref, p0, p1, p2, mine_ref, other_ref, *refs):
+def stacked(refs):
+    if len(refs) == 1:
+        return refs[0][...]
+    low, high = refs
+    pieces = []
+    for ki in range(3):
+        rows = slice(ki * BLK, (ki + 1) * BLK)
+        pieces += [low[rows, :], high[rows, :]]
+    return jnp.concatenate(pieces, axis=0)
+
+
+def project_kernel(which, has_in, parts, own_ref, x_ref, p0, p1, p2, *refs):
     n = len(which)
+    even = parity() == 0
+    mine, other = stacked(refs[:parts]), stacked(refs[parts : 2 * parts])
+    refs = refs[2 * parts :]
     carried, outs = (refs[:n], refs[n:]) if has_in else ((None,) * n, refs)
-    even = parity() == 0
-    mine, other = mine_ref[...], other_ref[...]
     lhs = jnp.concatenate([x_ref[...]] + [peer[0:ROWS, :] for peer in (p0, p1, p2)], axis=1)
     for c_ref, out, ti in zip(carried, outs, which):
         remote = lax.select(even, mine, other) if ti == 0 else lax.select(even, other, mine)
@@ -177,13 +199,13 @@
 
 def project(which, own, features, first_got, mine, other, carried, after=(), out_dtype=BF16):
     half = (ROWS, WIDTH)
-    n = len(which)
-    return call(
-        functools.partial(project_kernel, which, bool(carried)),
-        (own, features, *first_got, mine, other, *carried),
+    n, parts = len(which), len(mine)
+    return call(
+        functools.partial(project_kernel, which, bool(carried), parts),
+        (own, features, *first_got, *mine, *other, *carried),
         [whole(half)] * 2
         + [whole(first_got[0].shape)] * 3
-        + [whole((3 * TILE, TILE))] * 2
+        + [whole(mine[0].shape)] * (2 * parts)
         + [whole(half)] * len(carried),
         [shape((ROWS, TILE), out_dtype)] * n,
         [whole((ROWS, TILE))] * n,
@@ -443,38 +465,40 @@
     places = diagonal_block_index[0][:, 0]
     ids = row_variant_index.reshape(1, ROWS)
 
-    first, (own0, own1) = pack((0, 1), weight, features)
+    first, (own0,) = pack((0,), weight, features)
     got = [shift(value, Y, hop) for value, hop in zip(first, HOPS)]
     sent = dispatch(ids, features, (first[0],))
     items = [sent[0]] + [shift(sent[k], "pool", k) for k in (1, 2, 3)]
-    second, (own2, own3) = pack((2, 3), weight, None, (sent[0],))
+    second, (own1, own2, own3) = pack((1, 2, 3), weight, None, (sent[0],))
     later = [shift(value, Y, hop) for value, hop in zip(second, HOPS)]
     low = down(items, down_factor, (second[0],))
     low1 = exchanged_sum(low, Z, 1)
-    blocks = block_terms(items, mats, places, (low,))
+    mine0 = join(got, ROWS, (True,), (low,))
+    other0 = (shift(mine0[0], "pool", 1), shift(mine0[1], "pool", -1))
     low2 = exchanged_sum(low1, Z, 2)
-    mine0, mine1 = join(got, ROWS, (low1, blocks))
-    other0 = swapped(mine0, False)
-    other1 = swapped(mine1, True)
+    plus, minus = project((0, 1), own0, features, got, mine0, other0, (), (low1,))
+    carried = (shift(plus, Z, 1), shift(minus, Z, -1))
     low3 = exchanged_sum(low2, Z, 4)
-    plus, minus = project((0, 1), own0, features, got, mine0, other0, (), (low2,))
-    carried = (shift(plus, Z, 1), shift(minus, Z, -1))
-    mine2, mine3 = join(later, 0, (plus,))
+    *mine1, mine2, mine3 = join(later, 0, (True, False, False), (plus,))
+    other1 = (shift(mine1[0], "pool", 1), shift(mine1[1], "pool", -1))
     other2 = swapped(mine2, False)
     other3 = swapped(mine3, True)
-    low4 = exchanged_sum(low3, Y, 1)
     plus, minus = project((0, 1), own1, features, got, mine1, other1, carried)
     carried = (shift(plus, Z, 1), shift(minus, Z, -1))
+    blocks = block_terms(items, mats, places, (plus,))
+    low4 = exchanged_sum(low3, Y, 1, (blocks,))
     low5 = exchanged_sum(low4, Y, 2)
-    plus, minus = project((0, 1), own2, features, got, mine2, other2, carried)
+    plus, minus = project((0, 1), own2, features, got, (mine2,), (other2,), carried)
     carried = (shift(plus, Z, 1), shift(minus, Z, -1))
     served = up(items, low5, up_factor, blocks, (plus,))
     returned = [served[0]] + [shift(served[k], "pool", -k) for k in (1, 2, 3)]
     (plus,) = project(
-        (0,), own3, features, got, mine3, other3, carried[:1], (served[1],)
+        (0,), own3, features, got, (mine3,), (other3,), carried[:1], (served[1],)
     )
     arrived = shift(plus, Z, 1)
-    (own,) = project((1,), own3, features, got, mine3, other3, carried[1:], (plus,), F32)
+    (own,) = project(
+        (1,), own3, features, got, (mine3,), (other3,), carried[1:], (plus,), F32
+    )
     plus = arrived
 
     first_out, branch = combine(ids, hidden_input, own, plus, returned)

time: 103 us -> 108 us (1.049)
  waiting for transfers between devices: 35.7 us -> 40 us
    ppermute x19 -> x23, starting transfers between devices: 27.8 us -> 34.2 us  [shift(): lax.ppermute(value, axis, [(i, (i + steps) % count) for i in range(count)])]
    ppermute x19 -> x23, waiting for transfers between devices: 16 us -> 21.1 us  [shift(): lax.ppermute(value, axis, [(i, (i + steps) % count) for i in range(count)])]
    ppermute x4 -> x2, starting transfers between devices: 4.95 us -> 1.89 us  [swapped(): return lax.ppermute(value, 'pool', pairs)]
    ppermute x5, starting transfers between devices: 14.6 us -> 12.3 us  [exchanged_sum(): other = lax.ppermute(value, axis, [(i, i ^ bit) for i in range(count)])]
    ppermute x1, waiting for transfers between devices: 12.1 us -> 10.5 us  [steps(): carried = lax.ppermute(first_out, 'section', [(0, 1)])]
  transfers between devices with their start and end apart: 29 -> 31, of which waited for: 12 -> 12; matrix products, arithmetic and copies ran while one was open for 0% -> 0% of each run, Pallas kernels for 14% -> 13%
where the time goes in v2:
time: 108 us
  starting transfers between devices  49.6 us (46%)
  waiting for transfers between devices  40 us (37%)
  Pallas kernels  17.2 us (16%)
    ppermute x23, starting transfers between devices, shift(): lax.ppermute(value, axis, [(i, (i + steps) % count) for i in range(count)])  34.2 us
    ppermute x23, waiting for transfers between devices, shift(): lax.ppermute(value, axis, [(i, (i + steps) % count) for i in range(count)])  21.1 us
    pallas_call x19, Pallas kernels, call(): pl.pallas_call(body, out_shape=outs, in_specs=list(in_specs) + [ANY] * m,...  17.2 us
    ppermute x5, starting transfers between devices, exchanged_sum(): other = lax.ppermute(value, axis, [(i, i ^ bit) for i in range(count)])  12.3 us
    ppermute x1, waiting for transfers between devices, steps(): carried = lax.ppermute(first_out, 'section', [(0, 1)])  10.5 us
    ppermute x5, waiting for transfers between devices, exchanged_sum(): other = lax.ppermute(value, axis, [(i, i ^ bit) for i in range(count)])  8.37 us
  transfers between devices with their start and end apart: 31, of which 12 were waited for; matrix products, arithmetic and copies ran while one was open for 0% of the time, Pallas kernels for 13%

profile of v2, /device:TPU:1, one launch (start us, length us, event | category | flops | bytes accessed | tf_op | source)
XLA Modules:
  0.0 107.9 jit_solution(6185040186925067266)
XLA Ops:
  0.0 1.5 %shard_map.82 = (bf16[768,256]{1,0:T(8,128)(2,1)S(1)}, bf16[768,256]{1,0:T(8,128)(2,1)S(1)}, bf16[768,256]{1,0:T(8,128)(2,1)S(1)}, bf16[512,256]{1,0:T(8,128)(2,1)S(1)}) custom-call(bf16[256,8192]{1,0:T(8,128)(2,1)} %bitcast.22, bf16[512,256]{1,0:T(8,128)(2,1)} %bitcast.9), custom_call_target="tpu_custom_call" | custom-call | bytes 1179648 | tf_op jit(solution)/shard_map/pallas_call | solution.py:67
  2.4 2.1 %collective-permute-start.6 = (bf16[272,256]{1,0:T(8,128)(2,1)S(1)}, bf16[272,256]{1,0:T(8,128)(2,1)S(1)}, u32[]{:S(2)}, u32[]{:S(2)}) collective-permute-start(bf16[272,256]{1,0:T(8,128)(2,1)S(1)} %get-tuple-element.46), channel_id=1, source_target_pairs={{0,64},{64,128},{128,192},{192,0},{1,65},{65,129},{129,193},{193,1... | collective-permute-start | bytes 417800 | tf_op jit(solution)/shard_map/ppermute | solution.py:28
  7.3 1.6 %collective-permute-start.2 = (bf16[768,256]{1,0:T(8,128)(2,1)S(1)}, bf16[768,256]{1,0:T(8,128)(2,1)S(1)}, u32[]{:S(2)}, u32[]{:S(2)}) collective-permute-start(bf16[768,256]{1,0:T(8,128)(2,1)S(1)} %get-tuple-element.41), channel_id=1, source_target_pairs={{0,2},{1,3},{2,0},{3,1},{4,6},{5,7},{6,4},{7,5},{8,10},{9,11},{10,... | collective-permute-start | bytes 1179656 | tf_op jit(solution)/shard_map/ppermute | solution.py:28
  8.9 2.4 %collective-permute-start.7 = (bf16[272,256]{1,0:T(8,128)(2,1)S(1)}, bf16[272,256]{1,0:T(8,128)(2,1)S(1)}, u32[]{:S(2)}, u32[]{:S(2)}) collective-permute-start(bf16[272,256]{1,0:T(8,128)(2,1)S(1)} %get-tuple-element.47), channel_id=1, source_target_pairs={{0,128},{64,192},{128,0},{192,64},{1,129},{65,193},{129,1},{193,65... | collective-permute-start | bytes 417800 | tf_op jit(solution)/shard_map/ppermute | solution.py:28
  12.5 1.7 %shard_map.84 = (bf16[768,256]{1,0:T(8,128)(2,1)S(1)}, bf16[768,256]{1,0:T(8,128)(2,1)S(1)}, bf16[768,256]{1,0:T(8,128)(2,1)S(1)}, bf16[512,256]{1,0:T(8,128)(2,...) custom-call(bf16[256,8192]{1,0:T(8,128)(2,1)} %bitcast.23, ...), custom_call_target="tpu_custom_call" | custom-call | bytes 1179648 | tf_op jit(solution)/shard_map/pallas_call | solution.py:67
  14.3 2.3 %collective-permute-done.8.refs_3_ = bf16[272,256]{1,0:T(8,128)(2,1)S(1)} collective-permute-done((bf16[272,256]{1,0:T(8,128)(2,1)S(1)}, bf16[272,256]{1,0:T(8,128)(2,1)S(1)}, u32[]{:S(2)}, u32[]{:S(2)}) %collective-permute-start.8) | collective-permute-done | bytes 139296 | tf_op jit(solution)/shard_map/ppermute | solution.py:28
  16.7 2.5 %shard_map.85.refs_3_.refs_0_ = bf16[256,256]{1,0:T(8,128)(2,1)S(1)} custom-call(bf16[272,256]{1,0:T(8,128)(2,1)S(1)} %get-tuple-element.38.refs_1_.refs_0_, bf16[272,256]{1,0:T(8,128)(2,1)S(1)} %collective-permute-done.6.refs_1_, bf16[272,256]{1,0:T(8,128)(2,1)S(1)} %collective-permute-done.7.refs_2_, bf16[272,256]{1,0:T(8,128)(2,1)S(1)} %collective-permute-done.8.refs_3_, ...), custom_call_target="tpu_custom_call" | custom-call | flops 1073741824 | bytes 2097152 | tf_op jit(solution)/shard_map/pallas_call | solution.py:67
  19.2 1.7 %collective-permute-start.11 = (bf16[256,256]{1,0:T(8,128)(2,1)S(1)}, bf16[256,256]{1,0:T(8,128)(2,1)S(1)}, u32[]{:S(2)}, u32[]{:S(2)}) collective-permute-start(bf16[256,256]{1,0:T(8,128)(2,1)S(1)} %shard_map.85.refs_3_.refs_0_), channel_id=1, source_target_pairs={{0,4},{4,0},{8,12},{12,8},{16,20},{20,16},{24,28},{28,24},{1,5},{5... | collective-permute-start | bytes 393224 | tf_op jit(solution)/shard_map/ppermute | solution.py:358
  21.3 2.3 %collective-permute-start.4 = (bf16[768,256]{1,0:T(8,128)(2,1)S(1)}, bf16[768,256]{1,0:T(8,128)(2,1)S(1)}, u32[]{:S(2)}, u32[]{:S(2)}) collective-permute-start(bf16[768,256]{1,0:T(8,128)(2,1)S(1)} %get-tuple-element.43), channel_id=1, source_target_pairs={{0,3},{1,0},{2,1},{3,2},{4,7},{5,4},{6,5},{7,6},{8,11},{9,8},{10,9... | collective-permute-start | bytes 1179656 | tf_op jit(solution)/shard_map/ppermute | solution.py:28
  25.2 1.5 %collective-permute-start.10 = (bf16[384,256]{1,0:T(8,128)(2,1)S(1)}, bf16[384,256]{1,0:T(8,128)(2,1)S(1)}, u32[]{:S(2)}, u32[]{:S(2)}) collective-permute-start(bf16[384,256]{1,0:T(8,128)(2,1)S(1)} %get-tuple-element.50.refs_6_), channel_id=1, source_target_pairs={{0,192},{64,0},{128,64},{192,128},{1,193},{65,1},{129,65},{193,129... | collective-permute-start | bytes 589832 | tf_op jit(solution)/shard_map/ppermute | solution.py:28
  26.7 3.3 %collective-permute-done.10.refs_8_ = bf16[384,256]{1,0:T(8,128)(2,1)S(1)} collective-permute-done((bf16[384,256]{1,0:T(8,128)(2,1)S(1)}, bf16[384,256]{1,0:T(8,128)(2,1)S(1)}, u32[]{:S(2)}, u32[]{:S(2)}) %collective-permute-start.10) | collective-permute-done | bytes 196640 | tf_op jit(solution)/shard_map/ppermute | solution.py:28
  30.1 2.7 %collective-permute-done.9.refs_7_ = bf16[384,256]{1,0:T(8,128)(2,1)S(1)} collective-permute-done((bf16[384,256]{1,0:T(8,128)(2,1)S(1)}, bf16[384,256]{1,0:T(8,128)(2,1)S(1)}, u32[]{:S(2)}, u32[]{:S(2)}) %collective-permute-start.9) | collective-permute-done | bytes 196640 | tf_op jit(solution)/shard_map/ppermute | solution.py:28
  33.5 1.7 %collective-permute-start.16 = (bf16[512,256]{1,0:T(8,128)(2,1)S(1)}, bf16[512,256]{1,0:T(8,128)(2,1)S(1)}, u32[]{:S(2)}, u32[]{:S(2)}) collective-permute-start(bf16[512,256]{1,0:T(8,128)(2,1)S(1)} %get-tuple-element.51.refs_3_), channel_id=1, source_target_pairs={{0,4},{4,8},{8,12},{12,16},{16,20},{20,24},{24,28},{28,0},{1,5},{5... | collective-permute-start | bytes 786440 | tf_op jit(solution)/shard_map/ppermute | solution.py:28
  35.2 4.0 %collective-permute-start.17 = (bf16[512,256]{1,0:T(8,128)(2,1)S(1)}, bf16[512,256]{1,0:T(8,128)(2,1)S(1)}, u32[]{:S(2)}, u32[]{:S(2)}) collective-permute-start(bf16[512,256]{1,0:T(8,128)(2,1)S(1)} %get-tuple-element.58), channel_id=1, source_target_pairs={{0,28},{4,0},{8,4},{12,8},{16,12},{20,16},{24,20},{28,24},{1,29},{... | collective-permute-start | bytes 786440 | tf_op jit(solution)/shard_map/ppermute | solution.py:28
  39.2 2.8 %collective-permute-done.5.refs_2_ = bf16[768,256]{1,0:T(8,128)(2,1)S(1)} collective-permute-done((bf16[768,256]{1,0:T(8,128)(2,1)S(1)}, bf16[768,256]{1,0:T(8,128)(2,1)S(1)}, u32[]{:S(2)}, u32[]{:S(2)}) %collective-permute-start.5) | collective-permute-done | bytes 393248 | tf_op jit(solution)/shard_map/ppermute | solution.py:28
  45.0 3.1 %collective-permute-done.14.refs_7_ = bf16[384,256]{1,0:T(8,128)(2,1)S(1)} collective-permute-done((bf16[384,256]{1,0:T(8,128)(2,1)S(1)}, bf16[384,256]{1,0:T(8,128)(2,1)S(1)}, u32[]{:S(2)}, u32[]{:S(2)}) %collective-permute-start.14) | collective-permute-done | bytes 196640 | tf_op jit(solution)/shard_map/ppermute | solution.py:28
  48.1 3.0 %collective-permute-start.22 = (bf16[256,256]{1,0:T(8,128)(2,1)S(1)}, bf16[256,256]{1,0:T(8,128)(2,1)S(1)}, u32[]{:S(2)}, u32[]{:S(2)}) collective-permute-start(bf16[256,256]{1,0:T(8,128)(2,1)S(1)} %shard_map.87.refs_9_.refs_0_), channel_id=1, source_target_pairs={{0,8},{4,12},{8,0},{12,4},{16,24},{20,28},{24,16},{28,20},{1,9},{5... | collective-permute-start | bytes 393224 | tf_op jit(solution)/shard_map/ppermute | solution.py:358
  51.8 1.9 %collective-permute-start.18 = (bf16[512,256]{1,0:T(8,128)(2,1)S(1)}, bf16[512,256]{1,0:T(8,128)(2,1)S(1)}, u32[]{:S(2)}, u32[]{:S(2)}) collective-permute-start(bf16[512,256]{1,0:T(8,128)(2,1)S(1)} %get-tuple-element.59.refs_6_), channel_id=1, source_target_pairs={{0,4},{4,8},{8,12},{12,16},{16,20},{20,24},{24,28},{28,0},{1,5},{5... | collective-permute-start | bytes 786440 | tf_op jit(solution)/shard_map/ppermute | solution.py:28
  53.7 2.0 %collective-permute-start.19 = (bf16[512,256]{1,0:T(8,128)(2,1)S(1)}, bf16[512,256]{1,0:T(8,128)(2,1)S(1)}, u32[]{:S(2)}, u32[]{:S(2)}) collective-permute-start(bf16[512,256]{1,0:T(8,128)(2,1)S(1)} %get-tuple-element.60), channel_id=1, source_target_pairs={{0,28},{4,0},{8,4},{12,8},{16,12},{20,16},{24,20},{28,24},{1,29},{... | collective-permute-start | bytes 786440 | tf_op jit(solution)/shard_map/ppermute | solution.py:28
  55.7 5.6 %collective-permute-start.23 = (bf16[256,256]{1,0:T(8,128)(2,1)S(1)}, bf16[256,256]{1,0:T(8,128)(2,1)S(1)}, u32[]{:S(2)}, u32[]{:S(2)}) collective-permute-start(bf16[256,256]{1,0:T(8,128)(2,1)S(1)} %shard_map.92.refs_0_), channel_id=1, source_target_pairs={{0,16},{4,20},{8,24},{12,28},{16,0},{20,4},{24,8},{28,12},{1,17},{... | collective-permute-start | bytes 393224 | tf_op jit(solution)/shard_map/ppermute | solution.py:358
  61.3 4.1 %collective-permute-done.23.refs_1_ = bf16[256,256]{1,0:T(8,128)(2,1)S(1)} collective-permute-done((bf16[256,256]{1,0:T(8,128)(2,1)S(1)}, bf16[256,256]{1,0:T(8,128)(2,1)S(1)}, u32[]{:S(2)}, u32[]{:S(2)}) %collective-permute-start.23) | collective-permute-done | bytes 131104 | tf_op jit(solution)/shard_map/ppermute | solution.py:358
  65.8 1.9 %collective-permute-start.12 = (bf16[768,256]{1,0:T(8,128)(2,1)S(1)}, bf16[768,256]{1,0:T(8,128)(2,1)S(1)}, u32[]{:S(2)}, u32[]{:S(2)}) collective-permute-start(bf16[768,256]{1,0:T(8,128)(2,1)S(1)} %get-tuple-element.52.refs_5_), channel_id=1, source_target_pairs={{0,192},{192,0},{64,128},{128,64},{1,193},{193,1},{65,129},{129,65... | collective-permute-start | bytes 1179656 | tf_op jit(solution)/shard_map/ppermute | solution.py:170
  68.5 1.9 %collective-permute-start.21 = (bf16[512,256]{1,0:T(8,128)(2,1)S(1)}, bf16[512,256]{1,0:T(8,128)(2,1)S(1)}, u32[]{:S(2)}, u32[]{:S(2)}) collective-permute-start(bf16[512,256]{1,0:T(8,128)(2,1)S(1)} %get-tuple-element.62.refs_7_), channel_id=1, source_target_pairs={{0,4},{4,8},{8,12},{12,16},{16,20},{20,24},{24,28},{28,0},{1,5},{5... | collective-permute-start | bytes 786440 | tf_op jit(solution)/shard_map/ppermute | solution.py:28
  70.4 4.3 %shard_map.94.refs_2_.refs_6_ = f32[4,256,256]{2,1,0:T(8,128)S(1)} custom-call(bf16[272,256]{1,0:T(8,128)(2,1)S(1)} %get-tuple-element.38.refs_1_.refs_0_, bf16[272,256]{1,0:T(8,128)(2,1)S(1)} %collective-permute-done.6.refs_1_, bf16[272,256]{1,0:T(8,128)(2,1)S(1)} %collective-permute-done.7.refs_2_, bf16[272,256]{1,0:T(8,128)(2,1)S(1)} %collective-permute-done.8.refs_3_, ...), custom_call_target="tpu_custom_call" | custom-call | flops 2147483648 | bytes 3145728 | tf_op jit(solution)/shard_map/pallas_call | solution.py:67
  74.7 1.6 %collective-permute-start.25 = (bf16[256,256]{1,0:T(8,128)(2,1)S(1)}, bf16[256,256]{1,0:T(8,128)(2,1)S(1)}, u32[]{:S(2)}, u32[]{:S(2)}) collective-permute-start(bf16[256,256]{1,0:T(8,128)(2,1)S(1)} %shard_map.95.refs_0_), channel_id=1, source_target_pairs={{0,2},{1,3},{2,0},{3,1},{4,6},{5,7},{6,4},{7,5},{8,10},{9,11},{10,... | collective-permute-start | bytes 393224 | tf_op jit(solution)/shard_map/ppermute | solution.py:358
  76.2 4.3 %collective-permute-done.25.refs_1_ = bf16[256,256]{1,0:T(8,128)(2,1)S(1)} collective-permute-done((bf16[256,256]{1,0:T(8,128)(2,1)S(1)}, bf16[256,256]{1,0:T(8,128)(2,1)S(1)}, u32[]{:S(2)}, u32[]{:S(2)}) %collective-permute-start.25) | collective-permute-done | bytes 131104 | tf_op jit(solution)/shard_map/ppermute | solution.py:358
  80.6 2.1 %collective-permute-start.20 = (bf16[512,256]{1,0:T(8,128)(2,1)S(1)}, bf16[512,256]{1,0:T(8,128)(2,1)S(1)}, u32[]{:S(2)}, u32[]{:S(2)}) collective-permute-start(bf16[512,256]{1,0:T(8,128)(2,1)S(1)} %get-tuple-element.61), channel_id=1, source_target_pairs={{0,28},{4,0},{8,4},{12,8},{16,12},{20,16},{24,20},{28,24},{1,29},{... | collective-permute-start | bytes 786440 | tf_op jit(solution)/shard_map/ppermute | solution.py:28
  82.7 2.5 %shard_map.97 = (bf16[256,256]{1,0:T(8,128)(2,1)S(1)}, bf16[256,256]{1,0:T(8,128)(2,1)S(1)}, bf16[256,256]{1,0:T(8,128)(2,1)S(1)}, bf16[256,256]{1,0:T(8,128)(2,1)S(1)}) custom-call(bf16[272,256]{1,0:T(8,128)(2,1)S(1)} %get-tuple-element.38.refs_1_.refs_0_, bf16[272,256]{1,0:T(8,128)(2,1)S(1)} %collective-permute-done.6.refs_1_, ...), custom_call_target="tpu_custom_call" | custom-call | flops 1073741824 | bytes 3145728 | tf_op jit(solution)/shard_map/pallas_call | solution.py:67
  85.7 2.3 %collective-permute-start.27 = (bf16[256,256]{1,0:T(8,128)(2,1)S(1)}, bf16[256,256]{1,0:T(8,128)(2,1)S(1)}, u32[]{:S(2)}, u32[]{:S(2)}) collective-permute-start(bf16[256,256]{1,0:T(8,128)(2,1)S(1)} %get-tuple-element.63.refs_8_), channel_id=1, source_target_pairs={{0,192},{64,0},{128,64},{192,128},{1,193},{65,1},{129,65},{193,129... | collective-permute-start | bytes 393224 | tf_op jit(solution)/shard_map/ppermute | solution.py:28
  89.2 2.2 %collective-permute-done.27.refs_5_ = bf16[256,256]{1,0:T(8,128)(2,1)S(1)} collective-permute-done((bf16[256,256]{1,0:T(8,128)(2,1)S(1)}, bf16[256,256]{1,0:T(8,128)(2,1)S(1)}, u32[]{:S(2)}, u32[]{:S(2)}) %collective-permute-start.27) | collective-permute-done | bytes 131104 | tf_op jit(solution)/shard_map/ppermute | solution.py:28
  91.3 2.1 %collective-permute-done.28.refs_6_ = bf16[256,256]{1,0:T(8,128)(2,1)S(1)} collective-permute-done((bf16[256,256]{1,0:T(8,128)(2,1)S(1)}, bf16[256,256]{1,0:T(8,128)(2,1)S(1)}, u32[]{:S(2)}, u32[]{:S(2)}) %collective-permute-start.28) | collective-permute-done | bytes 131104 | tf_op jit(solution)/shard_map/ppermute | solution.py:28
  96.6 10.5 %collective-permute-done.30 = bf16[512,256]{1,0:T(8,128)(2,1)S(1)} collective-permute-done((bf16[512,256]{1,0:T(8,128)(2,1)S(1)}, bf16[512,256]{1,0:T(8,128)(2,1)S(1)}, u32[]{:S(2)}, u32[]{:S(2)}) %collective-permute-start.30) | collective-permute-done | bytes 262176 | tf_op jit(solution)/shard_map/ppermute | solution.py:505
  (64 shorter events, 18.2 us)
Async XLA Ops:
  2.4 8.9 %collective-permute-start.6 = (bf16[272,256]{1,0:T(8,128)(2,1)S(1)}, bf16[272,256]{1,0:T(8,128)(2,1)S(1)}, u32[]{:S(2)}, u32[]{:S(2)}) collective-permute-start(bf16[272,256]{1,0:T(8,128)(2,1)S(1)} %get-tuple-element.46), channel_id=1, source_target_pairs={{0,64},{64,128},{128,192},{192,0},{1,65},{65,129},{129,193},{193,1... | collective-permute-start | bytes 417800 | tf_op jit(solution)/shard_map/ppermute | solution.py:28
  4.5 16.8 %collective-permute-start = (bf16[768,256]{1,0:T(8,128)(2,1)S(1)}, bf16[768,256]{1,0:T(8,128)(2,1)S(1)}, u32[]{:S(2)}, u32[]{:S(2)}) collective-permute-start(bf16[768,256]{1,0:T(8,128)(2,1)S(1)} %get-tuple-element.37.refs_2_), channel_id=1, source_target_pairs={{0,1},{1,2},{2,3},{3,0},{4,5},{5,6},{6,7},{7,4},{8,9},{9,10},{10,1... | collective-permute-start | bytes 1179656 | tf_op jit(solution)/shard_map/ppermute | solution.py:28
  5.8 17.8 %collective-permute-start.1 = (bf16[768,256]{1,0:T(8,128)(2,1)S(1)}, bf16[768,256]{1,0:T(8,128)(2,1)S(1)}, u32[]{:S(2)}, u32[]{:S(2)}) collective-permute-start(bf16[768,256]{1,0:T(8,128)(2,1)S(1)} %get-tuple-element.40), channel_id=1, source_target_pairs={{0,3},{1,0},{2,1},{3,2},{4,7},{5,4},{6,5},{7,6},{8,11},{9,8},{10,9... | collective-permute-start | bytes 1179656 | tf_op jit(solution)/shard_map/ppermute | solution.py:28
  7.3 17.9 %collective-permute-start.2 = (bf16[768,256]{1,0:T(8,128)(2,1)S(1)}, bf16[768,256]{1,0:T(8,128)(2,1)S(1)}, u32[]{:S(2)}, u32[]{:S(2)}) collective-permute-start(bf16[768,256]{1,0:T(8,128)(2,1)S(1)} %get-tuple-element.41), channel_id=1, source_target_pairs={{0,2},{1,3},{2,0},{3,1},{4,6},{5,7},{6,4},{7,5},{8,10},{9,11},{10,... | collective-permute-start | bytes 1179656 | tf_op jit(solution)/shard_map/ppermute | solution.py:28
  8.9 5.4 %collective-permute-start.7 = (bf16[272,256]{1,0:T(8,128)(2,1)S(1)}, bf16[272,256]{1,0:T(8,128)(2,1)S(1)}, u32[]{:S(2)}, u32[]{:S(2)}) collective-permute-start(bf16[272,256]{1,0:T(8,128)(2,1)S(1)} %get-tuple-element.47), channel_id=1, source_target_pairs={{0,128},{64,192},{128,0},{192,64},{1,129},{65,193},{129,1},{193,65... | collective-permute-start | bytes 417800 | tf_op jit(solution)/shard_map/ppermute | solution.py:28
  11.4 5.3 %collective-permute-start.8 = (bf16[272,256]{1,0:T(8,128)(2,1)S(1)}, bf16[272,256]{1,0:T(8,128)(2,1)S(1)}, u32[]{:S(2)}, u32[]{:S(2)}) collective-permute-start(bf16[272,256]{1,0:T(8,128)(2,1)S(1)} %get-tuple-element.48), channel_id=1, source_target_pairs={{0,192},{64,0},{128,64},{192,128},{1,193},{65,1},{129,65},{193,129... | collective-permute-start | bytes 417800 | tf_op jit(solution)/shard_map/ppermute | solution.py:28
  19.2 7.5 %collective-permute-start.11 = (bf16[256,256]{1,0:T(8,128)(2,1)S(1)}, bf16[256,256]{1,0:T(8,128)(2,1)S(1)}, u32[]{:S(2)}, u32[]{:S(2)}) collective-permute-start(bf16[256,256]{1,0:T(8,128)(2,1)S(1)} %shard_map.85.refs_3_.refs_0_), channel_id=1, source_target_pairs={{0,4},{4,0},{8,12},{12,8},{16,20},{20,16},{24,28},{28,24},{1,5},{5... | collective-permute-start | bytes 393224 | tf_op jit(solution)/shard_map/ppermute | solution.py:358
  20.9 18.3 %collective-permute-start.3 = (bf16[768,256]{1,0:T(8,128)(2,1)S(1)}, bf16[768,256]{1,0:T(8,128)(2,1)S(1)}, u32[]{:S(2)}, u32[]{:S(2)}) collective-permute-start(bf16[768,256]{1,0:T(8,128)(2,1)S(1)} %get-tuple-element.42.refs_5_), channel_id=1, source_target_pairs={{0,1},{1,2},{2,3},{3,0},{4,5},{5,6},{6,7},{7,4},{8,9},{9,10},{10,1... | collective-permute-start | bytes 1179656 | tf_op jit(solution)/shard_map/ppermute | solution.py:28
  21.3 17.9 %collective-permute-start.4 = (bf16[768,256]{1,0:T(8,128)(2,1)S(1)}, bf16[768,256]{1,0:T(8,128)(2,1)S(1)}, u32[]{:S(2)}, u32[]{:S(2)}) collective-permute-start(bf16[768,256]{1,0:T(8,128)(2,1)S(1)} %get-tuple-element.43), channel_id=1, source_target_pairs={{0,3},{1,0},{2,1},{3,2},{4,7},{5,4},{6,5},{7,6},{8,11},{9,8},{10,9... | collective-permute-start | bytes 1179656 | tf_op jit(solution)/shard_map/ppermute | solution.py:28
  23.6 18.4 %collective-permute-start.5 = (bf16[768,256]{1,0:T(8,128)(2,1)S(1)}, bf16[768,256]{1,0:T(8,128)(2,1)S(1)}, u32[]{:S(2)}, u32[]{:S(2)}) collective-permute-start(bf16[768,256]{1,0:T(8,128)(2,1)S(1)} %get-tuple-element.44), channel_id=1, source_target_pairs={{0,2},{1,3},{2,0},{3,1},{4,6},{5,7},{6,4},{7,5},{8,10},{9,11},{10,... | collective-permute-start | bytes 1179656 | tf_op jit(solution)/shard_map/ppermute | solution.py:28
  25.2 4.9 %collective-permute-start.10 = (bf16[384,256]{1,0:T(8,128)(2,1)S(1)}, bf16[384,256]{1,0:T(8,128)(2,1)S(1)}, u32[]{:S(2)}, u32[]{:S(2)}) collective-permute-start(bf16[384,256]{1,0:T(8,128)(2,1)S(1)} %get-tuple-element.50.refs_6_), channel_id=1, source_target_pairs={{0,192},{64,0},{128,64},{192,128},{1,193},{65,1},{129,65},{193,129... | collective-permute-start | bytes 589832 | tf_op jit(solution)/shard_map/ppermute | solution.py:28
  26.7 6.0 %collective-permute-start.9 = (bf16[384,256]{1,0:T(8,128)(2,1)S(1)}, bf16[384,256]{1,0:T(8,128)(2,1)S(1)}, u32[]{:S(2)}, u32[]{:S(2)}) collective-permute-start(bf16[384,256]{1,0:T(8,128)(2,1)S(1)} %get-tuple-element.49.refs_5_), channel_id=1, source_target_pairs={{0,64},{64,128},{128,192},{192,0},{1,65},{65,129},{129,193},{193,1... | collective-permute-start | bytes 589832 | tf_op jit(solution)/shard_map/ppermute | solution.py:28
  33.4 36.9 %copy-start.4 = (bf16[1,32,1,128,128]{4,3,2,1,0:T(8,128)(2,1)S(1)}, bf16[1,32,1,128,128]{4,3,2,1,0:T(8,128)(2,1)}, u32[]{:S(2)}) copy-start(bf16[1,32,1,128,128]{4,3,2,1,0:T(8,128)(2,1)} %param.13) | copy-start | bytes 3145732
  33.5 17.6 %collective-permute-start.16 = (bf16[512,256]{1,0:T(8,128)(2,1)S(1)}, bf16[512,256]{1,0:T(8,128)(2,1)S(1)}, u32[]{:S(2)}, u32[]{:S(2)}) collective-permute-start(bf16[512,256]{1,0:T(8,128)(2,1)S(1)} %get-tuple-element.51.refs_3_), channel_id=1, source_target_pairs={{0,4},{4,8},{8,12},{12,16},{16,20},{20,24},{24,28},{28,0},{1,5},{5... | collective-permute-start | bytes 786440 | tf_op jit(solution)/shard_map/ppermute | solution.py:28
  35.2 15.9 %collective-permute-start.17 = (bf16[512,256]{1,0:T(8,128)(2,1)S(1)}, bf16[512,256]{1,0:T(8,128)(2,1)S(1)}, u32[]{:S(2)}, u32[]{:S(2)}) collective-permute-start(bf16[512,256]{1,0:T(8,128)(2,1)S(1)} %get-tuple-element.58), channel_id=1, source_target_pairs={{0,28},{4,0},{8,4},{12,8},{16,12},{20,16},{24,20},{28,24},{1,29},{... | collective-permute-start | bytes 786440 | tf_op jit(solution)/shard_map/ppermute | solution.py:28
  42.1 6.0 %collective-permute-start.14 = (bf16[384,256]{1,0:T(8,128)(2,1)S(1)}, bf16[384,256]{1,0:T(8,128)(2,1)S(1)}, u32[]{:S(2)}, u32[]{:S(2)}) collective-permute-start(bf16[384,256]{1,0:T(8,128)(2,1)S(1)} %get-tuple-element.56.refs_5_), channel_id=1, source_target_pairs={{0,64},{64,128},{128,192},{192,0},{1,65},{65,129},{129,193},{193,1... | collective-permute-start | bytes 589832 | tf_op jit(solution)/shard_map/ppermute | solution.py:28
  43.5 7.5 %collective-permute-start.15 = (bf16[384,256]{1,0:T(8,128)(2,1)S(1)}, bf16[384,256]{1,0:T(8,128)(2,1)S(1)}, u32[]{:S(2)}, u32[]{:S(2)}) collective-permute-start(bf16[384,256]{1,0:T(8,128)(2,1)S(1)} %get-tuple-element.57.refs_6_), channel_id=1, source_target_pairs={{0,192},{64,0},{128,64},{192,128},{1,193},{65,1},{129,65},{193,129... | collective-permute-start | bytes 589832 | tf_op jit(solution)/shard_map/ppermute | solution.py:28
  45.0 22.7 %collective-permute-start.13 = (bf16[768,256]{1,0:T(8,128)(2,1)S(1)}, bf16[768,256]{1,0:T(8,128)(2,1)S(1)}, u32[]{:S(2)}, u32[]{:S(2)}) collective-permute-start(bf16[768,256]{1,0:T(8,128)(2,1)S(1)} %get-tuple-element.54.refs_5_), channel_id=1, source_target_pairs={{0,64},{64,0},{128,192},{192,128},{1,65},{65,1},{129,193},{193,129... | collective-permute-start | bytes 1179656 | tf_op jit(solution)/shard_map/ppermute | solution.py:170
  48.1 7.6 %collective-permute-start.22 = (bf16[256,256]{1,0:T(8,128)(2,1)S(1)}, bf16[256,256]{1,0:T(8,128)(2,1)S(1)}, u32[]{:S(2)}, u32[]{:S(2)}) collective-permute-start(bf16[256,256]{1,0:T(8,128)(2,1)S(1)} %shard_map.87.refs_9_.refs_0_), channel_id=1, source_target_pairs={{0,8},{4,12},{8,0},{12,4},{16,24},{20,28},{24,16},{28,20},{1,9},{5... | collective-permute-start | bytes 393224 | tf_op jit(solution)/shard_map/ppermute | solution.py:358
  51.8 16.0 %collective-permute-start.18 = (bf16[512,256]{1,0:T(8,128)(2,1)S(1)}, bf16[512,256]{1,0:T(8,128)(2,1)S(1)}, u32[]{:S(2)}, u32[]{:S(2)}) collective-permute-start(bf16[512,256]{1,0:T(8,128)(2,1)S(1)} %get-tuple-element.59.refs_6_), channel_id=1, source_target_pairs={{0,4},{4,8},{8,12},{12,16},{16,20},{20,24},{24,28},{28,0},{1,5},{5... | collective-permute-start | bytes 786440 | tf_op jit(solution)/shard_map/ppermute | solution.py:28
  53.7 14.1 %collective-permute-start.19 = (bf16[512,256]{1,0:T(8,128)(2,1)S(1)}, bf16[512,256]{1,0:T(8,128)(2,1)S(1)}, u32[]{:S(2)}, u32[]{:S(2)}) collective-permute-start(bf16[512,256]{1,0:T(8,128)(2,1)S(1)} %get-tuple-element.60), channel_id=1, source_target_pairs={{0,28},{4,0},{8,4},{12,8},{16,12},{20,16},{24,20},{28,24},{1,29},{... | collective-permute-start | bytes 786440 | tf_op jit(solution)/shard_map/ppermute | solution.py:28
  55.7 9.7 %collective-permute-start.23 = (bf16[256,256]{1,0:T(8,128)(2,1)S(1)}, bf16[256,256]{1,0:T(8,128)(2,1)S(1)}, u32[]{:S(2)}, u32[]{:S(2)}) collective-permute-start(bf16[256,256]{1,0:T(8,128)(2,1)S(1)} %shard_map.92.refs_0_), channel_id=1, source_target_pairs={{0,16},{4,20},{8,24},{12,28},{16,0},{20,4},{24,8},{28,12},{1,17},{... | collective-permute-start | bytes 393224 | tf_op jit(solution)/shard_map/ppermute | solution.py:358
  65.4 9.2 %collective-permute-start.24 = (bf16[256,256]{1,0:T(8,128)(2,1)S(1)}, bf16[256,256]{1,0:T(8,128)(2,1)S(1)}, u32[]{:S(2)}, u32[]{:S(2)}) collective-permute-start(bf16[256,256]{1,0:T(8,128)(2,1)S(1)} %shard_map.93.refs_0_), channel_id=1, source_target_pairs={{0,1},{1,0},{2,3},{3,2},{4,5},{5,4},{6,7},{7,6},{8,9},{9,8},{10,11... | collective-permute-start | bytes 393224 | tf_op jit(solution)/shard_map/ppermute | solution.py:358
  65.8 19.3 %collective-permute-start.12 = (bf16[768,256]{1,0:T(8,128)(2,1)S(1)}, bf16[768,256]{1,0:T(8,128)(2,1)S(1)}, u32[]{:S(2)}, u32[]{:S(2)}) collective-permute-start(bf16[768,256]{1,0:T(8,128)(2,1)S(1)} %get-tuple-element.52.refs_5_), channel_id=1, source_target_pairs={{0,192},{192,0},{64,128},{128,64},{1,193},{193,1},{65,129},{129,65... | collective-permute-start | bytes 1179656 | tf_op jit(solution)/shard_map/ppermute | solution.py:170
  68.5 16.7 %collective-permute-start.21 = (bf16[512,256]{1,0:T(8,128)(2,1)S(1)}, bf16[512,256]{1,0:T(8,128)(2,1)S(1)}, u32[]{:S(2)}, u32[]{:S(2)}) collective-permute-start(bf16[512,256]{1,0:T(8,128)(2,1)S(1)} %get-tuple-element.62.refs_7_), channel_id=1, source_target_pairs={{0,4},{4,8},{8,12},{12,16},{16,20},{20,24},{24,28},{28,0},{1,5},{5... | collective-permute-start | bytes 786440 | tf_op jit(solution)/shard_map/ppermute | solution.py:28
  74.7 5.8 %collective-permute-start.25 = (bf16[256,256]{1,0:T(8,128)(2,1)S(1)}, bf16[256,256]{1,0:T(8,128)(2,1)S(1)}, u32[]{:S(2)}, u32[]{:S(2)}) collective-permute-start(bf16[256,256]{1,0:T(8,128)(2,1)S(1)} %shard_map.95.refs_0_), channel_id=1, source_target_pairs={{0,2},{1,3},{2,0},{3,1},{4,6},{5,7},{6,4},{7,5},{8,10},{9,11},{10,... | collective-permute-start | bytes 393224 | tf_op jit(solution)/shard_map/ppermute | solution.py:358
  80.6 8.2 %collective-permute-start.20 = (bf16[512,256]{1,0:T(8,128)(2,1)S(1)}, bf16[512,256]{1,0:T(8,128)(2,1)S(1)}, u32[]{:S(2)}, u32[]{:S(2)}) collective-permute-start(bf16[512,256]{1,0:T(8,128)(2,1)S(1)} %get-tuple-element.61), channel_id=1, source_target_pairs={{0,28},{4,0},{8,4},{12,8},{16,12},{20,16},{24,20},{28,24},{1,29},{... | collective-permute-start | bytes 786440 | tf_op jit(solution)/shard_map/ppermute | solution.py:28
  85.6 9.1 %collective-permute-start.26 = (bf16[512,256]{1,0:T(8,128)(2,1)S(1)}, bf16[512,256]{1,0:T(8,128)(2,1)S(1)}, u32[]{:S(2)}, u32[]{:S(2)}) collective-permute-start(bf16[512,256]{1,0:T(8,128)(2,1)S(1)} %shard_map.98.refs_8_), channel_id=1, source_target_pairs={{0,4},{4,8},{8,12},{12,16},{16,20},{20,24},{24,28},{28,0},{1,5},{5... | collective-permute-start | bytes 786440 | tf_op jit(solution)/shard_map/ppermute | solution.py:28
  85.7 5.6 %collective-permute-start.27 = (bf16[256,256]{1,0:T(8,128)(2,1)S(1)}, bf16[256,256]{1,0:T(8,128)(2,1)S(1)}, u32[]{:S(2)}, u32[]{:S(2)}) collective-permute-start(bf16[256,256]{1,0:T(8,128)(2,1)S(1)} %get-tuple-element.63.refs_8_), channel_id=1, source_target_pairs={{0,192},{64,0},{128,64},{192,128},{1,193},{65,1},{129,65},{193,129... | collective-permute-start | bytes 393224 | tf_op jit(solution)/shard_map/ppermute | solution.py:28
  88.0 5.4 %collective-permute-start.28 = (bf16[256,256]{1,0:T(8,128)(2,1)S(1)}, bf16[256,256]{1,0:T(8,128)(2,1)S(1)}, u32[]{:S(2)}, u32[]{:S(2)}) collective-permute-start(bf16[256,256]{1,0:T(8,128)(2,1)S(1)} %get-tuple-element.65), channel_id=1, source_target_pairs={{0,128},{64,192},{128,0},{192,64},{1,129},{65,193},{129,1},{193,65... | collective-permute-start | bytes 393224 | tf_op jit(solution)/shard_map/ppermute | solution.py:28
  88.7 6.1 %collective-permute-start.29 = (bf16[256,256]{1,0:T(8,128)(2,1)S(1)}, bf16[256,256]{1,0:T(8,128)(2,1)S(1)}, u32[]{:S(2)}, u32[]{:S(2)}) collective-permute-start(bf16[256,256]{1,0:T(8,128)(2,1)S(1)} %get-tuple-element.66), channel_id=1, source_target_pairs={{0,64},{64,128},{128,192},{192,0},{1,65},{65,129},{129,193},{193,1... | collective-permute-start | bytes 393224 | tf_op jit(solution)/shard_map/ppermute | solution.py:28
  95.3 11.8 %collective-permute-start.30 = (bf16[512,256]{1,0:T(8,128)(2,1)S(1)}, bf16[512,256]{1,0:T(8,128)(2,1)S(1)}, u32[]{:S(2)}, u32[]{:S(2)}) collective-permute-start(bf16[512,256]{1,0:T(8,128)(2,1)S(1)} %get-tuple-element.67), channel_id=1, source_target_pairs={{0,32},{1,33},{2,34},{3,35},{4,36},{5,37},{6,38},{7,39},{8,40},{9,... | collective-permute-start | bytes 786440 | tf_op jit(solution)/shard_map/ppermute | solution.py:505
  (6 other events, 78.6 us)

commit v3 on v2

--- a/solution.py
+++ b/solution.py
@@ -476,7 +476,8 @@
     mine0 = join(got, ROWS, (True,), (low,))
     other0 = (shift(mine0[0], "pool", 1), shift(mine0[1], "pool", -1))
     low2 = exchanged_sum(low1, Z, 2)
-    plus, minus = project((0, 1), own0, features, got, mine0, other0, (), (low1,))
+    blocks = block_terms(items, mats, places, (low1, mine0[0]))
+    plus, minus = project((0, 1), own0, features, got, mine0, other0, (), (blocks,))
     carried = (shift(plus, Z, 1), shift(minus, Z, -1))
     low3 = exchanged_sum(low2, Z, 4)
     *mine1, mine2, mine3 = join(later, 0, (True, False, False), (plus,))
@@ -485,8 +486,7 @@
     other3 = swapped(mine3, True)
     plus, minus = project((0, 1), own1, features, got, mine1, other1, carried)
     carried = (shift(plus, Z, 1), shift(minus, Z, -1))
-    blocks = block_terms(items, mats, places, (plus,))
-    low4 = exchanged_sum(low3, Y, 1, (blocks,))
+    low4 = exchanged_sum(low3, Y, 1)
     low5 = exchanged_sum(low4, Y, 2)
     plus, minus = project((0, 1), own2, features, got, (mine2,), (other2,), carried)
     carried = (shift(plus, Z, 1), shift(minus, Z, -1))

time: 108 us -> 107 us (level)
  waiting for transfers between devices: 40 us -> 35.2 us
  starting transfers between devices: 49.6 us -> 53.1 us
    ppermute x23, waiting for transfers between devices: 21.1 us -> 13.2 us  [shift(): lax.ppermute(value, axis, [(i, (i + steps) % count) for i in range(count)])]
    ppermute x5, starting transfers between devices: 12.3 us -> 15.2 us  [exchanged_sum(): other = lax.ppermute(value, axis, [(i, i ^ bit) for i in range(count)])]
    ppermute x23, starting transfers between devices: 34.2 us -> 36.4 us  [shift(): lax.ppermute(value, axis, [(i, (i + steps) % count) for i in range(count)])]
    ppermute x1, waiting for transfers between devices: 10.5 us -> 12.2 us  [steps(): carried = lax.ppermute(first_out, 'section', [(0, 1)])]
    ppermute x2, starting transfers between devices: 1.89 us -> 0.24 us  [swapped(): return lax.ppermute(value, 'pool', pairs)]
    ppermute x5, waiting for transfers between devices: 8.37 us -> 9.74 us  [exchanged_sum(): other = lax.ppermute(value, axis, [(i, i ^ bit) for i in range(count)])]
  transfers between devices with their start and end apart: 31 -> 31, of which waited for: 12 -> 11; matrix products, arithmetic and copies ran while one was open for 0% -> 0% of each run, Pallas kernels for 13% -> 13%
where the time goes in v3:
time: 107 us
  starting transfers between devices  53.1 us (50%)
  waiting for transfers between devices  35.2 us (33%)
  Pallas kernels  17.3 us (16%)
    ppermute x23, starting transfers between devices, shift(): lax.ppermute(value, axis, [(i, (i + steps) % count) for i in range(count)])  36.4 us
    pallas_call x19, Pallas kernels, call(): pl.pallas_call(body, out_shape=outs, in_specs=list(in_specs) + [ANY] * m,...  17.3 us
    ppermute x5, starting transfers between devices, exchanged_sum(): other = lax.ppermute(value, axis, [(i, i ^ bit) for i in range(count)])  15.2 us
    ppermute x23, waiting for transfers between devices, shift(): lax.ppermute(value, axis, [(i, (i + steps) % count) for i in range(count)])  13.2 us
    ppermute x1, waiting for transfers between devices, steps(): carried = lax.ppermute(first_out, 'section', [(0, 1)])  12.2 us
    ppermute x5, waiting for transfers between devices, exchanged_sum(): other = lax.ppermute(value, axis, [(i, i ^ bit) for i in range(count)])  9.74 us
  transfers between devices with their start and end apart: 31, of which 11 were waited for; matrix products, arithmetic and copies ran while one was open for 0% of the time, Pallas kernels for 13%

profile of v3, /device:TPU:1, one launch (start us, length us, event | category | flops | bytes accessed | tf_op | source)
XLA Modules:
  0.0 106.7 jit_solution(2770096813427880419)
XLA Ops:
  0.0 1.5 %shard_map.82 = (bf16[768,256]{1,0:T(8,128)(2,1)S(1)}, bf16[768,256]{1,0:T(8,128)(2,1)S(1)}, bf16[768,256]{1,0:T(8,128)(2,1)S(1)}, bf16[512,256]{1,0:T(8,128)(2,1)S(1)}) custom-call(bf16[256,8192]{1,0:T(8,128)(2,1)} %bitcast.22, bf16[512,256]{1,0:T(8,128)(2,1)} %bitcast.9), custom_call_target="tpu_custom_call" | custom-call | bytes 1179648 | tf_op jit(solution)/shard_map/pallas_call | solution.py:67
  2.4 2.1 %collective-permute-start.6 = (bf16[272,256]{1,0:T(8,128)(2,1)S(1)}, bf16[272,256]{1,0:T(8,128)(2,1)S(1)}, u32[]{:S(2)}, u32[]{:S(2)}) collective-permute-start(bf16[272,256]{1,0:T(8,128)(2,1)S(1)} %get-tuple-element.46), channel_id=1, source_target_pairs={{0,64},{64,128},{128,192},{192,0},{1,65},{65,129},{129,193},{193,1... | collective-permute-start | bytes 417800 | tf_op jit(solution)/shard_map/ppermute | solution.py:28
  5.8 2.5 %collective-permute-start.7 = (bf16[272,256]{1,0:T(8,128)(2,1)S(1)}, bf16[272,256]{1,0:T(8,128)(2,1)S(1)}, u32[]{:S(2)}, u32[]{:S(2)}) collective-permute-start(bf16[272,256]{1,0:T(8,128)(2,1)S(1)} %get-tuple-element.47), channel_id=1, source_target_pairs={{0,128},{64,192},{128,0},{192,64},{1,129},{65,193},{129,1},{193,65... | collective-permute-start | bytes 417800 | tf_op jit(solution)/shard_map/ppermute | solution.py:28
  9.5 1.4 %collective-permute-start.1 = (bf16[768,256]{1,0:T(8,128)(2,1)S(1)}, bf16[768,256]{1,0:T(8,128)(2,1)S(1)}, u32[]{:S(2)}, u32[]{:S(2)}) collective-permute-start(bf16[768,256]{1,0:T(8,128)(2,1)S(1)} %get-tuple-element.40), channel_id=1, source_target_pairs={{0,3},{1,0},{2,1},{3,2},{4,7},{5,4},{6,5},{7,6},{8,11},{9,8},{10,9... | collective-permute-start | bytes 1179656 | tf_op jit(solution)/shard_map/ppermute | solution.py:28
  10.9 1.7 %collective-permute-start.2 = (bf16[768,256]{1,0:T(8,128)(2,1)S(1)}, bf16[768,256]{1,0:T(8,128)(2,1)S(1)}, u32[]{:S(2)}, u32[]{:S(2)}) collective-permute-start(bf16[768,256]{1,0:T(8,128)(2,1)S(1)} %get-tuple-element.41), channel_id=1, source_target_pairs={{0,2},{1,3},{2,0},{3,1},{4,6},{5,7},{6,4},{7,5},{8,10},{9,11},{10,... | collective-permute-start | bytes 1179656 | tf_op jit(solution)/shard_map/ppermute | solution.py:28
  12.5 1.8 %shard_map.84 = (bf16[768,256]{1,0:T(8,128)(2,1)S(1)}, bf16[768,256]{1,0:T(8,128)(2,1)S(1)}, bf16[768,256]{1,0:T(8,128)(2,1)S(1)}, bf16[512,256]{1,0:T(8,128)(2,...) custom-call(bf16[256,8192]{1,0:T(8,128)(2,1)} %bitcast.23, ...), custom_call_target="tpu_custom_call" | custom-call | bytes 1179648 | tf_op jit(solution)/shard_map/pallas_call | solution.py:67
  14.4 2.5 %shard_map.85.refs_3_.refs_0_ = bf16[256,256]{1,0:T(8,128)(2,1)S(1)} custom-call(bf16[272,256]{1,0:T(8,128)(2,1)S(1)} %get-tuple-element.38.refs_1_.refs_0_, bf16[272,256]{1,0:T(8,128)(2,1)S(1)} %collective-permute-done.6.refs_1_, bf16[272,256]{1,0:T(8,128)(2,1)S(1)} %collective-permute-done.7.refs_2_, bf16[272,256]{1,0:T(8,128)(2,1)S(1)} %collective-permute-done.8.refs_3_, ...), custom_call_target="tpu_custom_call" | custom-call | flops 1073741824 | bytes 2097152 | tf_op jit(solution)/shard_map/pallas_call | solution.py:67
  16.9 1.7 %collective-permute-start.11 = (bf16[256,256]{1,0:T(8,128)(2,1)S(1)}, bf16[256,256]{1,0:T(8,128)(2,1)S(1)}, u32[]{:S(2)}, u32[]{:S(2)}) collective-permute-start(bf16[256,256]{1,0:T(8,128)(2,1)S(1)} %shard_map.85.refs_3_.refs_0_), channel_id=1, source_target_pairs={{0,4},{4,0},{8,12},{12,8},{16,20},{20,16},{24,28},{28,24},{1,5},{5... | collective-permute-start | bytes 393224 | tf_op jit(solution)/shard_map/ppermute | solution.py:358
  19.5 1.8 %collective-permute-done.11.refs_1_ = bf16[256,256]{1,0:T(8,128)(2,1)S(1)} collective-permute-done((bf16[256,256]{1,0:T(8,128)(2,1)S(1)}, bf16[256,256]{1,0:T(8,128)(2,1)S(1)}, u32[]{:S(2)}, u32[]{:S(2)}) %collective-permute-start.11) | collective-permute-done | bytes 131104 | tf_op jit(solution)/shard_map/ppermute | solution.py:358
  21.3 1.4 %collective-permute-start.4 = (bf16[768,256]{1,0:T(8,128)(2,1)S(1)}, bf16[768,256]{1,0:T(8,128)(2,1)S(1)}, u32[]{:S(2)}, u32[]{:S(2)}) collective-permute-start(bf16[768,256]{1,0:T(8,128)(2,1)S(1)} %get-tuple-element.43), channel_id=1, source_target_pairs={{0,3},{1,0},{2,1},{3,2},{4,7},{5,4},{6,5},{7,6},{8,11},{9,8},{10,9... | collective-permute-start | bytes 1179656 | tf_op jit(solution)/shard_map/ppermute | solution.py:28
  25.1 1.7 %collective-permute-start.10 = (bf16[384,256]{1,0:T(8,128)(2,1)S(1)}, bf16[384,256]{1,0:T(8,128)(2,1)S(1)}, u32[]{:S(2)}, u32[]{:S(2)}) collective-permute-start(bf16[384,256]{1,0:T(8,128)(2,1)S(1)} %get-tuple-element.50.refs_6_), channel_id=1, source_target_pairs={{0,192},{64,0},{128,64},{192,128},{1,193},{65,1},{129,65},{193,129... | collective-permute-start | bytes 589832 | tf_op jit(solution)/shard_map/ppermute | solution.py:28
  26.9 4.3 %shard_map.88.refs_9_.refs_6_ = f32[4,256,256]{2,1,0:T(8,128)S(1)} custom-call(bf16[272,256]{1,0:T(8,128)(2,1)S(1)} %get-tuple-element.38.refs_1_.refs_0_, bf16[272,256]{1,0:T(8,128)(2,1)S(1)} %collective-permute-done.6.refs_1_, bf16[272,256]{1,0:T(8,128)(2,1)S(1)} %collective-permute-done.7.refs_2_, bf16[272,256]{1,0:T(8,128)(2,1)S(1)} %collective-permute-done.8.refs_3_, ...), custom_call_target="tpu_custom_call" | custom-call | flops 2147483648 | bytes 3145728 | tf_op jit(solution)/shard_map/pallas_call | solution.py:67
  31.2 1.7 %collective-permute-done.9.refs_7_ = bf16[384,256]{1,0:T(8,128)(2,1)S(1)} collective-permute-done((bf16[384,256]{1,0:T(8,128)(2,1)S(1)}, bf16[384,256]{1,0:T(8,128)(2,1)S(1)}, u32[]{:S(2)}, u32[]{:S(2)}) %collective-permute-start.9) | collective-permute-done | bytes 196640 | tf_op jit(solution)/shard_map/ppermute | solution.py:28
  33.6 1.6 %collective-permute-start.16 = (bf16[512,256]{1,0:T(8,128)(2,1)S(1)}, bf16[512,256]{1,0:T(8,128)(2,1)S(1)}, u32[]{:S(2)}, u32[]{:S(2)}) collective-permute-start(bf16[512,256]{1,0:T(8,128)(2,1)S(1)} %get-tuple-element.51.refs_3_), channel_id=1, source_target_pairs={{0,4},{4,8},{8,12},{12,16},{16,20},{20,24},{24,28},{28,0},{1,5},{5... | collective-permute-start | bytes 786440 | tf_op jit(solution)/shard_map/ppermute | solution.py:28
  35.2 4.2 %collective-permute-start.17 = (bf16[512,256]{1,0:T(8,128)(2,1)S(1)}, bf16[512,256]{1,0:T(8,128)(2,1)S(1)}, u32[]{:S(2)}, u32[]{:S(2)}) collective-permute-start(bf16[512,256]{1,0:T(8,128)(2,1)S(1)} %get-tuple-element.58), channel_id=1, source_target_pairs={{0,28},{4,0},{8,4},{12,8},{16,12},{20,16},{24,20},{28,24},{1,29},{... | collective-permute-start | bytes 786440 | tf_op jit(solution)/shard_map/ppermute | solution.py:28
  39.4 2.5 %collective-permute-done.5.refs_2_ = bf16[768,256]{1,0:T(8,128)(2,1)S(1)} collective-permute-done((bf16[768,256]{1,0:T(8,128)(2,1)S(1)}, bf16[768,256]{1,0:T(8,128)(2,1)S(1)}, u32[]{:S(2)}, u32[]{:S(2)}) %collective-permute-start.5) | collective-permute-done | bytes 393248 | tf_op jit(solution)/shard_map/ppermute | solution.py:28
  42.0 1.4 %collective-permute-start.14 = (bf16[384,256]{1,0:T(8,128)(2,1)S(1)}, bf16[384,256]{1,0:T(8,128)(2,1)S(1)}, u32[]{:S(2)}, u32[]{:S(2)}) collective-permute-start(bf16[384,256]{1,0:T(8,128)(2,1)S(1)} %get-tuple-element.56.refs_5_), channel_id=1, source_target_pairs={{0,64},{64,128},{128,192},{192,0},{1,65},{65,129},{129,193},{193,1... | collective-permute-start | bytes 589832 | tf_op jit(solution)/shard_map/ppermute | solution.py:28
  44.9 3.0 %collective-permute-done.14.refs_7_ = bf16[384,256]{1,0:T(8,128)(2,1)S(1)} collective-permute-done((bf16[384,256]{1,0:T(8,128)(2,1)S(1)}, bf16[384,256]{1,0:T(8,128)(2,1)S(1)}, u32[]{:S(2)}, u32[]{:S(2)}) %collective-permute-start.14) | collective-permute-done | bytes 196640 | tf_op jit(solution)/shard_map/ppermute | solution.py:28
  47.8 3.1 %collective-permute-start.22 = (bf16[256,256]{1,0:T(8,128)(2,1)S(1)}, bf16[256,256]{1,0:T(8,128)(2,1)S(1)}, u32[]{:S(2)}, u32[]{:S(2)}) collective-permute-start(bf16[256,256]{1,0:T(8,128)(2,1)S(1)} %shard_map.87.refs_6_.refs_0_), channel_id=1, source_target_pairs={{0,8},{4,12},{8,0},{12,4},{16,24},{20,28},{24,16},{28,20},{1,9},{5... | collective-permute-start | bytes 393224 | tf_op jit(solution)/shard_map/ppermute | solution.py:358
  51.6 2.0 %collective-permute-start.18 = (bf16[512,256]{1,0:T(8,128)(2,1)S(1)}, bf16[512,256]{1,0:T(8,128)(2,1)S(1)}, u32[]{:S(2)}, u32[]{:S(2)}) collective-permute-start(bf16[512,256]{1,0:T(8,128)(2,1)S(1)} %get-tuple-element.59), channel_id=1, source_target_pairs={{0,4},{4,8},{8,12},{12,16},{16,20},{20,24},{24,28},{28,0},{1,5},{5... | collective-permute-start | bytes 786440 | tf_op jit(solution)/shard_map/ppermute | solution.py:28
  53.6 1.9 %collective-permute-start.19 = (bf16[512,256]{1,0:T(8,128)(2,1)S(1)}, bf16[512,256]{1,0:T(8,128)(2,1)S(1)}, u32[]{:S(2)}, u32[]{:S(2)}) collective-permute-start(bf16[512,256]{1,0:T(8,128)(2,1)S(1)} %get-tuple-element.60), channel_id=1, source_target_pairs={{0,28},{4,0},{8,4},{12,8},{16,12},{20,16},{24,20},{28,24},{1,29},{... | collective-permute-start | bytes 786440 | tf_op jit(solution)/shard_map/ppermute | solution.py:28
  55.6 5.6 %collective-permute-start.23 = (bf16[256,256]{1,0:T(8,128)(2,1)S(1)}, bf16[256,256]{1,0:T(8,128)(2,1)S(1)}, u32[]{:S(2)}, u32[]{:S(2)}) collective-permute-start(bf16[256,256]{1,0:T(8,128)(2,1)S(1)} %shard_map.93.refs_0_), channel_id=1, source_target_pairs={{0,16},{4,20},{8,24},{12,28},{16,0},{20,4},{24,8},{28,12},{1,17},{... | collective-permute-start | bytes 393224 | tf_op jit(solution)/shard_map/ppermute | solution.py:358
  61.3 3.9 %collective-permute-done.23.refs_1_ = bf16[256,256]{1,0:T(8,128)(2,1)S(1)} collective-permute-done((bf16[256,256]{1,0:T(8,128)(2,1)S(1)}, bf16[256,256]{1,0:T(8,128)(2,1)S(1)}, u32[]{:S(2)}, u32[]{:S(2)}) %collective-permute-start.23) | collective-permute-done | bytes 131104 | tf_op jit(solution)/shard_map/ppermute | solution.py:358
  65.3 3.5 %collective-permute-start.24 = (bf16[256,256]{1,0:T(8,128)(2,1)S(1)}, bf16[256,256]{1,0:T(8,128)(2,1)S(1)}, u32[]{:S(2)}, u32[]{:S(2)}) collective-permute-start(bf16[256,256]{1,0:T(8,128)(2,1)S(1)} %shard_map.94.refs_0_), channel_id=1, source_target_pairs={{0,1},{1,0},{2,3},{3,2},{4,5},{5,4},{6,7},{7,6},{8,9},{9,8},{10,11... | collective-permute-start | bytes 393224 | tf_op jit(solution)/shard_map/ppermute | solution.py:358
  69.5 3.7 %collective-permute-start.21 = (bf16[512,256]{1,0:T(8,128)(2,1)S(1)}, bf16[512,256]{1,0:T(8,128)(2,1)S(1)}, u32[]{:S(2)}, u32[]{:S(2)}) collective-permute-start(bf16[512,256]{1,0:T(8,128)(2,1)S(1)} %get-tuple-element.62.refs_7_), channel_id=1, source_target_pairs={{0,4},{4,8},{8,12},{12,16},{16,20},{20,24},{24,28},{28,0},{1,5},{5... | collective-permute-start | bytes 786440 | tf_op jit(solution)/shard_map/ppermute | solution.py:28
  73.2 1.4 %collective-permute-start.25 = (bf16[256,256]{1,0:T(8,128)(2,1)S(1)}, bf16[256,256]{1,0:T(8,128)(2,1)S(1)}, u32[]{:S(2)}, u32[]{:S(2)}) collective-permute-start(bf16[256,256]{1,0:T(8,128)(2,1)S(1)} %shard_map.95.refs_0_), channel_id=1, source_target_pairs={{0,2},{1,3},{2,0},{3,1},{4,6},{5,7},{6,4},{7,5},{8,10},{9,11},{10,... | collective-permute-start | bytes 393224 | tf_op jit(solution)/shard_map/ppermute | solution.py:358
  74.6 4.0 %collective-permute-done.25.refs_1_ = bf16[256,256]{1,0:T(8,128)(2,1)S(1)} collective-permute-done((bf16[256,256]{1,0:T(8,128)(2,1)S(1)}, bf16[256,256]{1,0:T(8,128)(2,1)S(1)}, u32[]{:S(2)}, u32[]{:S(2)}) %collective-permute-start.25) | collective-permute-done | bytes 131104 | tf_op jit(solution)/shard_map/ppermute | solution.py:358
  78.7 3.2 %collective-permute-start.20 = (bf16[512,256]{1,0:T(8,128)(2,1)S(1)}, bf16[512,256]{1,0:T(8,128)(2,1)S(1)}, u32[]{:S(2)}, u32[]{:S(2)}) collective-permute-start(bf16[512,256]{1,0:T(8,128)(2,1)S(1)} %get-tuple-element.61), channel_id=1, source_target_pairs={{0,28},{4,0},{8,4},{12,8},{16,12},{20,16},{24,20},{28,24},{1,29},{... | collective-permute-start | bytes 786440 | tf_op jit(solution)/shard_map/ppermute | solution.py:28
  81.9 2.5 %shard_map.97 = (bf16[256,256]{1,0:T(8,128)(2,1)S(1)}, bf16[256,256]{1,0:T(8,128)(2,1)S(1)}, bf16[256,256]{1,0:T(8,128)(2,1)S(1)}, bf16[256,256]{1,0:T(8,128)(2,1)S(1)}) custom-call(bf16[272,256]{1,0:T(8,128)(2,1)S(1)} %get-tuple-element.38.refs_1_.refs_0_, bf16[272,256]{1,0:T(8,128)(2,1)S(1)} %collective-permute-done.6.refs_1_, ...), custom_call_target="tpu_custom_call" | custom-call | flops 1073741824 | bytes 3145728 | tf_op jit(solution)/shard_map/pallas_call | solution.py:67
  86.9 1.9 %collective-permute-done.27.refs_5_ = bf16[256,256]{1,0:T(8,128)(2,1)S(1)} collective-permute-done((bf16[256,256]{1,0:T(8,128)(2,1)S(1)}, bf16[256,256]{1,0:T(8,128)(2,1)S(1)}, u32[]{:S(2)}, u32[]{:S(2)}) %collective-permute-start.27) | collective-permute-done | bytes 131104 | tf_op jit(solution)/shard_map/ppermute | solution.py:28
  88.8 1.7 %collective-permute-done.28.refs_6_ = bf16[256,256]{1,0:T(8,128)(2,1)S(1)} collective-permute-done((bf16[256,256]{1,0:T(8,128)(2,1)S(1)}, bf16[256,256]{1,0:T(8,128)(2,1)S(1)}, u32[]{:S(2)}, u32[]{:S(2)}) %collective-permute-start.28) | collective-permute-done | bytes 131104 | tf_op jit(solution)/shard_map/ppermute | solution.py:28
  93.7 12.2 %collective-permute-done.30 = bf16[512,256]{1,0:T(8,128)(2,1)S(1)} collective-permute-done((bf16[512,256]{1,0:T(8,128)(2,1)S(1)}, bf16[512,256]{1,0:T(8,128)(2,1)S(1)}, u32[]{:S(2)}, u32[]{:S(2)}) %collective-permute-start.30) | collective-permute-done | bytes 262176 | tf_op jit(solution)/shard_map/ppermute | solution.py:505
  (64 shorter events, 17.1 us)
Async XLA Ops:
  2.4 8.4 %collective-permute-start.6 = (bf16[272,256]{1,0:T(8,128)(2,1)S(1)}, bf16[272,256]{1,0:T(8,128)(2,1)S(1)}, u32[]{:S(2)}, u32[]{:S(2)}) collective-permute-start(bf16[272,256]{1,0:T(8,128)(2,1)S(1)} %get-tuple-element.46), channel_id=1, source_target_pairs={{0,64},{64,128},{128,192},{192,0},{1,65},{65,129},{129,193},{193,1... | collective-permute-start | bytes 417800 | tf_op jit(solution)/shard_map/ppermute | solution.py:28
  4.5 18.2 %collective-permute-start = (bf16[768,256]{1,0:T(8,128)(2,1)S(1)}, bf16[768,256]{1,0:T(8,128)(2,1)S(1)}, u32[]{:S(2)}, u32[]{:S(2)}) collective-permute-start(bf16[768,256]{1,0:T(8,128)(2,1)S(1)} %get-tuple-element.37.refs_2_), channel_id=1, source_target_pairs={{0,1},{1,2},{2,3},{3,0},{4,5},{5,6},{6,7},{7,4},{8,9},{9,10},{10,1... | collective-permute-start | bytes 1179656 | tf_op jit(solution)/shard_map/ppermute | solution.py:28
  5.8 8.5 %collective-permute-start.7 = (bf16[272,256]{1,0:T(8,128)(2,1)S(1)}, bf16[272,256]{1,0:T(8,128)(2,1)S(1)}, u32[]{:S(2)}, u32[]{:S(2)}) collective-permute-start(bf16[272,256]{1,0:T(8,128)(2,1)S(1)} %get-tuple-element.47), channel_id=1, source_target_pairs={{0,128},{64,192},{128,0},{192,64},{1,129},{65,193},{129,1},{193,65... | collective-permute-start | bytes 417800 | tf_op jit(solution)/shard_map/ppermute | solution.py:28
  8.3 6.1 %collective-permute-start.8 = (bf16[272,256]{1,0:T(8,128)(2,1)S(1)}, bf16[272,256]{1,0:T(8,128)(2,1)S(1)}, u32[]{:S(2)}, u32[]{:S(2)}) collective-permute-start(bf16[272,256]{1,0:T(8,128)(2,1)S(1)} %get-tuple-element.48), channel_id=1, source_target_pairs={{0,192},{64,0},{128,64},{192,128},{1,193},{65,1},{129,65},{193,129... | collective-permute-start | bytes 417800 | tf_op jit(solution)/shard_map/ppermute | solution.py:28
  9.5 14.5 %collective-permute-start.1 = (bf16[768,256]{1,0:T(8,128)(2,1)S(1)}, bf16[768,256]{1,0:T(8,128)(2,1)S(1)}, u32[]{:S(2)}, u32[]{:S(2)}) collective-permute-start(bf16[768,256]{1,0:T(8,128)(2,1)S(1)} %get-tuple-element.40), channel_id=1, source_target_pairs={{0,3},{1,0},{2,1},{3,2},{4,7},{5,4},{6,5},{7,6},{8,11},{9,8},{10,9... | collective-permute-start | bytes 1179656 | tf_op jit(solution)/shard_map/ppermute | solution.py:28
  10.9 14.2 %collective-permute-start.2 = (bf16[768,256]{1,0:T(8,128)(2,1)S(1)}, bf16[768,256]{1,0:T(8,128)(2,1)S(1)}, u32[]{:S(2)}, u32[]{:S(2)}) collective-permute-start(bf16[768,256]{1,0:T(8,128)(2,1)S(1)} %get-tuple-element.41), channel_id=1, source_target_pairs={{0,2},{1,3},{2,0},{3,1},{4,6},{5,7},{6,4},{7,5},{8,10},{9,11},{10,... | collective-permute-start | bytes 1179656 | tf_op jit(solution)/shard_map/ppermute | solution.py:28
  16.9 4.4 %collective-permute-start.11 = (bf16[256,256]{1,0:T(8,128)(2,1)S(1)}, bf16[256,256]{1,0:T(8,128)(2,1)S(1)}, u32[]{:S(2)}, u32[]{:S(2)}) collective-permute-start(bf16[256,256]{1,0:T(8,128)(2,1)S(1)} %shard_map.85.refs_3_.refs_0_), channel_id=1, source_target_pairs={{0,4},{4,0},{8,12},{12,8},{16,20},{20,16},{24,28},{28,24},{1,5},{5... | collective-permute-start | bytes 393224 | tf_op jit(solution)/shard_map/ppermute | solution.py:358
  18.6 20.8 %collective-permute-start.3 = (bf16[768,256]{1,0:T(8,128)(2,1)S(1)}, bf16[768,256]{1,0:T(8,128)(2,1)S(1)}, u32[]{:S(2)}, u32[]{:S(2)}) collective-permute-start(bf16[768,256]{1,0:T(8,128)(2,1)S(1)} %get-tuple-element.42.refs_5_), channel_id=1, source_target_pairs={{0,1},{1,2},{2,3},{3,0},{4,5},{5,6},{6,7},{7,4},{8,9},{9,10},{10,1... | collective-permute-start | bytes 1179656 | tf_op jit(solution)/shard_map/ppermute | solution.py:28
  21.3 18.1 %collective-permute-start.4 = (bf16[768,256]{1,0:T(8,128)(2,1)S(1)}, bf16[768,256]{1,0:T(8,128)(2,1)S(1)}, u32[]{:S(2)}, u32[]{:S(2)}) collective-permute-start(bf16[768,256]{1,0:T(8,128)(2,1)S(1)} %get-tuple-element.43), channel_id=1, source_target_pairs={{0,3},{1,0},{2,1},{3,2},{4,7},{5,4},{6,5},{7,6},{8,11},{9,8},{10,9... | collective-permute-start | bytes 1179656 | tf_op jit(solution)/shard_map/ppermute | solution.py:28
  22.7 19.2 %collective-permute-start.5 = (bf16[768,256]{1,0:T(8,128)(2,1)S(1)}, bf16[768,256]{1,0:T(8,128)(2,1)S(1)}, u32[]{:S(2)}, u32[]{:S(2)}) collective-permute-start(bf16[768,256]{1,0:T(8,128)(2,1)S(1)} %get-tuple-element.44), channel_id=1, source_target_pairs={{0,2},{1,3},{2,0},{3,1},{4,6},{5,7},{6,4},{7,5},{8,10},{9,11},{10,... | collective-permute-start | bytes 1179656 | tf_op jit(solution)/shard_map/ppermute | solution.py:28
  25.1 6.0 %collective-permute-start.10 = (bf16[384,256]{1,0:T(8,128)(2,1)S(1)}, bf16[384,256]{1,0:T(8,128)(2,1)S(1)}, u32[]{:S(2)}, u32[]{:S(2)}) collective-permute-start(bf16[384,256]{1,0:T(8,128)(2,1)S(1)} %get-tuple-element.50.refs_6_), channel_id=1, source_target_pairs={{0,192},{64,0},{128,64},{192,128},{1,193},{65,1},{129,65},{193,129... | collective-permute-start | bytes 589832 | tf_op jit(solution)/shard_map/ppermute | solution.py:28
  26.9 6.0 %collective-permute-start.9 = (bf16[384,256]{1,0:T(8,128)(2,1)S(1)}, bf16[384,256]{1,0:T(8,128)(2,1)S(1)}, u32[]{:S(2)}, u32[]{:S(2)}) collective-permute-start(bf16[384,256]{1,0:T(8,128)(2,1)S(1)} %get-tuple-element.49.refs_7_.refs_5_), channel_id=1, source_target_pairs={{0,64},{64,128},{128,192},{192,0},{1,65},{65,129},{129,193},{193,1... | collective-permute-start | bytes 589832 | tf_op jit(solution)/shard_map/ppermute | solution.py:28
  33.6 17.3 %collective-permute-start.16 = (bf16[512,256]{1,0:T(8,128)(2,1)S(1)}, bf16[512,256]{1,0:T(8,128)(2,1)S(1)}, u32[]{:S(2)}, u32[]{:S(2)}) collective-permute-start(bf16[512,256]{1,0:T(8,128)(2,1)S(1)} %get-tuple-element.51.refs_3_), channel_id=1, source_target_pairs={{0,4},{4,8},{8,12},{12,16},{16,20},{20,24},{24,28},{28,0},{1,5},{5... | collective-permute-start | bytes 786440 | tf_op jit(solution)/shard_map/ppermute | solution.py:28
  35.2 46.7 %copy-start.5 = (bf16[1,32,64,256]{3,2,1,0:T(8,128)(2,1)S(1)}, bf16[1,32,64,256]{3,2,1,0:T(8,128)(2,1)}, u32[]{:S(2)}) copy-start(bf16[1,32,64,256]{3,2,1,0:T(8,128)(2,1)} %param.12) | copy-start | bytes 3145732
  35.2 15.7 %collective-permute-start.17 = (bf16[512,256]{1,0:T(8,128)(2,1)S(1)}, bf16[512,256]{1,0:T(8,128)(2,1)S(1)}, u32[]{:S(2)}, u32[]{:S(2)}) collective-permute-start(bf16[512,256]{1,0:T(8,128)(2,1)S(1)} %get-tuple-element.58), channel_id=1, source_target_pairs={{0,28},{4,0},{8,4},{12,8},{16,12},{20,16},{24,20},{28,24},{1,29},{... | collective-permute-start | bytes 786440 | tf_op jit(solution)/shard_map/ppermute | solution.py:28
  42.0 5.8 %collective-permute-start.14 = (bf16[384,256]{1,0:T(8,128)(2,1)S(1)}, bf16[384,256]{1,0:T(8,128)(2,1)S(1)}, u32[]{:S(2)}, u32[]{:S(2)}) collective-permute-start(bf16[384,256]{1,0:T(8,128)(2,1)S(1)} %get-tuple-element.56.refs_5_), channel_id=1, source_target_pairs={{0,64},{64,128},{128,192},{192,0},{1,65},{65,129},{129,193},{193,1... | collective-permute-start | bytes 589832 | tf_op jit(solution)/shard_map/ppermute | solution.py:28
  43.4 7.5 %collective-permute-start.15 = (bf16[384,256]{1,0:T(8,128)(2,1)S(1)}, bf16[384,256]{1,0:T(8,128)(2,1)S(1)}, u32[]{:S(2)}, u32[]{:S(2)}) collective-permute-start(bf16[384,256]{1,0:T(8,128)(2,1)S(1)} %get-tuple-element.57.refs_6_), channel_id=1, source_target_pairs={{0,192},{64,0},{128,64},{192,128},{1,193},{65,1},{129,65},{193,129... | collective-permute-start | bytes 589832 | tf_op jit(solution)/shard_map/ppermute | solution.py:28
  44.8 24.0 %collective-permute-start.13 = (bf16[768,256]{1,0:T(8,128)(2,1)S(1)}, bf16[768,256]{1,0:T(8,128)(2,1)S(1)}, u32[]{:S(2)}, u32[]{:S(2)}) collective-permute-start(bf16[768,256]{1,0:T(8,128)(2,1)S(1)} %get-tuple-element.54.refs_5_), channel_id=1, source_target_pairs={{0,64},{64,0},{128,192},{192,128},{1,65},{65,1},{129,193},{193,129... | collective-permute-start | bytes 1179656 | tf_op jit(solution)/shard_map/ppermute | solution.py:170
  47.8 7.7 %collective-permute-start.22 = (bf16[256,256]{1,0:T(8,128)(2,1)S(1)}, bf16[256,256]{1,0:T(8,128)(2,1)S(1)}, u32[]{:S(2)}, u32[]{:S(2)}) collective-permute-start(bf16[256,256]{1,0:T(8,128)(2,1)S(1)} %shard_map.87.refs_6_.refs_0_), channel_id=1, source_target_pairs={{0,8},{4,12},{8,0},{12,4},{16,24},{20,28},{24,16},{28,20},{1,9},{5... | collective-permute-start | bytes 393224 | tf_op jit(solution)/shard_map/ppermute | solution.py:358
  51.6 17.1 %collective-permute-start.18 = (bf16[512,256]{1,0:T(8,128)(2,1)S(1)}, bf16[512,256]{1,0:T(8,128)(2,1)S(1)}, u32[]{:S(2)}, u32[]{:S(2)}) collective-permute-start(bf16[512,256]{1,0:T(8,128)(2,1)S(1)} %get-tuple-element.59), channel_id=1, source_target_pairs={{0,4},{4,8},{8,12},{12,16},{16,20},{20,24},{24,28},{28,0},{1,5},{5... | collective-permute-start | bytes 786440 | tf_op jit(solution)/shard_map/ppermute | solution.py:28
  53.6 15.1 %collective-permute-start.19 = (bf16[512,256]{1,0:T(8,128)(2,1)S(1)}, bf16[512,256]{1,0:T(8,128)(2,1)S(1)}, u32[]{:S(2)}, u32[]{:S(2)}) collective-permute-start(bf16[512,256]{1,0:T(8,128)(2,1)S(1)} %get-tuple-element.60), channel_id=1, source_target_pairs={{0,28},{4,0},{8,4},{12,8},{16,12},{20,16},{24,20},{28,24},{1,29},{... | collective-permute-start | bytes 786440 | tf_op jit(solution)/shard_map/ppermute | solution.py:28
  55.6 9.7 %collective-permute-start.23 = (bf16[256,256]{1,0:T(8,128)(2,1)S(1)}, bf16[256,256]{1,0:T(8,128)(2,1)S(1)}, u32[]{:S(2)}, u32[]{:S(2)}) collective-permute-start(bf16[256,256]{1,0:T(8,128)(2,1)S(1)} %shard_map.93.refs_0_), channel_id=1, source_target_pairs={{0,16},{4,20},{8,24},{12,28},{16,0},{20,4},{24,8},{28,12},{1,17},{... | collective-permute-start | bytes 393224 | tf_op jit(solution)/shard_map/ppermute | solution.py:358
  61.2 23.2 %collective-permute-start.12 = (bf16[768,256]{1,0:T(8,128)(2,1)S(1)}, bf16[768,256]{1,0:T(8,128)(2,1)S(1)}, u32[]{:S(2)}, u32[]{:S(2)}) collective-permute-start(bf16[768,256]{1,0:T(8,128)(2,1)S(1)} %get-tuple-element.52.refs_5_), channel_id=1, source_target_pairs={{0,192},{192,0},{64,128},{128,64},{1,193},{193,1},{65,129},{129,65... | collective-permute-start | bytes 1179656 | tf_op jit(solution)/shard_map/ppermute | solution.py:170
  65.3 7.9 %collective-permute-start.24 = (bf16[256,256]{1,0:T(8,128)(2,1)S(1)}, bf16[256,256]{1,0:T(8,128)(2,1)S(1)}, u32[]{:S(2)}, u32[]{:S(2)}) collective-permute-start(bf16[256,256]{1,0:T(8,128)(2,1)S(1)} %shard_map.94.refs_0_), channel_id=1, source_target_pairs={{0,1},{1,0},{2,3},{3,2},{4,5},{5,4},{6,7},{7,6},{8,9},{9,8},{10,11... | collective-permute-start | bytes 393224 | tf_op jit(solution)/shard_map/ppermute | solution.py:358
  69.5 14.9 %collective-permute-start.21 = (bf16[512,256]{1,0:T(8,128)(2,1)S(1)}, bf16[512,256]{1,0:T(8,128)(2,1)S(1)}, u32[]{:S(2)}, u32[]{:S(2)}) collective-permute-start(bf16[512,256]{1,0:T(8,128)(2,1)S(1)} %get-tuple-element.62.refs_7_), channel_id=1, source_target_pairs={{0,4},{4,8},{8,12},{12,16},{16,20},{20,24},{24,28},{28,0},{1,5},{5... | collective-permute-start | bytes 786440 | tf_op jit(solution)/shard_map/ppermute | solution.py:28
  73.2 5.4 %collective-permute-start.25 = (bf16[256,256]{1,0:T(8,128)(2,1)S(1)}, bf16[256,256]{1,0:T(8,128)(2,1)S(1)}, u32[]{:S(2)}, u32[]{:S(2)}) collective-permute-start(bf16[256,256]{1,0:T(8,128)(2,1)S(1)} %shard_map.95.refs_0_), channel_id=1, source_target_pairs={{0,2},{1,3},{2,0},{3,1},{4,6},{5,7},{6,4},{7,5},{8,10},{9,11},{10,... | collective-permute-start | bytes 393224 | tf_op jit(solution)/shard_map/ppermute | solution.py:358
  78.7 7.8 %collective-permute-start.20 = (bf16[512,256]{1,0:T(8,128)(2,1)S(1)}, bf16[512,256]{1,0:T(8,128)(2,1)S(1)}, u32[]{:S(2)}, u32[]{:S(2)}) collective-permute-start(bf16[512,256]{1,0:T(8,128)(2,1)S(1)} %get-tuple-element.61), channel_id=1, source_target_pairs={{0,28},{4,0},{8,4},{12,8},{16,12},{20,16},{24,20},{28,24},{1,29},{... | collective-permute-start | bytes 786440 | tf_op jit(solution)/shard_map/ppermute | solution.py:28
  84.8 7.0 %collective-permute-start.26 = (bf16[512,256]{1,0:T(8,128)(2,1)S(1)}, bf16[512,256]{1,0:T(8,128)(2,1)S(1)}, u32[]{:S(2)}, u32[]{:S(2)}) collective-permute-start(bf16[512,256]{1,0:T(8,128)(2,1)S(1)} %shard_map.98.refs_8_), channel_id=1, source_target_pairs={{0,4},{4,8},{8,12},{12,16},{16,20},{20,24},{24,28},{28,0},{1,5},{5... | collective-permute-start | bytes 786440 | tf_op jit(solution)/shard_map/ppermute | solution.py:28
  84.9 3.9 %collective-permute-start.27 = (bf16[256,256]{1,0:T(8,128)(2,1)S(1)}, bf16[256,256]{1,0:T(8,128)(2,1)S(1)}, u32[]{:S(2)}, u32[]{:S(2)}) collective-permute-start(bf16[256,256]{1,0:T(8,128)(2,1)S(1)} %get-tuple-element.63.refs_8_), channel_id=1, source_target_pairs={{0,192},{64,0},{128,64},{192,128},{1,193},{65,1},{129,65},{193,129... | collective-permute-start | bytes 393224 | tf_op jit(solution)/shard_map/ppermute | solution.py:28
  85.0 5.5 %collective-permute-start.28 = (bf16[256,256]{1,0:T(8,128)(2,1)S(1)}, bf16[256,256]{1,0:T(8,128)(2,1)S(1)}, u32[]{:S(2)}, u32[]{:S(2)}) collective-permute-start(bf16[256,256]{1,0:T(8,128)(2,1)S(1)} %get-tuple-element.65), channel_id=1, source_target_pairs={{0,128},{64,192},{128,0},{192,64},{1,129},{65,193},{129,1},{193,65... | collective-permute-start | bytes 393224 | tf_op jit(solution)/shard_map/ppermute | solution.py:28
  85.6 6.3 %collective-permute-start.29 = (bf16[256,256]{1,0:T(8,128)(2,1)S(1)}, bf16[256,256]{1,0:T(8,128)(2,1)S(1)}, u32[]{:S(2)}, u32[]{:S(2)}) collective-permute-start(bf16[256,256]{1,0:T(8,128)(2,1)S(1)} %get-tuple-element.66), channel_id=1, source_target_pairs={{0,64},{64,128},{128,192},{192,0},{1,65},{65,129},{129,193},{193,1... | collective-permute-start | bytes 393224 | tf_op jit(solution)/shard_map/ppermute | solution.py:28
  92.4 13.6 %collective-permute-start.30 = (bf16[512,256]{1,0:T(8,128)(2,1)S(1)}, bf16[512,256]{1,0:T(8,128)(2,1)S(1)}, u32[]{:S(2)}, u32[]{:S(2)}) collective-permute-start(bf16[512,256]{1,0:T(8,128)(2,1)S(1)} %get-tuple-element.67), channel_id=1, source_target_pairs={{0,32},{1,33},{2,34},{3,35},{4,36},{5,37},{6,38},{7,39},{8,40},{9,... | collective-permute-start | bytes 786440 | tf_op jit(solution)/shard_map/ppermute | solution.py:505
  (6 other events, 53.6 us)

commit v4 on v3

--- a/solution.py
+++ b/solution.py
@@ -89,12 +89,14 @@
     copies = []
     for gi, group in enumerate(groups):
         plus, minus = tiles_of(group)
-        mine = plus * (1 - odd) + minus * odd
+        wanted = (plus, minus) if ahead else (plus * (1 - odd) + minus * odd,)
         for ki, hop in enumerate(HOPS):
-            if ahead and gi == 0:
+            if ahead:
                 copies.append((refs[1], outs[ki].at[pl.ds(0, ROWS), :]))
-            source = w_ref.at[:, pl.ds(column(mine, lax.rem(y + hop, NY)), TILE)]
-            copies.append((source, outs[ki].at[pl.ds(ahead + gi * TILE, TILE), :]))
+            for ti, ztile in enumerate(wanted):
+                source = w_ref.at[:, pl.ds(column(ztile, lax.rem(y + hop, NY)), TILE)]
+                first = ahead + (gi + ti) * TILE
+                copies.append((source, outs[ki].at[pl.ds(first, TILE), :]))
     for gi, group in enumerate(groups):
         for ti, ztile in enumerate(tiles_of(group)):
             source = w_ref.at[:, pl.ds(column(ztile, y), TILE)]
@@ -110,12 +112,12 @@
 
 
 def pack(groups, weight, features=None, after=()):
-    ahead = 0 if features is None else ROWS
-    args, specs = [weight], [HBM]
-    if ahead:
+    args, specs, rows = [weight], [HBM], len(groups) * TILE
+    ahead = 0
+    if features is not None:
+        ahead, rows = ROWS, ROWS + 2 * TILE
         args.append(features)
         specs.append(HBM)
-    rows = ahead + len(groups) * TILE
     dims = [(rows, TILE)] * 3 + [(2 * TILE, TILE)] * len(groups)
     got = call(
         functools.partial(pack_kernel, groups, ahead),
@@ -123,7 +125,7 @@
         specs,
         [shape(d) for d in dims],
         [whole(d) for d in dims],
-        [pltpu.SemaphoreType.DMA((3 + 5 * len(groups),))],
+        [pltpu.SemaphoreType.DMA((11 if ahead else 5 * len(groups),))],
         (0, 6 * rows * TILE),
         8,
         after,
@@ -184,12 +186,19 @@
 def project_kernel(which, has_in, parts, own_ref, x_ref, p0, p1, p2, *refs):
     n = len(which)
     even = parity() == 0
-    mine, other = stacked(refs[:parts]), stacked(refs[parts : 2 * parts])
+    if parts:
+        mine, other = stacked(refs[:parts]), stacked(refs[parts : 2 * parts])
     refs = refs[2 * parts :]
     carried, outs = (refs[:n], refs[n:]) if has_in else ((None,) * n, refs)
     lhs = jnp.concatenate([x_ref[...]] + [peer[0:ROWS, :] for peer in (p0, p1, p2)], axis=1)
     for c_ref, out, ti in zip(carried, outs, which):
-        remote = lax.select(even, mine, other) if ti == 0 else lax.select(even, other, mine)
+        if parts == 0:
+            rows = slice(ROWS + ti * TILE, ROWS + (ti + 1) * TILE)
+            remote = jnp.concatenate([peer[rows, :] for peer in (p0, p1, p2)], axis=0)
+        elif ti == 0:
+            remote = lax.select(even, mine, other)
+        else:
+            remote = lax.select(even, other, mine)
         rhs = jnp.concatenate([own_ref[ti * TILE : (ti + 1) * TILE, :], remote], axis=0)
         total = jnp.dot(lhs, rhs, preferred_element_type=F32)
         if has_in:
@@ -205,7 +214,7 @@
         (own, features, *first_got, *mine, *other, *carried),
         [whole(half)] * 2
         + [whole(first_got[0].shape)] * 3
-        + [whole(mine[0].shape)] * (2 * parts)
+        + [whole(value.shape) for value in (*mine, *other)]
         + [whole(half)] * len(carried),
         [shape((ROWS, TILE), out_dtype)] * n,
         [whole((ROWS, TILE))] * n,
@@ -369,13 +378,15 @@
     )
 
 
-def up_kernel(i0, i1, i2, i3, low_ref, up_ref, block_ref, *refs):
+def up_kernel(i0, i1, i2, i3, l0, l1, l2, l3, up_ref, block_ref, *refs):
     outs, (item_ref, two_ref, out_ref) = refs[:NX], refs[NX:]
+    low = l0[...].astype(F32) + l1[...].astype(F32) + l2[...].astype(F32) + l3[...].astype(F32)
+    low = low.astype(BF16).astype(F32)
     for k, item in enumerate((i0, i1, i2, i3)):
         item_ref[k] = item[WINDOW : WINDOW + IDROWS, :]
     first = lax.broadcasted_iota(jnp.int32, (WINDOW, 128), 1) < RANK
     for h in range(2):
-        packed = low_ref[:, h * 128 : (h + 1) * 128].astype(F32)
+        packed = low[:, h * 128 : (h + 1) * 128]
         turned = pltpu.roll(packed, RANK, 1)
         two_ref[h] = jnp.where(first, packed, turned)
         two_ref[h + 2] = jnp.where(first, turned, packed)
@@ -397,12 +408,13 @@
         outs[k][...] = out_ref[k]
 
 
-def up(items, low, factor, blocks, after=()):
+def up(items, lows, factor, blocks, after=()):
     return call(
         up_kernel,
-        (*items, low, factor, blocks),
+        (*items, *lows, factor, blocks),
         [whole((WINDOW + IDROWS, WIDTH))] * NX
-        + [whole((WINDOW, 256)), whole((VARS * RANK, WIDTH)), whole((NX, WINDOW, 256))],
+        + [whole((WINDOW, 256))] * 4
+        + [whole((VARS * RANK, WIDTH)), whole((NX, WINDOW, 256))],
         [shape((WINDOW, WIDTH))] * NX,
         [whole((WINDOW, WIDTH))] * NX,
         [
@@ -469,28 +481,28 @@
     got = [shift(value, Y, hop) for value, hop in zip(first, HOPS)]
     sent = dispatch(ids, features, (first[0],))
     items = [sent[0]] + [shift(sent[k], "pool", k) for k in (1, 2, 3)]
-    second, (own1, own2, own3) = pack((1, 2, 3), weight, None, (sent[0],))
-    later = [shift(value, Y, hop) for value, hop in zip(second, HOPS)]
+    second, (own1,) = pack((1,), weight, None, (sent[0],))
+    got1 = [shift(value, Y, hop) for value, hop in zip(second, HOPS)]
     low = down(items, down_factor, (second[0],))
+    third, (own2, own3) = pack((2, 3), weight, None, (low,))
+    got2 = [shift(value, Y, hop) for value, hop in zip(third, HOPS)]
     low1 = exchanged_sum(low, Z, 1)
-    mine0 = join(got, ROWS, (True,), (low,))
-    other0 = (shift(mine0[0], "pool", 1), shift(mine0[1], "pool", -1))
     low2 = exchanged_sum(low1, Z, 2)
-    blocks = block_terms(items, mats, places, (low1, mine0[0]))
-    plus, minus = project((0, 1), own0, features, got, mine0, other0, (), (blocks,))
+    plus, minus = project((0, 1), own0, features, got, (), (), (), (low1,))
     carried = (shift(plus, Z, 1), shift(minus, Z, -1))
+    mine1 = join(got1, 0, (True,), (plus,))
+    other1 = (shift(mine1[0], "pool", 1), shift(mine1[1], "pool", -1))
     low3 = exchanged_sum(low2, Z, 4)
-    *mine1, mine2, mine3 = join(later, 0, (True, False, False), (plus,))
-    other1 = (shift(mine1[0], "pool", 1), shift(mine1[1], "pool", -1))
+    plus, minus = project((0, 1), own1, features, got, mine1, other1, carried)
+    mine2, mine3 = join(got2, 0, (False, False), (plus,))
     other2 = swapped(mine2, False)
+    carried = (shift(plus, Z, 1), shift(minus, Z, -1))
     other3 = swapped(mine3, True)
-    plus, minus = project((0, 1), own1, features, got, mine1, other1, carried)
+    lows = [low3] + [shift(low3, Y, hop) for hop in HOPS]
+    blocks = block_terms(items, mats, places, (plus,))
+    plus, minus = project((0, 1), own2, features, got, (mine2,), (other2,), carried, (blocks,))
     carried = (shift(plus, Z, 1), shift(minus, Z, -1))
-    low4 = exchanged_sum(low3, Y, 1)
-    low5 = exchanged_sum(low4, Y, 2)
-    plus, minus = project((0, 1), own2, features, got, (mine2,), (other2,), carried)
-    carried = (shift(plus, Z, 1), shift(minus, Z, -1))
-    served = up(items, low5, up_factor, blocks, (plus,))
+    served = up(items, lows, up_factor, blocks, (plus,))
     returned = [served[0]] + [shift(served[k], "pool", -k) for k in (1, 2, 3)]
     (plus,) = project(
         (0,), own3, features, got, (mine3,), (other3,), carried[:1], (served[1],)

time: 107 us -> 110 us (1.028)
  waiting for transfers between devices: 35.2 us -> 41.2 us
  starting transfers between devices: 53.1 us -> 49.5 us
    ppermute x23 -> x27, waiting for transfers between devices: 13.2 us -> 27.5 us  [shift(): lax.ppermute(value, axis, [(i, (i + steps) % count) for i in range(count)])]
    ppermute x5 -> x3, starting transfers between devices: 15.2 us -> 5.82 us  [exchanged_sum(): other = lax.ppermute(value, axis, [(i, i ^ bit) for i in range(count)])]
    ppermute x5 -> x3, waiting for transfers between devices: 9.74 us -> 5.19 us  [exchanged_sum(): other = lax.ppermute(value, axis, [(i, i ^ bit) for i in range(count)])]
    ppermute x23 -> x27, starting transfers between devices: 36.4 us -> 40.9 us  [shift(): lax.ppermute(value, axis, [(i, (i + steps) % count) for i in range(count)])]
    ppermute x1, waiting for transfers between devices: 12.2 us -> 8.49 us  [steps(): carried = lax.ppermute(first_out, 'section', [(0, 1)])]
    ppermute x2, starting transfers between devices: 0.24 us -> 1.51 us  [swapped(): return lax.ppermute(value, 'pool', pairs)]
    pallas_call x19 -> x18, Pallas kernels: 17.3 us -> 18.3 us  [call(): pl.pallas_call(body, out_shape=outs, in_specs=list(in_specs) + [ANY] * m,...]
  transfers between devices with their start and end apart: 31 -> 33, of which waited for: 11 -> 16; matrix products, arithmetic and copies ran while one was open for 0% -> 0% of each run, Pallas kernels for 13% -> 15%
where the time goes in v4:
time: 110 us
  starting transfers between devices  49.5 us (45%)
  waiting for transfers between devices  41.2 us (37%)
  Pallas kernels  18.3 us (17%)
    ppermute x27, starting transfers between devices, shift(): lax.ppermute(value, axis, [(i, (i + steps) % count) for i in range(count)])  40.9 us
    ppermute x27, waiting for transfers between devices, shift(): lax.ppermute(value, axis, [(i, (i + steps) % count) for i in range(count)])  27.5 us
    pallas_call x18, Pallas kernels, call(): pl.pallas_call(body, out_shape=outs, in_specs=list(in_specs) + [ANY] * m,...  18.3 us
    ppermute x1, waiting for transfers between devices, steps(): carried = lax.ppermute(first_out, 'section', [(0, 1)])  8.49 us
    ppermute x3, starting transfers between devices, exchanged_sum(): other = lax.ppermute(value, axis, [(i, i ^ bit) for i in range(count)])  5.82 us
    ppermute x3, waiting for transfers between devices, exchanged_sum(): other = lax.ppermute(value, axis, [(i, i ^ bit) for i in range(count)])  5.19 us
  transfers between devices with their start and end apart: 33, of which 16 were waited for; matrix products, arithmetic and copies ran while one was open for 0% of the time, Pallas kernels for 15%

profile of v4, /device:TPU:1, one launch (start us, length us, event | category | flops | bytes accessed | tf_op | source)
XLA Modules:
  0.0 110.1 jit_solution(354789102846827188)
XLA Ops:
  0.0 1.7 %shard_map.82 = (bf16[1024,256]{1,0:T(8,128)(2,1)S(1)}, bf16[1024,256]{1,0:T(8,128)(2,1)S(1)}, bf16[1024,256]{1,0:T(8,128)(2,1)S(1)}, bf16[512,256]{1,0:T(8,128)(2,1)S(1)}) custom-call(bf16[256,8192]{1,0:T(8,128)(2,1)} %bitcast.22, bf16[512,256]{1,0:T(8,128)(2,1)} %bitcast.9), custom_call_target="tpu_custom_call" | custom-call | bytes 1572864 | tf_op jit(solution)/shard_map/pallas_call | solution.py:67
  1.7 2.2 %collective-permute-start.3 = (bf16[1024,256]{1,0:T(8,128)(2,1)S(1)}, bf16[1024,256]{1,0:T(8,128)(2,1)S(1)}, u32[]{:S(2)}, u32[]{:S(2)}) collective-permute-start(bf16[1024,256]{1,0:T(8,128)(2,1)S(1)} %get-tuple-element.38.refs_2_), channel_id=1, source_target_pairs={{0,1},{1,2},{2,3},{3,0},{4,5},{5,6},{6,7},{7,4},{8,9},{9,10},{10,1... | collective-permute-start | bytes 1572872 | tf_op jit(solution)/shard_map/ppermute | solution.py:28
  6.1 1.5 %collective-permute-start.4 = (bf16[1024,256]{1,0:T(8,128)(2,1)S(1)}, bf16[1024,256]{1,0:T(8,128)(2,1)S(1)}, u32[]{:S(2)}, u32[]{:S(2)}) collective-permute-start(bf16[1024,256]{1,0:T(8,128)(2,1)S(1)} %get-tuple-element.45), channel_id=1, source_target_pairs={{0,3},{1,0},{2,1},{3,2},{4,7},{5,4},{6,5},{7,6},{8,11},{9,8},{10,9... | collective-permute-start | bytes 1572872 | tf_op jit(solution)/shard_map/ppermute | solution.py:28
  7.5 1.6 %collective-permute-start.5 = (bf16[1024,256]{1,0:T(8,128)(2,1)S(1)}, bf16[1024,256]{1,0:T(8,128)(2,1)S(1)}, u32[]{:S(2)}, u32[]{:S(2)}) collective-permute-start(bf16[1024,256]{1,0:T(8,128)(2,1)S(1)} %get-tuple-element.46), channel_id=1, source_target_pairs={{0,2},{1,3},{2,0},{3,1},{4,6},{5,7},{6,4},{7,5},{8,10},{9,11},{10,... | collective-permute-start | bytes 1572872 | tf_op jit(solution)/shard_map/ppermute | solution.py:28
  9.1 2.4 %collective-permute-start.1 = (bf16[272,256]{1,0:T(8,128)(2,1)S(1)}, bf16[272,256]{1,0:T(8,128)(2,1)S(1)}, u32[]{:S(2)}, u32[]{:S(2)}) collective-permute-start(bf16[272,256]{1,0:T(8,128)(2,1)S(1)} %get-tuple-element.41), channel_id=1, source_target_pairs={{0,128},{64,192},{128,0},{192,64},{1,129},{65,193},{129,1},{193,65... | collective-permute-start | bytes 417800 | tf_op jit(solution)/shard_map/ppermute | solution.py:28
  14.6 2.4 %collective-permute-done.2.refs_3_ = bf16[272,256]{1,0:T(8,128)(2,1)S(1)} collective-permute-done((bf16[272,256]{1,0:T(8,128)(2,1)S(1)}, bf16[272,256]{1,0:T(8,128)(2,1)S(1)}, u32[]{:S(2)}, u32[]{:S(2)}) %collective-permute-start.2) | collective-permute-done | bytes 139296 | tf_op jit(solution)/shard_map/ppermute | solution.py:28
  16.9 2.6 %shard_map.85.refs_1_.refs_0_ = bf16[256,256]{1,0:T(8,128)(2,1)S(1)} custom-call(bf16[272,256]{1,0:T(8,128)(2,1)S(1)} %get-tuple-element.39.refs_1_.refs_0_, bf16[272,256]{1,0:T(8,128)(2,1)S(1)} %collective-permute-done.refs_1_, bf16[272,256]{1,0:T(8,128)(2,1)S(1)} %collective-permute-done.1.refs_2_, bf16[272,256]{1,0:T(8,128)(2,1)S(1)} %collective-permute-done.2.refs_3_, ...), custom_call_target="tpu_custom_call" | custom-call | flops 1073741824 | bytes 2097152 | tf_op jit(solution)/shard_map/pallas_call | solution.py:67
  19.5 1.7 %collective-permute-start.12 = (bf16[256,256]{1,0:T(8,128)(2,1)S(1)}, bf16[256,256]{1,0:T(8,128)(2,1)S(1)}, u32[]{:S(2)}, u32[]{:S(2)}) collective-permute-start(bf16[256,256]{1,0:T(8,128)(2,1)S(1)} %shard_map.85.refs_1_.refs_0_), channel_id=1, source_target_pairs={{0,4},{4,0},{8,12},{12,8},{16,20},{20,16},{24,28},{28,24},{1,5},{5... | collective-permute-start | bytes 393224 | tf_op jit(solution)/shard_map/ppermute | solution.py:367
  21.6 2.3 %collective-permute-done.12.refs_1_ = bf16[256,256]{1,0:T(8,128)(2,1)S(1)} collective-permute-done((bf16[256,256]{1,0:T(8,128)(2,1)S(1)}, bf16[256,256]{1,0:T(8,128)(2,1)S(1)}, u32[]{:S(2)}, u32[]{:S(2)}) %collective-permute-start.12) | collective-permute-done | bytes 131104 | tf_op jit(solution)/shard_map/ppermute | solution.py:367
  24.6 1.4 %collective-permute-start.11 = (bf16[256,256]{1,0:T(8,128)(2,1)S(1)}, bf16[256,256]{1,0:T(8,128)(2,1)S(1)}, u32[]{:S(2)}, u32[]{:S(2)}) collective-permute-start(bf16[256,256]{1,0:T(8,128)(2,1)S(1)} %get-tuple-element.52), channel_id=1, source_target_pairs={{0,2},{1,3},{2,0},{3,1},{4,6},{5,7},{6,4},{7,5},{8,10},{9,11},{10,... | collective-permute-start | bytes 393224 | tf_op jit(solution)/shard_map/ppermute | solution.py:28
  26.1 3.0 %collective-permute-done.5.refs_4_ = bf16[1024,256]{1,0:T(8,128)(2,1)S(1)} collective-permute-done((bf16[1024,256]{1,0:T(8,128)(2,1)S(1)}, bf16[1024,256]{1,0:T(8,128)(2,1)S(1)}, u32[]{:S(2)}, u32[]{:S(2)}) %collective-permute-start.5) | collective-permute-done | bytes 524320 | tf_op jit(solution)/shard_map/ppermute | solution.py:28
  29.8 4.1 %collective-permute-done.9.refs_0_ = bf16[256,256]{1,0:T(8,128)(2,1)S(1)} collective-permute-done((bf16[256,256]{1,0:T(8,128)(2,1)S(1)}, bf16[256,256]{1,0:T(8,128)(2,1)S(1)}, u32[]{:S(2)}, u32[]{:S(2)}) %collective-permute-start.9) | collective-permute-done | bytes 131104 | tf_op jit(solution)/shard_map/ppermute | solution.py:28
  37.5 1.7 %collective-permute-start.15 = (bf16[512,256]{1,0:T(8,128)(2,1)S(1)}, bf16[512,256]{1,0:T(8,128)(2,1)S(1)}, u32[]{:S(2)}, u32[]{:S(2)}) collective-permute-start(bf16[512,256]{1,0:T(8,128)(2,1)S(1)} %get-tuple-element.54.refs_3_), channel_id=1, source_target_pairs={{0,4},{4,8},{8,12},{12,16},{16,20},{20,24},{24,28},{28,0},{1,5},{5... | collective-permute-start | bytes 786440 | tf_op jit(solution)/shard_map/ppermute | solution.py:28
  39.2 3.9 %collective-permute-start.16 = (bf16[512,256]{1,0:T(8,128)(2,1)S(1)}, bf16[512,256]{1,0:T(8,128)(2,1)S(1)}, u32[]{:S(2)}, u32[]{:S(2)}) collective-permute-start(bf16[512,256]{1,0:T(8,128)(2,1)S(1)} %get-tuple-element.57), channel_id=1, source_target_pairs={{0,28},{4,0},{8,4},{12,8},{16,12},{20,16},{24,20},{28,24},{1,29},{... | collective-permute-start | bytes 786440 | tf_op jit(solution)/shard_map/ppermute | solution.py:28
  43.1 1.5 %shard_map.86 = (bf16[512,256]{1,0:T(8,128)(2,1)S(1)}, bf16[512,256]{1,0:T(8,128)(2,1)S(1)}, bf16[512,256]{1,0:T(8,128)(2,1)S(1)}, bf16[512,256]{1,0:T(8,128)(2,1)S(1)}, bf16[512,256]{1,0:T(8,128)(2,1)S(1)}) custom-call(bf16[256,8192]{1,0:T(8,128)(2,1)} %bitcast.24, bf16[256,256]{1,0:T(8,128)(2,1)S(1)} %shard_map.85.refs_1_.refs_0_), custom_call_target="tpu_custom_call" | custom-call | bytes 786432 | tf_op jit(solution)/shard_map/pallas_call | solution.py:67
  44.6 2.9 %collective-permute-start.6 = (bf16[512,256]{1,0:T(8,128)(2,1)S(1)}, bf16[512,256]{1,0:T(8,128)(2,1)S(1)}, u32[]{:S(2)}, u32[]{:S(2)}) collective-permute-start(bf16[512,256]{1,0:T(8,128)(2,1)S(1)} %get-tuple-element.47), channel_id=1, source_target_pairs={{0,1},{1,2},{2,3},{3,0},{4,5},{5,6},{6,7},{7,4},{8,9},{9,10},{10,1... | collective-permute-start | bytes 786440 | tf_op jit(solution)/shard_map/ppermute | solution.py:28
  47.5 2.1 %collective-permute-start.7 = (bf16[512,256]{1,0:T(8,128)(2,1)S(1)}, bf16[512,256]{1,0:T(8,128)(2,1)S(1)}, u32[]{:S(2)}, u32[]{:S(2)}) collective-permute-start(bf16[512,256]{1,0:T(8,128)(2,1)S(1)} %get-tuple-element.48), channel_id=1, source_target_pairs={{0,3},{1,0},{2,1},{3,2},{4,7},{5,4},{6,5},{7,6},{8,11},{9,8},{10,9... | collective-permute-start | bytes 786440 | tf_op jit(solution)/shard_map/ppermute | solution.py:28
  51.5 3.3 %collective-permute-done.6.refs_0_ = bf16[512,256]{1,0:T(8,128)(2,1)S(1)} collective-permute-done((bf16[512,256]{1,0:T(8,128)(2,1)S(1)}, bf16[512,256]{1,0:T(8,128)(2,1)S(1)}, u32[]{:S(2)}, u32[]{:S(2)}) %collective-permute-start.6) | collective-permute-done | bytes 262176 | tf_op jit(solution)/shard_map/ppermute | solution.py:28
  55.8 5.4 %collective-permute-done.8.refs_2_ = bf16[512,256]{1,0:T(8,128)(2,1)S(1)} collective-permute-done((bf16[512,256]{1,0:T(8,128)(2,1)S(1)}, bf16[512,256]{1,0:T(8,128)(2,1)S(1)}, u32[]{:S(2)}, u32[]{:S(2)}) %collective-permute-start.8) | collective-permute-done | bytes 262176 | tf_op jit(solution)/shard_map/ppermute | solution.py:28
  61.5 2.0 %collective-permute-start.19 = (bf16[512,256]{1,0:T(8,128)(2,1)S(1)}, bf16[512,256]{1,0:T(8,128)(2,1)S(1)}, u32[]{:S(2)}, u32[]{:S(2)}) collective-permute-start(bf16[512,256]{1,0:T(8,128)(2,1)S(1)} %get-tuple-element.58.refs_3_.refs_6_), channel_id=1, source_target_pairs={{0,4},{4,8},{8,12},{12,16},{16,20},{20,24},{24,28},{28,0},{1,5},{5... | collective-permute-start | bytes 786440 | tf_op jit(solution)/shard_map/ppermute | solution.py:28
  64.2 2.9 %collective-permute-done.23.refs_1_ = bf16[256,256]{1,0:T(8,128)(2,1)S(1)} collective-permute-done((bf16[256,256]{1,0:T(8,128)(2,1)S(1)}, bf16[256,256]{1,0:T(8,128)(2,1)S(1)}, u32[]{:S(2)}, u32[]{:S(2)}) %collective-permute-start.23) | collective-permute-done | bytes 131104 | tf_op jit(solution)/shard_map/ppermute | solution.py:367
  67.2 4.0 %collective-permute-start.24 = (bf16[256,256]{1,0:T(8,128)(2,1)S(1)}, bf16[256,256]{1,0:T(8,128)(2,1)S(1)}, u32[]{:S(2)}, u32[]{:S(2)}) collective-permute-start(bf16[256,256]{1,0:T(8,128)(2,1)S(1)} %shard_map.94.refs_0_), channel_id=1, source_target_pairs={{0,16},{4,20},{8,24},{12,28},{16,0},{20,4},{24,8},{28,12},{1,17},{... | collective-permute-start | bytes 393224 | tf_op jit(solution)/shard_map/ppermute | solution.py:367
  71.2 1.4 %collective-permute-start.17 = (bf16[768,256]{1,0:T(8,128)(2,1)S(1)}, bf16[768,256]{1,0:T(8,128)(2,1)S(1)}, u32[]{:S(2)}, u32[]{:S(2)}) collective-permute-start(bf16[768,256]{1,0:T(8,128)(2,1)S(1)} %get-tuple-element.59.refs_5_), channel_id=1, source_target_pairs={{0,192},{192,0},{64,128},{128,64},{1,193},{193,1},{65,129},{129,65... | collective-permute-start | bytes 1179656 | tf_op jit(solution)/shard_map/ppermute | solution.py:172
  72.6 4.3 %shard_map.92.refs_9_ = f32[4,256,256]{2,1,0:T(8,128)S(1)} custom-call(bf16[272,256]{1,0:T(8,128)(2,1)S(1)} %get-tuple-element.39.refs_1_.refs_0_, bf16[272,256]{1,0:T(8,128)(2,1)S(1)} %collective-permute-done.refs_1_, bf16[272,256]{1,0:T(8,128)(2,1)S(1)} %collective-permute-done.1.refs_2_, bf16[272,256]{1,0:T(8,128)(2,1)S(1)} %collective-permute-done.2.refs_3_, ...), custom_call_target="tpu_custom_call" | custom-call | flops 2147483648 | bytes 3145728 | tf_op jit(solution)/shard_map/pallas_call | solution.py:67
  78.1 3.3 %collective-permute-start.26 = (bf16[256,256]{1,0:T(8,128)(2,1)S(1)}, bf16[256,256]{1,0:T(8,128)(2,1)S(1)}, u32[]{:S(2)}, u32[]{:S(2)}) collective-permute-start(bf16[256,256]{1,0:T(8,128)(2,1)S(1)} %shard_map.95.refs_4_), channel_id=1, source_target_pairs={{0,3},{1,0},{2,1},{3,2},{4,7},{5,4},{6,5},{7,6},{8,11},{9,8},{10,9... | collective-permute-start | bytes 393224 | tf_op jit(solution)/shard_map/ppermute | solution.py:28
  82.5 1.5 %collective-permute-done.25.refs_5_ = bf16[256,256]{1,0:T(8,128)(2,1)S(1)} collective-permute-done((bf16[256,256]{1,0:T(8,128)(2,1)S(1)}, bf16[256,256]{1,0:T(8,128)(2,1)S(1)}, u32[]{:S(2)}, u32[]{:S(2)}) %collective-permute-start.25) | collective-permute-done | bytes 131104 | tf_op jit(solution)/shard_map/ppermute | solution.py:28
  84.0 1.9 %collective-permute-start.21 = (bf16[512,256]{1,0:T(8,128)(2,1)S(1)}, bf16[512,256]{1,0:T(8,128)(2,1)S(1)}, u32[]{:S(2)}, u32[]{:S(2)}) collective-permute-start(bf16[512,256]{1,0:T(8,128)(2,1)S(1)} %get-tuple-element.63), channel_id=1, source_target_pairs={{0,28},{4,0},{8,4},{12,8},{16,12},{20,16},{24,20},{28,24},{1,29},{... | collective-permute-start | bytes 786440 | tf_op jit(solution)/shard_map/ppermute | solution.py:28
  86.7 2.5 %shard_map.96 = (bf16[256,256]{1,0:T(8,128)(2,1)S(1)}, bf16[256,256]{1,0:T(8,128)(2,1)S(1)}, bf16[256,256]{1,0:T(8,128)(2,1)S(1)}, bf16[256,256]{1,0:T(8,128)(2,1)S(1)}) custom-call(bf16[272,256]{1,0:T(8,128)(2,1)S(1)} %get-tuple-element.39.refs_1_.refs_0_, bf16[272,256]{1,0:T(8,128)(2,1)S(1)} %collective-permute-done.refs_1_, ...), custom_call_target="tpu_custom_call" | custom-call | flops 1073741824 | bytes 3145728 | tf_op jit(solution)/shard_map/pallas_call | solution.py:67
  92.2 1.7 %collective-permute-start.30 = (bf16[256,256]{1,0:T(8,128)(2,1)S(1)}, bf16[256,256]{1,0:T(8,128)(2,1)S(1)}, u32[]{:S(2)}, u32[]{:S(2)}) collective-permute-start(bf16[256,256]{1,0:T(8,128)(2,1)S(1)} %get-tuple-element.67), channel_id=1, source_target_pairs={{0,128},{64,192},{128,0},{192,64},{1,129},{65,193},{129,1},{193,65... | collective-permute-start | bytes 393224 | tf_op jit(solution)/shard_map/ppermute | solution.py:28
  95.0 2.5 %collective-permute-done.30.refs_6_ = bf16[256,256]{1,0:T(8,128)(2,1)S(1)} collective-permute-done((bf16[256,256]{1,0:T(8,128)(2,1)S(1)}, bf16[256,256]{1,0:T(8,128)(2,1)S(1)}, u32[]{:S(2)}, u32[]{:S(2)}) %collective-permute-start.30) | collective-permute-done | bytes 131104 | tf_op jit(solution)/shard_map/ppermute | solution.py:28
  97.5 1.4 %collective-permute-done.31.refs_7_ = bf16[256,256]{1,0:T(8,128)(2,1)S(1)} collective-permute-done((bf16[256,256]{1,0:T(8,128)(2,1)S(1)}, bf16[256,256]{1,0:T(8,128)(2,1)S(1)}, u32[]{:S(2)}, u32[]{:S(2)}) %collective-permute-start.31) | collective-permute-done | bytes 131104 | tf_op jit(solution)/shard_map/ppermute | solution.py:28
  100.8 8.5 %collective-permute-done.32 = bf16[512,256]{1,0:T(8,128)(2,1)S(1)} collective-permute-done((bf16[512,256]{1,0:T(8,128)(2,1)S(1)}, bf16[512,256]{1,0:T(8,128)(2,1)S(1)}, u32[]{:S(2)}, u32[]{:S(2)}) %collective-permute-start.32) | collective-permute-done | bytes 262176 | tf_op jit(solution)/shard_map/ppermute | solution.py:517
  (67 shorter events, 24.3 us)
Async XLA Ops:
  1.7 22.9 %collective-permute-start.3 = (bf16[1024,256]{1,0:T(8,128)(2,1)S(1)}, bf16[1024,256]{1,0:T(8,128)(2,1)S(1)}, u32[]{:S(2)}, u32[]{:S(2)}) collective-permute-start(bf16[1024,256]{1,0:T(8,128)(2,1)S(1)} %get-tuple-element.38.refs_2_), channel_id=1, source_target_pairs={{0,1},{1,2},{2,3},{3,0},{4,5},{5,6},{6,7},{7,4},{8,9},{9,10},{10,1... | collective-permute-start | bytes 1572872 | tf_op jit(solution)/shard_map/ppermute | solution.py:28
  4.8 6.8 %collective-permute-start = (bf16[272,256]{1,0:T(8,128)(2,1)S(1)}, bf16[272,256]{1,0:T(8,128)(2,1)S(1)}, u32[]{:S(2)}, u32[]{:S(2)}) collective-permute-start(bf16[272,256]{1,0:T(8,128)(2,1)S(1)} %get-tuple-element.40), channel_id=1, source_target_pairs={{0,64},{64,128},{128,192},{192,0},{1,65},{65,129},{129,193},{193,1... | collective-permute-start | bytes 417800 | tf_op jit(solution)/shard_map/ppermute | solution.py:28
  6.1 20.0 %collective-permute-start.4 = (bf16[1024,256]{1,0:T(8,128)(2,1)S(1)}, bf16[1024,256]{1,0:T(8,128)(2,1)S(1)}, u32[]{:S(2)}, u32[]{:S(2)}) collective-permute-start(bf16[1024,256]{1,0:T(8,128)(2,1)S(1)} %get-tuple-element.45), channel_id=1, source_target_pairs={{0,3},{1,0},{2,1},{3,2},{4,7},{5,4},{6,5},{7,6},{8,11},{9,8},{10,9... | collective-permute-start | bytes 1572872 | tf_op jit(solution)/shard_map/ppermute | solution.py:28
  7.5 21.6 %collective-permute-start.5 = (bf16[1024,256]{1,0:T(8,128)(2,1)S(1)}, bf16[1024,256]{1,0:T(8,128)(2,1)S(1)}, u32[]{:S(2)}, u32[]{:S(2)}) collective-permute-start(bf16[1024,256]{1,0:T(8,128)(2,1)S(1)} %get-tuple-element.46), channel_id=1, source_target_pairs={{0,2},{1,3},{2,0},{3,1},{4,6},{5,7},{6,4},{7,5},{8,10},{9,11},{10,... | collective-permute-start | bytes 1572872 | tf_op jit(solution)/shard_map/ppermute | solution.py:28
  9.1 5.4 %collective-permute-start.1 = (bf16[272,256]{1,0:T(8,128)(2,1)S(1)}, bf16[272,256]{1,0:T(8,128)(2,1)S(1)}, u32[]{:S(2)}, u32[]{:S(2)}) collective-permute-start(bf16[272,256]{1,0:T(8,128)(2,1)S(1)} %get-tuple-element.41), channel_id=1, source_target_pairs={{0,128},{64,192},{128,0},{192,64},{1,129},{65,193},{129,1},{193,65... | collective-permute-start | bytes 417800 | tf_op jit(solution)/shard_map/ppermute | solution.py:28
  11.6 5.3 %collective-permute-start.2 = (bf16[272,256]{1,0:T(8,128)(2,1)S(1)}, bf16[272,256]{1,0:T(8,128)(2,1)S(1)}, u32[]{:S(2)}, u32[]{:S(2)}) collective-permute-start(bf16[272,256]{1,0:T(8,128)(2,1)S(1)} %get-tuple-element.42), channel_id=1, source_target_pairs={{0,192},{64,0},{128,64},{192,128},{1,193},{65,1},{129,65},{193,129... | collective-permute-start | bytes 417800 | tf_op jit(solution)/shard_map/ppermute | solution.py:28
  19.5 4.4 %collective-permute-start.12 = (bf16[256,256]{1,0:T(8,128)(2,1)S(1)}, bf16[256,256]{1,0:T(8,128)(2,1)S(1)}, u32[]{:S(2)}, u32[]{:S(2)}) collective-permute-start(bf16[256,256]{1,0:T(8,128)(2,1)S(1)} %shard_map.85.refs_1_.refs_0_), channel_id=1, source_target_pairs={{0,4},{4,0},{8,12},{12,8},{16,20},{20,16},{24,28},{28,24},{1,5},{5... | collective-permute-start | bytes 393224 | tf_op jit(solution)/shard_map/ppermute | solution.py:367
  21.2 12.7 %collective-permute-start.9 = (bf16[256,256]{1,0:T(8,128)(2,1)S(1)}, bf16[256,256]{1,0:T(8,128)(2,1)S(1)}, u32[]{:S(2)}, u32[]{:S(2)}) collective-permute-start(bf16[256,256]{1,0:T(8,128)(2,1)S(1)} %get-tuple-element.43.refs_5_), channel_id=1, source_target_pairs={{0,1},{1,2},{2,3},{3,0},{4,5},{5,6},{6,7},{7,4},{8,9},{9,10},{10,1... | collective-permute-start | bytes 393224 | tf_op jit(solution)/shard_map/ppermute | solution.py:28
  23.9 10.1 %collective-permute-start.10 = (bf16[256,256]{1,0:T(8,128)(2,1)S(1)}, bf16[256,256]{1,0:T(8,128)(2,1)S(1)}, u32[]{:S(2)}, u32[]{:S(2)}) collective-permute-start(bf16[256,256]{1,0:T(8,128)(2,1)S(1)} %get-tuple-element.51), channel_id=1, source_target_pairs={{0,3},{1,0},{2,1},{3,2},{4,7},{5,4},{6,5},{7,6},{8,11},{9,8},{10,9... | collective-permute-start | bytes 393224 | tf_op jit(solution)/shard_map/ppermute | solution.py:28
  24.6 10.0 %collective-permute-start.11 = (bf16[256,256]{1,0:T(8,128)(2,1)S(1)}, bf16[256,256]{1,0:T(8,128)(2,1)S(1)}, u32[]{:S(2)}, u32[]{:S(2)}) collective-permute-start(bf16[256,256]{1,0:T(8,128)(2,1)S(1)} %get-tuple-element.52), channel_id=1, source_target_pairs={{0,2},{1,3},{2,0},{3,1},{4,6},{5,7},{6,4},{7,5},{8,10},{9,11},{10,... | collective-permute-start | bytes 393224 | tf_op jit(solution)/shard_map/ppermute | solution.py:28
  34.7 12.8 %collective-permute-start.13 = (bf16[384,256]{1,0:T(8,128)(2,1)S(1)}, bf16[384,256]{1,0:T(8,128)(2,1)S(1)}, u32[]{:S(2)}, u32[]{:S(2)}) collective-permute-start(bf16[384,256]{1,0:T(8,128)(2,1)S(1)} %get-tuple-element.55.refs_5_), channel_id=1, source_target_pairs={{0,64},{64,128},{128,192},{192,0},{1,65},{65,129},{129,193},{193,1... | collective-permute-start | bytes 589832 | tf_op jit(solution)/shard_map/ppermute | solution.py:28
  36.1 13.5 %collective-permute-start.14 = (bf16[384,256]{1,0:T(8,128)(2,1)S(1)}, bf16[384,256]{1,0:T(8,128)(2,1)S(1)}, u32[]{:S(2)}, u32[]{:S(2)}) collective-permute-start(bf16[384,256]{1,0:T(8,128)(2,1)S(1)} %get-tuple-element.56.refs_6_), channel_id=1, source_target_pairs={{0,192},{64,0},{128,64},{192,128},{1,193},{65,1},{129,65},{193,129... | collective-permute-start | bytes 589832 | tf_op jit(solution)/shard_map/ppermute | solution.py:28
  37.5 13.3 %collective-permute-start.15 = (bf16[512,256]{1,0:T(8,128)(2,1)S(1)}, bf16[512,256]{1,0:T(8,128)(2,1)S(1)}, u32[]{:S(2)}, u32[]{:S(2)}) collective-permute-start(bf16[512,256]{1,0:T(8,128)(2,1)S(1)} %get-tuple-element.54.refs_3_), channel_id=1, source_target_pairs={{0,4},{4,8},{8,12},{12,16},{16,20},{20,24},{24,28},{28,0},{1,5},{5... | collective-permute-start | bytes 786440 | tf_op jit(solution)/shard_map/ppermute | solution.py:28
  39.2 11.6 %collective-permute-start.16 = (bf16[512,256]{1,0:T(8,128)(2,1)S(1)}, bf16[512,256]{1,0:T(8,128)(2,1)S(1)}, u32[]{:S(2)}, u32[]{:S(2)}) collective-permute-start(bf16[512,256]{1,0:T(8,128)(2,1)S(1)} %get-tuple-element.57), channel_id=1, source_target_pairs={{0,28},{4,0},{8,4},{12,8},{16,12},{20,16},{24,20},{28,24},{1,29},{... | collective-permute-start | bytes 786440 | tf_op jit(solution)/shard_map/ppermute | solution.py:28
  44.6 10.1 %collective-permute-start.6 = (bf16[512,256]{1,0:T(8,128)(2,1)S(1)}, bf16[512,256]{1,0:T(8,128)(2,1)S(1)}, u32[]{:S(2)}, u32[]{:S(2)}) collective-permute-start(bf16[512,256]{1,0:T(8,128)(2,1)S(1)} %get-tuple-element.47), channel_id=1, source_target_pairs={{0,1},{1,2},{2,3},{3,0},{4,5},{5,6},{6,7},{7,4},{8,9},{9,10},{10,1... | collective-permute-start | bytes 786440 | tf_op jit(solution)/shard_map/ppermute | solution.py:28
  47.5 8.3 %collective-permute-start.7 = (bf16[512,256]{1,0:T(8,128)(2,1)S(1)}, bf16[512,256]{1,0:T(8,128)(2,1)S(1)}, u32[]{:S(2)}, u32[]{:S(2)}) collective-permute-start(bf16[512,256]{1,0:T(8,128)(2,1)S(1)} %get-tuple-element.48), channel_id=1, source_target_pairs={{0,3},{1,0},{2,1},{3,2},{4,7},{5,4},{6,5},{7,6},{8,11},{9,8},{10,9... | collective-permute-start | bytes 786440 | tf_op jit(solution)/shard_map/ppermute | solution.py:28
  49.6 11.7 %collective-permute-start.8 = (bf16[512,256]{1,0:T(8,128)(2,1)S(1)}, bf16[512,256]{1,0:T(8,128)(2,1)S(1)}, u32[]{:S(2)}, u32[]{:S(2)}) collective-permute-start(bf16[512,256]{1,0:T(8,128)(2,1)S(1)} %get-tuple-element.49), channel_id=1, source_target_pairs={{0,2},{1,3},{2,0},{3,1},{4,6},{5,7},{6,4},{7,5},{8,10},{9,11},{10,... | collective-permute-start | bytes 786440 | tf_op jit(solution)/shard_map/ppermute | solution.py:28
  61.3 15.7 %collective-permute-start.18 = (bf16[768,256]{1,0:T(8,128)(2,1)S(1)}, bf16[768,256]{1,0:T(8,128)(2,1)S(1)}, u32[]{:S(2)}, u32[]{:S(2)}) collective-permute-start(bf16[768,256]{1,0:T(8,128)(2,1)S(1)} %get-tuple-element.61.refs_5_), channel_id=1, source_target_pairs={{0,64},{64,0},{128,192},{192,128},{1,65},{65,1},{129,193},{193,129... | collective-permute-start | bytes 1179656 | tf_op jit(solution)/shard_map/ppermute | solution.py:172
  61.4 5.8 %collective-permute-start.23 = (bf16[256,256]{1,0:T(8,128)(2,1)S(1)}, bf16[256,256]{1,0:T(8,128)(2,1)S(1)}, u32[]{:S(2)}, u32[]{:S(2)}) collective-permute-start(bf16[256,256]{1,0:T(8,128)(2,1)S(1)} %shard_map.87.refs_5_.refs_0_), channel_id=1, source_target_pairs={{0,8},{4,12},{8,0},{12,4},{16,24},{20,28},{24,16},{28,20},{1,9},{5... | collective-permute-start | bytes 393224 | tf_op jit(solution)/shard_map/ppermute | solution.py:367
  61.5 15.4 %collective-permute-start.19 = (bf16[512,256]{1,0:T(8,128)(2,1)S(1)}, bf16[512,256]{1,0:T(8,128)(2,1)S(1)}, u32[]{:S(2)}, u32[]{:S(2)}) collective-permute-start(bf16[512,256]{1,0:T(8,128)(2,1)S(1)} %get-tuple-element.58.refs_3_.refs_6_), channel_id=1, source_target_pairs={{0,4},{4,8},{8,12},{12,16},{16,20},{20,24},{24,28},{28,0},{1,5},{5... | collective-permute-start | bytes 786440 | tf_op jit(solution)/shard_map/ppermute | solution.py:28
  63.5 13.5 %collective-permute-start.20 = (bf16[512,256]{1,0:T(8,128)(2,1)S(1)}, bf16[512,256]{1,0:T(8,128)(2,1)S(1)}, u32[]{:S(2)}, u32[]{:S(2)}) collective-permute-start(bf16[512,256]{1,0:T(8,128)(2,1)S(1)} %get-tuple-element.62), channel_id=1, source_target_pairs={{0,28},{4,0},{8,4},{12,8},{16,12},{20,16},{24,20},{28,24},{1,29},{... | collective-permute-start | bytes 786440 | tf_op jit(solution)/shard_map/ppermute | solution.py:28
  67.2 10.6 %collective-permute-start.24 = (bf16[256,256]{1,0:T(8,128)(2,1)S(1)}, bf16[256,256]{1,0:T(8,128)(2,1)S(1)}, u32[]{:S(2)}, u32[]{:S(2)}) collective-permute-start(bf16[256,256]{1,0:T(8,128)(2,1)S(1)} %shard_map.94.refs_0_), channel_id=1, source_target_pairs={{0,16},{4,20},{8,24},{12,28},{16,0},{20,4},{24,8},{28,12},{1,17},{... | collective-permute-start | bytes 393224 | tf_op jit(solution)/shard_map/ppermute | solution.py:367
  71.2 18.0 %collective-permute-start.17 = (bf16[768,256]{1,0:T(8,128)(2,1)S(1)}, bf16[768,256]{1,0:T(8,128)(2,1)S(1)}, u32[]{:S(2)}, u32[]{:S(2)}) collective-permute-start(bf16[768,256]{1,0:T(8,128)(2,1)S(1)} %get-tuple-element.59.refs_5_), channel_id=1, source_target_pairs={{0,192},{192,0},{64,128},{128,64},{1,193},{193,1},{65,129},{129,65... | collective-permute-start | bytes 1179656 | tf_op jit(solution)/shard_map/ppermute | solution.py:172
  77.7 11.6 %collective-permute-start.22 = (bf16[512,256]{1,0:T(8,128)(2,1)S(1)}, bf16[512,256]{1,0:T(8,128)(2,1)S(1)}, u32[]{:S(2)}, u32[]{:S(2)}) collective-permute-start(bf16[512,256]{1,0:T(8,128)(2,1)S(1)} %get-tuple-element.64.refs_10_), channel_id=1, source_target_pairs={{0,4},{4,8},{8,12},{12,16},{16,20},{20,24},{24,28},{28,0},{1,5},{5... | collective-permute-start | bytes 786440 | tf_op jit(solution)/shard_map/ppermute | solution.py:28
  77.8 6.2 %collective-permute-start.25 = (bf16[256,256]{1,0:T(8,128)(2,1)S(1)}, bf16[256,256]{1,0:T(8,128)(2,1)S(1)}, u32[]{:S(2)}, u32[]{:S(2)}) collective-permute-start(bf16[256,256]{1,0:T(8,128)(2,1)S(1)} %shard_map.95.refs_4_), channel_id=1, source_target_pairs={{0,1},{1,2},{2,3},{3,0},{4,5},{5,6},{6,7},{7,4},{8,9},{9,10},{10,1... | collective-permute-start | bytes 393224 | tf_op jit(solution)/shard_map/ppermute | solution.py:28
  78.1 7.8 %collective-permute-start.26 = (bf16[256,256]{1,0:T(8,128)(2,1)S(1)}, bf16[256,256]{1,0:T(8,128)(2,1)S(1)}, u32[]{:S(2)}, u32[]{:S(2)}) collective-permute-start(bf16[256,256]{1,0:T(8,128)(2,1)S(1)} %shard_map.95.refs_4_), channel_id=1, source_target_pairs={{0,3},{1,0},{2,1},{3,2},{4,7},{5,4},{6,5},{7,6},{8,11},{9,8},{10,9... | collective-permute-start | bytes 393224 | tf_op jit(solution)/shard_map/ppermute | solution.py:28
  81.4 5.3 %collective-permute-start.27 = (bf16[256,256]{1,0:T(8,128)(2,1)S(1)}, bf16[256,256]{1,0:T(8,128)(2,1)S(1)}, u32[]{:S(2)}, u32[]{:S(2)}) collective-permute-start(bf16[256,256]{1,0:T(8,128)(2,1)S(1)} %shard_map.95.refs_4_), channel_id=1, source_target_pairs={{0,2},{1,3},{2,0},{3,1},{4,6},{5,7},{6,4},{7,5},{8,10},{9,11},{10,... | collective-permute-start | bytes 393224 | tf_op jit(solution)/shard_map/ppermute | solution.py:28
  84.0 9.9 %collective-permute-start.21 = (bf16[512,256]{1,0:T(8,128)(2,1)S(1)}, bf16[512,256]{1,0:T(8,128)(2,1)S(1)}, u32[]{:S(2)}, u32[]{:S(2)}) collective-permute-start(bf16[512,256]{1,0:T(8,128)(2,1)S(1)} %get-tuple-element.63), channel_id=1, source_target_pairs={{0,28},{4,0},{8,4},{12,8},{16,12},{20,16},{24,20},{28,24},{1,29},{... | collective-permute-start | bytes 786440 | tf_op jit(solution)/shard_map/ppermute | solution.py:28
  89.7 9.2 %collective-permute-start.28 = (bf16[512,256]{1,0:T(8,128)(2,1)S(1)}, bf16[512,256]{1,0:T(8,128)(2,1)S(1)}, u32[]{:S(2)}, u32[]{:S(2)}) collective-permute-start(bf16[512,256]{1,0:T(8,128)(2,1)S(1)} %shard_map.97.refs_8_), channel_id=1, source_target_pairs={{0,4},{4,8},{8,12},{12,16},{16,20},{20,24},{24,28},{28,0},{1,5},{5... | collective-permute-start | bytes 786440 | tf_op jit(solution)/shard_map/ppermute | solution.py:28
  92.2 5.3 %collective-permute-start.30 = (bf16[256,256]{1,0:T(8,128)(2,1)S(1)}, bf16[256,256]{1,0:T(8,128)(2,1)S(1)}, u32[]{:S(2)}, u32[]{:S(2)}) collective-permute-start(bf16[256,256]{1,0:T(8,128)(2,1)S(1)} %get-tuple-element.67), channel_id=1, source_target_pairs={{0,128},{64,192},{128,0},{192,64},{1,129},{65,193},{129,1},{193,65... | collective-permute-start | bytes 393224 | tf_op jit(solution)/shard_map/ppermute | solution.py:28
  93.9 5.0 %collective-permute-start.31 = (bf16[256,256]{1,0:T(8,128)(2,1)S(1)}, bf16[256,256]{1,0:T(8,128)(2,1)S(1)}, u32[]{:S(2)}, u32[]{:S(2)}) collective-permute-start(bf16[256,256]{1,0:T(8,128)(2,1)S(1)} %get-tuple-element.68), channel_id=1, source_target_pairs={{0,64},{64,128},{128,192},{192,0},{1,65},{65,129},{129,193},{193,1... | collective-permute-start | bytes 393224 | tf_op jit(solution)/shard_map/ppermute | solution.py:28
  99.5 9.8 %collective-permute-start.32 = (bf16[512,256]{1,0:T(8,128)(2,1)S(1)}, bf16[512,256]{1,0:T(8,128)(2,1)S(1)}, u32[]{:S(2)}, u32[]{:S(2)}) collective-permute-start(bf16[512,256]{1,0:T(8,128)(2,1)S(1)} %get-tuple-element.69), channel_id=1, source_target_pairs={{0,32},{1,33},{2,34},{3,35},{4,36},{5,37},{6,38},{7,39},{8,40},{9,... | collective-permute-start | bytes 786440 | tf_op jit(solution)/shard_map/ppermute | solution.py:517
  (8 other events, 115.3 us)

commit v5 on v4

--- a/solution.py
+++ b/solution.py
@@ -322,23 +322,32 @@
     for k, item in enumerate((i0, i1, i2, i3)):
         item_ref[k] = item[...]
     shard = lax.axis_index(Z) * NY + lax.axis_index(Y)
-
-    def lanes_of(v):
-        return pl.ds(pl.multiple_of((place_ref[v] - shard * 2) * BLK, BLK), BLK)
-
     for v in range(VARS):
-        rhs_ref[v * BLK : (v + 1) * BLK, :] = jnp.zeros((BLK, 256), BF16)
-        rhs_ref[v * BLK : (v + 1) * BLK, lanes_of(v)] = mats_ref[v]
+        first = (v // 2) * BLK
+        lanes = slice((v % 2) * BLK, (v % 2 + 1) * BLK)
+        rhs_ref[first : first + BLK, lanes] = mats_ref[v]
 
     def window(k, carry):
         item = item_ref.at[k]
-        variant = variant_columns(item, 128)
-        pieces = []
+        ids = item[WINDOW : WINDOW + 1, :].astype(F32)
+        code = jnp.full(ids.shape, 64.0, F32)
         for v in range(VARS):
-            piece = item[0:WINDOW, lanes_of(v)].astype(F32)
-            pieces.append(jnp.where(variant == float(v), piece, 0.0).astype(BF16))
-        lhs = jnp.concatenate(pieces, axis=1)
-        out_ref[k] = jnp.dot(lhs, rhs_ref[...], preferred_element_type=F32)
+            place = (place_ref[v] - shard * 2).astype(F32)
+            code = jnp.where(ids == float(v), v // 2 + 16.0 * (v % 2) + 32.0 * place, code)
+        code = spread_columns(code, 128)
+        upper = (code >= 32.0) & (code < 64.0)
+        rest = jnp.where(upper, code - 32.0, code)
+        odd = rest >= 16.0
+        pair = jnp.where(odd, rest - 16.0, rest).astype(BF16)
+        low = item[0:WINDOW, 0:BLK].astype(F32)
+        high = item[0:WINDOW, BLK : 2 * BLK].astype(F32)
+        picked = jnp.where(upper, high, low).astype(BF16)
+        zero = jnp.zeros_like(picked)
+        pieces = [jnp.where(pair == jnp.bfloat16(p), picked, zero) for p in range(VARS // 2)]
+        both = jnp.dot(jnp.concatenate(pieces, axis=1), rhs_ref[...], preferred_element_type=F32)
+        one = jnp.where(odd, both[:, BLK:], both[:, 0:BLK])
+        out_ref[k, :, 0:BLK] = jnp.where(upper, 0.0, one)
+        out_ref[k, :, BLK : 2 * BLK] = jnp.where(upper, one, 0.0)
         return carry
 
     lax.fori_loop(0, NX, window, 0)
@@ -351,8 +360,8 @@
         [whole((WINDOW + IDROWS, WIDTH))] * NX + [whole((VARS, BLK, BLK)), SMEM],
         shape((NX, WINDOW, 256), F32),
         whole((NX, WINDOW, 256)),
-        [pltpu.VMEM((NX, WINDOW + IDROWS, WIDTH), BF16), pltpu.VMEM((VARS * BLK, 256), BF16)],
-        (2 * 1024 * 4096 * 256, 3 << 20),
+        [pltpu.VMEM((NX, WINDOW + IDROWS, WIDTH), BF16), pltpu.VMEM((VARS * BLK // 2, 256), BF16)],
+        (2 * 1024 * 2048 * 256, 3 << 20),
         10,
         after,
     )
@@ -393,11 +402,12 @@
     half = lax.div(lax.broadcasted_iota(jnp.int32, (1, 128), 1), jnp.int32(RANK)).astype(F32)
 
     def window(k, carry):
-        variant = spread_columns(item_ref[k, 0:1, :], 128)
-        two = two_ref[k]
+        variant = (spread_columns(item_ref[k, 0:1, :], 128) - half).astype(BF16)
+        two = two_ref[k].astype(BF16)
+        zero = jnp.zeros_like(two)
         pieces = []
         for i in range(VARS // 2):
-            pieces.append(jnp.where(variant == half + float(2 * i), two, 0.0).astype(BF16))
+            pieces.append(jnp.where(variant == jnp.bfloat16(2 * i), two, zero))
         lhs = jnp.concatenate(pieces, axis=1)
         total = block_ref[k] + jnp.dot(lhs, up_ref[...], preferred_element_type=F32)
         out_ref[k] = total.astype(BF16)

time: 110 us -> 116 us (1.055)
  waiting for transfers between devices: 41.2 us -> 47.4 us
    ppermute x3, waiting for transfers between devices: 5.19 us -> 9.82 us  [exchanged_sum(): other = lax.ppermute(value, axis, [(i, i ^ bit) for i in range(count)])]
    ppermute x1, waiting for transfers between devices: 8.49 us -> 9.92 us  [steps(): carried = lax.ppermute(first_out, 'section', [(0, 1)])]
  transfers between devices with their start and end apart: 33 -> 33, of which waited for: 16 -> 15; matrix products, arithmetic and copies ran while one was open for 0% -> 0% of each run, Pallas kernels for 15% -> 13%
where the time goes in v5:
time: 116 us
  starting transfers between devices  49.9 us (43%)
  waiting for transfers between devices  47.4 us (41%)
  Pallas kernels  17.2 us (15%)
    ppermute x27, starting transfers between devices, shift(): lax.ppermute(value, axis, [(i, (i + steps) % count) for i in range(count)])  41.6 us
    ppermute x27, waiting for transfers between devices, shift(): lax.ppermute(value, axis, [(i, (i + steps) % count) for i in range(count)])  27.7 us
    pallas_call x18, Pallas kernels, call(): pl.pallas_call(body, out_shape=outs, in_specs=list(in_specs) + [ANY] * m,...  17.2 us
    ppermute x1, waiting for transfers between devices, steps(): carried = lax.ppermute(first_out, 'section', [(0, 1)])  9.92 us
    ppermute x3, waiting for transfers between devices, exchanged_sum(): other = lax.ppermute(value, axis, [(i, i ^ bit) for i in range(count)])  9.82 us
    ppermute x3, starting transfers between devices, exchanged_sum(): other = lax.ppermute(value, axis, [(i, i ^ bit) for i in range(count)])  5.55 us
  transfers between devices with their start and end apart: 33, of which 15 were waited for; matrix products, arithmetic and copies ran while one was open for 0% of the time, Pallas kernels for 13%

profile of v5, /device:TPU:1, one launch (start us, length us, event | category | flops | bytes accessed | tf_op | source)
XLA Modules:
  0.0 115.6 jit_solution(12780849222013332286)
XLA Ops:
  0.0 1.7 %shard_map.82 = (bf16[1024,256]{1,0:T(8,128)(2,1)S(1)}, bf16[1024,256]{1,0:T(8,128)(2,1)S(1)}, bf16[1024,256]{1,0:T(8,128)(2,1)S(1)}, bf16[512,256]{1,0:T(8,128)(2,1)S(1)}) custom-call(bf16[256,8192]{1,0:T(8,128)(2,1)} %bitcast.22, bf16[512,256]{1,0:T(8,128)(2,1)} %bitcast.9), custom_call_target="tpu_custom_call" | custom-call | bytes 1572864 | tf_op jit(solution)/shard_map/pallas_call | solution.py:67
  1.7 2.2 %collective-permute-start.3 = (bf16[1024,256]{1,0:T(8,128)(2,1)S(1)}, bf16[1024,256]{1,0:T(8,128)(2,1)S(1)}, u32[]{:S(2)}, u32[]{:S(2)}) collective-permute-start(bf16[1024,256]{1,0:T(8,128)(2,1)S(1)} %get-tuple-element.38.refs_2_), channel_id=1, source_target_pairs={{0,1},{1,2},{2,3},{3,0},{4,5},{5,6},{6,7},{7,4},{8,9},{9,10},{10,1... | collective-permute-start | bytes 1572872 | tf_op jit(solution)/shard_map/ppermute | solution.py:28
  6.1 1.5 %collective-permute-start.4 = (bf16[1024,256]{1,0:T(8,128)(2,1)S(1)}, bf16[1024,256]{1,0:T(8,128)(2,1)S(1)}, u32[]{:S(2)}, u32[]{:S(2)}) collective-permute-start(bf16[1024,256]{1,0:T(8,128)(2,1)S(1)} %get-tuple-element.45), channel_id=1, source_target_pairs={{0,3},{1,0},{2,1},{3,2},{4,7},{5,4},{6,5},{7,6},{8,11},{9,8},{10,9... | collective-permute-start | bytes 1572872 | tf_op jit(solution)/shard_map/ppermute | solution.py:28
  7.5 1.6 %collective-permute-start.5 = (bf16[1024,256]{1,0:T(8,128)(2,1)S(1)}, bf16[1024,256]{1,0:T(8,128)(2,1)S(1)}, u32[]{:S(2)}, u32[]{:S(2)}) collective-permute-start(bf16[1024,256]{1,0:T(8,128)(2,1)S(1)} %get-tuple-element.46), channel_id=1, source_target_pairs={{0,2},{1,3},{2,0},{3,1},{4,6},{5,7},{6,4},{7,5},{8,10},{9,11},{10,... | collective-permute-start | bytes 1572872 | tf_op jit(solution)/shard_map/ppermute | solution.py:28
  9.1 2.4 %collective-permute-start.1 = (bf16[272,256]{1,0:T(8,128)(2,1)S(1)}, bf16[272,256]{1,0:T(8,128)(2,1)S(1)}, u32[]{:S(2)}, u32[]{:S(2)}) collective-permute-start(bf16[272,256]{1,0:T(8,128)(2,1)S(1)} %get-tuple-element.41), channel_id=1, source_target_pairs={{0,128},{64,192},{128,0},{192,64},{1,129},{65,193},{129,1},{193,65... | collective-permute-start | bytes 417800 | tf_op jit(solution)/shard_map/ppermute | solution.py:28
  14.6 2.4 %collective-permute-done.2.refs_3_ = bf16[272,256]{1,0:T(8,128)(2,1)S(1)} collective-permute-done((bf16[272,256]{1,0:T(8,128)(2,1)S(1)}, bf16[272,256]{1,0:T(8,128)(2,1)S(1)}, u32[]{:S(2)}, u32[]{:S(2)}) %collective-permute-start.2) | collective-permute-done | bytes 139296 | tf_op jit(solution)/shard_map/ppermute | solution.py:28
  16.9 2.6 %shard_map.85.refs_1_.refs_0_ = bf16[256,256]{1,0:T(8,128)(2,1)S(1)} custom-call(bf16[272,256]{1,0:T(8,128)(2,1)S(1)} %get-tuple-element.39.refs_1_.refs_0_, bf16[272,256]{1,0:T(8,128)(2,1)S(1)} %collective-permute-done.refs_1_, bf16[272,256]{1,0:T(8,128)(2,1)S(1)} %collective-permute-done.1.refs_2_, bf16[272,256]{1,0:T(8,128)(2,1)S(1)} %collective-permute-done.2.refs_3_, ...), custom_call_target="tpu_custom_call" | custom-call | flops 1073741824 | bytes 2097152 | tf_op jit(solution)/shard_map/pallas_call | solution.py:67
  19.5 1.7 %collective-permute-start.12 = (bf16[256,256]{1,0:T(8,128)(2,1)S(1)}, bf16[256,256]{1,0:T(8,128)(2,1)S(1)}, u32[]{:S(2)}, u32[]{:S(2)}) collective-permute-start(bf16[256,256]{1,0:T(8,128)(2,1)S(1)} %shard_map.85.refs_1_.refs_0_), channel_id=1, source_target_pairs={{0,4},{4,0},{8,12},{12,8},{16,20},{20,16},{24,28},{28,24},{1,5},{5... | collective-permute-start | bytes 393224 | tf_op jit(solution)/shard_map/ppermute | solution.py:376
  21.6 2.3 %collective-permute-done.12.refs_1_ = bf16[256,256]{1,0:T(8,128)(2,1)S(1)} collective-permute-done((bf16[256,256]{1,0:T(8,128)(2,1)S(1)}, bf16[256,256]{1,0:T(8,128)(2,1)S(1)}, u32[]{:S(2)}, u32[]{:S(2)}) %collective-permute-start.12) | collective-permute-done | bytes 131104 | tf_op jit(solution)/shard_map/ppermute | solution.py:376
  24.6 1.4 %collective-permute-start.11 = (bf16[256,256]{1,0:T(8,128)(2,1)S(1)}, bf16[256,256]{1,0:T(8,128)(2,1)S(1)}, u32[]{:S(2)}, u32[]{:S(2)}) collective-permute-start(bf16[256,256]{1,0:T(8,128)(2,1)S(1)} %get-tuple-element.52), channel_id=1, source_target_pairs={{0,2},{1,3},{2,0},{3,1},{4,6},{5,7},{6,4},{7,5},{8,10},{9,11},{10,... | collective-permute-start | bytes 393224 | tf_op jit(solution)/shard_map/ppermute | solution.py:28
  26.1 3.0 %collective-permute-done.5.refs_4_ = bf16[1024,256]{1,0:T(8,128)(2,1)S(1)} collective-permute-done((bf16[1024,256]{1,0:T(8,128)(2,1)S(1)}, bf16[1024,256]{1,0:T(8,128)(2,1)S(1)}, u32[]{:S(2)}, u32[]{:S(2)}) %collective-permute-start.5) | collective-permute-done | bytes 524320 | tf_op jit(solution)/shard_map/ppermute | solution.py:28
  29.8 4.1 %collective-permute-done.9.refs_0_ = bf16[256,256]{1,0:T(8,128)(2,1)S(1)} collective-permute-done((bf16[256,256]{1,0:T(8,128)(2,1)S(1)}, bf16[256,256]{1,0:T(8,128)(2,1)S(1)}, u32[]{:S(2)}, u32[]{:S(2)}) %collective-permute-start.9) | collective-permute-done | bytes 131104 | tf_op jit(solution)/shard_map/ppermute | solution.py:28
  37.5 1.7 %collective-permute-start.15 = (bf16[512,256]{1,0:T(8,128)(2,1)S(1)}, bf16[512,256]{1,0:T(8,128)(2,1)S(1)}, u32[]{:S(2)}, u32[]{:S(2)}) collective-permute-start(bf16[512,256]{1,0:T(8,128)(2,1)S(1)} %get-tuple-element.54.refs_3_), channel_id=1, source_target_pairs={{0,4},{4,8},{8,12},{12,16},{16,20},{20,24},{24,28},{28,0},{1,5},{5... | collective-permute-start | bytes 786440 | tf_op jit(solution)/shard_map/ppermute | solution.py:28
  39.2 3.9 %collective-permute-start.16 = (bf16[512,256]{1,0:T(8,128)(2,1)S(1)}, bf16[512,256]{1,0:T(8,128)(2,1)S(1)}, u32[]{:S(2)}, u32[]{:S(2)}) collective-permute-start(bf16[512,256]{1,0:T(8,128)(2,1)S(1)} %get-tuple-element.57), channel_id=1, source_target_pairs={{0,28},{4,0},{8,4},{12,8},{16,12},{20,16},{24,20},{28,24},{1,29},{... | collective-permute-start | bytes 786440 | tf_op jit(solution)/shard_map/ppermute | solution.py:28
  43.1 1.5 %shard_map.86 = (bf16[512,256]{1,0:T(8,128)(2,1)S(1)}, bf16[512,256]{1,0:T(8,128)(2,1)S(1)}, bf16[512,256]{1,0:T(8,128)(2,1)S(1)}, bf16[512,256]{1,0:T(8,128)(2,1)S(1)}, bf16[512,256]{1,0:T(8,128)(2,1)S(1)}) custom-call(bf16[256,8192]{1,0:T(8,128)(2,1)} %bitcast.24, bf16[256,256]{1,0:T(8,128)(2,1)S(1)} %shard_map.85.refs_1_.refs_0_), custom_call_target="tpu_custom_call" | custom-call | bytes 786432 | tf_op jit(solution)/shard_map/pallas_call | solution.py:67
  44.6 2.9 %collective-permute-start.6 = (bf16[512,256]{1,0:T(8,128)(2,1)S(1)}, bf16[512,256]{1,0:T(8,128)(2,1)S(1)}, u32[]{:S(2)}, u32[]{:S(2)}) collective-permute-start(bf16[512,256]{1,0:T(8,128)(2,1)S(1)} %get-tuple-element.47), channel_id=1, source_target_pairs={{0,1},{1,2},{2,3},{3,0},{4,5},{5,6},{6,7},{7,4},{8,9},{9,10},{10,1... | collective-permute-start | bytes 786440 | tf_op jit(solution)/shard_map/ppermute | solution.py:28
  47.5 2.1 %collective-permute-start.7 = (bf16[512,256]{1,0:T(8,128)(2,1)S(1)}, bf16[512,256]{1,0:T(8,128)(2,1)S(1)}, u32[]{:S(2)}, u32[]{:S(2)}) collective-permute-start(bf16[512,256]{1,0:T(8,128)(2,1)S(1)} %get-tuple-element.48), channel_id=1, source_target_pairs={{0,3},{1,0},{2,1},{3,2},{4,7},{5,4},{6,5},{7,6},{8,11},{9,8},{10,9... | collective-permute-start | bytes 786440 | tf_op jit(solution)/shard_map/ppermute | solution.py:28
  51.5 3.3 %collective-permute-done.6.refs_0_ = bf16[512,256]{1,0:T(8,128)(2,1)S(1)} collective-permute-done((bf16[512,256]{1,0:T(8,128)(2,1)S(1)}, bf16[512,256]{1,0:T(8,128)(2,1)S(1)}, u32[]{:S(2)}, u32[]{:S(2)}) %collective-permute-start.6) | collective-permute-done | bytes 262176 | tf_op jit(solution)/shard_map/ppermute | solution.py:28
  55.8 5.4 %collective-permute-done.8.refs_2_ = bf16[512,256]{1,0:T(8,128)(2,1)S(1)} collective-permute-done((bf16[512,256]{1,0:T(8,128)(2,1)S(1)}, bf16[512,256]{1,0:T(8,128)(2,1)S(1)}, u32[]{:S(2)}, u32[]{:S(2)}) %collective-permute-start.8) | collective-permute-done | bytes 262176 | tf_op jit(solution)/shard_map/ppermute | solution.py:28
  61.5 2.7 %collective-permute-start.20 = (bf16[512,256]{1,0:T(8,128)(2,1)S(1)}, bf16[512,256]{1,0:T(8,128)(2,1)S(1)}, u32[]{:S(2)}, u32[]{:S(2)}) collective-permute-start(bf16[512,256]{1,0:T(8,128)(2,1)S(1)} %get-tuple-element.62), channel_id=1, source_target_pairs={{0,28},{4,0},{8,4},{12,8},{16,12},{20,16},{24,20},{28,24},{1,29},{... | collective-permute-start | bytes 786440 | tf_op jit(solution)/shard_map/ppermute | solution.py:28
  64.1 7.5 %collective-permute-done.23.refs_1_ = bf16[256,256]{1,0:T(8,128)(2,1)S(1)} collective-permute-done((bf16[256,256]{1,0:T(8,128)(2,1)S(1)}, bf16[256,256]{1,0:T(8,128)(2,1)S(1)}, u32[]{:S(2)}, u32[]{:S(2)}) %collective-permute-start.23) | collective-permute-done | bytes 131104 | tf_op jit(solution)/shard_map/ppermute | solution.py:376
  71.7 3.8 %collective-permute-start.24 = (bf16[256,256]{1,0:T(8,128)(2,1)S(1)}, bf16[256,256]{1,0:T(8,128)(2,1)S(1)}, u32[]{:S(2)}, u32[]{:S(2)}) collective-permute-start(bf16[256,256]{1,0:T(8,128)(2,1)S(1)} %shard_map.94.refs_0_), channel_id=1, source_target_pairs={{0,16},{4,20},{8,24},{12,28},{16,0},{20,4},{24,8},{28,12},{1,17},{... | collective-permute-start | bytes 393224 | tf_op jit(solution)/shard_map/ppermute | solution.py:376
  75.5 1.4 %collective-permute-start.17 = (bf16[768,256]{1,0:T(8,128)(2,1)S(1)}, bf16[768,256]{1,0:T(8,128)(2,1)S(1)}, u32[]{:S(2)}, u32[]{:S(2)}) collective-permute-start(bf16[768,256]{1,0:T(8,128)(2,1)S(1)} %get-tuple-element.59.refs_5_), channel_id=1, source_target_pairs={{0,192},{192,0},{64,128},{128,64},{1,193},{193,1},{65,129},{129,65... | collective-permute-start | bytes 1179656 | tf_op jit(solution)/shard_map/ppermute | solution.py:172
  77.0 3.2 %shard_map.92.refs_9_ = f32[4,256,256]{2,1,0:T(8,128)S(1)} custom-call(bf16[272,256]{1,0:T(8,128)(2,1)S(1)} %get-tuple-element.39.refs_1_.refs_0_, bf16[272,256]{1,0:T(8,128)(2,1)S(1)} %collective-permute-done.refs_1_, bf16[272,256]{1,0:T(8,128)(2,1)S(1)} %collective-permute-done.1.refs_2_, bf16[272,256]{1,0:T(8,128)(2,1)S(1)} %collective-permute-done.2.refs_3_, ...), custom_call_target="tpu_custom_call" | custom-call | flops 1073741824 | bytes 3145728 | tf_op jit(solution)/shard_map/pallas_call | solution.py:67
  81.7 3.3 %collective-permute-start.26 = (bf16[256,256]{1,0:T(8,128)(2,1)S(1)}, bf16[256,256]{1,0:T(8,128)(2,1)S(1)}, u32[]{:S(2)}, u32[]{:S(2)}) collective-permute-start(bf16[256,256]{1,0:T(8,128)(2,1)S(1)} %shard_map.95.refs_4_), channel_id=1, source_target_pairs={{0,3},{1,0},{2,1},{3,2},{4,7},{5,4},{6,5},{7,6},{8,11},{9,8},{10,9... | collective-permute-start | bytes 393224 | tf_op jit(solution)/shard_map/ppermute | solution.py:28
  86.1 1.5 %collective-permute-done.25.refs_5_ = bf16[256,256]{1,0:T(8,128)(2,1)S(1)} collective-permute-done((bf16[256,256]{1,0:T(8,128)(2,1)S(1)}, bf16[256,256]{1,0:T(8,128)(2,1)S(1)}, u32[]{:S(2)}, u32[]{:S(2)}) %collective-permute-start.25) | collective-permute-done | bytes 131104 | tf_op jit(solution)/shard_map/ppermute | solution.py:28
  87.5 3.0 %collective-permute-start.21 = (bf16[512,256]{1,0:T(8,128)(2,1)S(1)}, bf16[512,256]{1,0:T(8,128)(2,1)S(1)}, u32[]{:S(2)}, u32[]{:S(2)}) collective-permute-start(bf16[512,256]{1,0:T(8,128)(2,1)S(1)} %get-tuple-element.63), channel_id=1, source_target_pairs={{0,28},{4,0},{8,4},{12,8},{16,12},{20,16},{24,20},{28,24},{1,29},{... | collective-permute-start | bytes 786440 | tf_op jit(solution)/shard_map/ppermute | solution.py:28
  90.5 2.5 %shard_map.96 = (bf16[256,256]{1,0:T(8,128)(2,1)S(1)}, bf16[256,256]{1,0:T(8,128)(2,1)S(1)}, bf16[256,256]{1,0:T(8,128)(2,1)S(1)}, bf16[256,256]{1,0:T(8,128)(2,1)S(1)}) custom-call(bf16[272,256]{1,0:T(8,128)(2,1)S(1)} %get-tuple-element.39.refs_1_.refs_0_, bf16[272,256]{1,0:T(8,128)(2,1)S(1)} %collective-permute-done.refs_1_, ...), custom_call_target="tpu_custom_call" | custom-call | flops 1073741824 | bytes 3145728 | tf_op jit(solution)/shard_map/pallas_call | solution.py:67
  93.8 2.5 %collective-permute-start.29 = (bf16[256,256]{1,0:T(8,128)(2,1)S(1)}, bf16[256,256]{1,0:T(8,128)(2,1)S(1)}, u32[]{:S(2)}, u32[]{:S(2)}) collective-permute-start(bf16[256,256]{1,0:T(8,128)(2,1)S(1)} %get-tuple-element.65.refs_8_), channel_id=1, source_target_pairs={{0,192},{64,0},{128,64},{192,128},{1,193},{65,1},{129,65},{193,129... | collective-permute-start | bytes 393224 | tf_op jit(solution)/shard_map/ppermute | solution.py:28
  97.4 2.2 %collective-permute-done.29.refs_5_ = bf16[256,256]{1,0:T(8,128)(2,1)S(1)} collective-permute-done((bf16[256,256]{1,0:T(8,128)(2,1)S(1)}, bf16[256,256]{1,0:T(8,128)(2,1)S(1)}, u32[]{:S(2)}, u32[]{:S(2)}) %collective-permute-start.29) | collective-permute-done | bytes 131104 | tf_op jit(solution)/shard_map/ppermute | solution.py:28
  99.6 2.1 %collective-permute-done.30.refs_6_ = bf16[256,256]{1,0:T(8,128)(2,1)S(1)} collective-permute-done((bf16[256,256]{1,0:T(8,128)(2,1)S(1)}, bf16[256,256]{1,0:T(8,128)(2,1)S(1)}, u32[]{:S(2)}, u32[]{:S(2)}) %collective-permute-start.30) | collective-permute-done | bytes 131104 | tf_op jit(solution)/shard_map/ppermute | solution.py:28
  104.9 9.9 %collective-permute-done.32 = bf16[512,256]{1,0:T(8,128)(2,1)S(1)} collective-permute-done((bf16[512,256]{1,0:T(8,128)(2,1)S(1)}, bf16[512,256]{1,0:T(8,128)(2,1)S(1)}, u32[]{:S(2)}, u32[]{:S(2)}) %collective-permute-start.32) | collective-permute-done | bytes 262176 | tf_op jit(solution)/shard_map/ppermute | solution.py:527
  (67 shorter events, 22.3 us)
Async XLA Ops:
  1.7 22.9 %collective-permute-start.3 = (bf16[1024,256]{1,0:T(8,128)(2,1)S(1)}, bf16[1024,256]{1,0:T(8,128)(2,1)S(1)}, u32[]{:S(2)}, u32[]{:S(2)}) collective-permute-start(bf16[1024,256]{1,0:T(8,128)(2,1)S(1)} %get-tuple-element.38.refs_2_), channel_id=1, source_target_pairs={{0,1},{1,2},{2,3},{3,0},{4,5},{5,6},{6,7},{7,4},{8,9},{9,10},{10,1... | collective-permute-start | bytes 1572872 | tf_op jit(solution)/shard_map/ppermute | solution.py:28
  4.8 6.8 %collective-permute-start = (bf16[272,256]{1,0:T(8,128)(2,1)S(1)}, bf16[272,256]{1,0:T(8,128)(2,1)S(1)}, u32[]{:S(2)}, u32[]{:S(2)}) collective-permute-start(bf16[272,256]{1,0:T(8,128)(2,1)S(1)} %get-tuple-element.40), channel_id=1, source_target_pairs={{0,64},{64,128},{128,192},{192,0},{1,65},{65,129},{129,193},{193,1... | collective-permute-start | bytes 417800 | tf_op jit(solution)/shard_map/ppermute | solution.py:28
  6.1 20.0 %collective-permute-start.4 = (bf16[1024,256]{1,0:T(8,128)(2,1)S(1)}, bf16[1024,256]{1,0:T(8,128)(2,1)S(1)}, u32[]{:S(2)}, u32[]{:S(2)}) collective-permute-start(bf16[1024,256]{1,0:T(8,128)(2,1)S(1)} %get-tuple-element.45), channel_id=1, source_target_pairs={{0,3},{1,0},{2,1},{3,2},{4,7},{5,4},{6,5},{7,6},{8,11},{9,8},{10,9... | collective-permute-start | bytes 1572872 | tf_op jit(solution)/shard_map/ppermute | solution.py:28
  7.5 21.6 %collective-permute-start.5 = (bf16[1024,256]{1,0:T(8,128)(2,1)S(1)}, bf16[1024,256]{1,0:T(8,128)(2,1)S(1)}, u32[]{:S(2)}, u32[]{:S(2)}) collective-permute-start(bf16[1024,256]{1,0:T(8,128)(2,1)S(1)} %get-tuple-element.46), channel_id=1, source_target_pairs={{0,2},{1,3},{2,0},{3,1},{4,6},{5,7},{6,4},{7,5},{8,10},{9,11},{10,... | collective-permute-start | bytes 1572872 | tf_op jit(solution)/shard_map/ppermute | solution.py:28
  9.1 5.4 %collective-permute-start.1 = (bf16[272,256]{1,0:T(8,128)(2,1)S(1)}, bf16[272,256]{1,0:T(8,128)(2,1)S(1)}, u32[]{:S(2)}, u32[]{:S(2)}) collective-permute-start(bf16[272,256]{1,0:T(8,128)(2,1)S(1)} %get-tuple-element.41), channel_id=1, source_target_pairs={{0,128},{64,192},{128,0},{192,64},{1,129},{65,193},{129,1},{193,65... | collective-permute-start | bytes 417800 | tf_op jit(solution)/shard_map/ppermute | solution.py:28
  11.6 5.3 %collective-permute-start.2 = (bf16[272,256]{1,0:T(8,128)(2,1)S(1)}, bf16[272,256]{1,0:T(8,128)(2,1)S(1)}, u32[]{:S(2)}, u32[]{:S(2)}) collective-permute-start(bf16[272,256]{1,0:T(8,128)(2,1)S(1)} %get-tuple-element.42), channel_id=1, source_target_pairs={{0,192},{64,0},{128,64},{192,128},{1,193},{65,1},{129,65},{193,129... | collective-permute-start | bytes 417800 | tf_op jit(solution)/shard_map/ppermute | solution.py:28
  21.2 12.7 %collective-permute-start.9 = (bf16[256,256]{1,0:T(8,128)(2,1)S(1)}, bf16[256,256]{1,0:T(8,128)(2,1)S(1)}, u32[]{:S(2)}, u32[]{:S(2)}) collective-permute-start(bf16[256,256]{1,0:T(8,128)(2,1)S(1)} %get-tuple-element.43.refs_5_), channel_id=1, source_target_pairs={{0,1},{1,2},{2,3},{3,0},{4,5},{5,6},{6,7},{7,4},{8,9},{9,10},{10,1... | collective-permute-start | bytes 393224 | tf_op jit(solution)/shard_map/ppermute | solution.py:28
  23.9 10.1 %collective-permute-start.10 = (bf16[256,256]{1,0:T(8,128)(2,1)S(1)}, bf16[256,256]{1,0:T(8,128)(2,1)S(1)}, u32[]{:S(2)}, u32[]{:S(2)}) collective-permute-start(bf16[256,256]{1,0:T(8,128)(2,1)S(1)} %get-tuple-element.51), channel_id=1, source_target_pairs={{0,3},{1,0},{2,1},{3,2},{4,7},{5,4},{6,5},{7,6},{8,11},{9,8},{10,9... | collective-permute-start | bytes 393224 | tf_op jit(solution)/shard_map/ppermute | solution.py:28
  24.6 10.0 %collective-permute-start.11 = (bf16[256,256]{1,0:T(8,128)(2,1)S(1)}, bf16[256,256]{1,0:T(8,128)(2,1)S(1)}, u32[]{:S(2)}, u32[]{:S(2)}) collective-permute-start(bf16[256,256]{1,0:T(8,128)(2,1)S(1)} %get-tuple-element.52), channel_id=1, source_target_pairs={{0,2},{1,3},{2,0},{3,1},{4,6},{5,7},{6,4},{7,5},{8,10},{9,11},{10,... | collective-permute-start | bytes 393224 | tf_op jit(solution)/shard_map/ppermute | solution.py:28
  34.7 12.8 %collective-permute-start.13 = (bf16[384,256]{1,0:T(8,128)(2,1)S(1)}, bf16[384,256]{1,0:T(8,128)(2,1)S(1)}, u32[]{:S(2)}, u32[]{:S(2)}) collective-permute-start(bf16[384,256]{1,0:T(8,128)(2,1)S(1)} %get-tuple-element.55.refs_5_), channel_id=1, source_target_pairs={{0,64},{64,128},{128,192},{192,0},{1,65},{65,129},{129,193},{193,1... | collective-permute-start | bytes 589832 | tf_op jit(solution)/shard_map/ppermute | solution.py:28
  36.1 13.5 %collective-permute-start.14 = (bf16[384,256]{1,0:T(8,128)(2,1)S(1)}, bf16[384,256]{1,0:T(8,128)(2,1)S(1)}, u32[]{:S(2)}, u32[]{:S(2)}) collective-permute-start(bf16[384,256]{1,0:T(8,128)(2,1)S(1)} %get-tuple-element.56.refs_6_), channel_id=1, source_target_pairs={{0,192},{64,0},{128,64},{192,128},{1,193},{65,1},{129,65},{193,129... | collective-permute-start | bytes 589832 | tf_op jit(solution)/shard_map/ppermute | solution.py:28
  37.5 13.3 %collective-permute-start.15 = (bf16[512,256]{1,0:T(8,128)(2,1)S(1)}, bf16[512,256]{1,0:T(8,128)(2,1)S(1)}, u32[]{:S(2)}, u32[]{:S(2)}) collective-permute-start(bf16[512,256]{1,0:T(8,128)(2,1)S(1)} %get-tuple-element.54.refs_3_), channel_id=1, source_target_pairs={{0,4},{4,8},{8,12},{12,16},{16,20},{20,24},{24,28},{28,0},{1,5},{5... | collective-permute-start | bytes 786440 | tf_op jit(solution)/shard_map/ppermute | solution.py:28
  39.2 11.6 %collective-permute-start.16 = (bf16[512,256]{1,0:T(8,128)(2,1)S(1)}, bf16[512,256]{1,0:T(8,128)(2,1)S(1)}, u32[]{:S(2)}, u32[]{:S(2)}) collective-permute-start(bf16[512,256]{1,0:T(8,128)(2,1)S(1)} %get-tuple-element.57), channel_id=1, source_target_pairs={{0,28},{4,0},{8,4},{12,8},{16,12},{20,16},{24,20},{28,24},{1,29},{... | collective-permute-start | bytes 786440 | tf_op jit(solution)/shard_map/ppermute | solution.py:28
  44.6 10.1 %collective-permute-start.6 = (bf16[512,256]{1,0:T(8,128)(2,1)S(1)}, bf16[512,256]{1,0:T(8,128)(2,1)S(1)}, u32[]{:S(2)}, u32[]{:S(2)}) collective-permute-start(bf16[512,256]{1,0:T(8,128)(2,1)S(1)} %get-tuple-element.47), channel_id=1, source_target_pairs={{0,1},{1,2},{2,3},{3,0},{4,5},{5,6},{6,7},{7,4},{8,9},{9,10},{10,1... | collective-permute-start | bytes 786440 | tf_op jit(solution)/shard_map/ppermute | solution.py:28
  47.5 8.3 %collective-permute-start.7 = (bf16[512,256]{1,0:T(8,128)(2,1)S(1)}, bf16[512,256]{1,0:T(8,128)(2,1)S(1)}, u32[]{:S(2)}, u32[]{:S(2)}) collective-permute-start(bf16[512,256]{1,0:T(8,128)(2,1)S(1)} %get-tuple-element.48), channel_id=1, source_target_pairs={{0,3},{1,0},{2,1},{3,2},{4,7},{5,4},{6,5},{7,6},{8,11},{9,8},{10,9... | collective-permute-start | bytes 786440 | tf_op jit(solution)/shard_map/ppermute | solution.py:28
  49.6 11.7 %collective-permute-start.8 = (bf16[512,256]{1,0:T(8,128)(2,1)S(1)}, bf16[512,256]{1,0:T(8,128)(2,1)S(1)}, u32[]{:S(2)}, u32[]{:S(2)}) collective-permute-start(bf16[512,256]{1,0:T(8,128)(2,1)S(1)} %get-tuple-element.49), channel_id=1, source_target_pairs={{0,2},{1,3},{2,0},{3,1},{4,6},{5,7},{6,4},{7,5},{8,10},{9,11},{10,... | collective-permute-start | bytes 786440 | tf_op jit(solution)/shard_map/ppermute | solution.py:28
  61.3 18.9 %collective-permute-start.18 = (bf16[768,256]{1,0:T(8,128)(2,1)S(1)}, bf16[768,256]{1,0:T(8,128)(2,1)S(1)}, u32[]{:S(2)}, u32[]{:S(2)}) collective-permute-start(bf16[768,256]{1,0:T(8,128)(2,1)S(1)} %get-tuple-element.61.refs_5_), channel_id=1, source_target_pairs={{0,64},{64,0},{128,192},{192,128},{1,65},{65,1},{129,193},{193,129... | collective-permute-start | bytes 1179656 | tf_op jit(solution)/shard_map/ppermute | solution.py:172
  61.4 18.8 %collective-permute-start.19 = (bf16[512,256]{1,0:T(8,128)(2,1)S(1)}, bf16[512,256]{1,0:T(8,128)(2,1)S(1)}, u32[]{:S(2)}, u32[]{:S(2)}) collective-permute-start(bf16[512,256]{1,0:T(8,128)(2,1)S(1)} %get-tuple-element.58.refs_3_.refs_6_), channel_id=1, source_target_pairs={{0,4},{4,8},{8,12},{12,16},{16,20},{20,24},{24,28},{28,0},{1,5},{5... | collective-permute-start | bytes 786440 | tf_op jit(solution)/shard_map/ppermute | solution.py:28
  61.5 18.7 %collective-permute-start.20 = (bf16[512,256]{1,0:T(8,128)(2,1)S(1)}, bf16[512,256]{1,0:T(8,128)(2,1)S(1)}, u32[]{:S(2)}, u32[]{:S(2)}) collective-permute-start(bf16[512,256]{1,0:T(8,128)(2,1)S(1)} %get-tuple-element.62), channel_id=1, source_target_pairs={{0,28},{4,0},{8,4},{12,8},{16,12},{20,16},{24,20},{28,24},{1,29},{... | collective-permute-start | bytes 786440 | tf_op jit(solution)/shard_map/ppermute | solution.py:28
  64.1 7.5 %collective-permute-start.23 = (bf16[256,256]{1,0:T(8,128)(2,1)S(1)}, bf16[256,256]{1,0:T(8,128)(2,1)S(1)}, u32[]{:S(2)}, u32[]{:S(2)}) collective-permute-start(bf16[256,256]{1,0:T(8,128)(2,1)S(1)} %shard_map.87.refs_5_.refs_0_), channel_id=1, source_target_pairs={{0,8},{4,12},{8,0},{12,4},{16,24},{20,28},{24,16},{28,20},{1,9},{5... | collective-permute-start | bytes 393224 | tf_op jit(solution)/shard_map/ppermute | solution.py:376
  71.7 9.3 %collective-permute-start.24 = (bf16[256,256]{1,0:T(8,128)(2,1)S(1)}, bf16[256,256]{1,0:T(8,128)(2,1)S(1)}, u32[]{:S(2)}, u32[]{:S(2)}) collective-permute-start(bf16[256,256]{1,0:T(8,128)(2,1)S(1)} %shard_map.94.refs_0_), channel_id=1, source_target_pairs={{0,16},{4,20},{8,24},{12,28},{16,0},{20,4},{24,8},{28,12},{1,17},{... | collective-permute-start | bytes 393224 | tf_op jit(solution)/shard_map/ppermute | solution.py:376
  75.5 17.5 %collective-permute-start.17 = (bf16[768,256]{1,0:T(8,128)(2,1)S(1)}, bf16[768,256]{1,0:T(8,128)(2,1)S(1)}, u32[]{:S(2)}, u32[]{:S(2)}) collective-permute-start(bf16[768,256]{1,0:T(8,128)(2,1)S(1)} %get-tuple-element.59.refs_5_), channel_id=1, source_target_pairs={{0,192},{192,0},{64,128},{128,64},{1,193},{193,1},{65,129},{129,65... | collective-permute-start | bytes 1179656 | tf_op jit(solution)/shard_map/ppermute | solution.py:172
  80.9 12.1 %collective-permute-start.22 = (bf16[512,256]{1,0:T(8,128)(2,1)S(1)}, bf16[512,256]{1,0:T(8,128)(2,1)S(1)}, u32[]{:S(2)}, u32[]{:S(2)}) collective-permute-start(bf16[512,256]{1,0:T(8,128)(2,1)S(1)} %get-tuple-element.64.refs_10_), channel_id=1, source_target_pairs={{0,4},{4,8},{8,12},{12,16},{16,20},{20,24},{24,28},{28,0},{1,5},{5... | collective-permute-start | bytes 786440 | tf_op jit(solution)/shard_map/ppermute | solution.py:28
  81.1 6.5 %collective-permute-start.25 = (bf16[256,256]{1,0:T(8,128)(2,1)S(1)}, bf16[256,256]{1,0:T(8,128)(2,1)S(1)}, u32[]{:S(2)}, u32[]{:S(2)}) collective-permute-start(bf16[256,256]{1,0:T(8,128)(2,1)S(1)} %shard_map.95.refs_4_), channel_id=1, source_target_pairs={{0,1},{1,2},{2,3},{3,0},{4,5},{5,6},{6,7},{7,4},{8,9},{9,10},{10,1... | collective-permute-start | bytes 393224 | tf_op jit(solution)/shard_map/ppermute | solution.py:28
  81.7 8.8 %collective-permute-start.26 = (bf16[256,256]{1,0:T(8,128)(2,1)S(1)}, bf16[256,256]{1,0:T(8,128)(2,1)S(1)}, u32[]{:S(2)}, u32[]{:S(2)}) collective-permute-start(bf16[256,256]{1,0:T(8,128)(2,1)S(1)} %shard_map.95.refs_4_), channel_id=1, source_target_pairs={{0,3},{1,0},{2,1},{3,2},{4,7},{5,4},{6,5},{7,6},{8,11},{9,8},{10,9... | collective-permute-start | bytes 393224 | tf_op jit(solution)/shard_map/ppermute | solution.py:28
  85.0 5.5 %collective-permute-start.27 = (bf16[256,256]{1,0:T(8,128)(2,1)S(1)}, bf16[256,256]{1,0:T(8,128)(2,1)S(1)}, u32[]{:S(2)}, u32[]{:S(2)}) collective-permute-start(bf16[256,256]{1,0:T(8,128)(2,1)S(1)} %shard_map.95.refs_4_), channel_id=1, source_target_pairs={{0,2},{1,3},{2,0},{3,1},{4,6},{5,7},{6,4},{7,5},{8,10},{9,11},{10,... | collective-permute-start | bytes 393224 | tf_op jit(solution)/shard_map/ppermute | solution.py:28
  87.5 9.5 %collective-permute-start.21 = (bf16[512,256]{1,0:T(8,128)(2,1)S(1)}, bf16[512,256]{1,0:T(8,128)(2,1)S(1)}, u32[]{:S(2)}, u32[]{:S(2)}) collective-permute-start(bf16[512,256]{1,0:T(8,128)(2,1)S(1)} %get-tuple-element.63), channel_id=1, source_target_pairs={{0,28},{4,0},{8,4},{12,8},{16,12},{20,16},{24,20},{28,24},{1,29},{... | collective-permute-start | bytes 786440 | tf_op jit(solution)/shard_map/ppermute | solution.py:28
  93.5 9.6 %collective-permute-start.28 = (bf16[512,256]{1,0:T(8,128)(2,1)S(1)}, bf16[512,256]{1,0:T(8,128)(2,1)S(1)}, u32[]{:S(2)}, u32[]{:S(2)}) collective-permute-start(bf16[512,256]{1,0:T(8,128)(2,1)S(1)} %shard_map.97.refs_8_), channel_id=1, source_target_pairs={{0,4},{4,8},{8,12},{12,16},{16,20},{20,24},{24,28},{28,0},{1,5},{5... | collective-permute-start | bytes 786440 | tf_op jit(solution)/shard_map/ppermute | solution.py:28
  93.8 5.8 %collective-permute-start.29 = (bf16[256,256]{1,0:T(8,128)(2,1)S(1)}, bf16[256,256]{1,0:T(8,128)(2,1)S(1)}, u32[]{:S(2)}, u32[]{:S(2)}) collective-permute-start(bf16[256,256]{1,0:T(8,128)(2,1)S(1)} %get-tuple-element.65.refs_8_), channel_id=1, source_target_pairs={{0,192},{64,0},{128,64},{192,128},{1,193},{65,1},{129,65},{193,129... | collective-permute-start | bytes 393224 | tf_op jit(solution)/shard_map/ppermute | solution.py:28
  96.3 5.4 %collective-permute-start.30 = (bf16[256,256]{1,0:T(8,128)(2,1)S(1)}, bf16[256,256]{1,0:T(8,128)(2,1)S(1)}, u32[]{:S(2)}, u32[]{:S(2)}) collective-permute-start(bf16[256,256]{1,0:T(8,128)(2,1)S(1)} %get-tuple-element.67), channel_id=1, source_target_pairs={{0,128},{64,192},{128,0},{192,64},{1,129},{65,193},{129,1},{193,65... | collective-permute-start | bytes 393224 | tf_op jit(solution)/shard_map/ppermute | solution.py:28
  96.9 6.1 %collective-permute-start.31 = (bf16[256,256]{1,0:T(8,128)(2,1)S(1)}, bf16[256,256]{1,0:T(8,128)(2,1)S(1)}, u32[]{:S(2)}, u32[]{:S(2)}) collective-permute-start(bf16[256,256]{1,0:T(8,128)(2,1)S(1)} %get-tuple-element.68), channel_id=1, source_target_pairs={{0,64},{64,128},{128,192},{192,0},{1,65},{65,129},{129,193},{193,1... | collective-permute-start | bytes 393224 | tf_op jit(solution)/shard_map/ppermute | solution.py:28
  103.6 11.2 %collective-permute-start.32 = (bf16[512,256]{1,0:T(8,128)(2,1)S(1)}, bf16[512,256]{1,0:T(8,128)(2,1)S(1)}, u32[]{:S(2)}, u32[]{:S(2)}) collective-permute-start(bf16[512,256]{1,0:T(8,128)(2,1)S(1)} %get-tuple-element.69), channel_id=1, source_target_pairs={{0,32},{1,33},{2,34},{3,35},{4,36},{5,37},{6,38},{7,39},{8,40},{9,... | collective-permute-start | bytes 786440 | tf_op jit(solution)/shard_map/ppermute | solution.py:527
  (8 other events, 128.2 us)

commit v6 on v5

--- a/solution.py
+++ b/solution.py
@@ -327,7 +327,8 @@
         lanes = slice((v % 2) * BLK, (v % 2 + 1) * BLK)
         rhs_ref[first : first + BLK, lanes] = mats_ref[v]
 
-    def window(k, carry):
+    rows, kept = [], []
+    for k in range(NX):
         item = item_ref.at[k]
         ids = item[WINDOW : WINDOW + 1, :].astype(F32)
         code = jnp.full(ids.shape, 64.0, F32)
@@ -344,13 +345,15 @@
         picked = jnp.where(upper, high, low).astype(BF16)
         zero = jnp.zeros_like(picked)
         pieces = [jnp.where(pair == jnp.bfloat16(p), picked, zero) for p in range(VARS // 2)]
-        both = jnp.dot(jnp.concatenate(pieces, axis=1), rhs_ref[...], preferred_element_type=F32)
+        rows.append(jnp.concatenate(pieces, axis=1))
+        kept.append((upper, odd))
+    lhs = jnp.concatenate(rows, axis=0)
+    every = jnp.dot(lhs, rhs_ref[...], preferred_element_type=F32)
+    for k, (upper, odd) in enumerate(kept):
+        both = every[k * WINDOW : (k + 1) * WINDOW, :]
         one = jnp.where(odd, both[:, BLK:], both[:, 0:BLK])
         out_ref[k, :, 0:BLK] = jnp.where(upper, 0.0, one)
         out_ref[k, :, BLK : 2 * BLK] = jnp.where(upper, one, 0.0)
-        return carry
-
-    lax.fori_loop(0, NX, window, 0)
 
 
 def block_terms(items, mats, places, after=()):
@@ -371,9 +374,8 @@
     out_ref[...] = (a_ref[...].astype(F32) + b_ref[...].astype(F32)).astype(BF16)
 
 
-def exchanged_sum(value, axis, bit, after=()):
-    count = lax.axis_size(axis)
-    other = lax.ppermute(value, axis, [(i, i ^ bit) for i in range(count)])
+def exchanged_sum(value, axis, partner, after=()):
+    other = lax.ppermute(value, axis, list(enumerate(partner)))
     return call(
         add_kernel,
         (value, other),
@@ -401,21 +403,19 @@
         two_ref[h + 2] = jnp.where(first, turned, packed)
     half = lax.div(lax.broadcasted_iota(jnp.int32, (1, 128), 1), jnp.int32(RANK)).astype(F32)
 
-    def window(k, carry):
+    rows = []
+    for k in range(NX):
         variant = (spread_columns(item_ref[k, 0:1, :], 128) - half).astype(BF16)
         two = two_ref[k].astype(BF16)
         zero = jnp.zeros_like(two)
         pieces = []
         for i in range(VARS // 2):
             pieces.append(jnp.where(variant == jnp.bfloat16(2 * i), two, zero))
-        lhs = jnp.concatenate(pieces, axis=1)
-        total = block_ref[k] + jnp.dot(lhs, up_ref[...], preferred_element_type=F32)
-        out_ref[k] = total.astype(BF16)
-        return carry
-
-    lax.fori_loop(0, NX, window, 0)
+        rows.append(jnp.concatenate(pieces, axis=1))
+    lhs = jnp.concatenate(rows, axis=0)
+    total = jnp.dot(lhs, up_ref[...], preferred_element_type=F32)
     for k in range(NX):
-        outs[k][...] = out_ref[k]
+        outs[k][...] = (block_ref[k] + total[k * WINDOW : (k + 1) * WINDOW, :]).astype(BF16)
 
 
 def up(items, lows, factor, blocks, after=()):
@@ -496,13 +496,13 @@
     low = down(items, down_factor, (second[0],))
     third, (own2, own3) = pack((2, 3), weight, None, (low,))
     got2 = [shift(value, Y, hop) for value, hop in zip(third, HOPS)]
-    low1 = exchanged_sum(low, Z, 1)
-    low2 = exchanged_sum(low1, Z, 2)
+    low1 = exchanged_sum(low, Z, (1, 0, 3, 2, 5, 4, 7, 6))
+    low2 = exchanged_sum(low1, Z, (2, 3, 0, 1, 6, 7, 4, 5))
     plus, minus = project((0, 1), own0, features, got, (), (), (), (low1,))
     carried = (shift(plus, Z, 1), shift(minus, Z, -1))
     mine1 = join(got1, 0, (True,), (plus,))
     other1 = (shift(mine1[0], "pool", 1), shift(mine1[1], "pool", -1))
-    low3 = exchanged_sum(low2, Z, 4)
+    low3 = exchanged_sum(low2, Z, (6, 7, 4, 5, 2, 3, 0, 1))
     plus, minus = project((0, 1), own1, features, got, mine1, other1, carried)
     mine2, mine3 = join(got2, 0, (False, False), (plus,))
     other2 = swapped(mine2, False)

time: 116 us -> 112 us (0.966)
  starting transfers between devices: 49.9 us -> 47.5 us
  Pallas kernels: 17.2 us -> 15.1 us
    ppermute x3, starting transfers between devices: 5.55 us -> 3.02 us  [exchanged_sum(): other = lax.ppermute(value, axis, list(enumerate(partner)))]
    ppermute x27, waiting for transfers between devices: 27.7 us -> 30.2 us  [shift(): lax.ppermute(value, axis, [(i, (i + steps) % count) for i in range(count)])]
    pallas_call x18, Pallas kernels: 17.2 us -> 15.1 us  [call(): pl.pallas_call(body, out_shape=outs, in_specs=list(in_specs) + [ANY] * m,...]
    ppermute x1, waiting for transfers between devices: 9.92 us -> 8.25 us  [steps(): carried = lax.ppermute(first_out, 'section', [(0, 1)])]
  transfers between devices with their start and end apart: 33 -> 33, of which waited for: 15 -> 16; matrix products, arithmetic and copies ran while one was open for 0% -> 0% of each run, Pallas kernels for 13% -> 11%
where the time goes in v6:
time: 112 us
  waiting for transfers between devices  48.2 us (43%)
  starting transfers between devices  47.5 us (42%)
  Pallas kernels  15.1 us (13%)
    ppermute x27, starting transfers between devices, shift(): lax.ppermute(value, axis, [(i, (i + steps) % count) for i in range(count)])  41.7 us
    ppermute x27, waiting for transfers between devices, shift(): lax.ppermute(value, axis, [(i, (i + steps) % count) for i in range(count)])  30.2 us
    pallas_call x18, Pallas kernels, call(): pl.pallas_call(body, out_shape=outs, in_specs=list(in_specs) + [ANY] * m,...  15.1 us
    ppermute x3, waiting for transfers between devices, exchanged_sum(): other = lax.ppermute(value, axis, list(enumerate(partner)))  9.78 us
    ppermute x1, waiting for transfers between devices, steps(): carried = lax.ppermute(first_out, 'section', [(0, 1)])  8.25 us
    ppermute x3, starting transfers between devices, exchanged_sum(): other = lax.ppermute(value, axis, list(enumerate(partner)))  3.02 us
  transfers between devices with their start and end apart: 33, of which 16 were waited for; matrix products, arithmetic and copies ran while one was open for 0% of the time, Pallas kernels for 11%

profile of v6, /device:TPU:1, one launch (start us, length us, event | category | flops | bytes accessed | tf_op | source)
XLA Modules:
  0.0 111.8 jit_solution(3372982291244317895)
XLA Ops:
  0.0 1.7 %shard_map.82 = (bf16[1024,256]{1,0:T(8,128)(2,1)S(1)}, bf16[1024,256]{1,0:T(8,128)(2,1)S(1)}, bf16[1024,256]{1,0:T(8,128)(2,1)S(1)}, bf16[512,256]{1,0:T(8,128)(2,1)S(1)}) custom-call(bf16[256,8192]{1,0:T(8,128)(2,1)} %bitcast.22, bf16[512,256]{1,0:T(8,128)(2,1)} %bitcast.9), custom_call_target="tpu_custom_call" | custom-call | bytes 1572864 | tf_op jit(solution)/shard_map/pallas_call | solution.py:67
  1.7 2.2 %collective-permute-start.3 = (bf16[1024,256]{1,0:T(8,128)(2,1)S(1)}, bf16[1024,256]{1,0:T(8,128)(2,1)S(1)}, u32[]{:S(2)}, u32[]{:S(2)}) collective-permute-start(bf16[1024,256]{1,0:T(8,128)(2,1)S(1)} %get-tuple-element.38.refs_2_), channel_id=1, source_target_pairs={{0,1},{1,2},{2,3},{3,0},{4,5},{5,6},{6,7},{7,4},{8,9},{9,10},{10,1... | collective-permute-start | bytes 1572872 | tf_op jit(solution)/shard_map/ppermute | solution.py:28
  6.1 1.5 %collective-permute-start.4 = (bf16[1024,256]{1,0:T(8,128)(2,1)S(1)}, bf16[1024,256]{1,0:T(8,128)(2,1)S(1)}, u32[]{:S(2)}, u32[]{:S(2)}) collective-permute-start(bf16[1024,256]{1,0:T(8,128)(2,1)S(1)} %get-tuple-element.45), channel_id=1, source_target_pairs={{0,3},{1,0},{2,1},{3,2},{4,7},{5,4},{6,5},{7,6},{8,11},{9,8},{10,9... | collective-permute-start | bytes 1572872 | tf_op jit(solution)/shard_map/ppermute | solution.py:28
  7.5 1.6 %collective-permute-start.5 = (bf16[1024,256]{1,0:T(8,128)(2,1)S(1)}, bf16[1024,256]{1,0:T(8,128)(2,1)S(1)}, u32[]{:S(2)}, u32[]{:S(2)}) collective-permute-start(bf16[1024,256]{1,0:T(8,128)(2,1)S(1)} %get-tuple-element.46), channel_id=1, source_target_pairs={{0,2},{1,3},{2,0},{3,1},{4,6},{5,7},{6,4},{7,5},{8,10},{9,11},{10,... | collective-permute-start | bytes 1572872 | tf_op jit(solution)/shard_map/ppermute | solution.py:28
  9.1 2.4 %collective-permute-start.1 = (bf16[272,256]{1,0:T(8,128)(2,1)S(1)}, bf16[272,256]{1,0:T(8,128)(2,1)S(1)}, u32[]{:S(2)}, u32[]{:S(2)}) collective-permute-start(bf16[272,256]{1,0:T(8,128)(2,1)S(1)} %get-tuple-element.41), channel_id=1, source_target_pairs={{0,128},{64,192},{128,0},{192,64},{1,129},{65,193},{129,1},{193,65... | collective-permute-start | bytes 417800 | tf_op jit(solution)/shard_map/ppermute | solution.py:28
  14.6 2.4 %collective-permute-done.2.refs_3_ = bf16[272,256]{1,0:T(8,128)(2,1)S(1)} collective-permute-done((bf16[272,256]{1,0:T(8,128)(2,1)S(1)}, bf16[272,256]{1,0:T(8,128)(2,1)S(1)}, u32[]{:S(2)}, u32[]{:S(2)}) %collective-permute-start.2) | collective-permute-done | bytes 139296 | tf_op jit(solution)/shard_map/ppermute | solution.py:28
  16.9 2.6 %shard_map.85.refs_1_.refs_0_ = bf16[256,256]{1,0:T(8,128)(2,1)S(1)} custom-call(bf16[272,256]{1,0:T(8,128)(2,1)S(1)} %get-tuple-element.39.refs_1_.refs_0_, bf16[272,256]{1,0:T(8,128)(2,1)S(1)} %collective-permute-done.refs_1_, bf16[272,256]{1,0:T(8,128)(2,1)S(1)} %collective-permute-done.1.refs_2_, bf16[272,256]{1,0:T(8,128)(2,1)S(1)} %collective-permute-done.2.refs_3_, ...), custom_call_target="tpu_custom_call" | custom-call | flops 1073741824 | bytes 2097152 | tf_op jit(solution)/shard_map/pallas_call | solution.py:67
  19.5 1.7 %collective-permute-start.12 = (bf16[256,256]{1,0:T(8,128)(2,1)S(1)}, bf16[256,256]{1,0:T(8,128)(2,1)S(1)}, u32[]{:S(2)}, u32[]{:S(2)}) collective-permute-start(bf16[256,256]{1,0:T(8,128)(2,1)S(1)} %shard_map.85.refs_1_.refs_0_), channel_id=1, source_target_pairs={{0,4},{4,0},{8,12},{12,8},{16,20},{20,16},{24,28},{28,24},{1,5},{5... | collective-permute-start | bytes 393224 | tf_op jit(solution)/shard_map/ppermute | solution.py:378
  21.6 2.3 %collective-permute-done.12.refs_1_ = bf16[256,256]{1,0:T(8,128)(2,1)S(1)} collective-permute-done((bf16[256,256]{1,0:T(8,128)(2,1)S(1)}, bf16[256,256]{1,0:T(8,128)(2,1)S(1)}, u32[]{:S(2)}, u32[]{:S(2)}) %collective-permute-start.12) | collective-permute-done | bytes 131104 | tf_op jit(solution)/shard_map/ppermute | solution.py:378
  24.6 1.4 %collective-permute-start.11 = (bf16[256,256]{1,0:T(8,128)(2,1)S(1)}, bf16[256,256]{1,0:T(8,128)(2,1)S(1)}, u32[]{:S(2)}, u32[]{:S(2)}) collective-permute-start(bf16[256,256]{1,0:T(8,128)(2,1)S(1)} %get-tuple-element.52), channel_id=1, source_target_pairs={{0,2},{1,3},{2,0},{3,1},{4,6},{5,7},{6,4},{7,5},{8,10},{9,11},{10,... | collective-permute-start | bytes 393224 | tf_op jit(solution)/shard_map/ppermute | solution.py:28
  26.1 3.0 %collective-permute-done.5.refs_4_ = bf16[1024,256]{1,0:T(8,128)(2,1)S(1)} collective-permute-done((bf16[1024,256]{1,0:T(8,128)(2,1)S(1)}, bf16[1024,256]{1,0:T(8,128)(2,1)S(1)}, u32[]{:S(2)}, u32[]{:S(2)}) %collective-permute-start.5) | collective-permute-done | bytes 524320 | tf_op jit(solution)/shard_map/ppermute | solution.py:28
  29.8 4.1 %collective-permute-done.9.refs_0_ = bf16[256,256]{1,0:T(8,128)(2,1)S(1)} collective-permute-done((bf16[256,256]{1,0:T(8,128)(2,1)S(1)}, bf16[256,256]{1,0:T(8,128)(2,1)S(1)}, u32[]{:S(2)}, u32[]{:S(2)}) %collective-permute-start.9) | collective-permute-done | bytes 131104 | tf_op jit(solution)/shard_map/ppermute | solution.py:28
  36.1 1.4 %collective-permute-start.14 = (bf16[384,256]{1,0:T(8,128)(2,1)S(1)}, bf16[384,256]{1,0:T(8,128)(2,1)S(1)}, u32[]{:S(2)}, u32[]{:S(2)}) collective-permute-start(bf16[384,256]{1,0:T(8,128)(2,1)S(1)} %get-tuple-element.56.refs_6_), channel_id=1, source_target_pairs={{0,192},{64,0},{128,64},{192,128},{1,193},{65,1},{129,65},{193,129... | collective-permute-start | bytes 589832 | tf_op jit(solution)/shard_map/ppermute | solution.py:28
  37.5 1.7 %collective-permute-start.15 = (bf16[512,256]{1,0:T(8,128)(2,1)S(1)}, bf16[512,256]{1,0:T(8,128)(2,1)S(1)}, u32[]{:S(2)}, u32[]{:S(2)}) collective-permute-start(bf16[512,256]{1,0:T(8,128)(2,1)S(1)} %get-tuple-element.54.refs_3_), channel_id=1, source_target_pairs={{0,4},{4,8},{8,12},{12,16},{16,20},{20,24},{24,28},{28,0},{1,5},{5... | collective-permute-start | bytes 786440 | tf_op jit(solution)/shard_map/ppermute | solution.py:28
  39.2 3.9 %collective-permute-start.16 = (bf16[512,256]{1,0:T(8,128)(2,1)S(1)}, bf16[512,256]{1,0:T(8,128)(2,1)S(1)}, u32[]{:S(2)}, u32[]{:S(2)}) collective-permute-start(bf16[512,256]{1,0:T(8,128)(2,1)S(1)} %get-tuple-element.57), channel_id=1, source_target_pairs={{0,28},{4,0},{8,4},{12,8},{16,12},{20,16},{24,20},{28,24},{1,29},{... | collective-permute-start | bytes 786440 | tf_op jit(solution)/shard_map/ppermute | solution.py:28
  43.1 1.5 %shard_map.86 = (bf16[512,256]{1,0:T(8,128)(2,1)S(1)}, bf16[512,256]{1,0:T(8,128)(2,1)S(1)}, bf16[512,256]{1,0:T(8,128)(2,1)S(1)}, bf16[512,256]{1,0:T(8,128)(2,1)S(1)}, bf16[512,256]{1,0:T(8,128)(2,1)S(1)}) custom-call(bf16[256,8192]{1,0:T(8,128)(2,1)} %bitcast.24, bf16[256,256]{1,0:T(8,128)(2,1)S(1)} %shard_map.85.refs_1_.refs_0_), custom_call_target="tpu_custom_call" | custom-call | bytes 786432 | tf_op jit(solution)/shard_map/pallas_call | solution.py:67
  44.6 2.9 %collective-permute-start.6 = (bf16[512,256]{1,0:T(8,128)(2,1)S(1)}, bf16[512,256]{1,0:T(8,128)(2,1)S(1)}, u32[]{:S(2)}, u32[]{:S(2)}) collective-permute-start(bf16[512,256]{1,0:T(8,128)(2,1)S(1)} %get-tuple-element.47), channel_id=1, source_target_pairs={{0,1},{1,2},{2,3},{3,0},{4,5},{5,6},{6,7},{7,4},{8,9},{9,10},{10,1... | collective-permute-start | bytes 786440 | tf_op jit(solution)/shard_map/ppermute | solution.py:28
  47.5 2.1 %collective-permute-start.7 = (bf16[512,256]{1,0:T(8,128)(2,1)S(1)}, bf16[512,256]{1,0:T(8,128)(2,1)S(1)}, u32[]{:S(2)}, u32[]{:S(2)}) collective-permute-start(bf16[512,256]{1,0:T(8,128)(2,1)S(1)} %get-tuple-element.48), channel_id=1, source_target_pairs={{0,3},{1,0},{2,1},{3,2},{4,7},{5,4},{6,5},{7,6},{8,11},{9,8},{10,9... | collective-permute-start | bytes 786440 | tf_op jit(solution)/shard_map/ppermute | solution.py:28
  51.5 3.3 %collective-permute-done.6.refs_0_ = bf16[512,256]{1,0:T(8,128)(2,1)S(1)} collective-permute-done((bf16[512,256]{1,0:T(8,128)(2,1)S(1)}, bf16[512,256]{1,0:T(8,128)(2,1)S(1)}, u32[]{:S(2)}, u32[]{:S(2)}) %collective-permute-start.6) | collective-permute-done | bytes 262176 | tf_op jit(solution)/shard_map/ppermute | solution.py:28
  55.8 5.4 %collective-permute-done.8.refs_2_ = bf16[512,256]{1,0:T(8,128)(2,1)S(1)} collective-permute-done((bf16[512,256]{1,0:T(8,128)(2,1)S(1)}, bf16[512,256]{1,0:T(8,128)(2,1)S(1)}, u32[]{:S(2)}, u32[]{:S(2)}) %collective-permute-start.8) | collective-permute-done | bytes 262176 | tf_op jit(solution)/shard_map/ppermute | solution.py:28
  61.5 2.7 %collective-permute-start.20 = (bf16[512,256]{1,0:T(8,128)(2,1)S(1)}, bf16[512,256]{1,0:T(8,128)(2,1)S(1)}, u32[]{:S(2)}, u32[]{:S(2)}) collective-permute-start(bf16[512,256]{1,0:T(8,128)(2,1)S(1)} %get-tuple-element.62), channel_id=1, source_target_pairs={{0,28},{4,0},{8,4},{12,8},{16,12},{20,16},{24,20},{28,24},{1,29},{... | collective-permute-start | bytes 786440 | tf_op jit(solution)/shard_map/ppermute | solution.py:28
  64.1 7.5 %collective-permute-done.23.refs_1_ = bf16[256,256]{1,0:T(8,128)(2,1)S(1)} collective-permute-done((bf16[256,256]{1,0:T(8,128)(2,1)S(1)}, bf16[256,256]{1,0:T(8,128)(2,1)S(1)}, u32[]{:S(2)}, u32[]{:S(2)}) %collective-permute-start.23) | collective-permute-done | bytes 131104 | tf_op jit(solution)/shard_map/ppermute | solution.py:378
  73.0 1.4 %collective-permute-start.17 = (bf16[768,256]{1,0:T(8,128)(2,1)S(1)}, bf16[768,256]{1,0:T(8,128)(2,1)S(1)}, u32[]{:S(2)}, u32[]{:S(2)}) collective-permute-start(bf16[768,256]{1,0:T(8,128)(2,1)S(1)} %get-tuple-element.59.refs_5_), channel_id=1, source_target_pairs={{0,192},{192,0},{64,128},{128,64},{1,193},{193,1},{65,129},{129,65... | collective-permute-start | bytes 1179656 | tf_op jit(solution)/shard_map/ppermute | solution.py:172
  74.4 2.2 %shard_map.92.refs_9_ = f32[4,256,256]{2,1,0:T(8,128)S(1)} custom-call(bf16[272,256]{1,0:T(8,128)(2,1)S(1)} %get-tuple-element.39.refs_1_.refs_0_, bf16[272,256]{1,0:T(8,128)(2,1)S(1)} %collective-permute-done.refs_1_, bf16[272,256]{1,0:T(8,128)(2,1)S(1)} %collective-permute-done.1.refs_2_, bf16[272,256]{1,0:T(8,128)(2,1)S(1)} %collective-permute-done.2.refs_3_, ...), custom_call_target="tpu_custom_call" | custom-call | flops 1073741824 | bytes 3145728 | tf_op jit(solution)/shard_map/pallas_call | solution.py:67
  77.3 1.6 %collective-permute-start.22 = (bf16[512,256]{1,0:T(8,128)(2,1)S(1)}, bf16[512,256]{1,0:T(8,128)(2,1)S(1)}, u32[]{:S(2)}, u32[]{:S(2)}) collective-permute-start(bf16[512,256]{1,0:T(8,128)(2,1)S(1)} %get-tuple-element.64.refs_10_), channel_id=1, source_target_pairs={{0,4},{4,8},{8,12},{12,16},{16,20},{20,24},{24,28},{28,0},{1,5},{5... | collective-permute-start | bytes 786440 | tf_op jit(solution)/shard_map/ppermute | solution.py:28
  79.0 5.6 %collective-permute-start.26 = (bf16[256,256]{1,0:T(8,128)(2,1)S(1)}, bf16[256,256]{1,0:T(8,128)(2,1)S(1)}, u32[]{:S(2)}, u32[]{:S(2)}) collective-permute-start(bf16[256,256]{1,0:T(8,128)(2,1)S(1)} %shard_map.95.refs_4_), channel_id=1, source_target_pairs={{0,3},{1,0},{2,1},{3,2},{4,7},{5,4},{6,5},{7,6},{8,11},{9,8},{10,9... | collective-permute-start | bytes 393224 | tf_op jit(solution)/shard_map/ppermute | solution.py:28
  85.7 1.5 %collective-permute-done.25.refs_5_ = bf16[256,256]{1,0:T(8,128)(2,1)S(1)} collective-permute-done((bf16[256,256]{1,0:T(8,128)(2,1)S(1)}, bf16[256,256]{1,0:T(8,128)(2,1)S(1)}, u32[]{:S(2)}, u32[]{:S(2)}) %collective-permute-start.25) | collective-permute-done | bytes 131104 | tf_op jit(solution)/shard_map/ppermute | solution.py:28
  87.3 2.7 %collective-permute-done.27.refs_7_ = bf16[256,256]{1,0:T(8,128)(2,1)S(1)} collective-permute-done((bf16[256,256]{1,0:T(8,128)(2,1)S(1)}, bf16[256,256]{1,0:T(8,128)(2,1)S(1)}, u32[]{:S(2)}, u32[]{:S(2)}) %collective-permute-start.27) | collective-permute-done | bytes 131104 | tf_op jit(solution)/shard_map/ppermute | solution.py:28
  92.0 2.5 %collective-permute-start.29 = (bf16[256,256]{1,0:T(8,128)(2,1)S(1)}, bf16[256,256]{1,0:T(8,128)(2,1)S(1)}, u32[]{:S(2)}, u32[]{:S(2)}) collective-permute-start(bf16[256,256]{1,0:T(8,128)(2,1)S(1)} %get-tuple-element.65.refs_8_), channel_id=1, source_target_pairs={{0,192},{64,0},{128,64},{192,128},{1,193},{65,1},{129,65},{193,129... | collective-permute-start | bytes 393224 | tf_op jit(solution)/shard_map/ppermute | solution.py:28
  95.5 2.3 %collective-permute-done.29.refs_5_ = bf16[256,256]{1,0:T(8,128)(2,1)S(1)} collective-permute-done((bf16[256,256]{1,0:T(8,128)(2,1)S(1)}, bf16[256,256]{1,0:T(8,128)(2,1)S(1)}, u32[]{:S(2)}, u32[]{:S(2)}) %collective-permute-start.29) | collective-permute-done | bytes 131104 | tf_op jit(solution)/shard_map/ppermute | solution.py:28
  97.8 2.1 %collective-permute-done.30.refs_6_ = bf16[256,256]{1,0:T(8,128)(2,1)S(1)} collective-permute-done((bf16[256,256]{1,0:T(8,128)(2,1)S(1)}, bf16[256,256]{1,0:T(8,128)(2,1)S(1)}, u32[]{:S(2)}, u32[]{:S(2)}) %collective-permute-start.30) | collective-permute-done | bytes 131104 | tf_op jit(solution)/shard_map/ppermute | solution.py:28
  102.8 8.2 %collective-permute-done.32 = bf16[512,256]{1,0:T(8,128)(2,1)S(1)} collective-permute-done((bf16[512,256]{1,0:T(8,128)(2,1)S(1)}, bf16[512,256]{1,0:T(8,128)(2,1)S(1)}, u32[]{:S(2)}, u32[]{:S(2)}) %collective-permute-start.32) | collective-permute-done | bytes 262176 | tf_op jit(solution)/shard_map/ppermute | solution.py:527
  (67 shorter events, 22.4 us)
Async XLA Ops:
  1.7 22.9 %collective-permute-start.3 = (bf16[1024,256]{1,0:T(8,128)(2,1)S(1)}, bf16[1024,256]{1,0:T(8,128)(2,1)S(1)}, u32[]{:S(2)}, u32[]{:S(2)}) collective-permute-start(bf16[1024,256]{1,0:T(8,128)(2,1)S(1)} %get-tuple-element.38.refs_2_), channel_id=1, source_target_pairs={{0,1},{1,2},{2,3},{3,0},{4,5},{5,6},{6,7},{7,4},{8,9},{9,10},{10,1... | collective-permute-start | bytes 1572872 | tf_op jit(solution)/shard_map/ppermute | solution.py:28
  4.8 6.8 %collective-permute-start = (bf16[272,256]{1,0:T(8,128)(2,1)S(1)}, bf16[272,256]{1,0:T(8,128)(2,1)S(1)}, u32[]{:S(2)}, u32[]{:S(2)}) collective-permute-start(bf16[272,256]{1,0:T(8,128)(2,1)S(1)} %get-tuple-element.40), channel_id=1, source_target_pairs={{0,64},{64,128},{128,192},{192,0},{1,65},{65,129},{129,193},{193,1... | collective-permute-start | bytes 417800 | tf_op jit(solution)/shard_map/ppermute | solution.py:28
  6.1 20.0 %collective-permute-start.4 = (bf16[1024,256]{1,0:T(8,128)(2,1)S(1)}, bf16[1024,256]{1,0:T(8,128)(2,1)S(1)}, u32[]{:S(2)}, u32[]{:S(2)}) collective-permute-start(bf16[1024,256]{1,0:T(8,128)(2,1)S(1)} %get-tuple-element.45), channel_id=1, source_target_pairs={{0,3},{1,0},{2,1},{3,2},{4,7},{5,4},{6,5},{7,6},{8,11},{9,8},{10,9... | collective-permute-start | bytes 1572872 | tf_op jit(solution)/shard_map/ppermute | solution.py:28
  7.5 21.6 %collective-permute-start.5 = (bf16[1024,256]{1,0:T(8,128)(2,1)S(1)}, bf16[1024,256]{1,0:T(8,128)(2,1)S(1)}, u32[]{:S(2)}, u32[]{:S(2)}) collective-permute-start(bf16[1024,256]{1,0:T(8,128)(2,1)S(1)} %get-tuple-element.46), channel_id=1, source_target_pairs={{0,2},{1,3},{2,0},{3,1},{4,6},{5,7},{6,4},{7,5},{8,10},{9,11},{10,... | collective-permute-start | bytes 1572872 | tf_op jit(solution)/shard_map/ppermute | solution.py:28
  9.1 5.4 %collective-permute-start.1 = (bf16[272,256]{1,0:T(8,128)(2,1)S(1)}, bf16[272,256]{1,0:T(8,128)(2,1)S(1)}, u32[]{:S(2)}, u32[]{:S(2)}) collective-permute-start(bf16[272,256]{1,0:T(8,128)(2,1)S(1)} %get-tuple-element.41), channel_id=1, source_target_pairs={{0,128},{64,192},{128,0},{192,64},{1,129},{65,193},{129,1},{193,65... | collective-permute-start | bytes 417800 | tf_op jit(solution)/shard_map/ppermute | solution.py:28
  11.6 5.3 %collective-permute-start.2 = (bf16[272,256]{1,0:T(8,128)(2,1)S(1)}, bf16[272,256]{1,0:T(8,128)(2,1)S(1)}, u32[]{:S(2)}, u32[]{:S(2)}) collective-permute-start(bf16[272,256]{1,0:T(8,128)(2,1)S(1)} %get-tuple-element.42), channel_id=1, source_target_pairs={{0,192},{64,0},{128,64},{192,128},{1,193},{65,1},{129,65},{193,129... | collective-permute-start | bytes 417800 | tf_op jit(solution)/shard_map/ppermute | solution.py:28
  21.2 12.7 %collective-permute-start.9 = (bf16[256,256]{1,0:T(8,128)(2,1)S(1)}, bf16[256,256]{1,0:T(8,128)(2,1)S(1)}, u32[]{:S(2)}, u32[]{:S(2)}) collective-permute-start(bf16[256,256]{1,0:T(8,128)(2,1)S(1)} %get-tuple-element.43.refs_5_), channel_id=1, source_target_pairs={{0,1},{1,2},{2,3},{3,0},{4,5},{5,6},{6,7},{7,4},{8,9},{9,10},{10,1... | collective-permute-start | bytes 393224 | tf_op jit(solution)/shard_map/ppermute | solution.py:28
  23.9 10.1 %collective-permute-start.10 = (bf16[256,256]{1,0:T(8,128)(2,1)S(1)}, bf16[256,256]{1,0:T(8,128)(2,1)S(1)}, u32[]{:S(2)}, u32[]{:S(2)}) collective-permute-start(bf16[256,256]{1,0:T(8,128)(2,1)S(1)} %get-tuple-element.51), channel_id=1, source_target_pairs={{0,3},{1,0},{2,1},{3,2},{4,7},{5,4},{6,5},{7,6},{8,11},{9,8},{10,9... | collective-permute-start | bytes 393224 | tf_op jit(solution)/shard_map/ppermute | solution.py:28
  24.6 10.0 %collective-permute-start.11 = (bf16[256,256]{1,0:T(8,128)(2,1)S(1)}, bf16[256,256]{1,0:T(8,128)(2,1)S(1)}, u32[]{:S(2)}, u32[]{:S(2)}) collective-permute-start(bf16[256,256]{1,0:T(8,128)(2,1)S(1)} %get-tuple-element.52), channel_id=1, source_target_pairs={{0,2},{1,3},{2,0},{3,1},{4,6},{5,7},{6,4},{7,5},{8,10},{9,11},{10,... | collective-permute-start | bytes 393224 | tf_op jit(solution)/shard_map/ppermute | solution.py:28
  34.7 12.8 %collective-permute-start.13 = (bf16[384,256]{1,0:T(8,128)(2,1)S(1)}, bf16[384,256]{1,0:T(8,128)(2,1)S(1)}, u32[]{:S(2)}, u32[]{:S(2)}) collective-permute-start(bf16[384,256]{1,0:T(8,128)(2,1)S(1)} %get-tuple-element.55.refs_5_), channel_id=1, source_target_pairs={{0,64},{64,128},{128,192},{192,0},{1,65},{65,129},{129,193},{193,1... | collective-permute-start | bytes 589832 | tf_op jit(solution)/shard_map/ppermute | solution.py:28
  36.1 13.5 %collective-permute-start.14 = (bf16[384,256]{1,0:T(8,128)(2,1)S(1)}, bf16[384,256]{1,0:T(8,128)(2,1)S(1)}, u32[]{:S(2)}, u32[]{:S(2)}) collective-permute-start(bf16[384,256]{1,0:T(8,128)(2,1)S(1)} %get-tuple-element.56.refs_6_), channel_id=1, source_target_pairs={{0,192},{64,0},{128,64},{192,128},{1,193},{65,1},{129,65},{193,129... | collective-permute-start | bytes 589832 | tf_op jit(solution)/shard_map/ppermute | solution.py:28
  37.5 13.3 %collective-permute-start.15 = (bf16[512,256]{1,0:T(8,128)(2,1)S(1)}, bf16[512,256]{1,0:T(8,128)(2,1)S(1)}, u32[]{:S(2)}, u32[]{:S(2)}) collective-permute-start(bf16[512,256]{1,0:T(8,128)(2,1)S(1)} %get-tuple-element.54.refs_3_), channel_id=1, source_target_pairs={{0,4},{4,8},{8,12},{12,16},{16,20},{20,24},{24,28},{28,0},{1,5},{5... | collective-permute-start | bytes 786440 | tf_op jit(solution)/shard_map/ppermute | solution.py:28
  39.2 11.6 %collective-permute-start.16 = (bf16[512,256]{1,0:T(8,128)(2,1)S(1)}, bf16[512,256]{1,0:T(8,128)(2,1)S(1)}, u32[]{:S(2)}, u32[]{:S(2)}) collective-permute-start(bf16[512,256]{1,0:T(8,128)(2,1)S(1)} %get-tuple-element.57), channel_id=1, source_target_pairs={{0,28},{4,0},{8,4},{12,8},{16,12},{20,16},{24,20},{28,24},{1,29},{... | collective-permute-start | bytes 786440 | tf_op jit(solution)/shard_map/ppermute | solution.py:28
  44.6 10.1 %collective-permute-start.6 = (bf16[512,256]{1,0:T(8,128)(2,1)S(1)}, bf16[512,256]{1,0:T(8,128)(2,1)S(1)}, u32[]{:S(2)}, u32[]{:S(2)}) collective-permute-start(bf16[512,256]{1,0:T(8,128)(2,1)S(1)} %get-tuple-element.47), channel_id=1, source_target_pairs={{0,1},{1,2},{2,3},{3,0},{4,5},{5,6},{6,7},{7,4},{8,9},{9,10},{10,1... | collective-permute-start | bytes 786440 | tf_op jit(solution)/shard_map/ppermute | solution.py:28
  47.5 8.3 %collective-permute-start.7 = (bf16[512,256]{1,0:T(8,128)(2,1)S(1)}, bf16[512,256]{1,0:T(8,128)(2,1)S(1)}, u32[]{:S(2)}, u32[]{:S(2)}) collective-permute-start(bf16[512,256]{1,0:T(8,128)(2,1)S(1)} %get-tuple-element.48), channel_id=1, source_target_pairs={{0,3},{1,0},{2,1},{3,2},{4,7},{5,4},{6,5},{7,6},{8,11},{9,8},{10,9... | collective-permute-start | bytes 786440 | tf_op jit(solution)/shard_map/ppermute | solution.py:28
  49.6 11.7 %collective-permute-start.8 = (bf16[512,256]{1,0:T(8,128)(2,1)S(1)}, bf16[512,256]{1,0:T(8,128)(2,1)S(1)}, u32[]{:S(2)}, u32[]{:S(2)}) collective-permute-start(bf16[512,256]{1,0:T(8,128)(2,1)S(1)} %get-tuple-element.49), channel_id=1, source_target_pairs={{0,2},{1,3},{2,0},{3,1},{4,6},{5,7},{6,4},{7,5},{8,10},{9,11},{10,... | collective-permute-start | bytes 786440 | tf_op jit(solution)/shard_map/ppermute | solution.py:28
  61.3 15.3 %collective-permute-start.18 = (bf16[768,256]{1,0:T(8,128)(2,1)S(1)}, bf16[768,256]{1,0:T(8,128)(2,1)S(1)}, u32[]{:S(2)}, u32[]{:S(2)}) collective-permute-start(bf16[768,256]{1,0:T(8,128)(2,1)S(1)} %get-tuple-element.61.refs_5_), channel_id=1, source_target_pairs={{0,64},{64,0},{128,192},{192,128},{1,65},{65,1},{129,193},{193,129... | collective-permute-start | bytes 1179656 | tf_op jit(solution)/shard_map/ppermute | solution.py:172
  61.4 15.2 %collective-permute-start.19 = (bf16[512,256]{1,0:T(8,128)(2,1)S(1)}, bf16[512,256]{1,0:T(8,128)(2,1)S(1)}, u32[]{:S(2)}, u32[]{:S(2)}) collective-permute-start(bf16[512,256]{1,0:T(8,128)(2,1)S(1)} %get-tuple-element.58.refs_3_.refs_6_), channel_id=1, source_target_pairs={{0,4},{4,8},{8,12},{12,16},{16,20},{20,24},{24,28},{28,0},{1,5},{5... | collective-permute-start | bytes 786440 | tf_op jit(solution)/shard_map/ppermute | solution.py:28
  61.5 15.1 %collective-permute-start.20 = (bf16[512,256]{1,0:T(8,128)(2,1)S(1)}, bf16[512,256]{1,0:T(8,128)(2,1)S(1)}, u32[]{:S(2)}, u32[]{:S(2)}) collective-permute-start(bf16[512,256]{1,0:T(8,128)(2,1)S(1)} %get-tuple-element.62), channel_id=1, source_target_pairs={{0,28},{4,0},{8,4},{12,8},{16,12},{20,16},{24,20},{28,24},{1,29},{... | collective-permute-start | bytes 786440 | tf_op jit(solution)/shard_map/ppermute | solution.py:28
  64.1 7.5 %collective-permute-start.23 = (bf16[256,256]{1,0:T(8,128)(2,1)S(1)}, bf16[256,256]{1,0:T(8,128)(2,1)S(1)}, u32[]{:S(2)}, u32[]{:S(2)}) collective-permute-start(bf16[256,256]{1,0:T(8,128)(2,1)S(1)} %shard_map.87.refs_5_.refs_0_), channel_id=1, source_target_pairs={{0,8},{4,12},{8,0},{12,4},{16,24},{20,28},{24,16},{28,20},{1,9},{5... | collective-permute-start | bytes 393224 | tf_op jit(solution)/shard_map/ppermute | solution.py:378
  71.7 7.2 %collective-permute-start.24 = (bf16[256,256]{1,0:T(8,128)(2,1)S(1)}, bf16[256,256]{1,0:T(8,128)(2,1)S(1)}, u32[]{:S(2)}, u32[]{:S(2)}) collective-permute-start(bf16[256,256]{1,0:T(8,128)(2,1)S(1)} %shard_map.94.refs_0_), channel_id=1, source_target_pairs={{0,24},{4,28},{8,16},{12,20},{16,8},{20,12},{24,0},{28,4},{1,25},{... | collective-permute-start | bytes 393224 | tf_op jit(solution)/shard_map/ppermute | solution.py:378
  73.0 18.4 %collective-permute-start.17 = (bf16[768,256]{1,0:T(8,128)(2,1)S(1)}, bf16[768,256]{1,0:T(8,128)(2,1)S(1)}, u32[]{:S(2)}, u32[]{:S(2)}) collective-permute-start(bf16[768,256]{1,0:T(8,128)(2,1)S(1)} %get-tuple-element.59.refs_5_), channel_id=1, source_target_pairs={{0,192},{192,0},{64,128},{128,64},{1,193},{193,1},{65,129},{129,65... | collective-permute-start | bytes 1179656 | tf_op jit(solution)/shard_map/ppermute | solution.py:172
  77.3 14.1 %collective-permute-start.22 = (bf16[512,256]{1,0:T(8,128)(2,1)S(1)}, bf16[512,256]{1,0:T(8,128)(2,1)S(1)}, u32[]{:S(2)}, u32[]{:S(2)}) collective-permute-start(bf16[512,256]{1,0:T(8,128)(2,1)S(1)} %get-tuple-element.64.refs_10_), channel_id=1, source_target_pairs={{0,4},{4,8},{8,12},{12,16},{16,20},{20,24},{24,28},{28,0},{1,5},{5... | collective-permute-start | bytes 786440 | tf_op jit(solution)/shard_map/ppermute | solution.py:28
  78.9 8.2 %collective-permute-start.25 = (bf16[256,256]{1,0:T(8,128)(2,1)S(1)}, bf16[256,256]{1,0:T(8,128)(2,1)S(1)}, u32[]{:S(2)}, u32[]{:S(2)}) collective-permute-start(bf16[256,256]{1,0:T(8,128)(2,1)S(1)} %shard_map.95.refs_4_), channel_id=1, source_target_pairs={{0,1},{1,2},{2,3},{3,0},{4,5},{5,6},{6,7},{7,4},{8,9},{9,10},{10,1... | collective-permute-start | bytes 393224 | tf_op jit(solution)/shard_map/ppermute | solution.py:28
  79.0 8.3 %collective-permute-start.26 = (bf16[256,256]{1,0:T(8,128)(2,1)S(1)}, bf16[256,256]{1,0:T(8,128)(2,1)S(1)}, u32[]{:S(2)}, u32[]{:S(2)}) collective-permute-start(bf16[256,256]{1,0:T(8,128)(2,1)S(1)} %shard_map.95.refs_4_), channel_id=1, source_target_pairs={{0,3},{1,0},{2,1},{3,2},{4,7},{5,4},{6,5},{7,6},{8,11},{9,8},{10,9... | collective-permute-start | bytes 393224 | tf_op jit(solution)/shard_map/ppermute | solution.py:28
  84.6 5.4 %collective-permute-start.27 = (bf16[256,256]{1,0:T(8,128)(2,1)S(1)}, bf16[256,256]{1,0:T(8,128)(2,1)S(1)}, u32[]{:S(2)}, u32[]{:S(2)}) collective-permute-start(bf16[256,256]{1,0:T(8,128)(2,1)S(1)} %shard_map.95.refs_4_), channel_id=1, source_target_pairs={{0,2},{1,3},{2,0},{3,1},{4,6},{5,7},{6,4},{7,5},{8,10},{9,11},{10,... | collective-permute-start | bytes 393224 | tf_op jit(solution)/shard_map/ppermute | solution.py:28
  87.2 7.9 %collective-permute-start.21 = (bf16[512,256]{1,0:T(8,128)(2,1)S(1)}, bf16[512,256]{1,0:T(8,128)(2,1)S(1)}, u32[]{:S(2)}, u32[]{:S(2)}) collective-permute-start(bf16[512,256]{1,0:T(8,128)(2,1)S(1)} %get-tuple-element.63), channel_id=1, source_target_pairs={{0,28},{4,0},{8,4},{12,8},{16,12},{20,16},{24,20},{28,24},{1,29},{... | collective-permute-start | bytes 786440 | tf_op jit(solution)/shard_map/ppermute | solution.py:28
  91.9 9.0 %collective-permute-start.28 = (bf16[512,256]{1,0:T(8,128)(2,1)S(1)}, bf16[512,256]{1,0:T(8,128)(2,1)S(1)}, u32[]{:S(2)}, u32[]{:S(2)}) collective-permute-start(bf16[512,256]{1,0:T(8,128)(2,1)S(1)} %shard_map.97.refs_8_), channel_id=1, source_target_pairs={{0,4},{4,8},{8,12},{12,16},{16,20},{20,24},{24,28},{28,0},{1,5},{5... | collective-permute-start | bytes 786440 | tf_op jit(solution)/shard_map/ppermute | solution.py:28
  92.0 5.8 %collective-permute-start.29 = (bf16[256,256]{1,0:T(8,128)(2,1)S(1)}, bf16[256,256]{1,0:T(8,128)(2,1)S(1)}, u32[]{:S(2)}, u32[]{:S(2)}) collective-permute-start(bf16[256,256]{1,0:T(8,128)(2,1)S(1)} %get-tuple-element.65.refs_8_), channel_id=1, source_target_pairs={{0,192},{64,0},{128,64},{192,128},{1,193},{65,1},{129,65},{193,129... | collective-permute-start | bytes 393224 | tf_op jit(solution)/shard_map/ppermute | solution.py:28
  94.5 5.4 %collective-permute-start.30 = (bf16[256,256]{1,0:T(8,128)(2,1)S(1)}, bf16[256,256]{1,0:T(8,128)(2,1)S(1)}, u32[]{:S(2)}, u32[]{:S(2)}) collective-permute-start(bf16[256,256]{1,0:T(8,128)(2,1)S(1)} %get-tuple-element.67), channel_id=1, source_target_pairs={{0,128},{64,192},{128,0},{192,64},{1,129},{65,193},{129,1},{193,65... | collective-permute-start | bytes 393224 | tf_op jit(solution)/shard_map/ppermute | solution.py:28
  94.5 6.4 %collective-permute-start.31 = (bf16[256,256]{1,0:T(8,128)(2,1)S(1)}, bf16[256,256]{1,0:T(8,128)(2,1)S(1)}, u32[]{:S(2)}, u32[]{:S(2)}) collective-permute-start(bf16[256,256]{1,0:T(8,128)(2,1)S(1)} %get-tuple-element.68), channel_id=1, source_target_pairs={{0,64},{64,128},{128,192},{192,0},{1,65},{65,129},{129,193},{193,1... | collective-permute-start | bytes 393224 | tf_op jit(solution)/shard_map/ppermute | solution.py:28
  101.5 9.6 %collective-permute-start.32 = (bf16[512,256]{1,0:T(8,128)(2,1)S(1)}, bf16[512,256]{1,0:T(8,128)(2,1)S(1)}, u32[]{:S(2)}, u32[]{:S(2)}) collective-permute-start(bf16[512,256]{1,0:T(8,128)(2,1)S(1)} %get-tuple-element.69), channel_id=1, source_target_pairs={{0,32},{1,33},{2,34},{3,35},{4,36},{5,37},{6,38},{7,39},{8,40},{9,... | collective-permute-start | bytes 786440 | tf_op jit(solution)/shard_map/ppermute | solution.py:527
  (8 other events, 124.7 us)

commit v7 on v6

--- a/solution.py
+++ b/solution.py
@@ -79,28 +79,28 @@
     return lax.rem(lax.axis_index("pool"), 2)
 
 
-def pack_kernel(groups, ahead, *refs):
-    w_ref = refs[0]
-    n_in = 2 if ahead else 1
-    outs = refs[n_in : n_in + 3]
-    owns = refs[n_in + 3 : n_in + 3 + len(groups)]
-    sems = refs[-1]
+def pack_body(sets, ahead, *refs):
+    w_ref, sems = refs[0], refs[-1]
+    groups = [group for members in sets for group in members]
+    rest = refs[2:] if ahead else refs[1:]
+    outs, owns = rest[: 3 * len(sets)], rest[3 * len(sets) : 3 * len(sets) + len(groups)]
     y, odd = lax.axis_index(Y), parity()
     copies = []
-    for gi, group in enumerate(groups):
-        plus, minus = tiles_of(group)
-        wanted = (plus, minus) if ahead else (plus * (1 - odd) + minus * odd,)
-        for ki, hop in enumerate(HOPS):
-            if ahead:
-                copies.append((refs[1], outs[ki].at[pl.ds(0, ROWS), :]))
-            for ti, ztile in enumerate(wanted):
-                source = w_ref.at[:, pl.ds(column(ztile, lax.rem(y + hop, NY)), TILE)]
-                first = ahead + (gi + ti) * TILE
-                copies.append((source, outs[ki].at[pl.ds(first, TILE), :]))
-    for gi, group in enumerate(groups):
+    for si, members in enumerate(sets):
+        for gi, group in enumerate(members):
+            plus, minus = tiles_of(group)
+            wanted = (plus, minus) if ahead else (plus * (1 - odd) + minus * odd,)
+            for ki, hop in enumerate(HOPS):
+                out = outs[3 * si + ki]
+                if ahead:
+                    copies.append((refs[1], out.at[pl.ds(0, ROWS), :]))
+                for ti, ztile in enumerate(wanted):
+                    source = w_ref.at[:, pl.ds(column(ztile, lax.rem(y + hop, NY)), TILE)]
+                    copies.append((source, out.at[pl.ds(ahead + (gi + ti) * TILE, TILE), :]))
+    for own, group in zip(owns, groups):
         for ti, ztile in enumerate(tiles_of(group)):
             source = w_ref.at[:, pl.ds(column(ztile, y), TILE)]
-            copies.append((source, owns[gi].at[pl.ds(ti * TILE, TILE), :]))
+            copies.append((source, own.at[pl.ds(ti * TILE, TILE), :]))
     copies = [
         pltpu.make_async_copy(source, target, sems.at[i])
         for i, (source, target) in enumerate(copies)
@@ -111,26 +111,29 @@
         copy.wait()
 
 
-def pack(groups, weight, features=None, after=()):
-    args, specs, rows = [weight], [HBM], len(groups) * TILE
-    ahead = 0
+def pack(sets, weight, features=None, after=()):
+    args, specs = [weight], [HBM]
+    ahead, count = 0, sum(len(members) for members in sets)
+    dims = []
     if features is not None:
-        ahead, rows = ROWS, ROWS + 2 * TILE
+        ahead = ROWS
         args.append(features)
         specs.append(HBM)
-    dims = [(rows, TILE)] * 3 + [(2 * TILE, TILE)] * len(groups)
+    for members in sets:
+        dims += [(ROWS + 2 * TILE if ahead else len(members) * TILE, TILE)] * 3
+    dims += [(2 * TILE, TILE)] * count
     got = call(
-        functools.partial(pack_kernel, groups, ahead),
+        functools.partial(pack_body, sets, ahead),
         args,
         specs,
         [shape(d) for d in dims],
         [whole(d) for d in dims],
-        [pltpu.SemaphoreType.DMA((11 if ahead else 5 * len(groups),))],
-        (0, 6 * rows * TILE),
+        [pltpu.SemaphoreType.DMA((11 if ahead else 5 * count,))],
+        (0, 20 * count * TILE * TILE),
         8,
         after,
     )
-    return got[:3], got[3:]
+    return [got[3 * i : 3 * i + 3] for i in range(len(sets))], got[3 * len(sets) :]
 
 
 def join_kernel(base, halves, a_ref, b_ref, c_ref, *outs):
@@ -487,14 +490,13 @@
     places = diagonal_block_index[0][:, 0]
     ids = row_variant_index.reshape(1, ROWS)
 
-    first, (own0,) = pack((0,), weight, features)
+    (first,), (own0,) = pack(((0,),), weight, features)
     got = [shift(value, Y, hop) for value, hop in zip(first, HOPS)]
     sent = dispatch(ids, features, (first[0],))
     items = [sent[0]] + [shift(sent[k], "pool", k) for k in (1, 2, 3)]
-    second, (own1,) = pack((1,), weight, None, (sent[0],))
+    (second, third), (own1, own2, own3) = pack(((1,), (2, 3)), weight, None, (sent[0],))
     got1 = [shift(value, Y, hop) for value, hop in zip(second, HOPS)]
     low = down(items, down_factor, (second[0],))
-    third, (own2, own3) = pack((2, 3), weight, None, (low,))
     got2 = [shift(value, Y, hop) for value, hop in zip(third, HOPS)]
     low1 = exchanged_sum(low, Z, (1, 0, 3, 2, 5, 4, 7, 6))
     low2 = exchanged_sum(low1, Z, (2, 3, 0, 1, 6, 7, 4, 5))

time: 112 us -> 112 us (level)
  starting transfers between devices: 47.5 us -> 49.3 us
    ppermute x3, starting transfers between devices: 3.02 us -> 4.86 us  [exchanged_sum(): other = lax.ppermute(value, axis, list(enumerate(partner)))]
    ppermute x27, waiting for transfers between devices: 30.2 us -> 28.9 us  [shift(): lax.ppermute(value, axis, [(i, (i + steps) % count) for i in range(count)])]
    pallas_call x18 -> x17, Pallas kernels: 15.1 us -> 14.1 us  [call(): pl.pallas_call(body, out_shape=outs, in_specs=list(in_specs) + [ANY] * m,...]
where the time goes in v7:
time: 112 us
  starting transfers between devices  49.3 us (44%)
  waiting for transfers between devices  47.1 us (42%)
  Pallas kernels  14.1 us (13%)
    ppermute x27, starting transfers between devices, shift(): lax.ppermute(value, axis, [(i, (i + steps) % count) for i in range(count)])  41.7 us
    ppermute x27, waiting for transfers between devices, shift(): lax.ppermute(value, axis, [(i, (i + steps) % count) for i in range(count)])  28.9 us
    pallas_call x17, Pallas kernels, call(): pl.pallas_call(body, out_shape=outs, in_specs=list(in_specs) + [ANY] * m,...  14.1 us
    ppermute x1, waiting for transfers between devices, steps(): carried = lax.ppermute(first_out, 'section', [(0, 1)])  9.23 us
    ppermute x3, waiting for transfers between devices, exchanged_sum(): other = lax.ppermute(value, axis, list(enumerate(partner)))  8.94 us
    ppermute x3, starting transfers between devices, exchanged_sum(): other = lax.ppermute(value, axis, list(enumerate(partner)))  4.86 us
  transfers between devices with their start and end apart: 33, of which 16 were waited for; matrix products, arithmetic and copies ran while one was open for 0% of the time, Pallas kernels for 11%

profile of v7, /device:TPU:1, one launch (start us, length us, event | category | flops | bytes accessed | tf_op | source)
XLA Modules:
  0.0 111.6 jit_solution(7149596105656707211)
XLA Ops:
  0.0 1.7 %shard_map.82 = (bf16[1024,256]{1,0:T(8,128)(2,1)S(1)}, bf16[1024,256]{1,0:T(8,128)(2,1)S(1)}, bf16[1024,256]{1,0:T(8,128)(2,1)S(1)}, bf16[512,256]{1,0:T(8,128)(2,1)S(1)}) custom-call(bf16[256,8192]{1,0:T(8,128)(2,1)} %bitcast.22, bf16[512,256]{1,0:T(8,128)(2,1)} %bitcast.9), custom_call_target="tpu_custom_call" | custom-call | bytes 1310720 | tf_op jit(solution)/shard_map/pallas_call | solution.py:67
  1.7 2.2 %collective-permute-start = (bf16[1024,256]{1,0:T(8,128)(2,1)S(1)}, bf16[1024,256]{1,0:T(8,128)(2,1)S(1)}, u32[]{:S(2)}, u32[]{:S(2)}) collective-permute-start(bf16[1024,256]{1,0:T(8,128)(2,1)S(1)} %get-tuple-element.38.refs_2_), channel_id=1, source_target_pairs={{0,1},{1,2},{2,3},{3,0},{4,5},{5,6},{6,7},{7,4},{8,9},{9,10},{10,1... | collective-permute-start | bytes 1572872 | tf_op jit(solution)/shard_map/ppermute | solution.py:28
  6.1 1.5 %collective-permute-start.1 = (bf16[1024,256]{1,0:T(8,128)(2,1)S(1)}, bf16[1024,256]{1,0:T(8,128)(2,1)S(1)}, u32[]{:S(2)}, u32[]{:S(2)}) collective-permute-start(bf16[1024,256]{1,0:T(8,128)(2,1)S(1)} %get-tuple-element.41), channel_id=1, source_target_pairs={{0,3},{1,0},{2,1},{3,2},{4,7},{5,4},{6,5},{7,6},{8,11},{9,8},{10,9... | collective-permute-start | bytes 1572872 | tf_op jit(solution)/shard_map/ppermute | solution.py:28
  7.5 1.6 %collective-permute-start.2 = (bf16[1024,256]{1,0:T(8,128)(2,1)S(1)}, bf16[1024,256]{1,0:T(8,128)(2,1)S(1)}, u32[]{:S(2)}, u32[]{:S(2)}) collective-permute-start(bf16[1024,256]{1,0:T(8,128)(2,1)S(1)} %get-tuple-element.42), channel_id=1, source_target_pairs={{0,2},{1,3},{2,0},{3,1},{4,6},{5,7},{6,4},{7,5},{8,10},{9,11},{10,... | collective-permute-start | bytes 1572872 | tf_op jit(solution)/shard_map/ppermute | solution.py:28
  9.1 2.4 %collective-permute-start.10 = (bf16[272,256]{1,0:T(8,128)(2,1)S(1)}, bf16[272,256]{1,0:T(8,128)(2,1)S(1)}, u32[]{:S(2)}, u32[]{:S(2)}) collective-permute-start(bf16[272,256]{1,0:T(8,128)(2,1)S(1)} %get-tuple-element.52), channel_id=1, source_target_pairs={{0,128},{64,192},{128,0},{192,64},{1,129},{65,193},{129,1},{193,65... | collective-permute-start | bytes 417800 | tf_op jit(solution)/shard_map/ppermute | solution.py:28
  12.8 1.7 %shard_map.84 = (bf16[256,256]{1,0:T(8,128)(2,1)S(1)}, bf16[256,256]{1,0:T(8,128)(2,1)S(1)}, bf16[256,256]{1,0:T(8,128)(2,1)S(1)}, bf16[512,256]{1,0:T(8,128)(2,...) custom-call(bf16[256,8192]{1,0:T(8,128)(2,1)} %bitcast.23, ...), custom_call_target="tpu_custom_call" | custom-call | bytes 3932160 | tf_op jit(solution)/shard_map/pallas_call | solution.py:67
  14.6 2.4 %collective-permute-done.11.refs_3_ = bf16[272,256]{1,0:T(8,128)(2,1)S(1)} collective-permute-done((bf16[272,256]{1,0:T(8,128)(2,1)S(1)}, bf16[272,256]{1,0:T(8,128)(2,1)S(1)}, u32[]{:S(2)}, u32[]{:S(2)}) %collective-permute-start.11) | collective-permute-done | bytes 139296 | tf_op jit(solution)/shard_map/ppermute | solution.py:28
  16.9 2.6 %shard_map.85.refs_0_ = bf16[256,256]{1,0:T(8,128)(2,1)S(1)} custom-call(bf16[272,256]{1,0:T(8,128)(2,1)S(1)} %get-tuple-element.39.refs_1_.refs_0_, bf16[272,256]{1,0:T(8,128)(2,1)S(1)} %collective-permute-done.9.refs_1_, bf16[272,256]{1,0:T(8,128)(2,1)S(1)} %collective-permute-done.10.refs_2_, bf16[272,256]{1,0:T(8,128)(2,1)S(1)} %collective-permute-done.11.refs_3_, ...), custom_call_target="tpu_custom_call" | custom-call | flops 1073741824 | bytes 2097152 | tf_op jit(solution)/shard_map/pallas_call | solution.py:67
  19.5 1.7 %collective-permute-start.12 = (bf16[256,256]{1,0:T(8,128)(2,1)S(1)}, bf16[256,256]{1,0:T(8,128)(2,1)S(1)}, u32[]{:S(2)}, u32[]{:S(2)}) collective-permute-start(bf16[256,256]{1,0:T(8,128)(2,1)S(1)} %shard_map.85.refs_0_), channel_id=1, source_target_pairs={{0,4},{4,0},{8,12},{12,8},{16,20},{20,16},{24,28},{28,24},{1,5},{5... | collective-permute-start | bytes 393224 | tf_op jit(solution)/shard_map/ppermute | solution.py:381
  21.6 2.3 %collective-permute-done.12.refs_1_ = bf16[256,256]{1,0:T(8,128)(2,1)S(1)} collective-permute-done((bf16[256,256]{1,0:T(8,128)(2,1)S(1)}, bf16[256,256]{1,0:T(8,128)(2,1)S(1)}, u32[]{:S(2)}, u32[]{:S(2)}) %collective-permute-start.12) | collective-permute-done | bytes 131104 | tf_op jit(solution)/shard_map/ppermute | solution.py:381
  24.7 1.4 %collective-permute-start.8 = (bf16[256,256]{1,0:T(8,128)(2,1)S(1)}, bf16[256,256]{1,0:T(8,128)(2,1)S(1)}, u32[]{:S(2)}, u32[]{:S(2)}) collective-permute-start(bf16[256,256]{1,0:T(8,128)(2,1)S(1)} %get-tuple-element.49), channel_id=1, source_target_pairs={{0,2},{1,3},{2,0},{3,1},{4,6},{5,7},{6,4},{7,5},{8,10},{9,11},{10,... | collective-permute-start | bytes 393224 | tf_op jit(solution)/shard_map/ppermute | solution.py:28
  26.1 3.0 %collective-permute-done.2.refs_4_ = bf16[1024,256]{1,0:T(8,128)(2,1)S(1)} collective-permute-done((bf16[1024,256]{1,0:T(8,128)(2,1)S(1)}, bf16[1024,256]{1,0:T(8,128)(2,1)S(1)}, u32[]{:S(2)}, u32[]{:S(2)}) %collective-permute-start.2) | collective-permute-done | bytes 524320 | tf_op jit(solution)/shard_map/ppermute | solution.py:28
  29.8 4.1 %collective-permute-done.6.refs_0_ = bf16[256,256]{1,0:T(8,128)(2,1)S(1)} collective-permute-done((bf16[256,256]{1,0:T(8,128)(2,1)S(1)}, bf16[256,256]{1,0:T(8,128)(2,1)S(1)}, u32[]{:S(2)}, u32[]{:S(2)}) %collective-permute-start.6) | collective-permute-done | bytes 131104 | tf_op jit(solution)/shard_map/ppermute | solution.py:28
  34.7 1.4 %collective-permute-start.13 = (bf16[384,256]{1,0:T(8,128)(2,1)S(1)}, bf16[384,256]{1,0:T(8,128)(2,1)S(1)}, u32[]{:S(2)}, u32[]{:S(2)}) collective-permute-start(bf16[384,256]{1,0:T(8,128)(2,1)S(1)} %get-tuple-element.55.refs_5_), channel_id=1, source_target_pairs={{0,64},{64,128},{128,192},{192,0},{1,65},{65,129},{129,193},{193,1... | collective-permute-start | bytes 589832 | tf_op jit(solution)/shard_map/ppermute | solution.py:28
  37.4 1.7 %collective-permute-start.15 = (bf16[512,256]{1,0:T(8,128)(2,1)S(1)}, bf16[512,256]{1,0:T(8,128)(2,1)S(1)}, u32[]{:S(2)}, u32[]{:S(2)}) collective-permute-start(bf16[512,256]{1,0:T(8,128)(2,1)S(1)} %get-tuple-element.54.refs_3_), channel_id=1, source_target_pairs={{0,4},{4,8},{8,12},{12,16},{16,20},{20,24},{24,28},{28,0},{1,5},{5... | collective-permute-start | bytes 786440 | tf_op jit(solution)/shard_map/ppermute | solution.py:28
  39.2 3.9 %collective-permute-start.16 = (bf16[512,256]{1,0:T(8,128)(2,1)S(1)}, bf16[512,256]{1,0:T(8,128)(2,1)S(1)}, u32[]{:S(2)}, u32[]{:S(2)}) collective-permute-start(bf16[512,256]{1,0:T(8,128)(2,1)S(1)} %get-tuple-element.57), channel_id=1, source_target_pairs={{0,28},{4,0},{8,4},{12,8},{16,12},{20,16},{24,20},{28,24},{1,29},{... | collective-permute-start | bytes 786440 | tf_op jit(solution)/shard_map/ppermute | solution.py:28
  43.1 2.6 %collective-permute-start.3 = (bf16[512,256]{1,0:T(8,128)(2,1)S(1)}, bf16[512,256]{1,0:T(8,128)(2,1)S(1)}, u32[]{:S(2)}, u32[]{:S(2)}) collective-permute-start(bf16[512,256]{1,0:T(8,128)(2,1)S(1)} %get-tuple-element.43), channel_id=1, source_target_pairs={{0,1},{1,2},{2,3},{3,0},{4,5},{5,6},{6,7},{7,4},{8,9},{9,10},{10,1... | collective-permute-start | bytes 786440 | tf_op jit(solution)/shard_map/ppermute | solution.py:28
  45.7 2.0 %collective-permute-start.4 = (bf16[512,256]{1,0:T(8,128)(2,1)S(1)}, bf16[512,256]{1,0:T(8,128)(2,1)S(1)}, u32[]{:S(2)}, u32[]{:S(2)}) collective-permute-start(bf16[512,256]{1,0:T(8,128)(2,1)S(1)} %get-tuple-element.44), channel_id=1, source_target_pairs={{0,3},{1,0},{2,1},{3,2},{4,7},{5,4},{6,5},{7,6},{8,11},{9,8},{10,9... | collective-permute-start | bytes 786440 | tf_op jit(solution)/shard_map/ppermute | solution.py:28
  49.7 3.3 %collective-permute-done.3.refs_0_ = bf16[512,256]{1,0:T(8,128)(2,1)S(1)} collective-permute-done((bf16[512,256]{1,0:T(8,128)(2,1)S(1)}, bf16[512,256]{1,0:T(8,128)(2,1)S(1)}, u32[]{:S(2)}, u32[]{:S(2)}) %collective-permute-start.3) | collective-permute-done | bytes 262176 | tf_op jit(solution)/shard_map/ppermute | solution.py:28
  53.9 5.6 %collective-permute-done.5.refs_2_ = bf16[512,256]{1,0:T(8,128)(2,1)S(1)} collective-permute-done((bf16[512,256]{1,0:T(8,128)(2,1)S(1)}, bf16[512,256]{1,0:T(8,128)(2,1)S(1)}, u32[]{:S(2)}, u32[]{:S(2)}) %collective-permute-start.5) | collective-permute-done | bytes 262176 | tf_op jit(solution)/shard_map/ppermute | solution.py:28
  59.7 3.3 %collective-permute-start.20 = (bf16[512,256]{1,0:T(8,128)(2,1)S(1)}, bf16[512,256]{1,0:T(8,128)(2,1)S(1)}, u32[]{:S(2)}, u32[]{:S(2)}) collective-permute-start(bf16[512,256]{1,0:T(8,128)(2,1)S(1)} %get-tuple-element.62), channel_id=1, source_target_pairs={{0,28},{4,0},{8,4},{12,8},{16,12},{20,16},{24,20},{28,24},{1,29},{... | collective-permute-start | bytes 786440 | tf_op jit(solution)/shard_map/ppermute | solution.py:28
  63.1 6.7 %collective-permute-done.23.refs_1_ = bf16[256,256]{1,0:T(8,128)(2,1)S(1)} collective-permute-done((bf16[256,256]{1,0:T(8,128)(2,1)S(1)}, bf16[256,256]{1,0:T(8,128)(2,1)S(1)}, u32[]{:S(2)}, u32[]{:S(2)}) %collective-permute-start.23) | collective-permute-done | bytes 131104 | tf_op jit(solution)/shard_map/ppermute | solution.py:381
  69.8 3.1 %collective-permute-start.24 = (bf16[256,256]{1,0:T(8,128)(2,1)S(1)}, bf16[256,256]{1,0:T(8,128)(2,1)S(1)}, u32[]{:S(2)}, u32[]{:S(2)}) collective-permute-start(bf16[256,256]{1,0:T(8,128)(2,1)S(1)} %shard_map.93.refs_0_), channel_id=1, source_target_pairs={{0,24},{4,28},{8,16},{12,20},{16,8},{20,12},{24,0},{28,4},{1,25},{... | collective-permute-start | bytes 393224 | tf_op jit(solution)/shard_map/ppermute | solution.py:381
  74.3 2.1 %shard_map.91.refs_9_ = f32[4,256,256]{2,1,0:T(8,128)S(1)} custom-call(bf16[272,256]{1,0:T(8,128)(2,1)S(1)} %get-tuple-element.39.refs_1_.refs_0_, bf16[272,256]{1,0:T(8,128)(2,1)S(1)} %collective-permute-done.9.refs_1_, bf16[272,256]{1,0:T(8,128)(2,1)S(1)} %collective-permute-done.10.refs_2_, bf16[272,256]{1,0:T(8,128)(2,1)S(1)} %collective-permute-done.11.refs_3_, ...), custom_call_target="tpu_custom_call" | custom-call | flops 1073741824 | bytes 3145728 | tf_op jit(solution)/shard_map/pallas_call | solution.py:67
  77.2 3.4 %collective-permute-start.22 = (bf16[512,256]{1,0:T(8,128)(2,1)S(1)}, bf16[512,256]{1,0:T(8,128)(2,1)S(1)}, u32[]{:S(2)}, u32[]{:S(2)}) collective-permute-start(bf16[512,256]{1,0:T(8,128)(2,1)S(1)} %get-tuple-element.64.refs_10_), channel_id=1, source_target_pairs={{0,4},{4,8},{8,12},{12,16},{16,20},{20,24},{24,28},{28,0},{1,5},{5... | collective-permute-start | bytes 786440 | tf_op jit(solution)/shard_map/ppermute | solution.py:28
  80.7 3.5 %collective-permute-start.26 = (bf16[256,256]{1,0:T(8,128)(2,1)S(1)}, bf16[256,256]{1,0:T(8,128)(2,1)S(1)}, u32[]{:S(2)}, u32[]{:S(2)}) collective-permute-start(bf16[256,256]{1,0:T(8,128)(2,1)S(1)} %shard_map.94.refs_4_), channel_id=1, source_target_pairs={{0,3},{1,0},{2,1},{3,2},{4,7},{5,4},{6,5},{7,6},{8,11},{9,8},{10,9... | collective-permute-start | bytes 393224 | tf_op jit(solution)/shard_map/ppermute | solution.py:28
  85.3 1.5 %collective-permute-done.25.refs_5_ = bf16[256,256]{1,0:T(8,128)(2,1)S(1)} collective-permute-done((bf16[256,256]{1,0:T(8,128)(2,1)S(1)}, bf16[256,256]{1,0:T(8,128)(2,1)S(1)}, u32[]{:S(2)}, u32[]{:S(2)}) %collective-permute-start.25) | collective-permute-done | bytes 131104 | tf_op jit(solution)/shard_map/ppermute | solution.py:28
  87.2 2.4 %collective-permute-done.27.refs_7_ = bf16[256,256]{1,0:T(8,128)(2,1)S(1)} collective-permute-done((bf16[256,256]{1,0:T(8,128)(2,1)S(1)}, bf16[256,256]{1,0:T(8,128)(2,1)S(1)}, u32[]{:S(2)}, u32[]{:S(2)}) %collective-permute-start.27) | collective-permute-done | bytes 131104 | tf_op jit(solution)/shard_map/ppermute | solution.py:28
  89.6 1.4 %shard_map.95 = (bf16[256,256]{1,0:T(8,128)(2,1)S(1)}, bf16[256,256]{1,0:T(8,128)(2,1)S(1)}, bf16[256,256]{1,0:T(8,128)(2,1)S(1)}, bf16[256,256]{1,0:T(8,128)(2,1)S(1)}) custom-call(bf16[272,256]{1,0:T(8,128)(2,1)S(1)} %get-tuple-element.39.refs_1_.refs_0_, bf16[272,256]{1,0:T(8,128)(2,1)S(1)} %collective-permute-done.9.refs_1_, ...), custom_call_target="tpu_custom_call" | custom-call | flops 1073741824 | bytes 3145728 | tf_op jit(solution)/shard_map/pallas_call | solution.py:67
  91.6 1.4 %collective-permute-start.29 = (bf16[256,256]{1,0:T(8,128)(2,1)S(1)}, bf16[256,256]{1,0:T(8,128)(2,1)S(1)}, u32[]{:S(2)}, u32[]{:S(2)}) collective-permute-start(bf16[256,256]{1,0:T(8,128)(2,1)S(1)} %get-tuple-element.65.refs_8_), channel_id=1, source_target_pairs={{0,192},{64,0},{128,64},{192,128},{1,193},{65,1},{129,65},{193,129... | collective-permute-start | bytes 393224 | tf_op jit(solution)/shard_map/ppermute | solution.py:28
  95.8 2.6 %collective-permute-done.30.refs_6_ = bf16[256,256]{1,0:T(8,128)(2,1)S(1)} collective-permute-done((bf16[256,256]{1,0:T(8,128)(2,1)S(1)}, bf16[256,256]{1,0:T(8,128)(2,1)S(1)}, u32[]{:S(2)}, u32[]{:S(2)}) %collective-permute-start.30) | collective-permute-done | bytes 131104 | tf_op jit(solution)/shard_map/ppermute | solution.py:28
  101.6 9.2 %collective-permute-done.32 = bf16[512,256]{1,0:T(8,128)(2,1)S(1)} collective-permute-done((bf16[512,256]{1,0:T(8,128)(2,1)S(1)}, bf16[512,256]{1,0:T(8,128)(2,1)S(1)}, u32[]{:S(2)}, u32[]{:S(2)}) %collective-permute-start.32) | collective-permute-done | bytes 262176 | tf_op jit(solution)/shard_map/ppermute | solution.py:529
  (66 shorter events, 21.6 us)
Async XLA Ops:
  1.7 23.0 %collective-permute-start = (bf16[1024,256]{1,0:T(8,128)(2,1)S(1)}, bf16[1024,256]{1,0:T(8,128)(2,1)S(1)}, u32[]{:S(2)}, u32[]{:S(2)}) collective-permute-start(bf16[1024,256]{1,0:T(8,128)(2,1)S(1)} %get-tuple-element.38.refs_2_), channel_id=1, source_target_pairs={{0,1},{1,2},{2,3},{3,0},{4,5},{5,6},{6,7},{7,4},{8,9},{9,10},{10,1... | collective-permute-start | bytes 1572872 | tf_op jit(solution)/shard_map/ppermute | solution.py:28
  4.8 6.8 %collective-permute-start.9 = (bf16[272,256]{1,0:T(8,128)(2,1)S(1)}, bf16[272,256]{1,0:T(8,128)(2,1)S(1)}, u32[]{:S(2)}, u32[]{:S(2)}) collective-permute-start(bf16[272,256]{1,0:T(8,128)(2,1)S(1)} %get-tuple-element.51), channel_id=1, source_target_pairs={{0,64},{64,128},{128,192},{192,0},{1,65},{65,129},{129,193},{193,1... | collective-permute-start | bytes 417800 | tf_op jit(solution)/shard_map/ppermute | solution.py:28
  6.1 20.0 %collective-permute-start.1 = (bf16[1024,256]{1,0:T(8,128)(2,1)S(1)}, bf16[1024,256]{1,0:T(8,128)(2,1)S(1)}, u32[]{:S(2)}, u32[]{:S(2)}) collective-permute-start(bf16[1024,256]{1,0:T(8,128)(2,1)S(1)} %get-tuple-element.41), channel_id=1, source_target_pairs={{0,3},{1,0},{2,1},{3,2},{4,7},{5,4},{6,5},{7,6},{8,11},{9,8},{10,9... | collective-permute-start | bytes 1572872 | tf_op jit(solution)/shard_map/ppermute | solution.py:28
  7.5 21.6 %collective-permute-start.2 = (bf16[1024,256]{1,0:T(8,128)(2,1)S(1)}, bf16[1024,256]{1,0:T(8,128)(2,1)S(1)}, u32[]{:S(2)}, u32[]{:S(2)}) collective-permute-start(bf16[1024,256]{1,0:T(8,128)(2,1)S(1)} %get-tuple-element.42), channel_id=1, source_target_pairs={{0,2},{1,3},{2,0},{3,1},{4,6},{5,7},{6,4},{7,5},{8,10},{9,11},{10,... | collective-permute-start | bytes 1572872 | tf_op jit(solution)/shard_map/ppermute | solution.py:28
  9.1 5.4 %collective-permute-start.10 = (bf16[272,256]{1,0:T(8,128)(2,1)S(1)}, bf16[272,256]{1,0:T(8,128)(2,1)S(1)}, u32[]{:S(2)}, u32[]{:S(2)}) collective-permute-start(bf16[272,256]{1,0:T(8,128)(2,1)S(1)} %get-tuple-element.52), channel_id=1, source_target_pairs={{0,128},{64,192},{128,0},{192,64},{1,129},{65,193},{129,1},{193,65... | collective-permute-start | bytes 417800 | tf_op jit(solution)/shard_map/ppermute | solution.py:28
  11.6 5.3 %collective-permute-start.11 = (bf16[272,256]{1,0:T(8,128)(2,1)S(1)}, bf16[272,256]{1,0:T(8,128)(2,1)S(1)}, u32[]{:S(2)}, u32[]{:S(2)}) collective-permute-start(bf16[272,256]{1,0:T(8,128)(2,1)S(1)} %get-tuple-element.53), channel_id=1, source_target_pairs={{0,192},{64,0},{128,64},{192,128},{1,193},{65,1},{129,65},{193,129... | collective-permute-start | bytes 417800 | tf_op jit(solution)/shard_map/ppermute | solution.py:28
  19.5 4.4 %collective-permute-start.12 = (bf16[256,256]{1,0:T(8,128)(2,1)S(1)}, bf16[256,256]{1,0:T(8,128)(2,1)S(1)}, u32[]{:S(2)}, u32[]{:S(2)}) collective-permute-start(bf16[256,256]{1,0:T(8,128)(2,1)S(1)} %shard_map.85.refs_0_), channel_id=1, source_target_pairs={{0,4},{4,0},{8,12},{12,8},{16,20},{20,16},{24,28},{28,24},{1,5},{5... | collective-permute-start | bytes 393224 | tf_op jit(solution)/shard_map/ppermute | solution.py:381
  21.2 12.7 %collective-permute-start.6 = (bf16[256,256]{1,0:T(8,128)(2,1)S(1)}, bf16[256,256]{1,0:T(8,128)(2,1)S(1)}, u32[]{:S(2)}, u32[]{:S(2)}) collective-permute-start(bf16[256,256]{1,0:T(8,128)(2,1)S(1)} %get-tuple-element.47.refs_5_), channel_id=1, source_target_pairs={{0,1},{1,2},{2,3},{3,0},{4,5},{5,6},{6,7},{7,4},{8,9},{9,10},{10,1... | collective-permute-start | bytes 393224 | tf_op jit(solution)/shard_map/ppermute | solution.py:28
  23.9 10.0 %collective-permute-start.7 = (bf16[256,256]{1,0:T(8,128)(2,1)S(1)}, bf16[256,256]{1,0:T(8,128)(2,1)S(1)}, u32[]{:S(2)}, u32[]{:S(2)}) collective-permute-start(bf16[256,256]{1,0:T(8,128)(2,1)S(1)} %get-tuple-element.48), channel_id=1, source_target_pairs={{0,3},{1,0},{2,1},{3,2},{4,7},{5,4},{6,5},{7,6},{8,11},{9,8},{10,9... | collective-permute-start | bytes 393224 | tf_op jit(solution)/shard_map/ppermute | solution.py:28
  24.7 10.0 %collective-permute-start.8 = (bf16[256,256]{1,0:T(8,128)(2,1)S(1)}, bf16[256,256]{1,0:T(8,128)(2,1)S(1)}, u32[]{:S(2)}, u32[]{:S(2)}) collective-permute-start(bf16[256,256]{1,0:T(8,128)(2,1)S(1)} %get-tuple-element.49), channel_id=1, source_target_pairs={{0,2},{1,3},{2,0},{3,1},{4,6},{5,7},{6,4},{7,5},{8,10},{9,11},{10,... | collective-permute-start | bytes 393224 | tf_op jit(solution)/shard_map/ppermute | solution.py:28
  34.7 11.1 %collective-permute-start.13 = (bf16[384,256]{1,0:T(8,128)(2,1)S(1)}, bf16[384,256]{1,0:T(8,128)(2,1)S(1)}, u32[]{:S(2)}, u32[]{:S(2)}) collective-permute-start(bf16[384,256]{1,0:T(8,128)(2,1)S(1)} %get-tuple-element.55.refs_5_), channel_id=1, source_target_pairs={{0,64},{64,128},{128,192},{192,0},{1,65},{65,129},{129,193},{193,1... | collective-permute-start | bytes 589832 | tf_op jit(solution)/shard_map/ppermute | solution.py:28
  36.1 11.7 %collective-permute-start.14 = (bf16[384,256]{1,0:T(8,128)(2,1)S(1)}, bf16[384,256]{1,0:T(8,128)(2,1)S(1)}, u32[]{:S(2)}, u32[]{:S(2)}) collective-permute-start(bf16[384,256]{1,0:T(8,128)(2,1)S(1)} %get-tuple-element.56.refs_6_), channel_id=1, source_target_pairs={{0,192},{64,0},{128,64},{192,128},{1,193},{65,1},{129,65},{193,129... | collective-permute-start | bytes 589832 | tf_op jit(solution)/shard_map/ppermute | solution.py:28
  37.4 11.6 %collective-permute-start.15 = (bf16[512,256]{1,0:T(8,128)(2,1)S(1)}, bf16[512,256]{1,0:T(8,128)(2,1)S(1)}, u32[]{:S(2)}, u32[]{:S(2)}) collective-permute-start(bf16[512,256]{1,0:T(8,128)(2,1)S(1)} %get-tuple-element.54.refs_3_), channel_id=1, source_target_pairs={{0,4},{4,8},{8,12},{12,16},{16,20},{20,24},{24,28},{28,0},{1,5},{5... | collective-permute-start | bytes 786440 | tf_op jit(solution)/shard_map/ppermute | solution.py:28
  39.2 9.8 %collective-permute-start.16 = (bf16[512,256]{1,0:T(8,128)(2,1)S(1)}, bf16[512,256]{1,0:T(8,128)(2,1)S(1)}, u32[]{:S(2)}, u32[]{:S(2)}) collective-permute-start(bf16[512,256]{1,0:T(8,128)(2,1)S(1)} %get-tuple-element.57), channel_id=1, source_target_pairs={{0,28},{4,0},{8,4},{12,8},{16,12},{20,16},{24,20},{28,24},{1,29},{... | collective-permute-start | bytes 786440 | tf_op jit(solution)/shard_map/ppermute | solution.py:28
  43.1 9.9 %collective-permute-start.3 = (bf16[512,256]{1,0:T(8,128)(2,1)S(1)}, bf16[512,256]{1,0:T(8,128)(2,1)S(1)}, u32[]{:S(2)}, u32[]{:S(2)}) collective-permute-start(bf16[512,256]{1,0:T(8,128)(2,1)S(1)} %get-tuple-element.43), channel_id=1, source_target_pairs={{0,1},{1,2},{2,3},{3,0},{4,5},{5,6},{6,7},{7,4},{8,9},{9,10},{10,1... | collective-permute-start | bytes 786440 | tf_op jit(solution)/shard_map/ppermute | solution.py:28
  45.7 8.2 %collective-permute-start.4 = (bf16[512,256]{1,0:T(8,128)(2,1)S(1)}, bf16[512,256]{1,0:T(8,128)(2,1)S(1)}, u32[]{:S(2)}, u32[]{:S(2)}) collective-permute-start(bf16[512,256]{1,0:T(8,128)(2,1)S(1)} %get-tuple-element.44), channel_id=1, source_target_pairs={{0,3},{1,0},{2,1},{3,2},{4,7},{5,4},{6,5},{7,6},{8,11},{9,8},{10,9... | collective-permute-start | bytes 786440 | tf_op jit(solution)/shard_map/ppermute | solution.py:28
  47.7 11.8 %collective-permute-start.5 = (bf16[512,256]{1,0:T(8,128)(2,1)S(1)}, bf16[512,256]{1,0:T(8,128)(2,1)S(1)}, u32[]{:S(2)}, u32[]{:S(2)}) collective-permute-start(bf16[512,256]{1,0:T(8,128)(2,1)S(1)} %get-tuple-element.45), channel_id=1, source_target_pairs={{0,2},{1,3},{2,0},{3,1},{4,6},{5,7},{6,4},{7,5},{8,10},{9,11},{10,... | collective-permute-start | bytes 786440 | tf_op jit(solution)/shard_map/ppermute | solution.py:28
  59.6 16.9 %collective-permute-start.18 = (bf16[768,256]{1,0:T(8,128)(2,1)S(1)}, bf16[768,256]{1,0:T(8,128)(2,1)S(1)}, u32[]{:S(2)}, u32[]{:S(2)}) collective-permute-start(bf16[768,256]{1,0:T(8,128)(2,1)S(1)} %get-tuple-element.61.refs_5_), channel_id=1, source_target_pairs={{0,64},{64,0},{128,192},{192,128},{1,65},{65,1},{129,193},{193,129... | collective-permute-start | bytes 1179656 | tf_op jit(solution)/shard_map/ppermute | solution.py:175
  59.7 16.8 %collective-permute-start.19 = (bf16[512,256]{1,0:T(8,128)(2,1)S(1)}, bf16[512,256]{1,0:T(8,128)(2,1)S(1)}, u32[]{:S(2)}, u32[]{:S(2)}) collective-permute-start(bf16[512,256]{1,0:T(8,128)(2,1)S(1)} %get-tuple-element.58.refs_3_.refs_6_), channel_id=1, source_target_pairs={{0,4},{4,8},{8,12},{12,16},{16,20},{20,24},{24,28},{28,0},{1,5},{5... | collective-permute-start | bytes 786440 | tf_op jit(solution)/shard_map/ppermute | solution.py:28
  59.7 16.7 %collective-permute-start.20 = (bf16[512,256]{1,0:T(8,128)(2,1)S(1)}, bf16[512,256]{1,0:T(8,128)(2,1)S(1)}, u32[]{:S(2)}, u32[]{:S(2)}) collective-permute-start(bf16[512,256]{1,0:T(8,128)(2,1)S(1)} %get-tuple-element.62), channel_id=1, source_target_pairs={{0,28},{4,0},{8,4},{12,8},{16,12},{20,16},{24,20},{28,24},{1,29},{... | collective-permute-start | bytes 786440 | tf_op jit(solution)/shard_map/ppermute | solution.py:28
  63.1 6.7 %collective-permute-start.23 = (bf16[256,256]{1,0:T(8,128)(2,1)S(1)}, bf16[256,256]{1,0:T(8,128)(2,1)S(1)}, u32[]{:S(2)}, u32[]{:S(2)}) collective-permute-start(bf16[256,256]{1,0:T(8,128)(2,1)S(1)} %shard_map.86.refs_5_.refs_0_), channel_id=1, source_target_pairs={{0,8},{4,12},{8,0},{12,4},{16,24},{20,28},{24,16},{28,20},{1,9},{5... | collective-permute-start | bytes 393224 | tf_op jit(solution)/shard_map/ppermute | solution.py:381
  69.8 10.8 %collective-permute-start.24 = (bf16[256,256]{1,0:T(8,128)(2,1)S(1)}, bf16[256,256]{1,0:T(8,128)(2,1)S(1)}, u32[]{:S(2)}, u32[]{:S(2)}) collective-permute-start(bf16[256,256]{1,0:T(8,128)(2,1)S(1)} %shard_map.93.refs_0_), channel_id=1, source_target_pairs={{0,24},{4,28},{8,16},{12,20},{16,8},{20,12},{24,0},{28,4},{1,25},{... | collective-permute-start | bytes 393224 | tf_op jit(solution)/shard_map/ppermute | solution.py:381
  72.9 18.1 %collective-permute-start.17 = (bf16[768,256]{1,0:T(8,128)(2,1)S(1)}, bf16[768,256]{1,0:T(8,128)(2,1)S(1)}, u32[]{:S(2)}, u32[]{:S(2)}) collective-permute-start(bf16[768,256]{1,0:T(8,128)(2,1)S(1)} %get-tuple-element.59.refs_5_), channel_id=1, source_target_pairs={{0,192},{192,0},{64,128},{128,64},{1,193},{193,1},{65,129},{129,65... | collective-permute-start | bytes 1179656 | tf_op jit(solution)/shard_map/ppermute | solution.py:175
  77.2 13.8 %collective-permute-start.22 = (bf16[512,256]{1,0:T(8,128)(2,1)S(1)}, bf16[512,256]{1,0:T(8,128)(2,1)S(1)}, u32[]{:S(2)}, u32[]{:S(2)}) collective-permute-start(bf16[512,256]{1,0:T(8,128)(2,1)S(1)} %get-tuple-element.64.refs_10_), channel_id=1, source_target_pairs={{0,4},{4,8},{8,12},{12,16},{16,20},{20,24},{24,28},{28,0},{1,5},{5... | collective-permute-start | bytes 786440 | tf_op jit(solution)/shard_map/ppermute | solution.py:28
  80.6 6.1 %collective-permute-start.25 = (bf16[256,256]{1,0:T(8,128)(2,1)S(1)}, bf16[256,256]{1,0:T(8,128)(2,1)S(1)}, u32[]{:S(2)}, u32[]{:S(2)}) collective-permute-start(bf16[256,256]{1,0:T(8,128)(2,1)S(1)} %shard_map.94.refs_4_), channel_id=1, source_target_pairs={{0,1},{1,2},{2,3},{3,0},{4,5},{5,6},{6,7},{7,4},{8,9},{9,10},{10,1... | collective-permute-start | bytes 393224 | tf_op jit(solution)/shard_map/ppermute | solution.py:28
  80.7 6.5 %collective-permute-start.26 = (bf16[256,256]{1,0:T(8,128)(2,1)S(1)}, bf16[256,256]{1,0:T(8,128)(2,1)S(1)}, u32[]{:S(2)}, u32[]{:S(2)}) collective-permute-start(bf16[256,256]{1,0:T(8,128)(2,1)S(1)} %shard_map.94.refs_4_), channel_id=1, source_target_pairs={{0,3},{1,0},{2,1},{3,2},{4,7},{5,4},{6,5},{7,6},{8,11},{9,8},{10,9... | collective-permute-start | bytes 393224 | tf_op jit(solution)/shard_map/ppermute | solution.py:28
  84.2 5.4 %collective-permute-start.27 = (bf16[256,256]{1,0:T(8,128)(2,1)S(1)}, bf16[256,256]{1,0:T(8,128)(2,1)S(1)}, u32[]{:S(2)}, u32[]{:S(2)}) collective-permute-start(bf16[256,256]{1,0:T(8,128)(2,1)S(1)} %shard_map.94.refs_4_), channel_id=1, source_target_pairs={{0,2},{1,3},{2,0},{3,1},{4,6},{5,7},{6,4},{7,5},{8,10},{9,11},{10,... | collective-permute-start | bytes 393224 | tf_op jit(solution)/shard_map/ppermute | solution.py:28
  86.8 7.5 %collective-permute-start.21 = (bf16[512,256]{1,0:T(8,128)(2,1)S(1)}, bf16[512,256]{1,0:T(8,128)(2,1)S(1)}, u32[]{:S(2)}, u32[]{:S(2)}) collective-permute-start(bf16[512,256]{1,0:T(8,128)(2,1)S(1)} %get-tuple-element.63), channel_id=1, source_target_pairs={{0,28},{4,0},{8,4},{12,8},{16,12},{20,16},{24,20},{28,24},{1,29},{... | collective-permute-start | bytes 786440 | tf_op jit(solution)/shard_map/ppermute | solution.py:28
  91.5 8.2 %collective-permute-start.28 = (bf16[512,256]{1,0:T(8,128)(2,1)S(1)}, bf16[512,256]{1,0:T(8,128)(2,1)S(1)}, u32[]{:S(2)}, u32[]{:S(2)}) collective-permute-start(bf16[512,256]{1,0:T(8,128)(2,1)S(1)} %shard_map.96.refs_8_), channel_id=1, source_target_pairs={{0,4},{4,8},{8,12},{12,16},{16,20},{20,24},{24,28},{28,0},{1,5},{5... | collective-permute-start | bytes 786440 | tf_op jit(solution)/shard_map/ppermute | solution.py:28
  93.0 5.4 %collective-permute-start.30 = (bf16[256,256]{1,0:T(8,128)(2,1)S(1)}, bf16[256,256]{1,0:T(8,128)(2,1)S(1)}, u32[]{:S(2)}, u32[]{:S(2)}) collective-permute-start(bf16[256,256]{1,0:T(8,128)(2,1)S(1)} %get-tuple-element.67), channel_id=1, source_target_pairs={{0,128},{64,192},{128,0},{192,64},{1,129},{65,193},{129,1},{193,65... | collective-permute-start | bytes 393224 | tf_op jit(solution)/shard_map/ppermute | solution.py:28
  93.5 6.2 %collective-permute-start.31 = (bf16[256,256]{1,0:T(8,128)(2,1)S(1)}, bf16[256,256]{1,0:T(8,128)(2,1)S(1)}, u32[]{:S(2)}, u32[]{:S(2)}) collective-permute-start(bf16[256,256]{1,0:T(8,128)(2,1)S(1)} %get-tuple-element.68), channel_id=1, source_target_pairs={{0,64},{64,128},{128,192},{192,0},{1,65},{65,129},{129,193},{193,1... | collective-permute-start | bytes 393224 | tf_op jit(solution)/shard_map/ppermute | solution.py:28
  100.3 10.5 %collective-permute-start.32 = (bf16[512,256]{1,0:T(8,128)(2,1)S(1)}, bf16[512,256]{1,0:T(8,128)(2,1)S(1)}, u32[]{:S(2)}, u32[]{:S(2)}) collective-permute-start(bf16[512,256]{1,0:T(8,128)(2,1)S(1)} %get-tuple-element.69), channel_id=1, source_target_pairs={{0,32},{1,33},{2,34},{3,35},{4,36},{5,37},{6,38},{7,39},{8,40},{9,... | collective-permute-start | bytes 786440 | tf_op jit(solution)/shard_map/ppermute | solution.py:529
  (8 other events, 162.5 us)

commit v8 on v7

--- a/solution.py
+++ b/solution.py
@@ -167,6 +167,13 @@
     )
 
 
+def spread_over_pools(values, sign):
+    moved = {0: values[0]}
+    for k in HOPS:
+        moved[k] = shift(values[k], "pool", sign * k)
+    return [moved[k] for k in range(NX)]
+
+
 def swapped(value, second_pairing):
     if second_pairing:
         pairs = [(0, 3), (3, 0), (1, 2), (2, 1)]
@@ -493,7 +500,7 @@
     (first,), (own0,) = pack(((0,),), weight, features)
     got = [shift(value, Y, hop) for value, hop in zip(first, HOPS)]
     sent = dispatch(ids, features, (first[0],))
-    items = [sent[0]] + [shift(sent[k], "pool", k) for k in (1, 2, 3)]
+    items = spread_over_pools(sent, 1)
     (second, third), (own1, own2, own3) = pack(((1,), (2, 3)), weight, None, (sent[0],))
     got1 = [shift(value, Y, hop) for value, hop in zip(second, HOPS)]
     low = down(items, down_factor, (second[0],))
@@ -515,7 +522,7 @@
     plus, minus = project((0, 1), own2, features, got, (mine2,), (other2,), carried, (blocks,))
     carried = (shift(plus, Z, 1), shift(minus, Z, -1))
     served = up(items, lows, up_factor, blocks, (plus,))
-    returned = [served[0]] + [shift(served[k], "pool", -k) for k in (1, 2, 3)]
+    returned = spread_over_pools(served, -1)
     (plus,) = project(
         (0,), own3, features, got, (mine3,), (other3,), carried[:1], (served[1],)
     )

time: 112 us -> 112 us (level)
  no operation moved by 1% of the time
where the time goes in v8:
time: 112 us
  starting transfers between devices  49.3 us (44%)
  waiting for transfers between devices  47.1 us (42%)
  Pallas kernels  14.1 us (13%)
    ppermute x27, starting transfers between devices, shift(): lax.ppermute(value, axis, [(i, (i + steps) % count) for i in range(count)])  41.7 us
    ppermute x27, waiting for transfers between devices, shift(): lax.ppermute(value, axis, [(i, (i + steps) % count) for i in range(count)])  28.9 us
    pallas_call x17, Pallas kernels, call(): pl.pallas_call(body, out_shape=outs, in_specs=list(in_specs) + [ANY] * m,...  14.1 us
    ppermute x1, waiting for transfers between devices, steps(): carried = lax.ppermute(first_out, 'section', [(0, 1)])  9.23 us
    ppermute x3, waiting for transfers between devices, exchanged_sum(): other = lax.ppermute(value, axis, list(enumerate(partner)))  8.94 us
    ppermute x3, starting transfers between devices, exchanged_sum(): other = lax.ppermute(value, axis, list(enumerate(partner)))  4.86 us
  transfers between devices with their start and end apart: 33, of which 16 were waited for; matrix products, arithmetic and copies ran while one was open for 0% of the time, Pallas kernels for 11%

profile of v8, /device:TPU:1, one launch (start us, length us, event | category | flops | bytes accessed | tf_op | source)
XLA Modules:
  0.0 111.6 jit_solution(7149596105656707211)
XLA Ops:
  0.0 1.7 %shard_map.82 = (bf16[1024,256]{1,0:T(8,128)(2,1)S(1)}, bf16[1024,256]{1,0:T(8,128)(2,1)S(1)}, bf16[1024,256]{1,0:T(8,128)(2,1)S(1)}, bf16[512,256]{1,0:T(8,128)(2,1)S(1)}) custom-call(bf16[256,8192]{1,0:T(8,128)(2,1)} %bitcast.22, bf16[512,256]{1,0:T(8,128)(2,1)} %bitcast.9), custom_call_target="tpu_custom_call" | custom-call | bytes 1310720 | tf_op jit(solution)/shard_map/pallas_call | solution.py:67
  1.7 2.2 %collective-permute-start = (bf16[1024,256]{1,0:T(8,128)(2,1)S(1)}, bf16[1024,256]{1,0:T(8,128)(2,1)S(1)}, u32[]{:S(2)}, u32[]{:S(2)}) collective-permute-start(bf16[1024,256]{1,0:T(8,128)(2,1)S(1)} %get-tuple-element.38.refs_2_), channel_id=1, source_target_pairs={{0,1},{1,2},{2,3},{3,0},{4,5},{5,6},{6,7},{7,4},{8,9},{9,10},{10,1... | collective-permute-start | bytes 1572872 | tf_op jit(solution)/shard_map/ppermute | solution.py:28
  6.1 1.5 %collective-permute-start.1 = (bf16[1024,256]{1,0:T(8,128)(2,1)S(1)}, bf16[1024,256]{1,0:T(8,128)(2,1)S(1)}, u32[]{:S(2)}, u32[]{:S(2)}) collective-permute-start(bf16[1024,256]{1,0:T(8,128)(2,1)S(1)} %get-tuple-element.41), channel_id=1, source_target_pairs={{0,3},{1,0},{2,1},{3,2},{4,7},{5,4},{6,5},{7,6},{8,11},{9,8},{10,9... | collective-permute-start | bytes 1572872 | tf_op jit(solution)/shard_map/ppermute | solution.py:28
  7.5 1.6 %collective-permute-start.2 = (bf16[1024,256]{1,0:T(8,128)(2,1)S(1)}, bf16[1024,256]{1,0:T(8,128)(2,1)S(1)}, u32[]{:S(2)}, u32[]{:S(2)}) collective-permute-start(bf16[1024,256]{1,0:T(8,128)(2,1)S(1)} %get-tuple-element.42), channel_id=1, source_target_pairs={{0,2},{1,3},{2,0},{3,1},{4,6},{5,7},{6,4},{7,5},{8,10},{9,11},{10,... | collective-permute-start | bytes 1572872 | tf_op jit(solution)/shard_map/ppermute | solution.py:28
  9.1 2.4 %collective-permute-start.10 = (bf16[272,256]{1,0:T(8,128)(2,1)S(1)}, bf16[272,256]{1,0:T(8,128)(2,1)S(1)}, u32[]{:S(2)}, u32[]{:S(2)}) collective-permute-start(bf16[272,256]{1,0:T(8,128)(2,1)S(1)} %get-tuple-element.52), channel_id=1, source_target_pairs={{0,128},{64,192},{128,0},{192,64},{1,129},{65,193},{129,1},{193,65... | collective-permute-start | bytes 417800 | tf_op jit(solution)/shard_map/ppermute | solution.py:28
  12.8 1.7 %shard_map.84 = (bf16[256,256]{1,0:T(8,128)(2,1)S(1)}, bf16[256,256]{1,0:T(8,128)(2,1)S(1)}, bf16[256,256]{1,0:T(8,128)(2,1)S(1)}, bf16[512,256]{1,0:T(8,128)(2,...) custom-call(bf16[256,8192]{1,0:T(8,128)(2,1)} %bitcast.23, ...), custom_call_target="tpu_custom_call" | custom-call | bytes 3932160 | tf_op jit(solution)/shard_map/pallas_call | solution.py:67
  14.6 2.4 %collective-permute-done.11.refs_3_ = bf16[272,256]{1,0:T(8,128)(2,1)S(1)} collective-permute-done((bf16[272,256]{1,0:T(8,128)(2,1)S(1)}, bf16[272,256]{1,0:T(8,128)(2,1)S(1)}, u32[]{:S(2)}, u32[]{:S(2)}) %collective-permute-start.11) | collective-permute-done | bytes 139296 | tf_op jit(solution)/shard_map/ppermute | solution.py:28
  16.9 2.6 %shard_map.85.refs_0_ = bf16[256,256]{1,0:T(8,128)(2,1)S(1)} custom-call(bf16[272,256]{1,0:T(8,128)(2,1)S(1)} %get-tuple-element.39.refs_1_.refs_0_, bf16[272,256]{1,0:T(8,128)(2,1)S(1)} %collective-permute-done.9.refs_1_, bf16[272,256]{1,0:T(8,128)(2,1)S(1)} %collective-permute-done.10.refs_2_, bf16[272,256]{1,0:T(8,128)(2,1)S(1)} %collective-permute-done.11.refs_3_, ...), custom_call_target="tpu_custom_call" | custom-call | flops 1073741824 | bytes 2097152 | tf_op jit(solution)/shard_map/pallas_call | solution.py:67
  19.5 1.7 %collective-permute-start.12 = (bf16[256,256]{1,0:T(8,128)(2,1)S(1)}, bf16[256,256]{1,0:T(8,128)(2,1)S(1)}, u32[]{:S(2)}, u32[]{:S(2)}) collective-permute-start(bf16[256,256]{1,0:T(8,128)(2,1)S(1)} %shard_map.85.refs_0_), channel_id=1, source_target_pairs={{0,4},{4,0},{8,12},{12,8},{16,20},{20,16},{24,28},{28,24},{1,5},{5... | collective-permute-start | bytes 393224 | tf_op jit(solution)/shard_map/ppermute | solution.py:388
  21.6 2.3 %collective-permute-done.12.refs_1_ = bf16[256,256]{1,0:T(8,128)(2,1)S(1)} collective-permute-done((bf16[256,256]{1,0:T(8,128)(2,1)S(1)}, bf16[256,256]{1,0:T(8,128)(2,1)S(1)}, u32[]{:S(2)}, u32[]{:S(2)}) %collective-permute-start.12) | collective-permute-done | bytes 131104 | tf_op jit(solution)/shard_map/ppermute | solution.py:388
  24.7 1.4 %collective-permute-start.8 = (bf16[256,256]{1,0:T(8,128)(2,1)S(1)}, bf16[256,256]{1,0:T(8,128)(2,1)S(1)}, u32[]{:S(2)}, u32[]{:S(2)}) collective-permute-start(bf16[256,256]{1,0:T(8,128)(2,1)S(1)} %get-tuple-element.49), channel_id=1, source_target_pairs={{0,2},{1,3},{2,0},{3,1},{4,6},{5,7},{6,4},{7,5},{8,10},{9,11},{10,... | collective-permute-start | bytes 393224 | tf_op jit(solution)/shard_map/ppermute | solution.py:28
  26.1 3.0 %collective-permute-done.2.refs_4_ = bf16[1024,256]{1,0:T(8,128)(2,1)S(1)} collective-permute-done((bf16[1024,256]{1,0:T(8,128)(2,1)S(1)}, bf16[1024,256]{1,0:T(8,128)(2,1)S(1)}, u32[]{:S(2)}, u32[]{:S(2)}) %collective-permute-start.2) | collective-permute-done | bytes 524320 | tf_op jit(solution)/shard_map/ppermute | solution.py:28
  29.8 4.1 %collective-permute-done.6.refs_0_ = bf16[256,256]{1,0:T(8,128)(2,1)S(1)} collective-permute-done((bf16[256,256]{1,0:T(8,128)(2,1)S(1)}, bf16[256,256]{1,0:T(8,128)(2,1)S(1)}, u32[]{:S(2)}, u32[]{:S(2)}) %collective-permute-start.6) | collective-permute-done | bytes 131104 | tf_op jit(solution)/shard_map/ppermute | solution.py:28
  34.7 1.4 %collective-permute-start.13 = (bf16[384,256]{1,0:T(8,128)(2,1)S(1)}, bf16[384,256]{1,0:T(8,128)(2,1)S(1)}, u32[]{:S(2)}, u32[]{:S(2)}) collective-permute-start(bf16[384,256]{1,0:T(8,128)(2,1)S(1)} %get-tuple-element.55.refs_5_), channel_id=1, source_target_pairs={{0,64},{64,128},{128,192},{192,0},{1,65},{65,129},{129,193},{193,1... | collective-permute-start | bytes 589832 | tf_op jit(solution)/shard_map/ppermute | solution.py:28
  37.4 1.7 %collective-permute-start.15 = (bf16[512,256]{1,0:T(8,128)(2,1)S(1)}, bf16[512,256]{1,0:T(8,128)(2,1)S(1)}, u32[]{:S(2)}, u32[]{:S(2)}) collective-permute-start(bf16[512,256]{1,0:T(8,128)(2,1)S(1)} %get-tuple-element.54.refs_3_), channel_id=1, source_target_pairs={{0,4},{4,8},{8,12},{12,16},{16,20},{20,24},{24,28},{28,0},{1,5},{5... | collective-permute-start | bytes 786440 | tf_op jit(solution)/shard_map/ppermute | solution.py:28
  39.2 3.9 %collective-permute-start.16 = (bf16[512,256]{1,0:T(8,128)(2,1)S(1)}, bf16[512,256]{1,0:T(8,128)(2,1)S(1)}, u32[]{:S(2)}, u32[]{:S(2)}) collective-permute-start(bf16[512,256]{1,0:T(8,128)(2,1)S(1)} %get-tuple-element.57), channel_id=1, source_target_pairs={{0,28},{4,0},{8,4},{12,8},{16,12},{20,16},{24,20},{28,24},{1,29},{... | collective-permute-start | bytes 786440 | tf_op jit(solution)/shard_map/ppermute | solution.py:28
  43.1 2.6 %collective-permute-start.3 = (bf16[512,256]{1,0:T(8,128)(2,1)S(1)}, bf16[512,256]{1,0:T(8,128)(2,1)S(1)}, u32[]{:S(2)}, u32[]{:S(2)}) collective-permute-start(bf16[512,256]{1,0:T(8,128)(2,1)S(1)} %get-tuple-element.43), channel_id=1, source_target_pairs={{0,1},{1,2},{2,3},{3,0},{4,5},{5,6},{6,7},{7,4},{8,9},{9,10},{10,1... | collective-permute-start | bytes 786440 | tf_op jit(solution)/shard_map/ppermute | solution.py:28
  45.7 2.0 %collective-permute-start.4 = (bf16[512,256]{1,0:T(8,128)(2,1)S(1)}, bf16[512,256]{1,0:T(8,128)(2,1)S(1)}, u32[]{:S(2)}, u32[]{:S(2)}) collective-permute-start(bf16[512,256]{1,0:T(8,128)(2,1)S(1)} %get-tuple-element.44), channel_id=1, source_target_pairs={{0,3},{1,0},{2,1},{3,2},{4,7},{5,4},{6,5},{7,6},{8,11},{9,8},{10,9... | collective-permute-start | bytes 786440 | tf_op jit(solution)/shard_map/ppermute | solution.py:28
  49.7 3.3 %collective-permute-done.3.refs_0_ = bf16[512,256]{1,0:T(8,128)(2,1)S(1)} collective-permute-done((bf16[512,256]{1,0:T(8,128)(2,1)S(1)}, bf16[512,256]{1,0:T(8,128)(2,1)S(1)}, u32[]{:S(2)}, u32[]{:S(2)}) %collective-permute-start.3) | collective-permute-done | bytes 262176 | tf_op jit(solution)/shard_map/ppermute | solution.py:28
  53.9 5.6 %collective-permute-done.5.refs_2_ = bf16[512,256]{1,0:T(8,128)(2,1)S(1)} collective-permute-done((bf16[512,256]{1,0:T(8,128)(2,1)S(1)}, bf16[512,256]{1,0:T(8,128)(2,1)S(1)}, u32[]{:S(2)}, u32[]{:S(2)}) %collective-permute-start.5) | collective-permute-done | bytes 262176 | tf_op jit(solution)/shard_map/ppermute | solution.py:28
  59.7 3.3 %collective-permute-start.20 = (bf16[512,256]{1,0:T(8,128)(2,1)S(1)}, bf16[512,256]{1,0:T(8,128)(2,1)S(1)}, u32[]{:S(2)}, u32[]{:S(2)}) collective-permute-start(bf16[512,256]{1,0:T(8,128)(2,1)S(1)} %get-tuple-element.62), channel_id=1, source_target_pairs={{0,28},{4,0},{8,4},{12,8},{16,12},{20,16},{24,20},{28,24},{1,29},{... | collective-permute-start | bytes 786440 | tf_op jit(solution)/shard_map/ppermute | solution.py:28
  63.1 6.7 %collective-permute-done.23.refs_1_ = bf16[256,256]{1,0:T(8,128)(2,1)S(1)} collective-permute-done((bf16[256,256]{1,0:T(8,128)(2,1)S(1)}, bf16[256,256]{1,0:T(8,128)(2,1)S(1)}, u32[]{:S(2)}, u32[]{:S(2)}) %collective-permute-start.23) | collective-permute-done | bytes 131104 | tf_op jit(solution)/shard_map/ppermute | solution.py:388
  69.8 3.1 %collective-permute-start.24 = (bf16[256,256]{1,0:T(8,128)(2,1)S(1)}, bf16[256,256]{1,0:T(8,128)(2,1)S(1)}, u32[]{:S(2)}, u32[]{:S(2)}) collective-permute-start(bf16[256,256]{1,0:T(8,128)(2,1)S(1)} %shard_map.93.refs_0_), channel_id=1, source_target_pairs={{0,24},{4,28},{8,16},{12,20},{16,8},{20,12},{24,0},{28,4},{1,25},{... | collective-permute-start | bytes 393224 | tf_op jit(solution)/shard_map/ppermute | solution.py:388
  74.3 2.1 %shard_map.91.refs_9_ = f32[4,256,256]{2,1,0:T(8,128)S(1)} custom-call(bf16[272,256]{1,0:T(8,128)(2,1)S(1)} %get-tuple-element.39.refs_1_.refs_0_, bf16[272,256]{1,0:T(8,128)(2,1)S(1)} %collective-permute-done.9.refs_1_, bf16[272,256]{1,0:T(8,128)(2,1)S(1)} %collective-permute-done.10.refs_2_, bf16[272,256]{1,0:T(8,128)(2,1)S(1)} %collective-permute-done.11.refs_3_, ...), custom_call_target="tpu_custom_call" | custom-call | flops 1073741824 | bytes 3145728 | tf_op jit(solution)/shard_map/pallas_call | solution.py:67
  77.2 3.4 %collective-permute-start.22 = (bf16[512,256]{1,0:T(8,128)(2,1)S(1)}, bf16[512,256]{1,0:T(8,128)(2,1)S(1)}, u32[]{:S(2)}, u32[]{:S(2)}) collective-permute-start(bf16[512,256]{1,0:T(8,128)(2,1)S(1)} %get-tuple-element.64.refs_10_), channel_id=1, source_target_pairs={{0,4},{4,8},{8,12},{12,16},{16,20},{20,24},{24,28},{28,0},{1,5},{5... | collective-permute-start | bytes 786440 | tf_op jit(solution)/shard_map/ppermute | solution.py:28
  80.7 3.5 %collective-permute-start.26 = (bf16[256,256]{1,0:T(8,128)(2,1)S(1)}, bf16[256,256]{1,0:T(8,128)(2,1)S(1)}, u32[]{:S(2)}, u32[]{:S(2)}) collective-permute-start(bf16[256,256]{1,0:T(8,128)(2,1)S(1)} %shard_map.94.refs_4_), channel_id=1, source_target_pairs={{0,3},{1,0},{2,1},{3,2},{4,7},{5,4},{6,5},{7,6},{8,11},{9,8},{10,9... | collective-permute-start | bytes 393224 | tf_op jit(solution)/shard_map/ppermute | solution.py:28
  85.3 1.5 %collective-permute-done.25.refs_5_ = bf16[256,256]{1,0:T(8,128)(2,1)S(1)} collective-permute-done((bf16[256,256]{1,0:T(8,128)(2,1)S(1)}, bf16[256,256]{1,0:T(8,128)(2,1)S(1)}, u32[]{:S(2)}, u32[]{:S(2)}) %collective-permute-start.25) | collective-permute-done | bytes 131104 | tf_op jit(solution)/shard_map/ppermute | solution.py:28
  87.2 2.4 %collective-permute-done.27.refs_7_ = bf16[256,256]{1,0:T(8,128)(2,1)S(1)} collective-permute-done((bf16[256,256]{1,0:T(8,128)(2,1)S(1)}, bf16[256,256]{1,0:T(8,128)(2,1)S(1)}, u32[]{:S(2)}, u32[]{:S(2)}) %collective-permute-start.27) | collective-permute-done | bytes 131104 | tf_op jit(solution)/shard_map/ppermute | solution.py:28
  89.6 1.4 %shard_map.95 = (bf16[256,256]{1,0:T(8,128)(2,1)S(1)}, bf16[256,256]{1,0:T(8,128)(2,1)S(1)}, bf16[256,256]{1,0:T(8,128)(2,1)S(1)}, bf16[256,256]{1,0:T(8,128)(2,1)S(1)}) custom-call(bf16[272,256]{1,0:T(8,128)(2,1)S(1)} %get-tuple-element.39.refs_1_.refs_0_, bf16[272,256]{1,0:T(8,128)(2,1)S(1)} %collective-permute-done.9.refs_1_, ...), custom_call_target="tpu_custom_call" | custom-call | flops 1073741824 | bytes 3145728 | tf_op jit(solution)/shard_map/pallas_call | solution.py:67
  91.6 1.4 %collective-permute-start.29 = (bf16[256,256]{1,0:T(8,128)(2,1)S(1)}, bf16[256,256]{1,0:T(8,128)(2,1)S(1)}, u32[]{:S(2)}, u32[]{:S(2)}) collective-permute-start(bf16[256,256]{1,0:T(8,128)(2,1)S(1)} %get-tuple-element.65.refs_8_), channel_id=1, source_target_pairs={{0,192},{64,0},{128,64},{192,128},{1,193},{65,1},{129,65},{193,129... | collective-permute-start | bytes 393224 | tf_op jit(solution)/shard_map/ppermute | solution.py:28
  95.8 2.6 %collective-permute-done.30.refs_6_ = bf16[256,256]{1,0:T(8,128)(2,1)S(1)} collective-permute-done((bf16[256,256]{1,0:T(8,128)(2,1)S(1)}, bf16[256,256]{1,0:T(8,128)(2,1)S(1)}, u32[]{:S(2)}, u32[]{:S(2)}) %collective-permute-start.30) | collective-permute-done | bytes 131104 | tf_op jit(solution)/shard_map/ppermute | solution.py:28
  101.6 9.2 %collective-permute-done.32 = bf16[512,256]{1,0:T(8,128)(2,1)S(1)} collective-permute-done((bf16[512,256]{1,0:T(8,128)(2,1)S(1)}, bf16[512,256]{1,0:T(8,128)(2,1)S(1)}, u32[]{:S(2)}, u32[]{:S(2)}) %collective-permute-start.32) | collective-permute-done | bytes 262176 | tf_op jit(solution)/shard_map/ppermute | solution.py:536
  (66 shorter events, 21.6 us)
Async XLA Ops:
  1.7 23.0 %collective-permute-start = (bf16[1024,256]{1,0:T(8,128)(2,1)S(1)}, bf16[1024,256]{1,0:T(8,128)(2,1)S(1)}, u32[]{:S(2)}, u32[]{:S(2)}) collective-permute-start(bf16[1024,256]{1,0:T(8,128)(2,1)S(1)} %get-tuple-element.38.refs_2_), channel_id=1, source_target_pairs={{0,1},{1,2},{2,3},{3,0},{4,5},{5,6},{6,7},{7,4},{8,9},{9,10},{10,1... | collective-permute-start | bytes 1572872 | tf_op jit(solution)/shard_map/ppermute | solution.py:28
  4.8 6.8 %collective-permute-start.9 = (bf16[272,256]{1,0:T(8,128)(2,1)S(1)}, bf16[272,256]{1,0:T(8,128)(2,1)S(1)}, u32[]{:S(2)}, u32[]{:S(2)}) collective-permute-start(bf16[272,256]{1,0:T(8,128)(2,1)S(1)} %get-tuple-element.51), channel_id=1, source_target_pairs={{0,64},{64,128},{128,192},{192,0},{1,65},{65,129},{129,193},{193,1... | collective-permute-start | bytes 417800 | tf_op jit(solution)/shard_map/ppermute | solution.py:28
  6.1 20.0 %collective-permute-start.1 = (bf16[1024,256]{1,0:T(8,128)(2,1)S(1)}, bf16[1024,256]{1,0:T(8,128)(2,1)S(1)}, u32[]{:S(2)}, u32[]{:S(2)}) collective-permute-start(bf16[1024,256]{1,0:T(8,128)(2,1)S(1)} %get-tuple-element.41), channel_id=1, source_target_pairs={{0,3},{1,0},{2,1},{3,2},{4,7},{5,4},{6,5},{7,6},{8,11},{9,8},{10,9... | collective-permute-start | bytes 1572872 | tf_op jit(solution)/shard_map/ppermute | solution.py:28
  7.5 21.6 %collective-permute-start.2 = (bf16[1024,256]{1,0:T(8,128)(2,1)S(1)}, bf16[1024,256]{1,0:T(8,128)(2,1)S(1)}, u32[]{:S(2)}, u32[]{:S(2)}) collective-permute-start(bf16[1024,256]{1,0:T(8,128)(2,1)S(1)} %get-tuple-element.42), channel_id=1, source_target_pairs={{0,2},{1,3},{2,0},{3,1},{4,6},{5,7},{6,4},{7,5},{8,10},{9,11},{10,... | collective-permute-start | bytes 1572872 | tf_op jit(solution)/shard_map/ppermute | solution.py:28
  9.1 5.4 %collective-permute-start.10 = (bf16[272,256]{1,0:T(8,128)(2,1)S(1)}, bf16[272,256]{1,0:T(8,128)(2,1)S(1)}, u32[]{:S(2)}, u32[]{:S(2)}) collective-permute-start(bf16[272,256]{1,0:T(8,128)(2,1)S(1)} %get-tuple-element.52), channel_id=1, source_target_pairs={{0,128},{64,192},{128,0},{192,64},{1,129},{65,193},{129,1},{193,65... | collective-permute-start | bytes 417800 | tf_op jit(solution)/shard_map/ppermute | solution.py:28
  11.6 5.3 %collective-permute-start.11 = (bf16[272,256]{1,0:T(8,128)(2,1)S(1)}, bf16[272,256]{1,0:T(8,128)(2,1)S(1)}, u32[]{:S(2)}, u32[]{:S(2)}) collective-permute-start(bf16[272,256]{1,0:T(8,128)(2,1)S(1)} %get-tuple-element.53), channel_id=1, source_target_pairs={{0,192},{64,0},{128,64},{192,128},{1,193},{65,1},{129,65},{193,129... | collective-permute-start | bytes 417800 | tf_op jit(solution)/shard_map/ppermute | solution.py:28
  19.5 4.4 %collective-permute-start.12 = (bf16[256,256]{1,0:T(8,128)(2,1)S(1)}, bf16[256,256]{1,0:T(8,128)(2,1)S(1)}, u32[]{:S(2)}, u32[]{:S(2)}) collective-permute-start(bf16[256,256]{1,0:T(8,128)(2,1)S(1)} %shard_map.85.refs_0_), channel_id=1, source_target_pairs={{0,4},{4,0},{8,12},{12,8},{16,20},{20,16},{24,28},{28,24},{1,5},{5... | collective-permute-start | bytes 393224 | tf_op jit(solution)/shard_map/ppermute | solution.py:388
  21.2 12.7 %collective-permute-start.6 = (bf16[256,256]{1,0:T(8,128)(2,1)S(1)}, bf16[256,256]{1,0:T(8,128)(2,1)S(1)}, u32[]{:S(2)}, u32[]{:S(2)}) collective-permute-start(bf16[256,256]{1,0:T(8,128)(2,1)S(1)} %get-tuple-element.47.refs_5_), channel_id=1, source_target_pairs={{0,1},{1,2},{2,3},{3,0},{4,5},{5,6},{6,7},{7,4},{8,9},{9,10},{10,1... | collective-permute-start | bytes 393224 | tf_op jit(solution)/shard_map/ppermute | solution.py:28
  23.9 10.0 %collective-permute-start.7 = (bf16[256,256]{1,0:T(8,128)(2,1)S(1)}, bf16[256,256]{1,0:T(8,128)(2,1)S(1)}, u32[]{:S(2)}, u32[]{:S(2)}) collective-permute-start(bf16[256,256]{1,0:T(8,128)(2,1)S(1)} %get-tuple-element.48), channel_id=1, source_target_pairs={{0,3},{1,0},{2,1},{3,2},{4,7},{5,4},{6,5},{7,6},{8,11},{9,8},{10,9... | collective-permute-start | bytes 393224 | tf_op jit(solution)/shard_map/ppermute | solution.py:28
  24.7 10.0 %collective-permute-start.8 = (bf16[256,256]{1,0:T(8,128)(2,1)S(1)}, bf16[256,256]{1,0:T(8,128)(2,1)S(1)}, u32[]{:S(2)}, u32[]{:S(2)}) collective-permute-start(bf16[256,256]{1,0:T(8,128)(2,1)S(1)} %get-tuple-element.49), channel_id=1, source_target_pairs={{0,2},{1,3},{2,0},{3,1},{4,6},{5,7},{6,4},{7,5},{8,10},{9,11},{10,... | collective-permute-start | bytes 393224 | tf_op jit(solution)/shard_map/ppermute | solution.py:28
  34.7 11.1 %collective-permute-start.13 = (bf16[384,256]{1,0:T(8,128)(2,1)S(1)}, bf16[384,256]{1,0:T(8,128)(2,1)S(1)}, u32[]{:S(2)}, u32[]{:S(2)}) collective-permute-start(bf16[384,256]{1,0:T(8,128)(2,1)S(1)} %get-tuple-element.55.refs_5_), channel_id=1, source_target_pairs={{0,64},{64,128},{128,192},{192,0},{1,65},{65,129},{129,193},{193,1... | collective-permute-start | bytes 589832 | tf_op jit(solution)/shard_map/ppermute | solution.py:28
  36.1 11.7 %collective-permute-start.14 = (bf16[384,256]{1,0:T(8,128)(2,1)S(1)}, bf16[384,256]{1,0:T(8,128)(2,1)S(1)}, u32[]{:S(2)}, u32[]{:S(2)}) collective-permute-start(bf16[384,256]{1,0:T(8,128)(2,1)S(1)} %get-tuple-element.56.refs_6_), channel_id=1, source_target_pairs={{0,192},{64,0},{128,64},{192,128},{1,193},{65,1},{129,65},{193,129... | collective-permute-start | bytes 589832 | tf_op jit(solution)/shard_map/ppermute | solution.py:28
  37.4 11.6 %collective-permute-start.15 = (bf16[512,256]{1,0:T(8,128)(2,1)S(1)}, bf16[512,256]{1,0:T(8,128)(2,1)S(1)}, u32[]{:S(2)}, u32[]{:S(2)}) collective-permute-start(bf16[512,256]{1,0:T(8,128)(2,1)S(1)} %get-tuple-element.54.refs_3_), channel_id=1, source_target_pairs={{0,4},{4,8},{8,12},{12,16},{16,20},{20,24},{24,28},{28,0},{1,5},{5... | collective-permute-start | bytes 786440 | tf_op jit(solution)/shard_map/ppermute | solution.py:28
  39.2 9.8 %collective-permute-start.16 = (bf16[512,256]{1,0:T(8,128)(2,1)S(1)}, bf16[512,256]{1,0:T(8,128)(2,1)S(1)}, u32[]{:S(2)}, u32[]{:S(2)}) collective-permute-start(bf16[512,256]{1,0:T(8,128)(2,1)S(1)} %get-tuple-element.57), channel_id=1, source_target_pairs={{0,28},{4,0},{8,4},{12,8},{16,12},{20,16},{24,20},{28,24},{1,29},{... | collective-permute-start | bytes 786440 | tf_op jit(solution)/shard_map/ppermute | solution.py:28
  43.1 9.9 %collective-permute-start.3 = (bf16[512,256]{1,0:T(8,128)(2,1)S(1)}, bf16[512,256]{1,0:T(8,128)(2,1)S(1)}, u32[]{:S(2)}, u32[]{:S(2)}) collective-permute-start(bf16[512,256]{1,0:T(8,128)(2,1)S(1)} %get-tuple-element.43), channel_id=1, source_target_pairs={{0,1},{1,2},{2,3},{3,0},{4,5},{5,6},{6,7},{7,4},{8,9},{9,10},{10,1... | collective-permute-start | bytes 786440 | tf_op jit(solution)/shard_map/ppermute | solution.py:28
  45.7 8.2 %collective-permute-start.4 = (bf16[512,256]{1,0:T(8,128)(2,1)S(1)}, bf16[512,256]{1,0:T(8,128)(2,1)S(1)}, u32[]{:S(2)}, u32[]{:S(2)}) collective-permute-start(bf16[512,256]{1,0:T(8,128)(2,1)S(1)} %get-tuple-element.44), channel_id=1, source_target_pairs={{0,3},{1,0},{2,1},{3,2},{4,7},{5,4},{6,5},{7,6},{8,11},{9,8},{10,9... | collective-permute-start | bytes 786440 | tf_op jit(solution)/shard_map/ppermute | solution.py:28
  47.7 11.8 %collective-permute-start.5 = (bf16[512,256]{1,0:T(8,128)(2,1)S(1)}, bf16[512,256]{1,0:T(8,128)(2,1)S(1)}, u32[]{:S(2)}, u32[]{:S(2)}) collective-permute-start(bf16[512,256]{1,0:T(8,128)(2,1)S(1)} %get-tuple-element.45), channel_id=1, source_target_pairs={{0,2},{1,3},{2,0},{3,1},{4,6},{5,7},{6,4},{7,5},{8,10},{9,11},{10,... | collective-permute-start | bytes 786440 | tf_op jit(solution)/shard_map/ppermute | solution.py:28
  59.6 16.9 %collective-permute-start.18 = (bf16[768,256]{1,0:T(8,128)(2,1)S(1)}, bf16[768,256]{1,0:T(8,128)(2,1)S(1)}, u32[]{:S(2)}, u32[]{:S(2)}) collective-permute-start(bf16[768,256]{1,0:T(8,128)(2,1)S(1)} %get-tuple-element.61.refs_5_), channel_id=1, source_target_pairs={{0,64},{64,0},{128,192},{192,128},{1,65},{65,1},{129,193},{193,129... | collective-permute-start | bytes 1179656 | tf_op jit(solution)/shard_map/ppermute | solution.py:182
  59.7 16.8 %collective-permute-start.19 = (bf16[512,256]{1,0:T(8,128)(2,1)S(1)}, bf16[512,256]{1,0:T(8,128)(2,1)S(1)}, u32[]{:S(2)}, u32[]{:S(2)}) collective-permute-start(bf16[512,256]{1,0:T(8,128)(2,1)S(1)} %get-tuple-element.58.refs_3_.refs_6_), channel_id=1, source_target_pairs={{0,4},{4,8},{8,12},{12,16},{16,20},{20,24},{24,28},{28,0},{1,5},{5... | collective-permute-start | bytes 786440 | tf_op jit(solution)/shard_map/ppermute | solution.py:28
  59.7 16.7 %collective-permute-start.20 = (bf16[512,256]{1,0:T(8,128)(2,1)S(1)}, bf16[512,256]{1,0:T(8,128)(2,1)S(1)}, u32[]{:S(2)}, u32[]{:S(2)}) collective-permute-start(bf16[512,256]{1,0:T(8,128)(2,1)S(1)} %get-tuple-element.62), channel_id=1, source_target_pairs={{0,28},{4,0},{8,4},{12,8},{16,12},{20,16},{24,20},{28,24},{1,29},{... | collective-permute-start | bytes 786440 | tf_op jit(solution)/shard_map/ppermute | solution.py:28
  63.1 6.7 %collective-permute-start.23 = (bf16[256,256]{1,0:T(8,128)(2,1)S(1)}, bf16[256,256]{1,0:T(8,128)(2,1)S(1)}, u32[]{:S(2)}, u32[]{:S(2)}) collective-permute-start(bf16[256,256]{1,0:T(8,128)(2,1)S(1)} %shard_map.86.refs_5_.refs_0_), channel_id=1, source_target_pairs={{0,8},{4,12},{8,0},{12,4},{16,24},{20,28},{24,16},{28,20},{1,9},{5... | collective-permute-start | bytes 393224 | tf_op jit(solution)/shard_map/ppermute | solution.py:388
  69.8 10.8 %collective-permute-start.24 = (bf16[256,256]{1,0:T(8,128)(2,1)S(1)}, bf16[256,256]{1,0:T(8,128)(2,1)S(1)}, u32[]{:S(2)}, u32[]{:S(2)}) collective-permute-start(bf16[256,256]{1,0:T(8,128)(2,1)S(1)} %shard_map.93.refs_0_), channel_id=1, source_target_pairs={{0,24},{4,28},{8,16},{12,20},{16,8},{20,12},{24,0},{28,4},{1,25},{... | collective-permute-start | bytes 393224 | tf_op jit(solution)/shard_map/ppermute | solution.py:388
  72.9 18.1 %collective-permute-start.17 = (bf16[768,256]{1,0:T(8,128)(2,1)S(1)}, bf16[768,256]{1,0:T(8,128)(2,1)S(1)}, u32[]{:S(2)}, u32[]{:S(2)}) collective-permute-start(bf16[768,256]{1,0:T(8,128)(2,1)S(1)} %get-tuple-element.59.refs_5_), channel_id=1, source_target_pairs={{0,192},{192,0},{64,128},{128,64},{1,193},{193,1},{65,129},{129,65... | collective-permute-start | bytes 1179656 | tf_op jit(solution)/shard_map/ppermute | solution.py:182
  77.2 13.8 %collective-permute-start.22 = (bf16[512,256]{1,0:T(8,128)(2,1)S(1)}, bf16[512,256]{1,0:T(8,128)(2,1)S(1)}, u32[]{:S(2)}, u32[]{:S(2)}) collective-permute-start(bf16[512,256]{1,0:T(8,128)(2,1)S(1)} %get-tuple-element.64.refs_10_), channel_id=1, source_target_pairs={{0,4},{4,8},{8,12},{12,16},{16,20},{20,24},{24,28},{28,0},{1,5},{5... | collective-permute-start | bytes 786440 | tf_op jit(solution)/shard_map/ppermute | solution.py:28
  80.6 6.1 %collective-permute-start.25 = (bf16[256,256]{1,0:T(8,128)(2,1)S(1)}, bf16[256,256]{1,0:T(8,128)(2,1)S(1)}, u32[]{:S(2)}, u32[]{:S(2)}) collective-permute-start(bf16[256,256]{1,0:T(8,128)(2,1)S(1)} %shard_map.94.refs_4_), channel_id=1, source_target_pairs={{0,1},{1,2},{2,3},{3,0},{4,5},{5,6},{6,7},{7,4},{8,9},{9,10},{10,1... | collective-permute-start | bytes 393224 | tf_op jit(solution)/shard_map/ppermute | solution.py:28
  80.7 6.5 %collective-permute-start.26 = (bf16[256,256]{1,0:T(8,128)(2,1)S(1)}, bf16[256,256]{1,0:T(8,128)(2,1)S(1)}, u32[]{:S(2)}, u32[]{:S(2)}) collective-permute-start(bf16[256,256]{1,0:T(8,128)(2,1)S(1)} %shard_map.94.refs_4_), channel_id=1, source_target_pairs={{0,3},{1,0},{2,1},{3,2},{4,7},{5,4},{6,5},{7,6},{8,11},{9,8},{10,9... | collective-permute-start | bytes 393224 | tf_op jit(solution)/shard_map/ppermute | solution.py:28
  84.2 5.4 %collective-permute-start.27 = (bf16[256,256]{1,0:T(8,128)(2,1)S(1)}, bf16[256,256]{1,0:T(8,128)(2,1)S(1)}, u32[]{:S(2)}, u32[]{:S(2)}) collective-permute-start(bf16[256,256]{1,0:T(8,128)(2,1)S(1)} %shard_map.94.refs_4_), channel_id=1, source_target_pairs={{0,2},{1,3},{2,0},{3,1},{4,6},{5,7},{6,4},{7,5},{8,10},{9,11},{10,... | collective-permute-start | bytes 393224 | tf_op jit(solution)/shard_map/ppermute | solution.py:28
  86.8 7.5 %collective-permute-start.21 = (bf16[512,256]{1,0:T(8,128)(2,1)S(1)}, bf16[512,256]{1,0:T(8,128)(2,1)S(1)}, u32[]{:S(2)}, u32[]{:S(2)}) collective-permute-start(bf16[512,256]{1,0:T(8,128)(2,1)S(1)} %get-tuple-element.63), channel_id=1, source_target_pairs={{0,28},{4,0},{8,4},{12,8},{16,12},{20,16},{24,20},{28,24},{1,29},{... | collective-permute-start | bytes 786440 | tf_op jit(solution)/shard_map/ppermute | solution.py:28
  91.5 8.2 %collective-permute-start.28 = (bf16[512,256]{1,0:T(8,128)(2,1)S(1)}, bf16[512,256]{1,0:T(8,128)(2,1)S(1)}, u32[]{:S(2)}, u32[]{:S(2)}) collective-permute-start(bf16[512,256]{1,0:T(8,128)(2,1)S(1)} %shard_map.96.refs_8_), channel_id=1, source_target_pairs={{0,4},{4,8},{8,12},{12,16},{16,20},{20,24},{24,28},{28,0},{1,5},{5... | collective-permute-start | bytes 786440 | tf_op jit(solution)/shard_map/ppermute | solution.py:28
  93.0 5.4 %collective-permute-start.30 = (bf16[256,256]{1,0:T(8,128)(2,1)S(1)}, bf16[256,256]{1,0:T(8,128)(2,1)S(1)}, u32[]{:S(2)}, u32[]{:S(2)}) collective-permute-start(bf16[256,256]{1,0:T(8,128)(2,1)S(1)} %get-tuple-element.67), channel_id=1, source_target_pairs={{0,128},{64,192},{128,0},{192,64},{1,129},{65,193},{129,1},{193,65... | collective-permute-start | bytes 393224 | tf_op jit(solution)/shard_map/ppermute | solution.py:28
  93.5 6.2 %collective-permute-start.31 = (bf16[256,256]{1,0:T(8,128)(2,1)S(1)}, bf16[256,256]{1,0:T(8,128)(2,1)S(1)}, u32[]{:S(2)}, u32[]{:S(2)}) collective-permute-start(bf16[256,256]{1,0:T(8,128)(2,1)S(1)} %get-tuple-element.68), channel_id=1, source_target_pairs={{0,64},{64,128},{128,192},{192,0},{1,65},{65,129},{129,193},{193,1... | collective-permute-start | bytes 393224 | tf_op jit(solution)/shard_map/ppermute | solution.py:28
  100.3 10.5 %collective-permute-start.32 = (bf16[512,256]{1,0:T(8,128)(2,1)S(1)}, bf16[512,256]{1,0:T(8,128)(2,1)S(1)}, u32[]{:S(2)}, u32[]{:S(2)}) collective-permute-start(bf16[512,256]{1,0:T(8,128)(2,1)S(1)} %get-tuple-element.69), channel_id=1, source_target_pairs={{0,32},{1,33},{2,34},{3,35},{4,36},{5,37},{6,38},{7,39},{8,40},{9,... | collective-permute-start | bytes 786440 | tf_op jit(solution)/shard_map/ppermute | solution.py:536
  (8 other events, 162.5 us)
